TPU v7x, 32 devices: a whole 2x2x4 slice. The times are simulated.
32 devices in a mesh: fsdp: 2 (over y), ctx: 4 (over z), tp: 4 (over x, core).
Axes of the slice: x: 2, y: 2, z: 4, core: 2. Of those that a mesh axis runs over, the one named last changes fastest.
Arguments:
- tokens: bfloat16 [4, 4, 1024, 1024], P(None, 'fsdp', 'ctx', 'tp'), may hold values from -6 to 6
- skip_tokens: bfloat16 [4, 4, 1024, 1024], P(None, 'fsdp', 'ctx', 'tp'), may hold values from -6 to 6
- merger_weight: bfloat16 [1024, 2, 1024], P(('fsdp', 'ctx'), None, 'tp'), may hold values from -0.125 to 0.125
- merger_bias: float32 [1024], P(('fsdp', 'ctx', 'tp')), may hold values from -3 to 3
- first_gain: float32 [1024], P(('fsdp', 'ctx', 'tp')), may hold values from 0.25 to 1.75
- first_shift: float32 [1024], P(('fsdp', 'ctx', 'tp')), may hold values from -2 to 2
- attend_weight: bfloat16 [1024, 3, 1024], P(('fsdp', 'ctx'), None, 'tp'), may hold values from -0.25 to 0.25
- output_weight: bfloat16 [1024, 1024], P(('fsdp', 'ctx'), 'tp'), may hold values from -0.75 to 0.75
- output_bias: float32 [1024], P(('fsdp', 'ctx', 'tp')), may hold values from -2 to 2
- second_gain: float32 [1024], P(('fsdp', 'ctx', 'tp')), may hold values from 0.25 to 1.75
- second_shift: float32 [1024], P(('fsdp', 'ctx', 'tp')), may hold values from -2 to 2
- expand_weight: bfloat16 [1024, 4096], P(('fsdp', 'ctx'), 'tp'), may hold values from -0.1875 to 0.1875
- widen_bias: float32 [4096], P(('fsdp', 'ctx', 'tp')), may hold values from -3 to 3
- shrink_weight: bfloat16 [1024, 4096], P(('fsdp', 'ctx'), 'tp'), may hold values from -0.125 to 0.125
- shrink_bias: float32 [1024], P(('fsdp', 'ctx', 'tp')), may hold values from -2 to 2
- live_slots: int32 [4, 4], P(None, 'fsdp'), may hold values from 0 to 1, as said below
- cotangent: bfloat16 [4, 4, 1024, 1024], P(None, 'fsdp', ('ctx', 'tp')), may hold values from -6 to 6
Outputs:
- layer_out: bfloat16 [4, 4, 1024, 1024], P(None, 'fsdp', ('ctx', 'tp'))
- grad_tokens: float32 [4, 4, 1024, 1024], P(None, 'fsdp', 'ctx', 'tp')
- grad_skip: float32 [4, 4, 1024, 1024], P(None, 'fsdp', 'ctx', 'tp')
- weight_merger: float32 [1024, 2, 1024], P(('fsdp', 'ctx'), None, 'tp')
- bias_merger: float32 [1024], P(('fsdp', 'ctx', 'tp'))
- gain_first: float32 [1024], P(('fsdp', 'ctx', 'tp'))
- shift_first: float32 [1024], P(('fsdp', 'ctx', 'tp'))
- weight_attend: float32 [1024, 3, 1024], P(('fsdp', 'ctx'), None, 'tp')
- weight_output: float32 [1024, 1024], P(('fsdp', 'ctx'), 'tp')
- bias_output: float32 [1024], P(('fsdp', 'ctx', 'tp'))
- gain_second: float32 [1024], P(('fsdp', 'ctx', 'tp'))
- shift_second: float32 [1024], P(('fsdp', 'ctx', 'tp'))
- weight_expand: float32 [1024, 4096], P(('fsdp', 'ctx'), 'tp')
- bias_expand: float32 [4096], P(('fsdp', 'ctx', 'tp'))
- weight_shrink: float32 [1024, 4096], P(('fsdp', 'ctx'), 'tp')
- bias_shrink: float32 [1024], P(('fsdp', 'ctx', 'tp'))
Inputs may be any that keep to these rules, and one draw needn't show every extreme that they name: `live_slots`: in every micro-batch but the last exactly one of the 4 slots is empty (0), in the last exactly two; the empty slots lie anywhere.
All inputs are finite; a program needn't handle non-finite values.
Results may differ from a plain program's by a relative error of at most 0.017.
Values may be sent and summed in bfloat16 or wider, within the bound.
No kernel may reach another device: no remote copies, remote signals or barrier semaphores. Data moves between devices by JAX's collectives and lax.ppermute only.
A program may use at most 256 MiB of HBM per device.

v0:
```python
import jax
import jax.numpy as jnp
from jax import lax
from jax.sharding import PartitionSpec as P

HD = 64


EPSILON = 1e-05


def layer_norm(matrix, scales, shifts):
    center = matrix - jnp.mean(matrix, axis=-1, keepdims=True)
    spread = jnp.mean(center * center, axis=-1, keepdims=True)
    return center * lax.rsqrt(spread + EPSILON) * scales + shifts


def gelu_exact(matrix):
    return jax.nn.gelu(matrix, approximate=False)


def fetch(merger_part, attend_part, output_part, expand_part, shrink_part):
    return (
        lax.all_gather(merger_part, ("fsdp", "ctx"), axis=0, tiled=True),
        lax.all_gather(attend_part, ("fsdp", "ctx"), axis=0, tiled=True),
        lax.all_gather(output_part, ("fsdp", "ctx"), axis=0, tiled=True),
        lax.all_gather(expand_part, ("fsdp", "ctx"), axis=0, tiled=True),
        lax.all_gather(shrink_part, ("fsdp", "ctx"), axis=0, tiled=True),
    )


def spread_rows(block):
    return lax.all_gather(block, "tp", axis=1, tiled=True)


def fold_rows(block):
    return lax.psum_scatter(block, "tp", scatter_dimension=1, tiled=True)


def reduce_weights(parts):
    return (
        lax.psum_scatter(parts[0], ("fsdp", "ctx"), scatter_dimension=0, tiled=True),
        lax.psum_scatter(parts[1], ("fsdp", "ctx"), scatter_dimension=0, tiled=True),
        lax.psum_scatter(parts[2], ("fsdp", "ctx"), scatter_dimension=0, tiled=True),
        lax.psum_scatter(parts[3], ("fsdp", "ctx"), scatter_dimension=0, tiled=True),
        lax.psum_scatter(parts[4], ("fsdp", "ctx"), scatter_dimension=0, tiled=True),
    )


def micro_step(weights, vectors, tokens_now, skips_now, live_now, cot_now, tensor_rank):
    merger_full, attend_full, output_full, expand_full, shrink_full = weights
    (
        merger_bias,
        first_gain,
        first_shift,
        output_bias,
        second_gain,
        second_shift,
        shrink_bias,
        widen_bias,
    ) = vectors
    groups = tokens_now.shape[0]
    local_len = tokens_now.shape[1]
    heads_dev = attend_full.shape[2] // HD
    hidden = expand_full.shape[1]
    scaling = HD ** (-0.5)
    stacked = jnp.stack([tokens_now, skips_now], axis=2)
    joined = (
        fold_rows(
            jnp.einsum("stci,oci->sto", stacked, merger_full, preferred_element_type=jnp.float32)
        )
        + merger_bias
    )
    normed, first_pull = jax.vjp(layer_norm, joined, first_gain, first_shift)
    normed_all = spread_rows(normed.astype(jnp.bfloat16))
    project = jnp.einsum(
        "std,dcj->stcj", normed_all, attend_full, preferred_element_type=jnp.float32
    ).astype(jnp.bfloat16)
    key_rows, value_rows = (
        lax.all_gather(project[:, :, 1], "ctx", axis=1, tiled=True),
        lax.all_gather(project[:, :, 2], "ctx", axis=1, tiled=True),
    )
    seq_len = key_rows.shape[1]
    query_heads = project[:, :, 0].reshape(groups, local_len, heads_dev, HD)
    key_heads = key_rows.reshape(groups, seq_len, heads_dev, HD)
    value_heads = value_rows.reshape(groups, seq_len, heads_dev, HD)
    scores = (
        jnp.einsum("sqhd,skhd->shqk", query_heads, key_heads, preferred_element_type=jnp.float32)
        * scaling
    )
    row_peak = jnp.max(scores, axis=-1, keepdims=True)
    logsum = row_peak + jnp.log(jnp.sum(jnp.exp(scores - row_peak), axis=-1, keepdims=True))
    probs_low = jnp.exp(scores - logsum).astype(jnp.bfloat16)
    attended = jnp.einsum(
        "shqk,skhd->sqhd", probs_low, value_heads, preferred_element_type=jnp.float32
    )
    attended = attended.astype(jnp.bfloat16).reshape(groups, local_len, heads_dev * HD)
    second = (
        joined
        + fold_rows(
            jnp.einsum("sti,oi->sto", attended, output_full, preferred_element_type=jnp.float32)
        )
        + output_bias
    )
    normed_two, second_pull = jax.vjp(layer_norm, second, second_gain, second_shift)
    normed_two_all = spread_rows(normed_two.astype(jnp.bfloat16))
    bias_slice = lax.dynamic_slice_in_dim(widen_bias, tensor_rank * hidden, hidden)
    widened_hidden = (
        jnp.einsum("std,df->stf", normed_two_all, expand_full, preferred_element_type=jnp.float32)
        + bias_slice
    )
    activated, gelu_pull = jax.vjp(gelu_exact, widened_hidden)
    activated_low = activated.astype(jnp.bfloat16)
    result = (
        second
        + fold_rows(
            jnp.einsum(
                "stf,of->sto", activated_low, shrink_full, preferred_element_type=jnp.float32
            )
        )
        + shrink_bias
    )
    live_mask = live_now.astype(jnp.float32)[:, None, None]
    layer_out = (result * live_mask).astype(jnp.bfloat16)
    upstream = cot_now.astype(jnp.float32) * live_mask
    grad_shrink_bias = jnp.sum(upstream, axis=(0, 1))
    branch_low = spread_rows(upstream.astype(jnp.bfloat16))
    grad_shrink = jnp.einsum(
        "sto,stf->of", branch_low, activated_low, preferred_element_type=jnp.float32
    )
    grad_activated = jnp.einsum(
        "sto,of->stf", branch_low, shrink_full, preferred_element_type=jnp.float32
    )
    grad_expanded = gelu_pull(grad_activated)[0].astype(jnp.bfloat16)
    grad_expand_bias = jnp.sum(grad_expanded, axis=(0, 1), dtype=jnp.float32)
    grad_expand = jnp.einsum(
        "std,stf->df", normed_two_all, grad_expanded, preferred_element_type=jnp.float32
    )
    grad_normed_two = fold_rows(
        jnp.einsum("stf,df->std", grad_expanded, expand_full, preferred_element_type=jnp.float32)
    )
    grad_second_norm, grad_second_gain, grad_second_shift = second_pull(grad_normed_two)
    grad_second = upstream + grad_second_norm
    grad_output_bias = jnp.sum(grad_second, axis=(0, 1))
    attn_low = spread_rows(grad_second.astype(jnp.bfloat16))
    grad_output = jnp.einsum("sto,sti->oi", attn_low, attended, preferred_element_type=jnp.float32)
    grad_attended = jnp.einsum(
        "sto,oi->sti", attn_low, output_full, preferred_element_type=jnp.float32
    )
    grad_attended = grad_attended.astype(jnp.bfloat16).reshape(groups, local_len, heads_dev, HD)
    scores_again = (
        jnp.einsum("sqhd,skhd->shqk", query_heads, key_heads, preferred_element_type=jnp.float32)
        * scaling
    )
    probs = jnp.exp(scores_again - logsum)
    grad_probs = jnp.einsum(
        "sqhd,skhd->shqk", grad_attended, value_heads, preferred_element_type=jnp.float32
    )
    row_inner = jnp.sum(probs * grad_probs, axis=-1, keepdims=True)
    grad_scores = (probs * (grad_probs - row_inner)).astype(jnp.bfloat16)
    grad_queries = (
        jnp.einsum("shqk,skhd->sqhd", grad_scores, key_heads, preferred_element_type=jnp.float32)
        * scaling
    )
    probs_again = probs.astype(jnp.bfloat16)
    key_terms = (
        jnp.einsum("shqk,sqhd->skhd", grad_scores, query_heads, preferred_element_type=jnp.float32)
        * scaling
    )
    value_terms = jnp.einsum(
        "shqk,sqhd->skhd", probs_again, grad_attended, preferred_element_type=jnp.float32
    )
    grad_keys, grad_values = (
        lax.psum_scatter(
            key_terms.reshape(groups, seq_len, heads_dev * HD).astype(jnp.bfloat16),
            "ctx",
            scatter_dimension=1,
            tiled=True,
        ).astype(jnp.float32),
        lax.psum_scatter(
            value_terms.reshape(groups, seq_len, heads_dev * HD).astype(jnp.bfloat16),
            "ctx",
            scatter_dimension=1,
            tiled=True,
        ).astype(jnp.float32),
    )
    grad_project = jnp.stack(
        [
            grad_queries.reshape(groups, local_len, heads_dev * HD).astype(jnp.bfloat16),
            grad_keys.astype(jnp.bfloat16),
            grad_values.astype(jnp.bfloat16),
        ],
        axis=2,
    )
    grad_attend = jnp.einsum(
        "std,stcj->dcj", normed_all, grad_project, preferred_element_type=jnp.float32
    )
    grad_normed = fold_rows(
        jnp.einsum("stcj,dcj->std", grad_project, attend_full, preferred_element_type=jnp.float32)
    )
    grad_first_norm, gradient_leading_gain, grad_first_shift = first_pull(grad_normed)
    grad_joined = grad_second + grad_first_norm
    grad_merger_bias = jnp.sum(grad_joined, axis=(0, 1))
    joined_low = spread_rows(grad_joined.astype(jnp.bfloat16))
    grad_merger = jnp.einsum(
        "sto,stci->oci", joined_low, stacked, preferred_element_type=jnp.float32
    )
    grad_stacked = jnp.einsum(
        "sto,oci->stci", joined_low, merger_full, preferred_element_type=jnp.float32
    )
    expand_whole = lax.dynamic_update_slice_in_dim(
        jnp.zeros((widen_bias.shape[0],), jnp.float32), grad_expand_bias, tensor_rank * hidden, 0
    )
    weight_part = (grad_merger, grad_attend, grad_output, grad_expand, grad_shrink)
    vector_portion = (
        grad_merger_bias,
        gradient_leading_gain,
        grad_first_shift,
        grad_output_bias,
        grad_second_gain,
        grad_second_shift,
        grad_shrink_bias,
        expand_whole,
    )
    return (layer_out, grad_stacked[:, :, 0], grad_stacked[:, :, 1], weight_part, vector_portion)


def on_device(
    tokens,
    skip_tokens,
    merger_weight,
    merger_bias,
    first_gain,
    first_shift,
    attend_weight,
    output_weight,
    output_bias,
    second_gain,
    second_shift,
    expand_weight,
    widen_bias,
    shrink_weight,
    shrink_bias,
    live_slots,
    cotangent,
):
    tensor_rank = lax.axis_index("tp")
    vectors = (
        lax.all_gather(merger_bias, ("fsdp", "ctx", "tp"), axis=0, tiled=True),
        lax.all_gather(first_gain, ("fsdp", "ctx", "tp"), axis=0, tiled=True),
        lax.all_gather(first_shift, ("fsdp", "ctx", "tp"), axis=0, tiled=True),
        lax.all_gather(output_bias, ("fsdp", "ctx", "tp"), axis=0, tiled=True),
        lax.all_gather(second_gain, ("fsdp", "ctx", "tp"), axis=0, tiled=True),
        lax.all_gather(second_shift, ("fsdp", "ctx", "tp"), axis=0, tiled=True),
        lax.all_gather(shrink_bias, ("fsdp", "ctx", "tp"), axis=0, tiled=True),
        lax.all_gather(widen_bias, ("fsdp", "ctx", "tp"), axis=0, tiled=True),
    )
    batches = tokens.shape[0]
    outs_list = []
    token_list = []
    skip_list = []
    weight_totals = None
    vector_totals = None
    for batch_index in range(batches):
        current = fetch(merger_weight, attend_weight, output_weight, expand_weight, shrink_weight)
        layer_out, grad_one, gradient_remaining, weight_part, vector_portion = micro_step(
            current,
            vectors,
            tokens[batch_index],
            skip_tokens[batch_index],
            live_slots[batch_index],
            cotangent[batch_index],
            tensor_rank,
        )
        if weight_totals is None:
            weight_totals = weight_part
            vector_totals = vector_portion
        else:
            weight_totals = tuple(
                (former + latter for former, latter in zip(weight_totals, weight_part))
            )
            vector_totals = tuple(
                (former + latter for former, latter in zip(vector_totals, vector_portion))
            )
        outs_list.append(layer_out)
        token_list.append(grad_one)
        skip_list.append(gradient_remaining)
    weight_totals = reduce_weights(weight_totals)
    vector_grads = (
        lax.psum_scatter(vector_totals[0], ("fsdp", "ctx", "tp"), scatter_dimension=0, tiled=True),
        lax.psum_scatter(vector_totals[1], ("fsdp", "ctx", "tp"), scatter_dimension=0, tiled=True),
        lax.psum_scatter(vector_totals[2], ("fsdp", "ctx", "tp"), scatter_dimension=0, tiled=True),
        lax.psum_scatter(vector_totals[3], ("fsdp", "ctx", "tp"), scatter_dimension=0, tiled=True),
        lax.psum_scatter(vector_totals[4], ("fsdp", "ctx", "tp"), scatter_dimension=0, tiled=True),
        lax.psum_scatter(vector_totals[5], ("fsdp", "ctx", "tp"), scatter_dimension=0, tiled=True),
        lax.psum_scatter(vector_totals[6], ("fsdp", "ctx", "tp"), scatter_dimension=0, tiled=True),
        lax.psum_scatter(vector_totals[7], ("fsdp", "ctx", "tp"), scatter_dimension=0, tiled=True),
    )
    return (
        jnp.stack(outs_list, axis=0),
        jnp.stack(token_list, axis=0),
        jnp.stack(skip_list, axis=0),
        weight_totals[0],
        vector_grads[0],
        vector_grads[1],
        vector_grads[2],
        weight_totals[1],
        weight_totals[2],
        vector_grads[3],
        vector_grads[4],
        vector_grads[5],
        weight_totals[3],
        vector_grads[7],
        weight_totals[4],
        vector_grads[6],
    )


def solution(mesh):
    placed = (
        P(None, "fsdp", "ctx", "tp"),
        P(None, "fsdp", "ctx", "tp"),
        P(("fsdp", "ctx"), None, "tp"),
        P(("fsdp", "ctx", "tp")),
        P(("fsdp", "ctx", "tp")),
        P(("fsdp", "ctx", "tp")),
        P(("fsdp", "ctx"), None, "tp"),
        P(("fsdp", "ctx"), "tp"),
        P(("fsdp", "ctx", "tp")),
        P(("fsdp", "ctx", "tp")),
        P(("fsdp", "ctx", "tp")),
        P(("fsdp", "ctx"), "tp"),
        P(("fsdp", "ctx", "tp")),
        P(("fsdp", "ctx"), "tp"),
        P(("fsdp", "ctx", "tp")),
        P(None, "fsdp"),
        P(None, "fsdp", ("ctx", "tp"), None),
    )
    return jax.shard_map(
        on_device,
        mesh=mesh,
        in_specs=placed,
        out_specs=(
            P(None, "fsdp", ("ctx", "tp"), None),
            P(None, "fsdp", "ctx", "tp"),
            P(None, "fsdp", "ctx", "tp"),
            P(("fsdp", "ctx"), None, "tp"),
            P(("fsdp", "ctx", "tp")),
            P(("fsdp", "ctx", "tp")),
            P(("fsdp", "ctx", "tp")),
            P(("fsdp", "ctx"), None, "tp"),
            P(("fsdp", "ctx"), "tp"),
            P(("fsdp", "ctx", "tp")),
            P(("fsdp", "ctx", "tp")),
            P(("fsdp", "ctx", "tp")),
            P(("fsdp", "ctx"), "tp"),
            P(("fsdp", "ctx", "tp")),
            P(("fsdp", "ctx"), "tp"),
            P(("fsdp", "ctx", "tp")),
        ),
        check_vma=False,
    )
```

profile of v0, /device:TPU:0, one launch (start us, length us, event | category | flops | bytes accessed | tf_op | source)
XLA Modules:
  0.0 2148.1 jit_solution(7706245499468301437)
XLA Ops:
  10.6 43.0 %all-gather.42.cloned.1.call-done = bf16[1024,2,256]{2,0,1:T(8,128)(2,1)} async-done(((bf16[128,2,256]{2,0,1:T(8,128)(2,1)}), bf16[1024,2,256]{2,0,1:T(8,128)(2,1)}) %all-gather.42.cloned.1.call-update) | async-done | bytes 1048592 | tf_op jit(solution)/shard_map/all_gather | solution.py:24
  66.0 38.9 %all-reduce.16 = (f32[1024]{0:T(1024)S(1)}, f32[1024]{0:T(1024)S(1)}, f32[1024]{0:T(1024)S(1)}, f32[1024]{0:T(1024)S(1)}, f32[1024]{0:T(1024)S(1)}, /*index=5*/f32[1024]{0:T(1024)S(1)}) all-reduce(f32[1024]{0:T(1024)S(1)} %dynamic-update-slice.3, ...), channel_id=1, replica_groups=mesh['fsdp'=2,'ctx'=4,'tp'=4] {'fsdp','ctx','tp'}, use_global_device_ids=true, to_apply=%add | all-reduce | flops 6144 | bytes 49152
  106.2 16.1 reduce-scatter.40.cloned.1.call-done
  122.3 33.8 %reduce-scatter.46.cloned.1.call-done = f32[2,64,1024]{2,1,0:T(8,128)} async-done(((f32[2,256,1024]{2,1,0:T(8,128)}), f32[2,64,1024]{2,1,0:T(8,128)}) %reduce-scatter.46.cloned.1.call-update) | async-done | bytes 524304 | tf_op jit(solution)/shard_map/reduce_scatter | solution.py:37
  156.1 34.0 %reduce-scatter.52.cloned.1.call-done = f32[2,64,1024]{2,1,0:T(8,128)} async-done(((f32[2,256,1024]{2,1,0:T(8,128)}), f32[2,64,1024]{2,1,0:T(8,128)}) %reduce-scatter.52.cloned.1.call-update) | async-done | bytes 524304 | tf_op jit(solution)/shard_map/reduce_scatter | solution.py:37
  196.6 41.2 %all-gather.46.cloned.1.call-done = bf16[1024,3,256]{0,2,1:T(8,128)(2,1)} async-done(((bf16[128,3,256]{0,2,1:T(8,128)(2,1)}), bf16[1024,3,256]{0,2,1:T(8,128)(2,1)}) %all-gather.46.cloned.1.call-update) | async-done | bytes 1572880 | tf_op jit(solution)/shard_map/all_gather | solution.py:25
  237.9 17.1 all-gather.54.cloned.1.call-done
  259.2 14.7 all-gather.58.cloned.1.call-done
  278.1 14.7 all-gather.62.cloned.1.call-done
  297.0 14.5 all-gather.44.cloned.1.call-done
  315.2 34.9 %all_gather.146 = bf16[1024,256]{1,0:T(8,128)(2,1)S(1)} all-gather(bf16[128,256]{1,0:T(8,128)(2,1)S(1)} %copy-done.113), channel_id=1, replica_groups=mesh['fsdp'=2,'ctx'=4,'tp'=4] {'fsdp','ctx'}, dimensions={0}, use_global_device_ids=true | all-gather | bytes 589824 | tf_op jit(solution)/shard_map/all_gather | solution.py:26
  356.6 24.6 %all-gather.94.cloned.1.call-done = bf16[2,1024,1,256]{1,3,2,0:T(8,128)(2,1)} async-done(((bf16[2,256,1,256]{1,3,2,0:T(8,128)(2,1)}), bf16[2,1024,1,256]{1,3,2,0:T(8,128)(2,1)}) %all-gather.94.cloned.1.call-update) | async-done | bytes 1048592 | tf_op jit(solution)/shard_map/all_gather | solution.py:81
  388.5 23.4 %all-gather.100.cloned.1.call-done = bf16[2,1024,1,256]{1,3,2,0:T(8,128)(2,1)} async-done(((bf16[2,256,1,256]{1,3,2,0:T(8,128)(2,1)}), bf16[2,1024,1,256]{1,3,2,0:T(8,128)(2,1)}) %all-gather.100.cloned.1.call-update) | async-done | bytes 1048592 | tf_op jit(solution)/shard_map/all_gather | solution.py:80
  417.8 24.6 %all-gather.98.cloned.1.call-done = bf16[2,1024,1,256]{1,3,2,0:T(8,128)(2,1)} async-done(((bf16[2,256,1,256]{1,3,2,0:T(8,128)(2,1)}), bf16[2,1024,1,256]{1,3,2,0:T(8,128)(2,1)}) %all-gather.98.cloned.1.call-update) | async-done | bytes 1048592 | tf_op jit(solution)/shard_map/all_gather | solution.py:81
  449.9 23.1 %all-gather.104.cloned.1.call-done = bf16[2,1024,1,256]{1,3,2,0:T(8,128)(2,1)} async-done(((bf16[2,256,1,256]{1,3,2,0:T(8,128)(2,1)}), bf16[2,1024,1,256]{1,3,2,0:T(8,128)(2,1)}) %all-gather.104.cloned.1.call-update) | async-done | bytes 1048592 | tf_op jit(solution)/shard_map/all_gather | solution.py:80
  478.8 24.1 %all-gather.102.cloned.1.call-done = bf16[2,1024,1,256]{1,3,2,0:T(8,128)(2,1)} async-done(((bf16[2,256,1,256]{1,3,2,0:T(8,128)(2,1)}), bf16[2,1024,1,256]{1,3,2,0:T(8,128)(2,1)}) %all-gather.102.cloned.1.call-update) | async-done | bytes 1048592 | tf_op jit(solution)/shard_map/all_gather | solution.py:81
  510.2 23.3 %all-gather.92.cloned.1.call-done = bf16[2,1024,1,256]{1,3,2,0:T(8,128)(2,1)} async-done(((bf16[2,256,1,256]{1,3,2,0:T(8,128)(2,1)}), bf16[2,1024,1,256]{1,3,2,0:T(8,128)(2,1)}) %all-gather.92.cloned.1.call-update) | async-done | bytes 1048592 | tf_op jit(solution)/shard_map/all_gather | solution.py:80
  539.4 24.0 %all-gather.90.cloned.1.call-done = bf16[2,1024,1,256]{1,3,2,0:T(8,128)(2,1)} async-done(((bf16[2,256,1,256]{1,3,2,0:T(8,128)(2,1)}), bf16[2,1024,1,256]{1,3,2,0:T(8,128)(2,1)}) %all-gather.90.cloned.1.call-update) | async-done | bytes 1048592 | tf_op jit(solution)/shard_map/all_gather | solution.py:81
  571.4 24.9 %reduce-scatter.42.cloned.1.call-done = f32[2,64,1024]{2,1,0:T(8,128)} async-done(((f32[2,256,1024]{2,1,0:T(8,128)}), f32[2,64,1024]{2,1,0:T(8,128)}) %reduce-scatter.42.cloned.1.call-update) | async-done | bytes 524304 | tf_op jit(solution)/shard_map/reduce_scatter | solution.py:37
  596.2 34.6 %reduce-scatter.48.cloned.1.call-done = f32[2,64,1024]{2,1,0:T(8,128)} async-done(((f32[2,256,1024]{2,1,0:T(8,128)}), f32[2,64,1024]{2,1,0:T(8,128)}) %reduce-scatter.48.cloned.1.call-update) | async-done | bytes 524304 | tf_op jit(solution)/shard_map/reduce_scatter | solution.py:37
  630.8 34.0 %reduce-scatter.54.cloned.1.call-done = f32[2,64,1024]{2,1,0:T(8,128)} async-done(((f32[2,256,1024]{2,1,0:T(8,128)}), f32[2,64,1024]{2,1,0:T(8,128)}) %reduce-scatter.54.cloned.1.call-update) | async-done | bytes 524304 | tf_op jit(solution)/shard_map/reduce_scatter | solution.py:37
  664.8 34.2 %reduce-scatter.36.cloned.1.call-done = f32[2,64,1024]{2,1,0:T(8,128)} async-done(((f32[2,256,1024]{2,1,0:T(8,128)}), f32[2,64,1024]{2,1,0:T(8,128)}) %reduce-scatter.36.cloned.1.call-update) | async-done | bytes 524304 | tf_op jit(solution)/shard_map/reduce_scatter | solution.py:37
  711.8 40.9 %all-gather.8 = f32[32,1,128]{2,1,0:T(1,128)S(1)} all-gather(f32[1,1,128]{2,1,0:T(1,128)S(1)} %bitcast.612), channel_id=1, replica_groups=mesh['fsdp'=2,'ctx'=4,'tp'=4] {'fsdp','ctx','tp'}, dimensions={0}, use_global_device_ids=true | all-gather | bytes 16896 | tf_op jit(solution)/shard_map/all_gather | solution.py:256
  752.7 15.0 all-gather.60.cloned.1.call-done
  772.2 14.4 all-gather.64.cloned.1.call-done
  791.1 14.3 all-gather.56.cloned.1.call-done
  809.9 14.2 all-gather.48.cloned.1.call-done
  824.1 8.2 fusion.169
  833.6 21.7 %multiply_convert_fusion.9 = (bf16[2,256,1024]{2,1,0:T(8,128)(2,1)}, f32[2,256,1024]{2,1,0:T(8,128)}, bf16[2,256,1024]{2,1,0:T(8,128)(2,1)}, f32[2,256,1024]{2,1...) fusion(f32[2,256,1024]{2,1,0:T(8,128)S(1)} %copy-done.65, ...), kind=kLoop, calls=%fused_computation.120 | loop fusion | flops 147324928 | bytes 23072768 | tf_op jit(solution)/shard_map/convert_element_type | solution.py:113
  855.3 38.6 %all-gather.52.cloned.1.call-done = bf16[1024,1024]{1,0:T(8,128)(2,1)} async-done(((bf16[128,1024]{1,0:T(8,128)(2,1)}), bf16[1024,1024]{1,0:T(8,128)(2,1)}) %all-gather.52.cloned.1.call-update) | async-done | bytes 2097168 | tf_op jit(solution)/shard_map/all_gather | solution.py:28
  893.9 5.8 convert_reduce_fusion
  903.4 7.2 all-gather.78.cloned.1.call-done
  910.6 5.8 convert_reduce_fusion.1
  920.0 8.9 all-gather.72.cloned.1.call-done
  928.9 5.8 convert_reduce_fusion.2
  938.5 8.7 all-gather.66.cloned.1.call-done
  947.2 5.8 convert_reduce_fusion.3
  956.7 24.9 %reduce-scatter.82.cloned.1.call-done = f32[2,64,1024]{2,1,0:T(8,128)} async-done(((f32[2,256,1024]{2,1,0:T(8,128)}), f32[2,64,1024]{2,1,0:T(8,128)}) %reduce-scatter.82.cloned.1.call-update) | async-done | bytes 524304 | tf_op jit(solution)/shard_map/reduce_scatter | solution.py:37
  983.5 32.9 %reduce-scatter.74.cloned.1.call-done = f32[2,64,1024]{2,1,0:T(8,128)} async-done(((f32[2,256,1024]{2,1,0:T(8,128)}), f32[2,64,1024]{2,1,0:T(8,128)}) %reduce-scatter.74.cloned.1.call-update) | async-done | bytes 524304 | tf_op jit(solution)/shard_map/reduce_scatter | solution.py:37
  1016.4 34.0 %reduce-scatter.66.cloned.1.call-done = f32[2,64,1024]{2,1,0:T(8,128)} async-done(((f32[2,256,1024]{2,1,0:T(8,128)}), f32[2,64,1024]{2,1,0:T(8,128)}) %reduce-scatter.66.cloned.1.call-update) | async-done | bytes 524304 | tf_op jit(solution)/shard_map/reduce_scatter | solution.py:37
  1050.4 34.0 %reduce-scatter.58.cloned.1.call-done = f32[2,64,1024]{2,1,0:T(8,128)} async-done(((f32[2,256,1024]{2,1,0:T(8,128)}), f32[2,64,1024]{2,1,0:T(8,128)}) %reduce-scatter.58.cloned.1.call-update) | async-done | bytes 524304 | tf_op jit(solution)/shard_map/reduce_scatter | solution.py:37
  1094.6 12.5 all-gather.86.cloned.1.call-done
  1196.5 24.8 %reduce-scatter.84.cloned.1.call-done = bf16[2,256,256]{2,1,0:T(8,128)(2,1)} async-done(((bf16[2,1024,256]{2,1,0:T(8,128)(2,1)}), bf16[2,256,256]{2,1,0:T(8,128)(2,1)}) %reduce-scatter.84.cloned.1.call-update) | async-done | bytes 262160 | tf_op jit(solution)/shard_map/reduce_scatter | solution.py:174
  1230.3 19.0 reduce-scatter.70.cloned.1.call-done
  1249.3 28.2 %reduce-scatter.68.cloned.1.call-done = bf16[2,256,256]{2,1,0:T(8,128)(2,1)} async-done(((bf16[2,1024,256]{2,1,0:T(8,128)(2,1)}), bf16[2,256,256]{2,1,0:T(8,128)(2,1)}) %reduce-scatter.68.cloned.1.call-update) | async-done | bytes 262160 | tf_op jit(solution)/shard_map/reduce_scatter | solution.py:174
  1286.5 19.0 reduce-scatter.62.cloned.1.call-done
  1305.5 28.0 %reduce-scatter.60.cloned.1.call-done = bf16[2,256,256]{2,1,0:T(8,128)(2,1)} async-done(((bf16[2,1024,256]{2,1,0:T(8,128)(2,1)}), bf16[2,256,256]{2,1,0:T(8,128)(2,1)}) %reduce-scatter.60.cloned.1.call-update) | async-done | bytes 262160 | tf_op jit(solution)/shard_map/reduce_scatter | solution.py:174
  1342.6 18.9 reduce-scatter.78.cloned.1.call-done
  1361.5 28.1 %reduce-scatter.76.cloned.1.call-done = bf16[2,256,256]{2,1,0:T(8,128)(2,1)} async-done(((bf16[2,1024,256]{2,1,0:T(8,128)(2,1)}), bf16[2,256,256]{2,1,0:T(8,128)(2,1)}) %reduce-scatter.76.cloned.1.call-update) | async-done | bytes 262160 | tf_op jit(solution)/shard_map/reduce_scatter | solution.py:174
  1393.7 28.9 %reduce-scatter.88.cloned.1.call-done = f32[2,64,1024]{2,1,0:T(8,128)} async-done(((f32[2,256,1024]{2,1,0:T(8,128)}), f32[2,64,1024]{2,1,0:T(8,128)}) %reduce-scatter.88.cloned.1.call-update) | async-done | bytes 524304 | tf_op jit(solution)/shard_map/reduce_scatter | solution.py:37
  1422.6 34.7 %reduce-scatter.72.cloned.1.call-done = f32[2,64,1024]{2,1,0:T(8,128)} async-done(((f32[2,256,1024]{2,1,0:T(8,128)}), f32[2,64,1024]{2,1,0:T(8,128)}) %reduce-scatter.72.cloned.1.call-update) | async-done | bytes 524304 | tf_op jit(solution)/shard_map/reduce_scatter | solution.py:37
  1457.4 33.8 %reduce-scatter.64.cloned.1.call-done = f32[2,64,1024]{2,1,0:T(8,128)} async-done(((f32[2,256,1024]{2,1,0:T(8,128)}), f32[2,64,1024]{2,1,0:T(8,128)}) %reduce-scatter.64.cloned.1.call-update) | async-done | bytes 524304 | tf_op jit(solution)/shard_map/reduce_scatter | solution.py:37
  1491.2 34.2 %reduce-scatter.80.cloned.1.call-done = f32[2,64,1024]{2,1,0:T(8,128)} async-done(((f32[2,256,1024]{2,1,0:T(8,128)}), f32[2,64,1024]{2,1,0:T(8,128)}) %reduce-scatter.80.cloned.1.call-update) | async-done | bytes 524304 | tf_op jit(solution)/shard_map/reduce_scatter | solution.py:37
  1556.3 9.4 all-gather.76.cloned.1.call-done
  1569.0 15.6 all-gather.70.cloned.1.call-done
  1587.9 15.5 all-gather.88.cloned.1.call-done
  1645.5 40.4 %all-reduce.15 = (f32[1024]{0:T(1024)S(1)}, f32[1024]{0:T(1024)S(1)}, f32[1024]{0:T(1024)S(1)}, f32[1024]{0:T(1024)S(1)}, f32[1024]{0:T(1024)S(1)}, /*index=5*/f...) all-reduce(f32[1024]{0:T(1024)S(1)} %dynamic-update-slice.9, ...), channel_id=1, replica_groups=mesh['fsdp'=2,'ctx'=4,'tp'=4] {'fsdp','ctx','tp'}, use_global_device_ids=true, to_apply=%add.6 | all-reduce | flops 12288 | bytes 98304
  1690.6 15.9 reduce-scatter.50.cloned.1.call-done
  1706.5 34.2 %reduce-scatter.56.cloned.1.call-done = f32[2,64,1024]{2,1,0:T(8,128)} async-done(((f32[2,256,1024]{2,1,0:T(8,128)}), f32[2,64,1024]{2,1,0:T(8,128)}) %reduce-scatter.56.cloned.1.call-update) | async-done | bytes 524304 | tf_op jit(solution)/shard_map/reduce_scatter | solution.py:37
  1752.1 60.0 %reduce-scatter.90.cloned.1.call-done = f32[128,2,256]{2,0,1:T(8,128)} async-done(((f32[1024,2,256]{2,0,1:T(8,128)}), f32[128,2,256]{2,0,1:T(8,128)}) %reduce-scatter.90.cloned.1.call-update) | async-done | bytes 262160 | tf_op jit(solution)/shard_map/reduce_scatter | solution.py:42
  1813.9 64.6 %reduce-scatter.94.cloned.1.call-done = f32[128,256]{1,0:T(8,128)} async-done(((f32[1024,256]{1,0:T(8,128)}), f32[128,256]{1,0:T(8,128)}) %reduce-scatter.94.cloned.1.call-update) | async-done | bytes 131088 | tf_op jit(solution)/shard_map/reduce_scatter | solution.py:44
  1878.6 91.6 %reduce-scatter.96.cloned.1.call-done = f32[128,1024]{1,0:T(8,128)} async-done(((f32[1024,1024]{1,0:T(8,128)}), f32[128,1024]{1,0:T(8,128)}) %reduce-scatter.96.cloned.1.call-update) | async-done | bytes 524304 | tf_op jit(solution)/shard_map/reduce_scatter | solution.py:45
  1970.1 91.9 %reduce-scatter.98.cloned.1.call-done = f32[128,1024]{1,0:T(8,128)} async-done(((f32[1024,1024]{1,0:T(8,128)}), f32[128,1024]{1,0:T(8,128)}) %reduce-scatter.98.cloned.1.call-update) | async-done | bytes 524304 | tf_op jit(solution)/shard_map/reduce_scatter | solution.py:46
  2062.1 79.1 %reduce-scatter.92.cloned.1.call-done = f32[128,3,256]{2,0,1:T(8,128)} async-done(((f32[1024,3,256]{2,0,1:T(8,128)}), f32[128,3,256]{2,0,1:T(8,128)}) %reduce-scatter.92.cloned.1.call-update) | async-done | bytes 393232 | tf_op jit(solution)/shard_map/reduce_scatter | solution.py:43
  (737 shorter events, 363.6 us)
Async XLA Ops:
  7.2 46.4 %all-gather.42.cloned.1.call-start = ((), (), s32[]{:S(2)}) async-start(), calls=%async_computation.33 | async-start | bytes 1179648 | tf_op jit(solution)/shard_map/all_gather | solution.py:24
  8.8 96.1 %reduce-scatter.34.cloned.1.call-start = ((), (), s32[]{:S(2)}) async-start(), calls=%async_computation.34 | async-start | bytes 2621440 | tf_op jit(solution)/shard_map/reduce_scatter | solution.py:37
  57.0 65.2 %reduce-scatter.40.cloned.1.call-start = ((), (), s32[]{:S(2)}) async-start(), calls=%async_computation.42 | async-start | bytes 2621440 | tf_op jit(solution)/shard_map/reduce_scatter | solution.py:37
  59.2 96.9 %reduce-scatter.46.cloned.1.call-start = ((), (), s32[]{:S(2)}) async-start(), calls=%async_computation.47 | async-start | bytes 2621440 | tf_op jit(solution)/shard_map/reduce_scatter | solution.py:37
  61.4 128.7 %reduce-scatter.52.cloned.1.call-start = ((), (), s32[]{:S(2)}) async-start(), calls=%async_computation.52 | async-start | bytes 2621440 | tf_op jit(solution)/shard_map/reduce_scatter | solution.py:37
  63.6 174.2 %all-gather.46.cloned.1.call-start = ((), (), s32[]{:S(2)}) async-start(), calls=%async_computation.36 | async-start | bytes 1769472 | tf_op jit(solution)/shard_map/all_gather | solution.py:25
  64.5 190.4 %all-gather.54.cloned.1.call-start = ((), (), s32[]{:S(2)}) async-start(), calls=%async_computation.43 | async-start | bytes 1310720 | tf_op jit(solution)/shard_map/all_gather | solution.py:33
  194.5 79.4 %all-gather.58.cloned.1.call-start = ((), (), s32[]{:S(2)}) async-start(), calls=%async_computation.48 | async-start | bytes 1310720 | tf_op jit(solution)/shard_map/all_gather | solution.py:33
  195.2 97.5 %all-gather.62.cloned.1.call-start = ((), (), s32[]{:S(2)}) async-start(), calls=%async_computation.53 | async-start | bytes 1310720 | tf_op jit(solution)/shard_map/all_gather | solution.py:33
  195.9 115.5 %all-gather.44.cloned.1.call-start = ((), (), s32[]{:S(2)}) async-start(), calls=%async_computation.35 | async-start | bytes 1310720 | tf_op jit(solution)/shard_map/all_gather | solution.py:33
  196.6 154.1 %all-gather.96.cloned.1.call-start = ((), (), s32[]{:S(2)}) async-start(), calls=%async_computation.93 | async-start | bytes 1310720 | tf_op jit(solution)/shard_map/all_gather | solution.py:80
  258.5 122.7 %all-gather.94.cloned.1.call-start = ((), (), s32[]{:S(2)}) async-start(), calls=%async_computation.92 | async-start | bytes 1310720 | tf_op jit(solution)/shard_map/all_gather | solution.py:81
  259.1 152.8 %all-gather.100.cloned.1.call-start = ((), (), s32[]{:S(2)}) async-start(), calls=%async_computation.95 | async-start | bytes 1310720 | tf_op jit(solution)/shard_map/all_gather | solution.py:80
  277.4 165.0 %all-gather.98.cloned.1.call-start = ((), (), s32[]{:S(2)}) async-start(), calls=%async_computation.94 | async-start | bytes 1310720 | tf_op jit(solution)/shard_map/all_gather | solution.py:81
  278.0 194.9 %all-gather.104.cloned.1.call-start = ((), (), s32[]{:S(2)}) async-start(), calls=%async_computation.97 | async-start | bytes 1310720 | tf_op jit(solution)/shard_map/all_gather | solution.py:80
  296.4 206.6 %all-gather.102.cloned.1.call-start = ((), (), s32[]{:S(2)}) async-start(), calls=%async_computation.96 | async-start | bytes 1310720 | tf_op jit(solution)/shard_map/all_gather | solution.py:81
  296.9 236.5 %all-gather.92.cloned.1.call-start = ((), (), s32[]{:S(2)}) async-start(), calls=%async_computation.91 | async-start | bytes 1310720 | tf_op jit(solution)/shard_map/all_gather | solution.py:80
  315.1 248.3 %all-gather.90.cloned.1.call-start = ((), (), s32[]{:S(2)}) async-start(), calls=%async_computation.90 | async-start | bytes 1310720 | tf_op jit(solution)/shard_map/all_gather | solution.py:81
  350.1 246.2 %reduce-scatter.42.cloned.1.call-start = ((), (), s32[]{:S(2)}) async-start(), calls=%async_computation.44 | async-start | bytes 2621440 | tf_op jit(solution)/shard_map/reduce_scatter | solution.py:37
  388.4 242.4 %reduce-scatter.48.cloned.1.call-start = ((), (), s32[]{:S(2)}) async-start(), calls=%async_computation.49 | async-start | bytes 2621440 | tf_op jit(solution)/shard_map/reduce_scatter | solution.py:37
  449.6 215.2 %reduce-scatter.54.cloned.1.call-start = ((), (), s32[]{:S(2)}) async-start(), calls=%async_computation.54 | async-start | bytes 2621440 | tf_op jit(solution)/shard_map/reduce_scatter | solution.py:37
  510.1 188.9 %reduce-scatter.36.cloned.1.call-start = ((), (), s32[]{:S(2)}) async-start(), calls=%async_computation.37 | async-start | bytes 2621440 | tf_op jit(solution)/shard_map/reduce_scatter | solution.py:37
  570.6 182.1 %all-gather.50.cloned.1.call-start = ((), (), s32[]{:S(2)}) async-start(), calls=%async_computation.39 | async-start | bytes 2359296 | tf_op jit(solution)/shard_map/all_gather | solution.py:27
  571.3 196.4 %all-gather.60.cloned.1.call-start = ((), (), s32[]{:S(2)}) async-start(), calls=%async_computation.50 | async-start | bytes 1310720 | tf_op jit(solution)/shard_map/all_gather | solution.py:33
  703.7 82.9 %all-gather.64.cloned.1.call-start = ((), (), s32[]{:S(2)}) async-start(), calls=%async_computation.55 | async-start | bytes 1310720 | tf_op jit(solution)/shard_map/all_gather | solution.py:33
  704.4 100.9 %all-gather.56.cloned.1.call-start = ((), (), s32[]{:S(2)}) async-start(), calls=%async_computation.45 | async-start | bytes 1310720 | tf_op jit(solution)/shard_map/all_gather | solution.py:33
  705.0 119.1 %all-gather.48.cloned.1.call-start = ((), (), s32[]{:S(2)}) async-start(), calls=%async_computation.38 | async-start | bytes 1310720 | tf_op jit(solution)/shard_map/all_gather | solution.py:33
  705.6 149.7 %all-gather.84.cloned.1.call-start = ((), (), s32[]{:S(2)}) async-start(), calls=%async_computation.78 | async-start | bytes 1310720 | tf_op jit(solution)/shard_map/all_gather | solution.py:33
  709.0 184.9 %all-gather.52.cloned.1.call-start = ((), (), s32[]{:S(2)}) async-start(), calls=%async_computation.40 | async-start | bytes 2359296 | tf_op jit(solution)/shard_map/all_gather | solution.py:28
  709.7 200.8 %all-gather.78.cloned.1.call-start = ((), (), s32[]{:S(2)}) async-start(), calls=%async_computation.71 | async-start | bytes 1310720 | tf_op jit(solution)/shard_map/all_gather | solution.py:33
  710.3 218.6 %all-gather.72.cloned.1.call-start = ((), (), s32[]{:S(2)}) async-start(), calls=%async_computation.64 | async-start | bytes 1310720 | tf_op jit(solution)/shard_map/all_gather | solution.py:33
  711.0 236.2 %all-gather.66.cloned.1.call-start = ((), (), s32[]{:S(2)}) async-start(), calls=%async_computation.57 | async-start | bytes 1310720 | tf_op jit(solution)/shard_map/all_gather | solution.py:33
  711.8 269.9 %reduce-scatter.82.cloned.1.call-start = ((), (), s32[]{:S(2)}) async-start(), calls=%async_computation.79 | async-start | bytes 2621440 | tf_op jit(solution)/shard_map/reduce_scatter | solution.py:37
  903.3 113.0 %reduce-scatter.74.cloned.1.call-start = ((), (), s32[]{:S(2)}) async-start(), calls=%async_computation.72 | async-start | bytes 2621440 | tf_op jit(solution)/shard_map/reduce_scatter | solution.py:37
  920.0 130.4 %reduce-scatter.66.cloned.1.call-start = ((), (), s32[]{:S(2)}) async-start(), calls=%async_computation.65 | async-start | bytes 2621440 | tf_op jit(solution)/shard_map/reduce_scatter | solution.py:37
  938.3 146.0 %reduce-scatter.58.cloned.1.call-start = ((), (), s32[]{:S(2)}) async-start(), calls=%async_computation.58 | async-start | bytes 2621440 | tf_op jit(solution)/shard_map/reduce_scatter | solution.py:37
  956.7 150.4 %all-gather.86.cloned.1.call-start = ((), (), s32[]{:S(2)}) async-start(), calls=%async_computation.80 | async-start | bytes 1310720 | tf_op jit(solution)/shard_map/all_gather | solution.py:33
  1090.2 38.4 %all-gather.74.cloned.1.call-start = ((), (), s32[]{:S(2)}) async-start(), calls=%async_computation.66 | async-start | bytes 1310720 | tf_op jit(solution)/shard_map/all_gather | solution.py:33
  1093.2 56.6 %all-gather.68.cloned.1.call-start = ((), (), s32[]{:S(2)}) async-start(), calls=%async_computation.59 | async-start | bytes 1310720 | tf_op jit(solution)/shard_map/all_gather | solution.py:33
  1093.8 77.8 %all-gather.80.cloned.1.call-start = ((), (), s32[]{:S(2)}) async-start(), calls=%async_computation.73 | async-start | bytes 1310720 | tf_op jit(solution)/shard_map/all_gather | solution.py:33
  1094.6 101.9 %reduce-scatter.86.cloned.1.call-start = ((), (), s32[]{:S(2)}) async-start(), calls=%async_computation.82 | async-start | bytes 1310720 | tf_op jit(solution)/shard_map/reduce_scatter | solution.py:180
  1115.1 106.2 %reduce-scatter.84.cloned.1.call-start = ((), (), s32[]{:S(2)}) async-start(), calls=%async_computation.81 | async-start | bytes 1310720 | tf_op jit(solution)/shard_map/reduce_scatter | solution.py:174
  1128.3 121.0 %reduce-scatter.70.cloned.1.call-start = ((), (), s32[]{:S(2)}) async-start(), calls=%async_computation.68 | async-start | bytes 1310720 | tf_op jit(solution)/shard_map/reduce_scatter | solution.py:180
  1136.8 140.7 %reduce-scatter.68.cloned.1.call-start = ((), (), s32[]{:S(2)}) async-start(), calls=%async_computation.67 | async-start | bytes 1310720 | tf_op jit(solution)/shard_map/reduce_scatter | solution.py:174
  1149.8 155.7 %reduce-scatter.62.cloned.1.call-start = ((), (), s32[]{:S(2)}) async-start(), calls=%async_computation.61 | async-start | bytes 1310720 | tf_op jit(solution)/shard_map/reduce_scatter | solution.py:180
  1158.3 175.3 %reduce-scatter.60.cloned.1.call-start = ((), (), s32[]{:S(2)}) async-start(), calls=%async_computation.60 | async-start | bytes 1310720 | tf_op jit(solution)/shard_map/reduce_scatter | solution.py:174
  1171.1 190.4 %reduce-scatter.78.cloned.1.call-start = ((), (), s32[]{:S(2)}) async-start(), calls=%async_computation.75 | async-start | bytes 1310720 | tf_op jit(solution)/shard_map/reduce_scatter | solution.py:180
  1179.7 209.9 %reduce-scatter.76.cloned.1.call-start = ((), (), s32[]{:S(2)}) async-start(), calls=%async_computation.74 | async-start | bytes 1310720 | tf_op jit(solution)/shard_map/reduce_scatter | solution.py:174
  1192.7 230.0 %reduce-scatter.88.cloned.1.call-start = ((), (), s32[]{:S(2)}) async-start(), calls=%async_computation.83 | async-start | bytes 2621440 | tf_op jit(solution)/shard_map/reduce_scatter | solution.py:37
  1225.2 232.1 %reduce-scatter.72.cloned.1.call-start = ((), (), s32[]{:S(2)}) async-start(), calls=%async_computation.69 | async-start | bytes 2621440 | tf_op jit(solution)/shard_map/reduce_scatter | solution.py:37
  1281.4 209.8 %reduce-scatter.64.cloned.1.call-start = ((), (), s32[]{:S(2)}) async-start(), calls=%async_computation.62 | async-start | bytes 2621440 | tf_op jit(solution)/shard_map/reduce_scatter | solution.py:37
  1337.5 187.9 %reduce-scatter.80.cloned.1.call-start = ((), (), s32[]{:S(2)}) async-start(), calls=%async_computation.76 | async-start | bytes 2621440 | tf_op jit(solution)/shard_map/reduce_scatter | solution.py:37
  1393.7 158.4 %all-gather.82.cloned.1.call-start = ((), (), s32[]{:S(2)}) async-start(), calls=%async_computation.77 | async-start | bytes 1310720 | tf_op jit(solution)/shard_map/all_gather | solution.py:33
  1532.6 51.9 %all-gather.70.cloned.1.call-start = ((), (), s32[]{:S(2)}) async-start(), calls=%async_computation.63 | async-start | bytes 1310720 | tf_op jit(solution)/shard_map/all_gather | solution.py:33
  1534.7 68.8 %all-gather.88.cloned.1.call-start = ((), (), s32[]{:S(2)}) async-start(), calls=%async_computation.84 | async-start | bytes 1310720 | tf_op jit(solution)/shard_map/all_gather | solution.py:33
  1535.9 154.6 %reduce-scatter.38.cloned.1.call-start = ((), (), s32[]{:S(2)}) async-start(), calls=%async_computation.41 | async-start | bytes 2621440 | tf_op jit(solution)/shard_map/reduce_scatter | solution.py:37
  1540.4 150.1 %reduce-scatter.44.cloned.1.call-start = ((), (), s32[]{:S(2)}) async-start(), calls=%async_computation.46 | async-start | bytes 2621440 | tf_op jit(solution)/shard_map/reduce_scatter | solution.py:37
  1544.3 162.2 %reduce-scatter.50.cloned.1.call-start = ((), (), s32[]{:S(2)}) async-start(), calls=%async_computation.51 | async-start | bytes 2621440 | tf_op jit(solution)/shard_map/reduce_scatter | solution.py:37
  1548.1 192.5 %reduce-scatter.56.cloned.1.call-start = ((), (), s32[]{:S(2)}) async-start(), calls=%async_computation.56 | async-start | bytes 2621440 | tf_op jit(solution)/shard_map/reduce_scatter | solution.py:37
  1552.0 260.1 %reduce-scatter.90.cloned.1.call-start = ((), (), s32[]{:S(2)}) async-start(), calls=%async_computation.85 | async-start | bytes 2359296 | tf_op jit(solution)/shard_map/reduce_scatter | solution.py:42
  1608.8 269.8 %reduce-scatter.94.cloned.1.call-start = ((), (), s32[]{:S(2)}) async-start(), calls=%async_computation.87 | async-start | bytes 1179648 | tf_op jit(solution)/shard_map/reduce_scatter | solution.py:44
  1615.1 355.0 %reduce-scatter.96.cloned.1.call-start = ((), (), s32[]{:S(2)}) async-start(), calls=%async_computation.88 | async-start | bytes 4718592 | tf_op jit(solution)/shard_map/reduce_scatter | solution.py:45
  1624.7 437.4 %reduce-scatter.98.cloned.1.call-start = ((), (), s32[]{:S(2)}) async-start(), calls=%async_computation.89 | async-start | bytes 4718592 | tf_op jit(solution)/shard_map/reduce_scatter | solution.py:46
  1635.1 506.0 %reduce-scatter.92.cloned.1.call-start = ((), (), s32[]{:S(2)}) async-start(), calls=%async_computation.86 | async-start | bytes 3538944 | tf_op jit(solution)/shard_map/reduce_scatter | solution.py:43
  (194 other events, 8016.1 us)
Sparse Core Ops, SparseCore 0:
  10.7 42.8 all-gather.41
  57.1 30.3 reduce-scatter.33
  90.8 31.4 reduce-scatter.39
  124.7 31.3 reduce-scatter.45
  158.6 31.3 reduce-scatter.51
  192.5 45.3 all-gather.45
  257.1 16.7 all-gather.57
  276.0 16.7 all-gather.61
  294.7 16.7 all-gather.43
  313.6 37.0 all-gather.95
  352.7 28.5 all-gather.93
  383.4 28.4 all-gather.99
  413.9 28.4 all-gather.97
  444.4 28.5 all-gather.103
  474.4 28.4 all-gather.101
  504.9 28.4 all-gather.91
  534.9 28.4 all-gather.89
  566.5 29.7 reduce-scatter.41
  599.3 31.4 reduce-scatter.47
  633.4 31.3 reduce-scatter.53
  667.5 31.4 reduce-scatter.35
  701.1 49.2 all-gather.49
  752.4 15.2 all-gather.59
  769.8 16.7 all-gather.63
  788.6 16.7 all-gather.55
  807.3 16.7 all-gather.47
  825.7 16.7 all-gather.83
  844.6 49.3 all-gather.51
  895.3 15.1 all-gather.77
  912.1 16.7 all-gather.71
  930.5 16.7 all-gather.65
  950.2 31.4 reduce-scatter.81
  984.9 31.3 reduce-scatter.73
  1018.9 31.4 reduce-scatter.65
  1052.9 31.3 reduce-scatter.57
  1090.3 16.7 all-gather.85
  1108.6 16.7 all-gather.73
  1126.8 16.7 all-gather.67
  1145.7 16.7 all-gather.79
  1165.3 27.1 reduce-scatter.85
  1195.5 25.7 reduce-scatter.83
  1223.5 25.8 reduce-scatter.69
  1251.7 25.7 reduce-scatter.67
  1279.7 25.8 reduce-scatter.61
  1307.8 25.7 reduce-scatter.59
  1335.7 25.7 reduce-scatter.77
  1363.8 25.7 reduce-scatter.75
  1392.6 30.0 reduce-scatter.87
  1425.9 31.4 reduce-scatter.71
  1459.8 31.4 reduce-scatter.63
  1493.9 31.4 reduce-scatter.79
  1530.5 16.7 all-gather.81
  1548.9 16.7 all-gather.75
  1567.8 16.7 all-gather.69
  1586.7 16.7 all-gather.87
  1606.5 31.4 reduce-scatter.37
  1641.1 31.5 reduce-scatter.43
  1675.1 31.3 reduce-scatter.49
  1709.2 31.4 reduce-scatter.55
  1744.2 67.8 reduce-scatter.89
  1816.1 62.4 reduce-scatter.93
  1883.0 87.0 reduce-scatter.95
  1974.2 87.8 reduce-scatter.97
  2066.7 74.4 reduce-scatter.91
  (1 shorter events, 14.8 us)
where the time goes:
time: 2160 us; the launch traced here: 2150 us
  waiting for transfers between devices  1570 us (73%)
  matrix products  256 us (12%)
  blocking collectives  155 us (7%)
  other arithmetic  86.6 us (4%)
  local copies, waits for them, and re-layouts  58.6 us (3%)
    reduce_scatter x20, waiting for transfers between devices, fold_rows(): return lax.psum_scatter(block, 'tp', scatter_dimension=1, tiled=True)  519 us
    all_gather x20, waiting for transfers between devices, spread_rows(): return lax.all_gather(block, 'tp', axis=1, tiled=True)  197 us
    reduce_scatter x4, waiting for transfers between devices, micro_step(): lax.psum_scatter(key_terms.reshape(groups, seq_len, heads_dev * HD).astyp...  109 us
    all_gather x4, waiting for transfers between devices, micro_step(): lax.all_gather(project[:, :, 2], 'ctx', axis=1, tiled=True)  97.3 us
    reduce_scatter x1, waiting for transfers between devices, reduce_weights(): lax.psum_scatter(parts[4], ('fsdp', 'ctx'), scatter_dimension=0, tiled=True)  91.9 us
    reduce_scatter x1, waiting for transfers between devices, reduce_weights(): lax.psum_scatter(parts[3], ('fsdp', 'ctx'), scatter_dimension=0, tiled=True)  91.6 us
    unnamed x2, blocking collectives  79.3 us
    reduce_scatter x1, waiting for transfers between devices, reduce_weights(): lax.psum_scatter(parts[1], ('fsdp', 'ctx'), scatter_dimension=0, tiled=True)  79.1 us
  transfers between devices with their start and end apart: 65, of which 55 were waited for; matrix products, arithmetic and copies ran while one was open for 16% of the time, Pallas kernels for 0%

commit v1 on v0

v1 whole, which is shorter than its diff:
```python
import functools

import jax
import jax.numpy as jnp
from jax import lax
from jax.experimental import pallas as pl
from jax.experimental.pallas import tpu as pltpu
from jax.sharding import PartitionSpec as P

HD = 64
EPSILON = 1e-05
F32 = jnp.float32
BF16 = jnp.bfloat16
ALL = ("fsdp", "ctx", "tp")


def dot(form, a, b):
    return jnp.einsum(form, a, b, preferred_element_type=F32)


def attend_forward_body(heads, q_ref, k_ref, v_ref, p_ref, o_ref):
    q = q_ref[0] * jnp.asarray(HD**-0.5, BF16)
    k = k_ref[0]
    v = v_ref[0]
    width = heads * HD
    lanes = lax.broadcasted_iota(jnp.int32, q.shape, 1) // HD
    rows = lax.broadcasted_iota(jnp.int32, (width, q.shape[0]), 0) // HD
    total = jnp.zeros((width, q.shape[0]), F32)
    for h in range(heads):
        q_h = jnp.where(lanes == h, q, jnp.zeros_like(q))
        s = lax.dot_general(k, q_h, (((1,), (1,)), ((), ())), preferred_element_type=F32)
        p = jnp.exp(s - jnp.max(s, axis=0, keepdims=True))
        low = (p * (1.0 / jnp.sum(p, axis=0, keepdims=True))).astype(BF16)
        p_ref[0, h] = low
        o_h = lax.dot_general(v, low, (((0,), (0,)), ((), ())), preferred_element_type=F32)
        total = total + jnp.where(rows == h, o_h, 0.0)
    o_ref[0] = total.T.astype(BF16)


def attend_forward(q, k, v):
    blocks, count, width = q.shape
    keys = k.shape[1]
    per = min(width, 128)
    heads = per // HD
    cols = width // per
    return pl.pallas_call(
        functools.partial(attend_forward_body, heads),
        grid=(blocks, cols),
        in_specs=[
            pl.BlockSpec((1, count, per), lambda t, j: (t, 0, j)),
            pl.BlockSpec((1, keys, per), lambda t, j: (t, 0, j)),
            pl.BlockSpec((1, keys, per), lambda t, j: (t, 0, j)),
        ],
        out_specs=[
            pl.BlockSpec((1, heads, keys, count), lambda t, j: (t, j, 0, 0)),
            pl.BlockSpec((1, count, per), lambda t, j: (t, 0, j)),
        ],
        out_shape=[
            jax.ShapeDtypeStruct((blocks, width // HD, keys, count), BF16),
            jax.ShapeDtypeStruct((blocks, count, width), BF16),
        ],
        compiler_params=pltpu.CompilerParams(vmem_limit_bytes=48 * 1024 * 1024),
        name="attend_forward",
    )(q, k, v)


def attend_backward_body(heads, q_ref, k_ref, v_ref, p_ref, o_ref, g_ref, dq_ref, dk_ref, dv_ref):
    q = q_ref[0] * jnp.asarray(HD**-0.5, BF16)
    k = k_ref[0]
    v = v_ref[0]
    g = g_ref[0]
    width = heads * HD
    count = q.shape[0]
    keys = k.shape[0]
    lanes = lax.broadcasted_iota(jnp.int32, q.shape, 1) // HD
    rows = lax.broadcasted_iota(jnp.int32, (width, count), 0) // HD
    prod = (g.astype(F32) * o_ref[0].astype(F32)).T
    dq = jnp.zeros((width, count), F32)
    dk = jnp.zeros((keys, width), F32)
    dv = jnp.zeros((keys, width), F32)
    for h in range(heads):
        q_h = jnp.where(lanes == h, q, jnp.zeros_like(q))
        g_h = jnp.where(lanes == h, g, jnp.zeros_like(g))
        p = p_ref[0, h]
        dp = lax.dot_general(v, g_h, (((1,), (1,)), ((), ())), preferred_element_type=F32)
        delta = jnp.sum(prod[h * HD : (h + 1) * HD], axis=0, keepdims=True)
        ds = (p.astype(F32) * (dp - delta)).astype(BF16)
        dq_h = lax.dot_general(k, ds, (((0,), (0,)), ((), ())), preferred_element_type=F32)
        dq = dq + jnp.where(rows == h, dq_h, 0.0)
        dk = dk + lax.dot_general(ds, q_h, (((1,), (0,)), ((), ())), preferred_element_type=F32)
        dv = dv + lax.dot_general(p, g_h, (((1,), (0,)), ((), ())), preferred_element_type=F32)
    dq_ref[0] = (dq.T * (HD**-0.5)).astype(BF16)
    dk_ref[0] = dk.astype(BF16)
    dv_ref[0] = dv.astype(BF16)


def attend_backward(q, k, v, p, o, g):
    blocks, count, width = q.shape
    keys = k.shape[1]
    per = min(width, 128)
    heads = per // HD
    cols = width // per
    q_spec = pl.BlockSpec((1, count, per), lambda t, j: (t, 0, j))
    k_spec = pl.BlockSpec((1, keys, per), lambda t, j: (t, 0, j))
    p_spec = pl.BlockSpec((1, heads, keys, count), lambda t, j: (t, j, 0, 0))
    return pl.pallas_call(
        functools.partial(attend_backward_body, heads),
        grid=(blocks, cols),
        in_specs=[q_spec, k_spec, k_spec, p_spec, q_spec, q_spec],
        out_specs=[q_spec, k_spec, k_spec],
        out_shape=[
            jax.ShapeDtypeStruct(q.shape, BF16),
            jax.ShapeDtypeStruct(k.shape, BF16),
            jax.ShapeDtypeStruct(v.shape, BF16),
        ],
        compiler_params=pltpu.CompilerParams(vmem_limit_bytes=48 * 1024 * 1024),
        name="attend_backward",
    )(q, k, v, p, o, g)


def norm_stats(matrix):
    center = matrix - jnp.mean(matrix, axis=-1, keepdims=True)
    spread = jnp.mean(center * center, axis=-1, keepdims=True)
    scale = lax.rsqrt(spread + EPSILON)
    return center * scale, scale


def norm_back(grad, unit, scale, gain):
    z = grad * gain
    inner = z - jnp.mean(z, axis=-1, keepdims=True) - unit * jnp.mean(z * unit, axis=-1, keepdims=True)
    return scale * inner


def gelu_pair(v):
    half = 0.5 * (1.0 + lax.erf(v * (0.5**0.5)))
    slope = half + v * jnp.exp(-0.5 * v * v) * 0.3989422804014327
    return v * half, slope


def pick(array, index, axis):
    return lax.dynamic_index_in_dim(array, index, axis, keepdims=False)


def swap_pairs(size, bit):
    if bit == 0:
        return [(i, i ^ 1) for i in range(size)]
    half = size // 2
    return [(i, (i // 2 + half // 2) % half * 2 + i % 2) for i in range(size)]


def chain_reduce(part, axis, size, rank, lead):
    up_pairs = [(i, i + 1) for i in range(size - 1)]
    down_pairs = [(i + 1, i) for i in range(size - 1)]
    up = down = None
    for step in range(size - 1):
        up_send = pick(part, jnp.clip(size - 1 - step + rank, 0, size - 1), lead)
        down_send = pick(part, jnp.clip(step - (size - 1 - rank), 0, size - 1), lead)
        if step:
            up_send = (up_send.astype(F32) + up.astype(F32)).astype(BF16)
            down_send = (down_send.astype(F32) + down.astype(F32)).astype(BF16)
        up = lax.ppermute(up_send, axis, up_pairs)
        down = lax.ppermute(down_send, axis, down_pairs)
    own = pick(part, rank, lead).astype(F32)
    if size > 1:
        own = own + up.astype(F32) + down.astype(F32)
    return own


def swap_reduce(part, axis, pairs, index, lead):
    got = lax.ppermute(pick(part, 1 - index, lead), axis, pairs)
    return (pick(part, index, lead).astype(F32) + got.astype(F32)).astype(BF16)


def sum_to_owner(grad, sizes, ranks, y_first):
    fs, cs, ts = sizes
    f_rank, c_rank, t_rank = ranks
    rows = grad.shape[1] // (fs * cs)
    part = grad.reshape(ts // 2, 2, fs, cs, rows, grad.shape[2])
    part = swap_reduce(part, "tp", swap_pairs(ts, 0), t_rank % 2, 1)

    def over_x(part):
        if ts == 2:
            return pick(part, 0, 0)
        if ts == 4:
            return swap_reduce(part, "tp", swap_pairs(ts, 1), t_rank // 2, 0)
        raise NotImplementedError

    def over_y(part, lead):
        if fs == 1:
            return pick(part, 0, lead)
        if fs == 2:
            return swap_reduce(part, "fsdp", [(0, 1), (1, 0)], f_rank, lead)
        return chain_reduce(part, "fsdp", fs, f_rank, lead).astype(BF16)

    if y_first:
        part = over_x(over_y(part, 1))
    else:
        part = over_y(over_x(part), 0)
    return chain_reduce(part, "ctx", cs, c_rank, 0)


def on_device(
    sizes,
    tokens,
    skip_tokens,
    merger_weight,
    merger_bias,
    first_gain,
    first_shift,
    attend_weight,
    output_weight,
    output_bias,
    second_gain,
    second_shift,
    expand_weight,
    widen_bias,
    shrink_weight,
    shrink_bias,
    live_slots,
    cotangent,
):
    fs, cs, ts = sizes
    f_rank, c_rank, t_rank = (lax.axis_index(a) for a in ALL)
    ranks = (f_rank, c_rank, t_rank)
    group = cs * ts
    batches, local_seqs, local_len, part_width = tokens.shape
    slots = batches * local_seqs
    share = group // slots
    fine = cotangent.shape[2] // share
    width = cotangent.shape[3]
    count = cs * ts * fine
    device = c_rank * ts + t_rank

    def gather(part):
        full = lax.all_gather(part, ("tp", "fsdp", "ctx"), axis=0, tiled=True)
        return full.reshape(ts, width, part.shape[1])

    merger = gather(merger_weight.reshape(merger_weight.shape[0], -1))
    attend = gather(attend_weight.reshape(attend_weight.shape[0], -1))
    output = gather(output_weight)
    expand = gather(expand_weight)
    shrink = gather(shrink_weight)

    packed = jnp.concatenate(
        [merger_bias, first_gain, first_shift, output_bias, second_gain, second_shift, shrink_bias, widen_bias]
    )
    packed = lax.all_gather(packed, ALL, axis=0, tiled=False)
    small = merger_bias.shape[0]
    vectors = [packed[:, i * small : (i + 1) * small].reshape(-1) for i in range(7)]
    merger_bias, first_gain, first_shift, output_bias, second_gain, second_shift, shrink_bias = vectors
    hidden = expand_weight.shape[1]
    widen_bias = packed[:, 7 * small :].reshape(ts, 1, hidden)

    def to_group(array):
        return lax.all_to_all(array, ("ctx", "tp"), 0, 0, tiled=True)

    def split_rows(array):
        feats = array.shape[-1]
        array = array.reshape(slots, ts, share, fine, feats).transpose(0, 2, 1, 3, 4)
        return array.reshape(group, ts * fine, feats)

    both = to_group(split_rows(jnp.concatenate([tokens, skip_tokens], axis=-1)).reshape(group * ts * fine, -1))
    both = both.reshape(cs, ts, ts * fine, 2 * part_width).transpose(1, 0, 2, 3).reshape(ts, count, 2 * part_width)
    cot = to_group(cotangent.reshape(group * fine, width)).reshape(count, width)
    live = pick(live_slots.reshape(slots), device // share, 0).astype(F32)

    joined = dot("tsi,toi->so", both, merger) + merger_bias
    unit_one, scale_one = norm_stats(joined)
    normed = (unit_one * first_gain + first_shift).astype(BF16)
    project = dot("sd,tdj->tsj", normed, attend).astype(BF16)
    third = project.shape[2] // 3
    queries = project[:, :, :third]
    own_keys = project[:, :, third:]

    def shift_pairs(step):
        return [(i, i // share * share + (i % share + step) % share) for i in range(ts)]

    blocks = [own_keys] + [lax.ppermute(own_keys, "tp", shift_pairs(d)) for d in range(1, share)]
    both_keys = jnp.concatenate(blocks, axis=1)
    key_rows = both_keys[:, :, :third]
    value_rows = both_keys[:, :, third:]
    probs, attended = attend_forward(queries, key_rows, value_rows)
    second = joined + dot("tsi,toi->so", attended, output) + output_bias
    unit_two, scale_two = norm_stats(second)
    normed_two = (unit_two * second_gain + second_shift).astype(BF16)
    expanded = dot("sd,tdf->tsf", normed_two, expand) + widen_bias
    activated, slope = gelu_pair(expanded)
    activated = activated.astype(BF16)
    result = second + dot("tsf,tof->so", activated, shrink) + shrink_bias
    layer_out = (result * live).astype(BF16)
    layer_out = to_group(layer_out.reshape(group * fine, width)).reshape(batches, local_seqs, share * fine, width)

    upstream = cot.astype(F32) * live
    branch_low = upstream.astype(BF16)
    grad_shrink = dot("so,tsf->tof", branch_low, activated).astype(BF16)
    grad_expanded = (dot("so,tof->tsf", branch_low, shrink) * slope).astype(BF16)
    grad_expand = dot("sd,tsf->tdf", normed_two, grad_expanded).astype(BF16)
    grad_normed_two = dot("tsf,tdf->sd", grad_expanded, expand)
    grad_second = upstream + norm_back(grad_normed_two, unit_two, scale_two, second_gain)
    attn_low = grad_second.astype(BF16)
    grad_output = dot("so,tsi->toi", attn_low, attended).astype(BF16)
    grad_attended = dot("so,toi->tsi", attn_low, output).astype(BF16)
    grad_queries, grad_keys, grad_values = attend_backward(
        queries, key_rows, value_rows, probs, attended, grad_attended
    )
    grad_both = jnp.concatenate([grad_keys, grad_values], axis=-1)
    total = grad_both[:, :count].astype(F32)
    for d in range(1, share):
        total = total + lax.ppermute(
            grad_both[:, d * count : (d + 1) * count], "tp", shift_pairs(share - d)
        ).astype(F32)
    grad_project = jnp.concatenate([grad_queries, total.astype(BF16)], axis=-1)
    grad_attend = dot("sd,tsj->tdj", normed, grad_project).astype(BF16)
    grad_normed = dot("tsj,tdj->sd", grad_project, attend)
    grad_joined = grad_second + norm_back(grad_normed, unit_one, scale_one, first_gain)
    joined_low = grad_joined.astype(BF16)
    grad_merger = dot("so,tsi->toi", joined_low, both).astype(BF16)
    grad_inputs = dot("so,toi->tsi", joined_low, merger).astype(BF16)

    out = grad_inputs.reshape(ts, cs, ts * fine, 2 * part_width).transpose(1, 0, 2, 3)
    out = to_group(out.reshape(group * ts * fine, 2 * part_width))
    out = out.reshape(slots, share, ts, fine, 2 * part_width).transpose(0, 2, 1, 3, 4)
    out = out.reshape(batches, local_seqs, local_len, 2 * part_width).astype(F32)

    def rows_sum(array):
        return jnp.sum(array.astype(F32), axis=0)

    sums = [
        rows_sum(grad_joined),
        rows_sum(grad_normed * unit_one),
        rows_sum(grad_normed),
        rows_sum(grad_second),
        rows_sum(grad_normed_two * unit_two),
        rows_sum(grad_normed_two),
        rows_sum(upstream),
    ]
    devices = fs * cs * ts
    vec = jnp.concatenate(
        [v.reshape(devices, small) for v in sums]
        + [jnp.sum(grad_expanded.astype(F32), axis=1).reshape(devices, -1)],
        axis=1,
    )
    vec = jnp.sum(lax.all_to_all(vec, ALL, 0, 0, tiled=True), axis=0)
    vec_out = [vec[i * small : (i + 1) * small] for i in range(7)] + [vec[7 * small :]]

    reduced = [
        sum_to_owner(g, sizes, ranks, y_first)
        for g, y_first in (
            (grad_merger, False),
            (grad_attend, True),
            (grad_output, False),
            (grad_expand, True),
            (grad_shrink, False),
        )
    ]
    return (
        layer_out,
        out[..., :part_width],
        out[..., part_width:],
        reduced[0].reshape(merger_weight.shape),
        vec_out[0],
        vec_out[1],
        vec_out[2],
        reduced[1].reshape(attend_weight.shape),
        reduced[2],
        vec_out[3],
        vec_out[4],
        vec_out[5],
        reduced[3],
        vec_out[7],
        reduced[4],
        vec_out[6],
    )


def solution(mesh):
    sizes = tuple(mesh.shape[a] for a in ALL)
    act = P(None, "fsdp", "ctx", "tp")
    vec = P(ALL)
    flat = P(None, "fsdp", ("ctx", "tp"), None)
    w_three = P(("fsdp", "ctx"), None, "tp")
    w_two = P(("fsdp", "ctx"), "tp")
    return jax.shard_map(
        functools.partial(on_device, sizes),
        mesh=mesh,
        in_specs=(
            act, act, w_three, vec, vec, vec, w_three, w_two, vec, vec, vec, w_two, vec, w_two, vec,
            P(None, "fsdp"), flat,
        ),
        out_specs=(
            flat, act, act, w_three, vec, vec, vec, w_three, w_two, vec, vec, vec, w_two, vec, w_two, vec,
        ),
        check_vma=False,
    )
```

time: 2160 us -> 851 us (0.39)
  waiting for transfers between devices: 1570 us -> 300 us
  matrix products: 256 us -> 96.6 us
  starting transfers between devices: 4.72 us -> 132 us
  blocking collectives: 155 us -> 77.8 us
  local copies, waits for them, and re-layouts: 58.6 us -> 124 us
  Pallas kernels: 0 us -> 41.3 us
  other arithmetic: 86.6 us -> 57.3 us
    reduce_scatter x33 -> x0, waiting for transfers between devices: 1070 us -> none  [the longest x20 519 us: fold_rows(): return lax.psum_scatter(block, 'tp', scatter_dimension=1, tiled=True)]
    all_gather x32 -> x5, waiting for transfers between devices: 487 us -> 223 us  [gather(): full = lax.all_gather(part, ('tp', 'fsdp', 'ctx'), axis=0, tiled=True)]
    dot_general x84 -> x15, matrix products: 256 us -> 96.6 us  [dot(): return jnp.einsum(form, a, b, preferred_element_type=F32)]
    ppermute x0 -> x47, starting transfers between devices: none -> 101 us  [the longest x15 65.5 us: chain_reduce(): up = lax.ppermute(up_send, axis, up_pairs)]
    all_gather x2 -> x0, blocking collectives: 75.7 us -> none  [the longest x1 40.9 us: on_device(): lax.all_gather(widen_bias, ('fsdp', 'ctx', 'tp'), axis=0, tiled=True)]
    ppermute x0 -> x47, waiting for transfers between devices: none -> 74.4 us  [the longest x15 65.4 us: swap_reduce(): got = lax.ppermute(pick(part, 1 - index, lead), axis, pairs)]
    pallas_call x0 -> x2, Pallas kernels: none -> 41.3 us  [the longest x1 20.7 us: attend_forward(): pl.pallas_call(functools.partial(attend_forward_body, heads), grid=(block...]
    dynamic_slice x1 -> x9, local copies, waits for them, and re-layouts: 0.01 us -> 34.1 us  [pick(): return lax.dynamic_index_in_dim(array, index, axis, keepdims=False)]
  transfers between devices with their start and end apart: 65 -> 57, of which waited for: 55 -> 12; matrix products, arithmetic and copies ran while one was open for 16% -> 27% of each run, Pallas kernels for 0% -> 5%
where the time goes in v1:
time: 851 us; the launch traced here: 845 us
  waiting for transfers between devices  300 us (35%)
  starting transfers between devices  132 us (16%)
  local copies, waits for them, and re-layouts  124 us (15%)
  matrix products  96.6 us (11%)
  blocking collectives  77.8 us (9%)
  other arithmetic  57.3 us (7%)
  Pallas kernels  41.3 us (5%)
  between operations  16.4 us (2%)
    all_gather x5, waiting for transfers between devices, gather(): full = lax.all_gather(part, ('tp', 'fsdp', 'ctx'), axis=0, tiled=True)  223 us
    dot_general x15, matrix products, dot(): return jnp.einsum(form, a, b, preferred_element_type=F32)  96.6 us
    unnamed x1, blocking collectives  77.8 us
    ppermute x15, starting transfers between devices, chain_reduce(): up = lax.ppermute(up_send, axis, up_pairs)  65.5 us
    ppermute x15, waiting for transfers between devices, swap_reduce(): got = lax.ppermute(pick(part, 1 - index, lead), axis, pairs)  65.4 us
    dynamic_slice x9, local copies, waits for them, and re-layouts, pick(): return lax.dynamic_index_in_dim(array, index, axis, keepdims=False)  34.1 us
    convert_element_type x15, other arithmetic, swap_reduce(): return (pick(part, index, lead).astype(F32) + got.astype(F32)).astype(BF16)  29.3 us
    unnamed x113, local copies, waits for them, and re-layouts  27.3 us
  transfers between devices with their start and end apart: 57, of which 12 were waited for; matrix products, arithmetic and copies ran while one was open for 27% of the time, Pallas kernels for 5%

profile of v1, /device:TPU:0, one launch (start us, length us, event | category | flops | bytes accessed | tf_op | source)
XLA Modules:
  0.0 845.3 jit_solution(1003752839086575956)
XLA Ops:
  15.6 7.5 all-to-all-start
  23.5 77.8 %all-reduce = f32[11264]{0:T(1024)S(1)} all-reduce(f32[11264]{0:T(1024)S(1)} %dynamic-update-slice), channel_id=2, replica_groups=mesh['fsdp'=2,'ctx'=4,'tp'=4] {'fsdp','ctx','tp'}, use_global_device_ids=true, to_apply=%add | all-reduce | flops 11264 | bytes 90112
  101.7 6.0 all-to-all-start.2
  109.2 5.3 fusion.31
  114.9 71.7 %all-gather.9.cloned.1.call-done = bf16[4096,768]{0,1:T(8,128)(2,1)} async-done(((bf16[128,768]{0,1:T(8,128)(2,1)}), bf16[4096,768]{0,1:T(8,128)(2,1)}) %all-gather.9.cloned.1.call-update) | async-done | bytes 6291472 | tf_op jit(solution)/shard_map/all_gather | solution.py:235
  186.6 8.6 %copy.100 = bf16[4096,768]{1,0:T(8,128)(2,1)} copy(bf16[4096,768]{0,1:T(8,128)(2,1)} %all-gather.9.cloned.1.call-done) | data formatting | bytes 12582912 | tf_op jit(solution)/shard_map/all_gather | solution.py:235
  195.3 6.7 convert_bitcast_fusion.3
  211.5 3.4 pad_maximum_fusion.1
  214.9 20.7 %attend_forward.1 = (bf16[4,4,1024,512]{3,2,1,0:T(8,128)(2,1)}, bf16[4,512,256]{2,1,0:T(8,128)(2,1)S(1)}) custom-call(bf16[4,512,256]{2,1,0:T(8,128)(2,1)S(1)} %slice.99.q_ref, bf16[4,1024,256]{2,1,0:T(8,128)(2,1)S(1)} %get-tuple-element.95.k_ref, bf16[4,1024,256]{2,1,0:T(8,128)(2,1)} %get-tuple-element.94.v_ref), custom_call_target="tpu_custom_call" | custom-call | tf_op jit(solution)/shard_map/attend_forward/pallas_call | solution.py:46
  236.6 7.8 all-gather.11.cloned.1.call-done
  244.4 3.9 fusion.87
  248.7 74.8 %all-gather.13.cloned.1.call-done = bf16[4096,1024]{1,0:T(8,128)(2,1)} async-done(((bf16[128,1024]{1,0:T(8,128)(2,1)}), bf16[4096,1024]{1,0:T(8,128)(2,1)}) %all-gather.13.cloned.1.call-update) | async-done | bytes 8388624 | tf_op jit(solution)/shard_map/all_gather | solution.py:235
  323.5 10.1 %fusion.11 = (bf16[4,512,1024]{2,1,0:T(8,128)(2,1)}, f32[512,4,1024]{2,0,1:T(8,128)}) fusion(f32[4,1024]{1,0:T(4,128)S(1)} %add.390, bf16[4,1024,1024]{2,1,0:T(8,128)(2,1)} %bitcast.383, f32[512,1024]{1,0:T(8,128)S(1)} %get-tuple-element.138, f32[1024]{0:T(1024)S(1)} %add.387, f32[1024]{0:T(1024)S(1)} %mul.159, f32[512]{0:T(512)S(1)} %add_rsqrt_fusion, ...), kind=kOutput, calls=%fused_computation.16 | convolution fusion | flops 4310171648 | bytes 23097344 | tf_op jit(solution)/shard_map/sd,tdf->tsf/dot_general | solution.py:18
  333.6 68.7 %all-gather.15.cloned.1.call-done = bf16[4096,1024]{1,0:T(8,128)(2,1)} async-done(((bf16[128,1024]{1,0:T(8,128)(2,1)}), bf16[4096,1024]{1,0:T(8,128)(2,1)}) %all-gather.15.cloned.1.call-update) | async-done | bytes 8388624 | tf_op jit(solution)/shard_map/all_gather | solution.py:235
  402.4 12.2 %convert_reduce_fusion = (f32[4,1024]{1,0:T(4,128)S(1)}, bf16[4,512,1024]{2,1,0:T(8,128)(2,1)}) fusion(f32[512,4,1024]{2,0,1:T(8,128)} %get-tuple-element.144, f32[4,1024]{1,0:T(4,128)S(1)} %add.390, bf16[512,1024,1]{1,0,2:T(8,128)(2,1)} %bitcast.375, bf16[4,1024,1024]{2,1,0:T(8,128)(2,1)} %bitcast.381), kind=kOutput, calls=%fused_computation.17 | convolution fusion | flops 4322226176 | bytes 22052864 | tf_op jit(solution)/shard_map/so,tof->tsf/dot_general | solution.py:18
  414.6 7.2 fusion.23
  428.2 4.4 reshape.299
  432.6 3.3 constant_dynamic-slice_fusion.3
  437.6 10.7 %fusion.26 = bf16[512,1024]{1,0:T(8,128)(2,1)} fusion(f32[512,1024]{1,0:T(8,128)} %copy-done.22, bf16[4,512,1024]{2,1,0:T(8,128)(2,1)} %get-tuple-element.143, bf16[4,1024,1024]{2,1,0:T(8,128)(2,1)} %bitcast.382, f32[]{:T(128)} %bitcast.19, f32[1024]{0:T(1024)S(1)} %add.397), kind=kOutput, calls=%fused_computation.65 | convolution fusion | flops 4297064448 | bytes 15732740 | tf_op jit(solution)/shard_map/tsf,tof->so/dot_general | solution.py:18
  448.3 4.7 all-to-all-start.1
  453.1 3.5 fusion.33.g_ref
  456.5 20.6 %attend_backward.1 = (bf16[4,512,256]{2,1,0:T(8,128)(2,1)S(1)}, bf16[4,1024,256]{2,1,0:T(8,128)(2,1)}, bf16[4,1024,256]{2,1,0:T(8,128)(2,1)}) custom-call(bf16[4,512,256]{2,1,0:T(8,128)(2,1)S(1)} %slice.99.q_ref, bf16[4,1024,256]{2,1,0:T(8,128)(2,1)} %copy-done, bf16[4,1024,256]{2,1,0:T(8,128)(2,1)} %get-tuple-element.94.v_ref, ...), custom_call_target="tpu_custom_call" | custom-call | tf_op jit(solution)/shard_map/attend_backward/pallas_call | solution.py:106
  488.8 8.1 convolution_convert_fusion.1
  496.9 4.4 collective-permute-done.21
  503.0 3.5 constant_dynamic-slice_fusion.1
  511.1 3.9 collective-permute-start.23
  515.1 5.9 convolution_convert_fusion
  522.4 4.7 collective-permute-start.24
  531.8 4.7 collective-permute-start.25
  538.7 3.9 fusion.22
  544.6 4.4 convert_bitcast_fusion.2
  549.0 7.7 reshape.287
  556.7 5.7 constant_dynamic-slice_fusion.7
  562.3 4.3 copy.106
  569.6 7.2 convert_bitcast_fusion
  576.8 11.0 %reshape.297 = bf16[2,2,2,4,128,768]{4,3,2,5,1,0:T(4,128)(2,1)} reshape(bf16[4,1024,768]{1,2,0:T(8,128)(2,1)} %convert_bitcast_fusion) | data formatting | bytes 12582912 | tf_op jit(solution)/shard_map/reshape | solution.py:178
  587.9 6.6 constant_dynamic-slice_fusion.5
  598.1 5.9 copy.109
  603.9 7.1 all-to-all-start.4
  611.4 4.8 convolution_convert_fusion.2
  618.4 5.4 all-to-all-start.3
  625.4 4.3 copy.127
  629.6 4.3 copy.128
  635.2 3.0 fusion.15
  640.4 4.4 fusion.7
  649.0 4.3 fusion.6
  653.3 20.9 %collective-permute-done.3 = bf16[2,4,128,512]{3,2,1,0:T(8,128)(2,1)S(1)} collective-permute-done((bf16[2,4,128,512]{3,2,1,0:T(8,128)(2,1)S(1)}, bf16[2,4,128,512]{3,2,1,0:T(8,128)(2,1)S(1)}, u32[]{:S(2)}, u32[]{:S(2)}) %collective-permute-start.3) | collective-permute-done | bytes 1048608 | tf_op jit(solution)/shard_map/ppermute | solution.py:170
  683.3 23.1 %collective-permute-done.4 = bf16[4,128,512]{2,1,0:T(8,128)(2,1)S(1)} collective-permute-done((bf16[4,128,512]{2,1,0:T(8,128)(2,1)S(1)}, bf16[4,128,512]{2,1,0:T(8,128)(2,1)S(1)}, u32[]{:S(2)}, u32[]{:S(2)}) %collective-permute-start.4) | collective-permute-done | bytes 524320 | tf_op jit(solution)/shard_map/ppermute | solution.py:170
  706.6 3.4 collective-permute-start.5
  714.1 5.2 collective-permute-start.6
  727.4 4.7 collective-permute-start.7
  744.6 4.2 collective-permute-done.12
  751.3 12.7 %collective-permute-done.31 = bf16[4,128,1024]{2,1,0:T(8,128)(2,1)} collective-permute-done((bf16[4,128,1024]{2,1,0:T(8,128)(2,1)}, bf16[4,128,1024]{2,1,0:T(8,128)(2,1)}, u32[]{:S(2)}, u32[]{:S(2)}) %collective-permute-start.31) | collective-permute-done | bytes 1048608 | tf_op jit(solution)/shard_map/ppermute | solution.py:170
  765.7 4.6 collective-permute-start.32
  773.3 4.6 collective-permute-start.41
  779.5 4.6 collective-permute-start.14
  785.4 4.6 collective-permute-start.33
  790.1 3.7 collective-permute-start.42
  793.8 3.1 collective-permute-start.15
  799.1 4.8 collective-permute-start.34
  806.2 4.6 collective-permute-start.43
  812.2 4.6 collective-permute-start.16
  817.5 3.1 collective-permute-done.18
  825.3 5.8 collective-permute-done.19
  (306 shorter events, 137.7 us)
Async XLA Ops:
  7.2 102.0 %all-gather.7.cloned.1.call-start = ((), (), s32[]{:S(2)}) async-start(), calls=%async_computation.5 | async-start | bytes 4325376 | tf_op jit(solution)/shard_map/all_gather | solution.py:235
  8.9 177.7 %all-gather.9.cloned.1.call-start = ((), (), s32[]{:S(2)}) async-start(), calls=%async_computation.6 | async-start | bytes 6488064 | tf_op jit(solution)/shard_map/all_gather | solution.py:235
  10.7 233.6 %all-gather.11.cloned.1.call-start = ((), (), s32[]{:S(2)}) async-start(), calls=%async_computation.7 | async-start | bytes 2162688 | tf_op jit(solution)/shard_map/all_gather | solution.py:235
  11.5 312.0 %all-gather.13.cloned.1.call-start = ((), (), s32[]{:S(2)}) async-start(), calls=%async_computation.8 | async-start | bytes 8650752 | tf_op jit(solution)/shard_map/all_gather | solution.py:235
  12.0 390.3 %all-gather.15.cloned.1.call-start = ((), (), s32[]{:S(2)}) async-start(), calls=%async_computation.9 | async-start | bytes 8650752 | tf_op jit(solution)/shard_map/all_gather | solution.py:235
  15.6 86.2 %all-to-all-start = ((bf16[16,128,512]{2,1,0:T(8,128)(2,1)}), bf16[16,128,512]{2,1,0:T(8,128)(2,1)S(1)}, u32[]{:S(2)}, u32[]{:S(2)}) async-start(bf16[16,128,512]{2,1,0:T(8,128)(2,1)} %bitcast.363), calls=%async_computation | async-start | bytes 4194304 | tf_op jit(solution)/shard_map/all_to_all | solution.py:255
  101.6 93.7 %copy-start.34 = (f32[1024]{0:T(1024)}, f32[1024]{0:T(1024)S(1)}, u32[]{:S(2)}) copy-start(f32[1024]{0:T(1024)S(1)} %add.379) | copy-start | bytes 12292
  101.7 104.7 %all-to-all-start.2 = ((bf16[16,32,1024]{2,1,0:T(8,128)(2,1)}), bf16[16,32,1024]{2,1,0:T(8,128)(2,1)S(1)}, u32[]{:S(2)}, u32[]{:S(2)}) async-start(bf16[16,32,1024]{2,1,0:T(8,128)(2,1)} %bitcast.376), calls=%async_computation.2 | async-start | bytes 2097152 | tf_op jit(solution)/shard_map/all_to_all | solution.py:255
  114.5 80.8 %copy-start.13 = (f32[512,1024,1]{1,0,2:T(8,128)}, f32[512,1024,1]{1,0,2:T(8,128)S(1)}, u32[]{:S(2)}) copy-start(f32[512,1024,1]{1,0,2:T(8,128)S(1)} %get-tuple-element.136) | copy-start | bytes 6291460
  204.3 7.2 collective-permute-start
  248.3 166.2 %copy-start.22 = (f32[512,1024]{1,0:T(8,128)}, f32[512,1024]{1,0:T(8,128)S(1)}, u32[]{:S(2)}) copy-start(f32[512,1024]{1,0:T(8,128)S(1)} %get-tuple-element.138) | copy-start | bytes 6291460
  437.4 48.0 %collective-permute-start.20 = (bf16[2,2,4,128,256]{4,3,2,1,0:T(8,128)(2,1)}, bf16[2,2,4,128,256]{4,3,2,1,0:T(8,128)(2,1)}, u32[]{:S(2)}, u32[]{:S(2)}) collective-permute-start(bf16[2,2,4,128,256]{4,3,2,1,0:T(8,128)(2,1)} %bitcast.377), channel_id=1, source_target_pairs={{0,1},{1,0},{2,3},{3,2},{4,5},{5,4},{6,7},{7,6},{8,9},{9,8},{10,11... | collective-permute-start | bytes 3145736 | tf_op jit(solution)/shard_map/ppermute | solution.py:170
  448.3 155.6 %all-to-all-start.1 = ((bf16[16,32,1024]{2,1,0:T(8,128)(2,1)}), bf16[16,32,1024]{2,1,0:T(8,128)(2,1)}, u32[]{:S(2)}, u32[]{:S(2)}) async-start(bf16[16,32,1024]{2,1,0:T(8,128)(2,1)} %bitcast.20), calls=%async_computation.1 | async-start | bytes 2097152 | tf_op jit(solution)/shard_map/all_to_all | solution.py:255
  482.2 54.3 %collective-permute-start.1 = (bf16[4,512,512]{2,1,0:T(8,128)(2,1)}, bf16[4,512,512]{2,1,0:T(8,128)(2,1)}, u32[]{:S(2)}, u32[]{:S(2)}) collective-permute-start(bf16[4,512,512]{2,1,0:T(8,128)(2,1)} %slice.109), channel_id=1, source_target_pairs={{0,1},{1,0},{2,3},{3,2},{4,5},{5,4},{6,7},{7,6},{8,9},{9,8},{10,11... | collective-permute-start | bytes 6291464 | tf_op jit(solution)/shard_map/ppermute | solution.py:309
  487.1 14.2 %collective-permute-start.21 = (bf16[2,4,128,256]{3,2,1,0:T(8,128)(2,1)S(1)}, bf16[2,4,128,256]{3,2,1,0:T(8,128)(2,1)S(1)}, u32[]{:S(2)}, u32[]{:S(2)}) collective-permute-start(bf16[2,4,128,256]{3,2,1,0:T(8,128)(2,1)S(1)} %dynamic-slice_bitcast_fusion.8), channel_id=1, source_target_pairs={{0,2},{1,3},{2,0},{3,1},{4,6},{5,7},{6,4},{7,5},{8,10},{9,11},{10,... | collective-permute-start | bytes 1572872 | tf_op jit(solution)/shard_map/ppermute | solution.py:170
  501.4 7.9 collective-permute-start.22
  506.4 32.3 %slice-start.2 = ((s8[6291456]{0:T(1024)(128)(4,1)}), s8[2097152]{0:T(1024)(128)(4,1)S(1)}, s32[]{:S(2)}) async-start(s8[6291456]{0:T(1024)(128)(4,1)} %bitcast.366), calls=%async_computation.12 | async-start | bytes 4194304
  509.3 131.1 %collective-permute-start.29 = (bf16[2,2,4,128,1024]{4,3,2,0,1:T(8,128)(2,1)}, bf16[2,2,4,128,1024]{4,3,2,0,1:T(8,128)(2,1)}, u32[]{:S(2)}, u32[]{:S(2)}) collective-permute-start(bf16[2,2,4,128,1024]{4,3,2,0,1:T(8,128)(2,1)} %bitcast.354), channel_id=1, source_target_pairs={{0,1},{1,0},{2,3},{3,2},{4,5},{5,4},{6,7},{7,6},{8,9},{9,8},{10,11... | collective-permute-start | bytes 12582920 | tf_op jit(solution)/shard_map/ppermute | solution.py:170
  511.1 27.6 %slice-start.3 = ((s8[6291456]{0:T(1024)(128)(4,1)}), s8[4194304]{0:T(1024)(128)(4,1)S(1)}, s32[]{:S(2)}) async-start(s8[6291456]{0:T(1024)(128)(4,1)} %bitcast.366), calls=%async_computation.13 | async-start | bytes 8388608
  511.1 11.2 %collective-permute-start.23 = (bf16[128,256]{1,0:T(8,128)(2,1)S(1)}, bf16[128,256]{1,0:T(8,128)(2,1)S(1)}, u32[]{:S(2)}, u32[]{:S(2)}) collective-permute-start(bf16[128,256]{1,0:T(8,128)(2,1)S(1)} %get-tuple-element.119), channel_id=1, source_target_pairs={{0,4},{4,8},{8,12},{1,5},{5,9},{9,13},{2,6},{6,10},{10,14},{3,7},{... | collective-permute-start | bytes 196616 | tf_op jit(solution)/shard_map/ppermute | solution.py:161
  521.0 8.7 %collective-permute-start.26 = (bf16[128,256]{1,0:T(8,128)(2,1)S(1)}, bf16[128,256]{1,0:T(8,128)(2,1)S(1)}, u32[]{:S(2)}, u32[]{:S(2)}) collective-permute-start(bf16[128,256]{1,0:T(8,128)(2,1)S(1)} %get-tuple-element.120), channel_id=1, source_target_pairs={{4,0},{8,4},{12,8},{5,1},{9,5},{13,9},{6,2},{10,6},{14,10},{7,3},{... | collective-permute-start | bytes 196616 | tf_op jit(solution)/shard_map/ppermute | solution.py:162
  522.4 7.4 collective-permute-start.24
  529.8 119.2 %collective-permute-start.38 = (bf16[2,2,4,128,1024]{4,3,2,1,0:T(8,128)(2,1)}, bf16[2,2,4,128,1024]{4,3,2,1,0:T(8,128)(2,1)}, u32[]{:S(2)}, u32[]{:S(2)}) collective-permute-start(bf16[2,2,4,128,1024]{4,3,2,1,0:T(8,128)(2,1)} %dynamic-slice_bitcast_fusion), channel_id=1, source_target_pairs={{0,1},{1,0},{2,3},{3,2},{4,5},{5,4},{6,7},{7,6},{8,9},{9,8},{10,11... | collective-permute-start | bytes 12582920 | tf_op jit(solution)/shard_map/ppermute | solution.py:170
  530.5 36.2 %collective-permute-start.27 = (bf16[128,256]{1,0:T(8,128)(2,1)}, bf16[128,256]{1,0:T(8,128)(2,1)}, u32[]{:S(2)}, u32[]{:S(2)}) collective-permute-start(bf16[128,256]{1,0:T(8,128)(2,1)} %get-tuple-element.118), channel_id=1, source_target_pairs={{4,0},{8,4},{12,8},{5,1},{9,5},{13,9},{6,2},{10,6},{14,10},{7,3},{... | collective-permute-start | bytes 196616 | tf_op jit(solution)/shard_map/ppermute | solution.py:162
  531.8 79.3 %collective-permute-start.25 = (bf16[128,256]{1,0:T(8,128)(2,1)}, bf16[128,256]{1,0:T(8,128)(2,1)S(1)}, u32[]{:S(2)}, u32[]{:S(2)}) collective-permute-start(bf16[128,256]{1,0:T(8,128)(2,1)} %get-tuple-element.117), channel_id=1, source_target_pairs={{0,4},{4,8},{8,12},{1,5},{5,9},{9,13},{2,6},{6,10},{10,14},{3,7},{... | collective-permute-start | bytes 196616 | tf_op jit(solution)/shard_map/ppermute | solution.py:161
  566.6 68.5 %collective-permute-start.2 = (bf16[2,2,4,128,512]{4,3,2,1,0:T(8,128)(2,1)}, bf16[2,2,4,128,512]{4,3,2,1,0:T(8,128)(2,1)}, u32[]{:S(2)}, u32[]{:S(2)}) collective-permute-start(bf16[2,2,4,128,512]{4,3,2,1,0:T(8,128)(2,1)} %bitcast.372), channel_id=1, source_target_pairs={{0,1},{1,0},{2,3},{3,2},{4,5},{5,4},{6,7},{7,6},{8,9},{9,8},{10,11... | collective-permute-start | bytes 6291464 | tf_op jit(solution)/shard_map/ppermute | solution.py:170
  568.1 55.7 %collective-permute-start.28 = (bf16[128,256]{1,0:T(8,128)(2,1)}, bf16[128,256]{1,0:T(8,128)(2,1)}, u32[]{:S(2)}, u32[]{:S(2)}) collective-permute-start(bf16[128,256]{1,0:T(8,128)(2,1)} %fusion.71), channel_id=1, source_target_pairs={{4,0},{8,4},{12,8},{5,1},{9,5},{13,9},{6,2},{10,6},{14,10},{7,3},{... | collective-permute-start | bytes 196616 | tf_op jit(solution)/shard_map/ppermute | solution.py:162
  603.9 14.5 %all-to-all-start.4 = ((f32[32,1,352]{2,1,0:T(1,128)}), f32[32,1,352]{2,1,0:T(1,128)S(1)}, u32[]{:S(2)}, u32[]{:S(2)}) async-start(f32[32,1,352]{2,1,0:T(1,128)} %all_to_all.38), calls=%async_computation.4 | async-start | bytes 98304 | tf_op jit(solution)/shard_map/all_to_all | solution.py:343
  611.1 69.3 %collective-permute-start.11 = (bf16[2,2,4,128,768]{4,3,2,0,1:T(8,128)(2,1)}, bf16[2,2,4,128,768]{4,3,2,0,1:T(8,128)(2,1)}, u32[]{:S(2)}, u32[]{:S(2)}) collective-permute-start(bf16[2,2,4,128,768]{4,3,2,0,1:T(8,128)(2,1)} %bitcast.369), channel_id=1, source_target_pairs={{0,1},{1,0},{2,3},{3,2},{4,5},{5,4},{6,7},{7,6},{8,9},{9,8},{10,11... | collective-permute-start | bytes 9437192 | tf_op jit(solution)/shard_map/ppermute | solution.py:170
  618.4 100.9 %all-to-all-start.3 = ((bf16[16,128,512]{2,1,0:T(8,128)(2,1)}), bf16[16,128,512]{2,1,0:T(8,128)(2,1)}, u32[]{:S(2)}, u32[]{:S(2)}) async-start(bf16[16,128,512]{2,1,0:T(8,128)(2,1)} %bitcast.361), calls=%async_computation.3 | async-start | bytes 4194304 | tf_op jit(solution)/shard_map/all_to_all | solution.py:255
  638.3 36.0 %collective-permute-start.3 = (bf16[2,4,128,512]{3,2,1,0:T(8,128)(2,1)S(1)}, bf16[2,4,128,512]{3,2,1,0:T(8,128)(2,1)S(1)}, u32[]{:S(2)}, u32[]{:S(2)}) collective-permute-start(bf16[2,4,128,512]{3,2,1,0:T(8,128)(2,1)S(1)} %dynamic-slice_bitcast_fusion.6), channel_id=1, source_target_pairs={{0,2},{1,3},{2,0},{3,1},{4,6},{5,7},{6,4},{7,5},{8,10},{9,11},{10,... | collective-permute-start | bytes 3145736 | tf_op jit(solution)/shard_map/ppermute | solution.py:170
  647.5 86.2 %collective-permute-start.30 = (bf16[2,4,128,1024]{3,2,1,0:T(8,128)(2,1)}, bf16[2,4,128,1024]{3,2,1,0:T(8,128)(2,1)}, u32[]{:S(2)}, u32[]{:S(2)}) collective-permute-start(bf16[2,4,128,1024]{3,2,1,0:T(8,128)(2,1)} %dynamic-slice_bitcast_fusion.2), channel_id=1, source_target_pairs={{0,16},{16,0},{1,17},{17,1},{2,18},{18,2},{3,19},{19,3},{4,20},{20... | collective-permute-start | bytes 6291464 | tf_op jit(solution)/shard_map/ppermute | solution.py:170
  653.3 22.9 %copy-start.7 = (bf16[2,2,4,128,1024]{4,3,2,1,0:T(8,128)(2,1)}, bf16[2,2,4,128,1024]{4,3,2,1,0:T(8,128)(2,1)S(1)}, u32[]{:S(2)}) copy-start(bf16[2,2,4,128,1024]{4,3,2,1,0:T(8,128)(2,1)S(1)} %fusion.6) | copy-start | bytes 12582916
  674.7 31.7 %collective-permute-start.4 = (bf16[4,128,512]{2,1,0:T(8,128)(2,1)S(1)}, bf16[4,128,512]{2,1,0:T(8,128)(2,1)S(1)}, u32[]{:S(2)}, u32[]{:S(2)}) collective-permute-start(bf16[4,128,512]{2,1,0:T(8,128)(2,1)S(1)} %dynamic-slice_bitcast_fusion.9), channel_id=1, source_target_pairs={{0,16},{16,0},{1,17},{17,1},{2,18},{18,2},{3,19},{19,3},{4,20},{20... | collective-permute-start | bytes 1572872 | tf_op jit(solution)/shard_map/ppermute | solution.py:170
  677.9 60.3 %collective-permute-start.39 = (bf16[2,4,128,1024]{3,2,1,0:T(8,128)(2,1)}, bf16[2,4,128,1024]{3,2,1,0:T(8,128)(2,1)}, u32[]{:S(2)}, u32[]{:S(2)}) collective-permute-start(bf16[2,4,128,1024]{3,2,1,0:T(8,128)(2,1)} %dynamic-slice_bitcast_fusion.1), channel_id=1, source_target_pairs={{0,2},{1,3},{2,0},{3,1},{4,6},{5,7},{6,4},{7,5},{8,10},{9,11},{10,... | collective-permute-start | bytes 6291464 | tf_op jit(solution)/shard_map/ppermute | solution.py:170
  706.6 7.4 collective-permute-start.5
  711.2 37.6 %collective-permute-start.12 = (bf16[2,4,128,768]{3,2,1,0:T(8,128)(2,1)}, bf16[2,4,128,768]{3,2,1,0:T(8,128)(2,1)}, u32[]{:S(2)}, u32[]{:S(2)}) collective-permute-start(bf16[2,4,128,768]{3,2,1,0:T(8,128)(2,1)} %dynamic-slice_bitcast_fusion.3), channel_id=1, source_target_pairs={{0,16},{16,0},{1,17},{17,1},{2,18},{18,2},{3,19},{19,3},{4,20},{20... | collective-permute-start | bytes 4718600 | tf_op jit(solution)/shard_map/ppermute | solution.py:170
  712.7 9.6 %collective-permute-start.8 = (bf16[128,512]{1,0:T(8,128)(2,1)S(1)}, bf16[128,512]{1,0:T(8,128)(2,1)S(1)}, u32[]{:S(2)}, u32[]{:S(2)}) collective-permute-start(bf16[128,512]{1,0:T(8,128)(2,1)S(1)} %get-tuple-element.116), channel_id=1, source_target_pairs={{4,0},{8,4},{12,8},{5,1},{9,5},{13,9},{6,2},{10,6},{14,10},{7,3},{... | collective-permute-start | bytes 393224 | tf_op jit(solution)/shard_map/ppermute | solution.py:162
  714.1 8.2 collective-permute-start.6
  723.5 8.6 %collective-permute-start.9 = (bf16[128,512]{1,0:T(8,128)(2,1)S(1)}, bf16[128,512]{1,0:T(8,128)(2,1)S(1)}, u32[]{:S(2)}, u32[]{:S(2)}) collective-permute-start(bf16[128,512]{1,0:T(8,128)(2,1)S(1)} %get-tuple-element.114), channel_id=1, source_target_pairs={{4,0},{8,4},{12,8},{5,1},{9,5},{13,9},{6,2},{10,6},{14,10},{7,3},{... | collective-permute-start | bytes 393224 | tf_op jit(solution)/shard_map/ppermute | solution.py:162
  727.4 16.3 %collective-permute-start.7 = (bf16[128,512]{1,0:T(8,128)(2,1)S(1)}, bf16[128,512]{1,0:T(8,128)(2,1)S(1)}, u32[]{:S(2)}, u32[]{:S(2)}) collective-permute-start(bf16[128,512]{1,0:T(8,128)(2,1)S(1)} %get-tuple-element.113), channel_id=1, source_target_pairs={{0,4},{4,8},{8,12},{1,5},{5,9},{9,13},{2,6},{6,10},{10,14},{3,7},{... | collective-permute-start | bytes 393224 | tf_op jit(solution)/shard_map/ppermute | solution.py:161
  732.1 11.6 %collective-permute-start.10 = (bf16[128,512]{1,0:T(8,128)(2,1)S(1)}, bf16[128,512]{1,0:T(8,128)(2,1)S(1)}, u32[]{:S(2)}, u32[]{:S(2)}) collective-permute-start(bf16[128,512]{1,0:T(8,128)(2,1)S(1)} %fusion.66), channel_id=1, source_target_pairs={{4,0},{8,4},{12,8},{5,1},{9,5},{13,9},{6,2},{10,6},{14,10},{7,3},{... | collective-permute-start | bytes 393224 | tf_op jit(solution)/shard_map/ppermute | solution.py:162
  737.6 26.4 %collective-permute-start.31 = (bf16[4,128,1024]{2,1,0:T(8,128)(2,1)}, bf16[4,128,1024]{2,1,0:T(8,128)(2,1)}, u32[]{:S(2)}, u32[]{:S(2)}) collective-permute-start(bf16[4,128,1024]{2,1,0:T(8,128)(2,1)} %dynamic-slice_bitcast_fusion.5), channel_id=1, source_target_pairs={{0,2},{1,3},{2,0},{3,1},{4,6},{5,7},{6,4},{7,5},{8,10},{9,11},{10,... | collective-permute-start | bytes 3145736 | tf_op jit(solution)/shard_map/ppermute | solution.py:170
  743.2 28.4 %collective-permute-start.40 = (bf16[4,128,1024]{2,1,0:T(8,128)(2,1)}, bf16[4,128,1024]{2,1,0:T(8,128)(2,1)}, u32[]{:S(2)}, u32[]{:S(2)}) collective-permute-start(bf16[4,128,1024]{2,1,0:T(8,128)(2,1)} %dynamic-slice_bitcast_fusion.4), channel_id=1, source_target_pairs={{0,16},{16,0},{1,17},{17,1},{2,18},{18,2},{3,19},{19,3},{4,20},{20... | collective-permute-start | bytes 3145736 | tf_op jit(solution)/shard_map/ppermute | solution.py:170
  750.7 20.9 %copy-start.16 = (bf16[2,4,128,1024]{3,2,1,0:T(8,128)(2,1)S(1)}, bf16[2,4,128,1024]{3,2,1,0:T(8,128)(2,1)}, u32[]{:S(2)}) copy-start(bf16[2,4,128,1024]{3,2,1,0:T(8,128)(2,1)} %copy-done.15) | copy-start | bytes 6291460
  750.7 28.5 %collective-permute-start.13 = (bf16[4,128,768]{2,1,0:T(8,128)(2,1)S(1)}, bf16[4,128,768]{2,1,0:T(8,128)(2,1)S(1)}, u32[]{:S(2)}, u32[]{:S(2)}) collective-permute-start(bf16[4,128,768]{2,1,0:T(8,128)(2,1)S(1)} %dynamic-slice_bitcast_fusion.7), channel_id=1, source_target_pairs={{0,2},{1,3},{2,0},{3,1},{4,6},{5,7},{6,4},{7,5},{8,10},{9,11},{10,... | collective-permute-start | bytes 2359304 | tf_op jit(solution)/shard_map/ppermute | solution.py:170
  765.7 18.3 %collective-permute-start.32 = (bf16[128,1024]{1,0:T(8,128)(2,1)S(1)}, bf16[128,1024]{1,0:T(8,128)(2,1)S(1)}, u32[]{:S(2)}, u32[]{:S(2)}) collective-permute-start(bf16[128,1024]{1,0:T(8,128)(2,1)S(1)} %get-tuple-element.104), channel_id=1, source_target_pairs={{0,4},{4,8},{8,12},{1,5},{5,9},{9,13},{2,6},{6,10},{10,14},{3,7},{... | collective-permute-start | bytes 786440 | tf_op jit(solution)/shard_map/ppermute | solution.py:161
  770.3 23.5 %collective-permute-start.35 = (bf16[128,1024]{1,0:T(8,128)(2,1)S(1)}, bf16[128,1024]{1,0:T(8,128)(2,1)S(1)}, u32[]{:S(2)}, u32[]{:S(2)}) collective-permute-start(bf16[128,1024]{1,0:T(8,128)(2,1)S(1)} %get-tuple-element.105), channel_id=1, source_target_pairs={{4,0},{8,4},{12,8},{5,1},{9,5},{13,9},{6,2},{10,6},{14,10},{7,3},{... | collective-permute-start | bytes 786440 | tf_op jit(solution)/shard_map/ppermute | solution.py:162
  773.3 12.1 %collective-permute-start.41 = (bf16[128,1024]{1,0:T(8,128)(2,1)S(1)}, bf16[128,1024]{1,0:T(8,128)(2,1)S(1)}, u32[]{:S(2)}, u32[]{:S(2)}) collective-permute-start(bf16[128,1024]{1,0:T(8,128)(2,1)S(1)} %get-tuple-element.100), channel_id=1, source_target_pairs={{0,4},{4,8},{8,12},{1,5},{5,9},{9,13},{2,6},{6,10},{10,14},{3,7},{... | collective-permute-start | bytes 786440 | tf_op jit(solution)/shard_map/ppermute | solution.py:161
  777.9 21.2 %collective-permute-start.44 = (bf16[128,1024]{1,0:T(8,128)(2,1)S(1)}, bf16[128,1024]{1,0:T(8,128)(2,1)S(1)}, u32[]{:S(2)}, u32[]{:S(2)}) collective-permute-start(bf16[128,1024]{1,0:T(8,128)(2,1)S(1)} %get-tuple-element.101), channel_id=1, source_target_pairs={{4,0},{8,4},{12,8},{5,1},{9,5},{13,9},{6,2},{10,6},{14,10},{7,3},{... | collective-permute-start | bytes 786440 | tf_op jit(solution)/shard_map/ppermute | solution.py:162
  779.5 10.6 %collective-permute-start.14 = (bf16[128,768]{1,0:T(8,128)(2,1)S(1)}, bf16[128,768]{1,0:T(8,128)(2,1)S(1)}, u32[]{:S(2)}, u32[]{:S(2)}) collective-permute-start(bf16[128,768]{1,0:T(8,128)(2,1)S(1)} %get-tuple-element.111), channel_id=1, source_target_pairs={{0,4},{4,8},{8,12},{1,5},{5,9},{9,13},{2,6},{6,10},{10,14},{3,7},{... | collective-permute-start | bytes 589832 | tf_op jit(solution)/shard_map/ppermute | solution.py:161
  784.0 22.1 %collective-permute-start.17 = (bf16[128,768]{1,0:T(8,128)(2,1)S(1)}, bf16[128,768]{1,0:T(8,128)(2,1)S(1)}, u32[]{:S(2)}, u32[]{:S(2)}) collective-permute-start(bf16[128,768]{1,0:T(8,128)(2,1)S(1)} %get-tuple-element.112), channel_id=1, source_target_pairs={{4,0},{8,4},{12,8},{5,1},{9,5},{13,9},{6,2},{10,6},{14,10},{7,3},{... | collective-permute-start | bytes 589832 | tf_op jit(solution)/shard_map/ppermute | solution.py:162
  785.4 11.5 %collective-permute-start.33 = (bf16[128,1024]{1,0:T(8,128)(2,1)S(1)}, bf16[128,1024]{1,0:T(8,128)(2,1)S(1)}, u32[]{:S(2)}, u32[]{:S(2)}) collective-permute-start(bf16[128,1024]{1,0:T(8,128)(2,1)S(1)} %fusion.52), channel_id=1, source_target_pairs={{0,4},{4,8},{8,12},{1,5},{5,9},{9,13},{2,6},{6,10},{10,14},{3,7},{... | collective-permute-start | bytes 786440 | tf_op jit(solution)/shard_map/ppermute | solution.py:161
  790.1 13.9 %collective-permute-start.42 = (bf16[128,1024]{1,0:T(8,128)(2,1)S(1)}, bf16[128,1024]{1,0:T(8,128)(2,1)S(1)}, u32[]{:S(2)}, u32[]{:S(2)}) collective-permute-start(bf16[128,1024]{1,0:T(8,128)(2,1)S(1)} %fusion.47), channel_id=1, source_target_pairs={{0,4},{4,8},{8,12},{1,5},{5,9},{9,13},{2,6},{6,10},{10,14},{3,7},{... | collective-permute-start | bytes 786440 | tf_op jit(solution)/shard_map/ppermute | solution.py:161
  793.8 16.9 %collective-permute-start.15 = (bf16[128,768]{1,0:T(8,128)(2,1)S(1)}, bf16[128,768]{1,0:T(8,128)(2,1)S(1)}, u32[]{:S(2)}, u32[]{:S(2)}) collective-permute-start(bf16[128,768]{1,0:T(8,128)(2,1)S(1)} %fusion.62), channel_id=1, source_target_pairs={{0,4},{4,8},{8,12},{1,5},{5,9},{9,13},{2,6},{6,10},{10,14},{3,7},{... | collective-permute-start | bytes 589832 | tf_op jit(solution)/shard_map/ppermute | solution.py:161
  797.8 14.4 %collective-permute-start.36 = (bf16[128,1024]{1,0:T(8,128)(2,1)S(1)}, bf16[128,1024]{1,0:T(8,128)(2,1)S(1)}, u32[]{:S(2)}, u32[]{:S(2)}) collective-permute-start(bf16[128,1024]{1,0:T(8,128)(2,1)S(1)} %get-tuple-element.103), channel_id=1, source_target_pairs={{4,0},{8,4},{12,8},{5,1},{9,5},{13,9},{6,2},{10,6},{14,10},{7,3},{... | collective-permute-start | bytes 786440 | tf_op jit(solution)/shard_map/ppermute | solution.py:162
  799.1 33.2 %collective-permute-start.34 = (bf16[128,1024]{1,0:T(8,128)(2,1)}, bf16[128,1024]{1,0:T(8,128)(2,1)S(1)}, u32[]{:S(2)}, u32[]{:S(2)}) collective-permute-start(bf16[128,1024]{1,0:T(8,128)(2,1)} %get-tuple-element.102), channel_id=1, source_target_pairs={{0,4},{4,8},{8,12},{1,5},{5,9},{9,13},{2,6},{6,10},{10,14},{3,7},{... | collective-permute-start | bytes 786440 | tf_op jit(solution)/shard_map/ppermute | solution.py:161
  804.9 17.1 %collective-permute-start.45 = (bf16[128,1024]{1,0:T(8,128)(2,1)S(1)}, bf16[128,1024]{1,0:T(8,128)(2,1)S(1)}, u32[]{:S(2)}, u32[]{:S(2)}) collective-permute-start(bf16[128,1024]{1,0:T(8,128)(2,1)S(1)} %get-tuple-element.99), channel_id=1, source_target_pairs={{4,0},{8,4},{12,8},{5,1},{9,5},{13,9},{6,2},{10,6},{14,10},{7,3},{... | collective-permute-start | bytes 786440 | tf_op jit(solution)/shard_map/ppermute | solution.py:162
  806.2 28.0 %collective-permute-start.43 = (bf16[128,1024]{1,0:T(8,128)(2,1)}, bf16[128,1024]{1,0:T(8,128)(2,1)S(1)}, u32[]{:S(2)}, u32[]{:S(2)}) collective-permute-start(bf16[128,1024]{1,0:T(8,128)(2,1)} %get-tuple-element.98), channel_id=1, source_target_pairs={{0,4},{4,8},{8,12},{1,5},{5,9},{9,13},{2,6},{6,10},{10,14},{3,7},{... | collective-permute-start | bytes 786440 | tf_op jit(solution)/shard_map/ppermute | solution.py:161
  810.9 9.7 %collective-permute-start.18 = (bf16[128,768]{1,0:T(8,128)(2,1)S(1)}, bf16[128,768]{1,0:T(8,128)(2,1)S(1)}, u32[]{:S(2)}, u32[]{:S(2)}) collective-permute-start(bf16[128,768]{1,0:T(8,128)(2,1)S(1)} %get-tuple-element.110), channel_id=1, source_target_pairs={{4,0},{8,4},{12,8},{5,1},{9,5},{13,9},{6,2},{10,6},{14,10},{7,3},{... | collective-permute-start | bytes 589832 | tf_op jit(solution)/shard_map/ppermute | solution.py:162
  812.2 11.9 %collective-permute-start.16 = (bf16[128,768]{1,0:T(8,128)(2,1)S(1)}, bf16[128,768]{1,0:T(8,128)(2,1)S(1)}, u32[]{:S(2)}, u32[]{:S(2)}) collective-permute-start(bf16[128,768]{1,0:T(8,128)(2,1)S(1)} %get-tuple-element.109), channel_id=1, source_target_pairs={{0,4},{4,8},{8,12},{1,5},{5,9},{9,13},{2,6},{6,10},{10,14},{3,7},{... | collective-permute-start | bytes 589832 | tf_op jit(solution)/shard_map/ppermute | solution.py:161
  820.6 11.7 %collective-permute-start.37 = (bf16[128,1024]{1,0:T(8,128)(2,1)}, bf16[128,1024]{1,0:T(8,128)(2,1)}, u32[]{:S(2)}, u32[]{:S(2)}) collective-permute-start(bf16[128,1024]{1,0:T(8,128)(2,1)} %fusion.51), channel_id=1, source_target_pairs={{4,0},{8,4},{12,8},{5,1},{9,5},{13,9},{6,2},{10,6},{14,10},{7,3},{... | collective-permute-start | bytes 786440 | tf_op jit(solution)/shard_map/ppermute | solution.py:162
  822.0 9.2 %collective-permute-start.19 = (bf16[128,768]{1,0:T(8,128)(2,1)S(1)}, bf16[128,768]{1,0:T(8,128)(2,1)S(1)}, u32[]{:S(2)}, u32[]{:S(2)}) collective-permute-start(bf16[128,768]{1,0:T(8,128)(2,1)S(1)} %fusion.61), channel_id=1, source_target_pairs={{4,0},{8,4},{12,8},{5,1},{9,5},{13,9},{6,2},{10,6},{14,10},{7,3},{... | collective-permute-start | bytes 589832 | tf_op jit(solution)/shard_map/ppermute | solution.py:162
  824.0 10.2 %collective-permute-start.46 = (bf16[128,1024]{1,0:T(8,128)(2,1)}, bf16[128,1024]{1,0:T(8,128)(2,1)}, u32[]{:S(2)}, u32[]{:S(2)}) collective-permute-start(bf16[128,1024]{1,0:T(8,128)(2,1)} %fusion.46), channel_id=1, source_target_pairs={{4,0},{8,4},{12,8},{5,1},{9,5},{13,9},{6,2},{10,6},{14,10},{7,3},{... | collective-permute-start | bytes 786440 | tf_op jit(solution)/shard_map/ppermute | solution.py:162
  (44 other events, 270.7 us)
Sparse Core Ops, SparseCore 0:
  11.6 84.6 all-gather.6
  99.7 86.8 all-gather.8
  189.6 54.7 all-gather.10
  247.2 76.2 all-gather.12
  326.3 75.9 all-gather.14

commit v2 on v1

v2 whole, which is shorter than its diff:
```python
import functools

import jax
import jax.numpy as jnp
from jax import lax
from jax.experimental import pallas as pl
from jax.experimental.pallas import tpu as pltpu
from jax.sharding import PartitionSpec as P

HD = 64
EPSILON = 1e-05
F32 = jnp.float32
BF16 = jnp.bfloat16
ALL = ("fsdp", "ctx", "tp")
PARAMS = pltpu.CompilerParams(vmem_limit_bytes=56 * 1024 * 1024)
CHUNK = 128


def mxu(a, b, a_dim, b_dim):
    return lax.dot_general(a, b, (((a_dim,), (b_dim,)), ((), ())), preferred_element_type=F32)


def whole(shape):
    return pl.BlockSpec(shape, lambda n: (0,) * len(shape))


def call(body, after, *, in_specs, out_specs, out_shape, grid, name, scratch_shapes=()):
    n_in, n_after, n_out = len(in_specs), len(after), len(out_specs)

    def run(*refs):
        outs = refs[n_in + n_after :]
        outs[n_out][...] = jnp.zeros((8, 128), F32)
        body(*refs[:n_in], *outs[:n_out], *outs[n_out + 1 :])

    def apply(*args):
        outs = pl.pallas_call(
            run,
            grid=grid,
            in_specs=[*in_specs, *[pl.BlockSpec(memory_space=pl.ANY)] * n_after],
            out_specs=[*out_specs, pl.BlockSpec((8, 128), lambda n: (0, 0))],
            out_shape=[*out_shape, jax.ShapeDtypeStruct((8, 128), F32)],
            scratch_shapes=scratch_shapes,
            compiler_params=PARAMS,
            cost_estimate=pl.CostEstimate(flops=1, bytes_accessed=1, transcendentals=0),
            name=name,
        )(*args, *after)
        return outs[:-1], outs[-1]

    return apply


def attend_forward_body(share, heads, *refs):
    own, others = refs[0], refs[1:share]
    p_ref, o_ref = refs[share:]
    part = heads * HD
    rows = lax.broadcasted_iota(jnp.int32, (part, own.shape[1]), 0) // HD
    lanes = lax.broadcasted_iota(jnp.int32, (own.shape[1], part), 1) // HD
    q = own[0, :, :part] * jnp.asarray(HD**-0.5, BF16)
    k = jnp.concatenate([r[0, :, part : 2 * part] for r in (own, *others)], axis=0)
    v = jnp.concatenate([r[0, :, 2 * part :] for r in (own, *others)], axis=0)
    total = jnp.zeros((part, q.shape[0]), F32)
    for h in range(heads):
        s = mxu(k, jnp.where(lanes == h, q, jnp.zeros_like(q)), 1, 1)
        p = jnp.exp(s - jnp.max(s, axis=0, keepdims=True))
        low = (p * (1.0 / jnp.sum(p, axis=0, keepdims=True))).astype(BF16)
        p_ref[0, h] = low
        total = total + jnp.where(rows == h, mxu(v, low, 0, 0), 0.0)
    o_ref[0] = total.T.astype(BF16)


def other_specs(share, shape):
    return [pl.BlockSpec(shape, lambda x, d=d: (x ^ (d >> 1), 0, 0)) for d in range(1, share)]


def attend_forward(after, own, others):
    blocks, count, cols = own.shape
    share = 1 + len(others)
    part = cols // 3
    heads = part // HD
    return call(
        functools.partial(attend_forward_body, share, heads),
        after,
        grid=(blocks,),
        in_specs=[pl.BlockSpec((1, count, cols), lambda x: (x, 0, 0))] + other_specs(share, (1, count, cols)),
        out_specs=[
            pl.BlockSpec((1, heads, share * count, count), lambda x: (x, 0, 0, 0)),
            pl.BlockSpec((1, count, part), lambda x: (x, 0, 0)),
        ],
        out_shape=[
            jax.ShapeDtypeStruct((blocks, heads, share * count, count), BF16),
            jax.ShapeDtypeStruct((blocks, count, part), BF16),
        ],
        name="attend_forward",
    )(own, *others)


def attend_backward_body(share, heads, *refs):
    own, others = refs[0], refs[1:share]
    p_ref, o_ref, g_ref = refs[share : share + 3]
    outs = refs[share + 3 :]
    part = heads * HD
    count = own.shape[1]
    q = own[0, :, :part] * jnp.asarray(HD**-0.5, BF16)
    k = jnp.concatenate([r[0, :, part : 2 * part] for r in (own, *others)], axis=0)
    v = jnp.concatenate([r[0, :, 2 * part :] for r in (own, *others)], axis=0)
    g = g_ref[0]
    rows = lax.broadcasted_iota(jnp.int32, (part, count), 0) // HD
    lanes = lax.broadcasted_iota(jnp.int32, (count, part), 1) // HD
    prod = (g.astype(F32) * o_ref[0].astype(F32)).T
    dq = jnp.zeros((part, count), F32)
    dk = jnp.zeros((share * count, part), F32)
    dv = jnp.zeros((share * count, part), F32)
    for h in range(heads):
        q_h = jnp.where(lanes == h, q, jnp.zeros_like(q))
        g_h = jnp.where(lanes == h, g, jnp.zeros_like(g))
        p = p_ref[0, h]
        delta = jnp.sum(prod[h * HD : (h + 1) * HD], axis=0, keepdims=True)
        ds = (p.astype(F32) * (mxu(v, g_h, 1, 1) - delta)).astype(BF16)
        dq = dq + jnp.where(rows == h, mxu(k, ds, 0, 0), 0.0)
        dk = dk + mxu(ds, q_h, 1, 0)
        dv = dv + mxu(p, g_h, 1, 0)
    outs[0][0, :, :part] = (dq.T * (HD**-0.5)).astype(BF16)
    outs[0][0, :, part : 2 * part] = dk[:count].astype(BF16)
    outs[0][0, :, 2 * part :] = dv[:count].astype(BF16)
    for d in range(1, share):
        outs[d][0, :, :part] = dk[d * count : (d + 1) * count].astype(BF16)
        outs[d][0, :, part:] = dv[d * count : (d + 1) * count].astype(BF16)


def attend_backward(after, own, others, probs, attended, grad):
    blocks, count, cols = own.shape
    share = 1 + len(others)
    part = cols // 3
    heads = part // HD
    spec = pl.BlockSpec((1, count, cols), lambda x: (x, 0, 0))
    o_spec = pl.BlockSpec((1, count, part), lambda x: (x, 0, 0))
    p_spec = pl.BlockSpec((1, heads, share * count, count), lambda x: (x, 0, 0, 0))
    return call(
        functools.partial(attend_backward_body, share, heads),
        after,
        grid=(blocks,),
        in_specs=[spec] + other_specs(share, (1, count, cols)) + [p_spec, o_spec, o_spec],
        out_specs=[spec] + other_specs(share, (1, count, 2 * part)),
        out_shape=[jax.ShapeDtypeStruct((blocks, count, cols), BF16)]
        + [jax.ShapeDtypeStruct((blocks, count, 2 * part), BF16)] * (share - 1),
        name="attend_backward",
    )(own, *others, probs, attended, grad)


def tree(w):
    return [h[0] for k in w for x in k for h in x]


def weight_specs(w, shape, index):
    return [
        pl.BlockSpec((None, *shape), lambda n, h=h, lead=lead: (lead, *index(h, n)))
        for k in w
        for x in k
        for h, (_, lead) in enumerate(x)
    ]


def up_body(ks, parts, step, *refs):
    left = refs[0]
    count = len(ks) * 2 * parts
    rows = left.shape[1] // parts
    for i in range(len(ks)):
        for x in range(2):
            total = None
            for h in range(parts):
                term = mxu(left[:, h * rows : (h + 1) * rows], refs[1 + (i * 2 + x) * parts + h][...], 1, 0)
                total = term if total is None else total + term
            step(i, x, total, refs[1 + count :])


def up(after, name, left, weights, width, col, step, extras, outs, tile):
    parts = len(weights[0][0])
    rows = weights[0][0][0][0].shape[1]
    per = width // tile
    count = left.shape[0]
    return call(
        functools.partial(up_body, range(len(weights)), parts, step),
        after,
        grid=(per,),
        in_specs=[whole((count, parts * rows))]
        + weight_specs(weights, (rows, tile), lambda h, n: (0, col * per + n))
        + [pl.BlockSpec((2, e.shape[1], tile), lambda n: (0, 0, n)) for e in extras],
        out_specs=[pl.BlockSpec((2, o[0], tile), lambda n: (0, 0, n)) for o in outs],
        out_shape=[jax.ShapeDtypeStruct((2, o[0], width), o[1]) for o in outs],
        name=name,
    )(left, *tree(weights), *extras)


def plain_step(i, x, total, refs):
    refs[i][x] = total.astype(BF16)


def gelu_step(i, x, total, refs):
    bias, act, slope = refs
    v = total + bias[x]
    half = 0.5 * (1.0 + lax.erf(v * (0.5**0.5)))
    act[x] = (v * half).astype(BF16)
    slope[x] = (half + v * jnp.exp(-0.5 * v * v) * 0.3989422804014327).astype(BF16)


def slope_step(i, x, total, refs):
    slope, grad, sums = refs
    low = (total * slope[x].astype(F32)).astype(BF16)
    grad[x] = low
    sums[x] = jnp.sum(low.astype(F32), axis=0, keepdims=True)


def down_body(parts, per, finish, n_out, *refs):
    lefts = refs[:2]
    weights = refs[2 : 2 + 4 * parts]
    rest = refs[2 + 4 * parts : -1]
    acc = refs[-1]
    n = pl.program_id(0)
    for h in range(parts):

        @pl.when(n // per == h)
        def _():
            total = None
            for k in range(2):
                for x in range(2):
                    term = mxu(lefts[k][x], weights[(k * 2 + x) * parts + h][...], 1, 1)
                    total = term if total is None else total + term
            acc[n] = total

    @pl.when(n == parts * per - 1)
    def _():
        finish(acc, rest)


def down(after, name, lefts, weights, width, col, finish, extras, outs):
    parts = len(weights[0][0])
    rows = weights[0][0][0][0].shape[1]
    tile = min(256, rows)
    per = rows // tile
    count = lefts[0].shape[1]
    return call(
        functools.partial(down_body, parts, per, finish, len(outs)),
        after,
        grid=(parts * per,),
        in_specs=[whole((2, count, width))] * 2
        + weight_specs(weights, (tile, width), lambda h, n: (jnp.clip(n - h * per, 0, per - 1), col))
        + [whole(e.shape) for e in extras],
        out_specs=[whole(o[0]) for o in outs],
        out_shape=[jax.ShapeDtypeStruct(*o) for o in outs],
        scratch_shapes=[pltpu.VMEM((parts * per, count, tile), F32)],
        name=name,
    )(*lefts, *tree(weights), *extras)


def row_mean(tiles):
    total = sum(jnp.sum(t, axis=-1, keepdims=True) for t in tiles)
    return total / sum(t.shape[-1] for t in tiles)


def norm_finish(has_residual, acc, refs):
    refs = list(refs)
    residual = refs.pop(0) if has_residual else None
    rows, total_ref, low_ref, low_t_ref = refs
    tiles, count, width = acc.shape
    for r in range(0, count, CHUNK):
        rr = pl.ds(r, CHUNK)
        total = []
        for i in range(tiles):
            cc = slice(i * width, (i + 1) * width)
            v = acc[i, rr, :] + rows[0:1, cc]
            if residual is not None:
                v = v + residual[rr, cc]
            total_ref[rr, cc] = v
            total.append(v)
        mean = row_mean(total)
        center = [t - mean for t in total]
        scale = lax.rsqrt(row_mean([c * c for c in center]) + EPSILON)
        for i in range(tiles):
            cc = slice(i * width, (i + 1) * width)
            v = center[i] * scale * rows[1:2, cc] + rows[2:3, cc]
            low_ref[rr, cc] = v.astype(BF16)
            low_t_ref[cc, rr] = v.T.astype(BF16)


def norm_back_finish(keep, acc, refs):
    total_ref, up_ref, rows, *outs = refs
    full_ref = outs.pop(0) if keep else None
    low_ref, low_t_ref, sums_ref = outs
    tiles, count, width = acc.shape
    zero = jnp.zeros((1, width), F32)
    sums = [[zero] * tiles for _ in range(4)]
    for r in range(0, count, CHUNK):
        rr = pl.ds(r, CHUNK)
        cuts = [slice(i * width, (i + 1) * width) for i in range(tiles)]
        total = [total_ref[rr, cc] for cc in cuts]
        mean = row_mean(total)
        center = [t - mean for t in total]
        scale = lax.rsqrt(row_mean([c * c for c in center]) + EPSILON)
        unit = [c * scale for c in center]
        grad = [acc[i, rr, :] for i in range(tiles)]
        z = [g * rows[0:1, cc] for g, cc in zip(grad, cuts)]
        z_mean = row_mean(z)
        zu_mean = row_mean([a * b for a, b in zip(z, unit)])
        for i, cc in enumerate(cuts):
            up_now = up_ref[rr, cc].astype(F32)
            v = up_now + scale * (z[i] - z_mean - unit[i] * zu_mean)
            if keep:
                full_ref[rr, cc] = v
            low_ref[rr, cc] = v.astype(BF16)
            low_t_ref[cc, rr] = v.T.astype(BF16)
            for j, s in enumerate((v, grad[i] * unit[i], grad[i], up_now)):
                sums[j][i] = sums[j][i] + jnp.sum(s, axis=0, keepdims=True)
    for j in range(4):
        for i in range(tiles):
            sums_ref[j : j + 1, i * width : (i + 1) * width] = sums[j][i]


def out_finish(acc, refs):
    total_ref, rows, low_ref = refs
    tiles, count, width = acc.shape
    for i in range(tiles):
        cc = slice(i * width, (i + 1) * width)
        v = (acc[i] + total_ref[:, cc] + rows[0:1, cc]) * rows[1:2, cc]
        low_ref[:, cc] = v.astype(BF16)


def weight_grad_body(n_parts, parts, by_x, has_more, *refs):
    lefts = refs[: n_parts * parts]
    rights = refs[n_parts * parts : n_parts * (parts + 1)]
    more = refs[n_parts * (parts + 1) :]
    n_out = 2 if by_x else parts
    outs = more[-n_out:]
    for x in range(2):
        for h in range(parts):
            i, j = (x, h) if by_x else (h, x)
            at = 0
            for p in range(n_parts):
                total = mxu(lefts[p * parts + h][...], rights[p][x], 1, 0)
                cc = slice(at, at + total.shape[1])
                at = cc.stop
                if has_more:
                    total = total + more[i][j, :, cc].astype(F32)
                outs[i][j, :, cc] = total.astype(BF16)


def weight_grad(after, lefts, rights, parts, by_x, more=()):
    depth, count = lefts[0].shape
    rows = depth // parts
    tile = min(256, rows)
    per = rows // tile
    cols = sum(r.shape[2] for r in rights)
    n_out, lead = (2, parts) if by_x else (parts, 2)
    out_spec = pl.BlockSpec((lead, tile, cols), lambda n: (0, n, 0))
    return call(
        functools.partial(weight_grad_body, len(lefts), parts, by_x, bool(more)),
        after,
        grid=(per,),
        in_specs=[
            pl.BlockSpec((tile, count), lambda n, h=h: (h * per + n, 0)) for _ in lefts for h in range(parts)
        ]
        + [whole(r.shape) for r in rights]
        + [out_spec] * len(more),
        out_specs=[out_spec] * n_out,
        out_shape=[jax.ShapeDtypeStruct((lead, rows, cols), BF16)] * n_out,
        name="weight_grad",
    )(*[left for left in lefts for _ in range(parts)], *rights, *more)


def pick(array, index, axis=0):
    return lax.dynamic_index_in_dim(array, index, axis, keepdims=False)


def add(*terms):
    return sum(t.astype(F32) for t in terms).astype(BF16)


class Line:
    def __init__(self):
        self.marks = []

    def gate(self, *arrays):
        leaves, form = jax.tree.flatten(arrays)
        places = [i for i, leaf in enumerate(leaves) if isinstance(leaf, jax.Array)]
        held, self.marks = lax.optimization_barrier(([leaves[i] for i in places], self.marks))
        for i, array in zip(places, held):
            leaves[i] = array
        arrays = jax.tree.unflatten(form, leaves)
        return arrays[0] if len(arrays) == 1 else arrays

    def plain(self, step, *args):
        out = step(*self.gate(args, ())[0])
        self.marks = self.marks + jax.tree.leaves(out)
        return out

    def __call__(self, step, *args):
        args = self.gate(args, ())[0]
        out, mark = step(self.marks, *args)
        self.marks = [mark]
        return out


def on_device(
    sizes,
    tokens,
    skip_tokens,
    merger_weight,
    merger_bias,
    first_gain,
    first_shift,
    attend_weight,
    output_weight,
    output_bias,
    second_gain,
    second_shift,
    expand_weight,
    widen_bias,
    shrink_weight,
    shrink_bias,
    live_slots,
    cotangent,
):
    fs, cs, ts = sizes
    assert ts == 4
    f_rank, c_rank, t_rank = (lax.axis_index(a) for a in ALL)
    group = cs * ts
    devices = fs * group
    batches, local_seqs, local_len, part_width = tokens.shape
    slots = batches * local_seqs
    share = group // slots
    assert share in (1, 2, 4)
    fine = cotangent.shape[2] // share
    width = cotangent.shape[3]
    count = group * fine
    hidden = expand_weight.shape[1]
    rows = width // (fs * cs)
    line = Line()

    def to_group(array):
        return lax.all_to_all(array, ("ctx", "tp"), 0, 0, tiled=True)

    def over_tp(array, flip):
        return lax.ppermute(array, "tp", [(i, i ^ flip) for i in range(ts)])

    def over_ctx(array, d):
        return lax.ppermute(array, "ctx", [(i, (i + d) % cs) for i in range(cs)])

    def over_fsdp(array, d):
        return lax.ppermute(array, "fsdp", [(i, (i + d) % fs) for i in range(fs)])

    def gather_ctx(pair):
        return [pair] + [over_ctx(pair, d) for d in range(1, cs)]

    def stack_parts(*moved):
        return [jnp.concatenate([m[i] for m in moved], axis=0) for i in range(2)]

    def gather_one(moved):
        a, b = line.plain(stack_parts, *moved)
        return a, [over_fsdp(a, h) for h in range(1, fs)], b, over_tp(b, 2)

    def gather_two(a, a_f, b, b_x):
        def stacks(a, a_f, b, b_x):
            return jnp.stack([a, *a_f]), jnp.stack([b, b_x])

        a, b = line.plain(stacks, a, a_f, b, b_x)
        return a, over_tp(a, 2), b, [over_fsdp(b, h) for h in range(1, fs)]

    def gather_three(a, a_x, b, b_f):
        whole_a, whole_b = [], []
        for _ in range(2):
            whole_a.append([[(p, h) for h in range(fs)] for p in (a, a_x)])
            whole_b.append([[(p, x) for p in (b, *b_f)] for x in range(2)])
            a, a_x, b, *b_f = [over_tp(p, 1) for p in (a, a_x, b, *b_f)]
        return whole_a, whole_b

    def chip(blocks):
        return [over_tp(b, 1) for b in blocks]

    def reduce_mid_a(a, move):
        return line.plain(lambda a, m: [add(a[h], m[h]) for h in range(fs)], a, move)

    def reduce_mid_b(b, moves):
        return line.plain(lambda b, m: [add(b[x], *[p[x] for p in m]) for x in range(2)], b, moves)

    def reduce_end(a, a_move, b, b_move):
        def both(a, a_move, b, b_move):
            a = add(a, *a_move).reshape(cs, rows, -1)
            b = add(b, b_move).reshape(cs, rows, -1)
            return [jnp.stack([a[d], b[d]]) for d in range(cs)]

        pieces = line.plain(both, a, a_move, b, b_move)
        return pieces[0], [over_ctx(pieces[d], -d) for d in range(1, cs)]

    def finish(own, moved):
        return sum(p.astype(F32) for p in (own, *moved))

    spread = lambda blocks: [blocks[0][0], blocks[1][0], blocks[0][1], blocks[1][1]]
    owner = jnp.stack(
        [(f_rank - h) % fs * cs + (c_rank - d) % cs for h in range(fs) for d in range(cs)]
    )
    features = lax.broadcasted_iota(jnp.int32, (width, width), 0)
    places = (owner[:, None] * rows + jnp.arange(rows)[None, :]).reshape(1, width)
    permute = (features == places).astype(BF16)

    def relative(array, axis=0):
        return [
            jnp.stack([pick(array, t_rank ^ (2 * x + k), axis) for x in range(2)]) for k in range(2)
        ]

    def absolute(blocks):
        blocks = jnp.stack(spread(blocks))
        return jnp.stack([pick(blocks, t_rank ^ t) for t in range(ts)])

    flat = lambda w: w.reshape(w.shape[0], -1)
    side = merger_weight.shape[1] * merger_weight.shape[2]
    heads_width = output_weight.shape[1]

    def start_att(a, m, o):
        return jnp.stack([flat(a), jnp.concatenate([flat(m), o], axis=1)])

    def split_rows(one, two):
        array = jnp.concatenate([one, two], axis=-1)
        array = array.reshape(slots, ts, share, fine, -1).transpose(0, 2, 1, 3, 4)
        return array.reshape(group * ts * fine, -1)

    small = merger_bias.shape[0]
    att = gather_ctx(line.plain(start_att, attend_weight, merger_weight, output_weight))
    packed = line.plain(
        lambda *v: jnp.broadcast_to(jnp.concatenate(v), (devices, sum(x.shape[0] for x in v))),
        merger_bias, first_gain, first_shift, output_bias, second_gain, second_shift, shrink_bias, widen_bias,
    )
    packed = lax.all_to_all(packed, ALL, 0, 0, tiled=True)
    both = line.plain(split_rows, tokens, skip_tokens)
    ffn = line.plain(lambda a, b: jnp.stack([a, b]), expand_weight, shrink_weight)
    packed = line.gate(packed)
    att = gather_one(att)
    both, ffn = line.gate(both, ffn)
    both = to_group(both)
    ffn = gather_ctx(ffn)
    attend, merger_output = gather_three(*gather_two(*att))

    def vectors_of(packed):
        vectors = packed[:, : 7 * small].reshape(fs * cs, ts, 7, small).transpose(0, 2, 1, 3)
        vectors = vectors.reshape(fs * cs, 7, rows)
        vectors = jnp.stack([pick(vectors, owner[i]) for i in range(fs * cs)], axis=1).reshape(7, width)
        return vectors, relative(packed[:, 7 * small :].reshape(ts, 1, hidden))

    def blocks_of(both):
        both = relative(both.reshape(cs, ts, ts * fine, side), 1)
        return [b.reshape(2, count, side) for b in both]

    vectors, widen = line.plain(vectors_of, packed)
    both = line.plain(blocks_of, both)
    act = (count, width)
    turned = (width, count)

    joined, normed, normed_t = line(
        lambda after, b, w, v: down(
            after, "joined", b, w, side, 0, functools.partial(norm_finish, False), [v[0:3]],
            [(act, F32), (act, BF16), (turned, BF16)],
        ),
        both, merger_output, vectors,
    )
    ffn = gather_one(ffn)
    project = line(
        lambda after, n, w: up(
            after, "project", n, w, 3 * heads_width, 0, plain_step, [], [(count, BF16)] * 2, heads_width
        ),
        normed, attend,
    )
    cot = to_group(line.gate(cotangent).reshape(group * fine, width))
    others = [[over_tp(project[k ^ (d & 1)], d) for d in range(1, share)] for k in range(2)]
    inner = [None, None]
    inner[0] = line(attend_forward, project[0], others[0])
    ffn = gather_two(*ffn)
    inner[1] = line(attend_forward, project[1], others[1])
    probs, attended = zip(*inner)
    second, normed_two, normed_two_t = line(
        lambda after, a, w, r, v: down(
            after, "second", a, w, heads_width, side // heads_width, functools.partial(norm_finish, True), [r, v[3:6]],
            [(act, F32), (act, BF16), (turned, BF16)],
        ),
        attended, merger_output, joined, vectors,
    )
    live = pick(live_slots.reshape(slots), (c_rank * ts + t_rank) // share).astype(F32)

    def arrived(cot, permute):
        ours = (mxu(cot.reshape(count, width), permute, 1, 0) * live).astype(BF16)
        return ours, ours.T

    branch_low, branch_low_t = line.plain(arrived, cot, permute)
    expand, shrink = gather_three(*line.gate(*ffn))

    def hidden_step(after, left, w, b):
        return up(after, "hidden", left, [w], hidden, 0, gelu_step, [b], [(count, BF16)] * 2, 256)

    activated, slope = [None, None], [None, None]
    activated[0], slope[0] = line(hidden_step, normed_two, expand[0], widen[0])
    activated[1], slope[1] = line(hidden_step, normed_two, expand[1], widen[1])

    def grads(by_x):
        return lambda after, lefts, rights, more=(): weight_grad(after, lefts, rights, fs, by_x, more)

    def hidden_back(after, left, w, s):
        return up(
            after, "hidden_back", left, [w], hidden, 0, slope_step, [s], [(count, BF16), (1, F32)], 256
        )

    grad_expanded, wide = [None, None], [None, None]
    other = chip(line(grads(True), [branch_low_t], [activated[1]]))
    grad_expanded[1], wide[1] = line(hidden_back, branch_low, shrink[1], slope[1])
    grad_shrink = line(grads(True), [branch_low_t], [activated[0]], other)
    shrink_move = over_tp(grad_shrink[1], 2)
    grad_expanded[0], wide[0] = line(hidden_back, branch_low, shrink[0], slope[0])
    other = chip(line(grads(False), [normed_two_t], [grad_expanded[1]]))
    grad_second, attn_low, attn_low_t, sums_two = line(
        lambda after, g, w, t, u, v: down(
            after, "second_back", g, w, hidden, 0, functools.partial(norm_back_finish, True), [t, u, v[4:5]],
            [(act, F32), (act, BF16), (turned, BF16), ((4, width), F32)],
        ),
        grad_expanded, expand, second, branch_low, vectors,
    )
    grad_expand = line(grads(False), [normed_two_t], [grad_expanded[0]], other)
    expand_move = [over_fsdp(grad_expand[h], -h) for h in range(1, fs)]
    grad_attended = line(
        lambda after, a, w: up(
            after, "attended_back", a, w, heads_width, side // heads_width, plain_step, [], [(count, BF16)] * 2,
            heads_width // 2,
        ),
        attn_low, merger_output,
    )

    def layer_end(after, a, w, t, v):
        ends = jnp.stack([v[6], jnp.full((width,), live)])
        return down(after, "layer_out", a, w, hidden, 0, out_finish, [t, ends], [(act, BF16)])

    (layer_out,) = line(layer_end, activated, shrink, second, vectors)
    layer_out = line.plain(lambda a, p: mxu(a, p, 1, 1).astype(BF16), layer_out, permute)
    layer_out = to_group(layer_out.reshape(group * fine, width))
    inner = [None, None]
    inner[1] = line(attend_backward, project[1], others[1], probs[1], attended[1], grad_attended[1])
    grad_shrink = reduce_mid_a(grad_shrink[0], shrink_move)
    shrink_move = [over_fsdp(grad_shrink[h], -h) for h in range(1, fs)]
    inner[0] = line(attend_backward, project[0], others[0], probs[0], attended[0], grad_attended[0])
    grad_expand = reduce_mid_b(grad_expand[0], expand_move)
    expand_move = over_tp(grad_expand[1], 2)

    def close(k):
        def total(own, *moves):
            third = own.shape[2] // 3
            return jnp.concatenate([own[:, :, :third], add(own[:, :, third:], *moves)], axis=-1)

        moves = [over_tp(inner[k ^ (d & 1)][d], d) for d in range(1, share)]
        return line.plain(total, inner[k][0], *moves)

    grad_project = [None, None]
    grad_project[1] = close(1)
    other = chip(line(grads(True), [normed_t], [grad_project[1]]))
    grad_project[0] = close(0)
    joined_low, joined_low_t, sums_one = line(
        lambda after, g, w, t, u, v: down(
            after, "first_back", g, w, 3 * heads_width, 0, functools.partial(norm_back_finish, False), [t, u, v[1:2]],
            [(act, BF16), (turned, BF16), ((4, width), F32)],
        ),
        grad_project, attend, joined, grad_second, vectors,
    )
    def vector_sums(one, two, wide):
        sums = jnp.concatenate([one[0:3], two]).reshape(7, fs * cs, rows)
        places = [(f_rank - f) % fs * cs + (c_rank - c) % cs for f in range(fs) for c in range(cs)]
        sums = jnp.stack([pick(sums, p, 1) for p in places])
        sums = sums.reshape(fs * cs, 7, ts, small).transpose(0, 2, 1, 3).reshape(devices, 7 * small)
        return jnp.concatenate([sums, absolute(wide).reshape(devices, -1)], axis=1)

    vec = lax.all_to_all(line.plain(vector_sums, sums_one, sums_two, wide), ALL, 0, 0, tiled=True)
    rest_other = chip(line(grads(False), [joined_low_t, attn_low_t], [both[1], attended[1]]))
    grad_attend = line(grads(True), [normed_t], [grad_project[0]], other)
    attend_move = over_tp(grad_attend[1], 2)
    grad_rest = line(grads(False), [joined_low_t, attn_low_t], [both[0], attended[0]], rest_other)
    rest_move = [over_fsdp(grad_rest[h], -h) for h in range(1, fs)]
    out = line(
        lambda after, a, w: up(after, "inputs_back", a, w, side, 0, plain_step, [], [(count, BF16)] * 2, 256),
        joined_low, merger_output,
    )

    def turn_back(out):
        out = absolute(out).reshape(ts, cs, ts * fine, side)
        return out.transpose(1, 0, 2, 3).reshape(group * ts * fine, side)

    out = to_group(line.plain(turn_back, out))
    ffn = reduce_end(grad_shrink[0], shrink_move, grad_expand[0], expand_move)
    grad_attend = reduce_mid_a(grad_attend[0], attend_move)
    attend_move = [over_fsdp(grad_attend[h], -h) for h in range(1, fs)]
    grad_rest = reduce_mid_b(grad_rest[0], rest_move)
    rest_move = over_tp(grad_rest[1], 2)
    att = reduce_end(grad_attend[0], attend_move, grad_rest[0], rest_move)
    ffn = line.plain(finish, *ffn)

    def unpack(out, layer_out, vec):
        out = out.reshape(slots, share, ts, fine, side).transpose(0, 2, 1, 3, 4)
        out = out.reshape(batches, local_seqs, local_len, side).astype(F32)
        layer_out = layer_out.reshape(batches, local_seqs, share * fine, width)
        return out[..., :part_width], out[..., part_width:], layer_out, jnp.sum(vec, axis=0)

    grad_tokens, grad_skip, layer_out, vec = line.plain(unpack, out, layer_out, vec)
    att = line.plain(finish, *att)
    vec_out = [vec[i * small : (i + 1) * small] for i in range(7)] + [vec[7 * small :]]
    return (
        layer_out,
        grad_tokens,
        grad_skip,
        att[1, :, :side].reshape(merger_weight.shape),
        vec_out[0],
        vec_out[1],
        vec_out[2],
        att[0].reshape(attend_weight.shape),
        att[1, :, side:],
        vec_out[3],
        vec_out[4],
        vec_out[5],
        ffn[1],
        vec_out[7],
        ffn[0],
        vec_out[6],
    )


def solution(mesh):
    sizes = tuple(mesh.shape[a] for a in ALL)
    act = P(None, "fsdp", "ctx", "tp")
    vec = P(ALL)
    flat = P(None, "fsdp", ("ctx", "tp"), None)
    w_three = P(("fsdp", "ctx"), None, "tp")
    w_two = P(("fsdp", "ctx"), "tp")
    return jax.shard_map(
        functools.partial(on_device, sizes),
        mesh=mesh,
        in_specs=(
            act, act, w_three, vec, vec, vec, w_three, w_two, vec, vec, vec, w_two, vec, w_two, vec,
            P(None, "fsdp"), flat,
        ),
        out_specs=(
            flat, act, act, w_three, vec, vec, vec, w_three, w_two, vec, vec, vec, w_two, vec, w_two, vec,
        ),
        check_vma=False,
    )
```

time: 851 us -> 642 us (0.75)
  Pallas kernels: 41.3 us -> 200 us
  waiting for transfers between devices: 300 us -> 209 us
  matrix products: 96.6 us -> 6.68 us
  local copies, waits for them, and re-layouts: 124 us -> 43.9 us
  blocking collectives: 77.8 us -> 0 us
  between operations: 16.4 us -> 2.59 us
  other arithmetic: 57.3 us -> 46.3 us
    all_gather x5 -> x0, waiting for transfers between devices: 223 us -> none  [gather(): full = lax.all_gather(part, ('tp', 'fsdp', 'ctx'), axis=0, tiled=True)]
    pallas_call x2 -> x24, Pallas kernels: 41.3 us -> 200 us  [apply(): pl.pallas_call(run, grid=grid, in_specs=[*in_specs, *[pl.BlockSpec(memory...]
    dot_general x15 -> x2, matrix products: 96.6 us -> 6.68 us  [mxu(): lax.dot_general(a, b, (((a_dim,), (b_dim,)), ((), ())), preferred_element...]
    ppermute x47 -> x48, waiting for transfers between devices: 74.4 us -> 154 us  [the longest x28 59.5 us: over_tp(): return lax.ppermute(array, 'tp', [(i, i ^ flip) for i in range(ts)])]
    unnamed x1 -> x0, blocking collectives: 77.8 us -> none
    all_to_all x1 -> x2, waiting for transfers between devices: 0.7 us -> 54.5 us  [the longest x1 28.2 us: on_device(): lax.all_to_all(line.plain(vector_sums, sums_one, sums_two, wide), ALL, 0,...]
    dynamic_slice x9 -> x6, local copies, waits for them, and re-layouts: 34.1 us -> 2.55 us  [pick(): return lax.dynamic_index_in_dim(array, index, axis, keepdims=False)]
    reshape x14 -> x6, local copies, waits for them, and re-layouts: 29.6 us -> 3.36 us  [the longest x1 1.53 us: turn_back(): out = absolute(out).reshape(ts, cs, ts * fine, side)]
  transfers between devices with their start and end apart: 57 -> 54, of which waited for: 12 -> 17; matrix products, arithmetic and copies ran while one was open for 27% -> 13% of each run, Pallas kernels for 5% -> 27%
where the time goes in v2:
time: 642 us; the launch traced here: 634 us
  waiting for transfers between devices  209 us (33%)
  Pallas kernels  200 us (31%)
  starting transfers between devices  126 us (20%)
  other arithmetic  46.3 us (7%)
  local copies, waits for them, and re-layouts  43.9 us (7%)
  matrix products  6.68 us (1%)
    pallas_call x24, Pallas kernels, apply(): pl.pallas_call(run, grid=grid, in_specs=[*in_specs, *[pl.BlockSpec(memory...  200 us
    ppermute x12, starting transfers between devices, over_ctx(): return lax.ppermute(array, 'ctx', [(i, (i + d) % cs) for i in range(cs)])  69.3 us
    ppermute x28, waiting for transfers between devices, over_tp(): return lax.ppermute(array, 'tp', [(i, i ^ flip) for i in range(ts)])  59.5 us
    ppermute x8, waiting for transfers between devices, over_fsdp(): return lax.ppermute(array, 'fsdp', [(i, (i + d) % fs) for i in range(fs)])  54.9 us
    ppermute x12, waiting for transfers between devices, over_ctx(): return lax.ppermute(array, 'ctx', [(i, (i + d) % cs) for i in range(cs)])  39.9 us
    all_to_all x1, waiting for transfers between devices, on_device(): lax.all_to_all(line.plain(vector_sums, sums_one, sums_two, wide), ALL, 0,...  28.2 us
    all_to_all x4, starting transfers between devices, to_group(): return lax.all_to_all(array, ('ctx', 'tp'), 0, 0, tiled=True)  26.4 us
    all_to_all x1, waiting for transfers between devices, on_device(): packed = lax.all_to_all(packed, ALL, 0, 0, tiled=True)  26.3 us
  transfers between devices with their start and end apart: 54, of which 17 were waited for; matrix products, arithmetic and copies ran while one was open for 13% of the time, Pallas kernels for 27%

profile of v2, /device:TPU:0, one launch (start us, length us, event | category | flops | bytes accessed | tf_op | source)
XLA Modules:
  0.0 634.4 jit_solution(14019464048847565441)
XLA Ops:
  4.0 5.1 collective-permute-start.2
  10.9 5.1 all-to-all-start
  19.1 26.3 %all-to-all-done = f32[32,1,352]{2,1,0:T(1,128)S(1)} async-done(((f32[32,1,352]{2,1,0:T(1,128)}), f32[32,1,352]{2,1,0:T(1,128)S(1)}, u32[]{:S(2)}, u32[]{:S(2)}) %all-to-all-start) | async-done | bytes 45088 | tf_op jit(solution)/shard_map/all_to_all | solution.py:531
  48.1 5.9 all-to-all-start.1
  54.0 12.2 %collective-permute-done.3 = bf16[512,768]{1,0:T(8,128)(2,1)S(1)} collective-permute-done((bf16[512,768]{1,0:T(8,128)(2,1)S(1)}, bf16[512,768]{1,0:T(8,128)(2,1)S(1)}, u32[]{:S(2)}, u32[]{:S(2)}) %collective-permute-start.3) | collective-permute-done | bytes 786464 | tf_op jit(solution)/shard_map/ppermute | solution.py:448
  66.3 12.0 %collective-permute-done.4 = bf16[512,768]{1,0:T(8,128)(2,1)S(1)} collective-permute-done((bf16[512,768]{1,0:T(8,128)(2,1)S(1)}, bf16[512,768]{1,0:T(8,128)(2,1)S(1)}, u32[]{:S(2)}, u32[]{:S(2)}) %collective-permute-start.4) | collective-permute-done | bytes 786464 | tf_op jit(solution)/shard_map/ppermute | solution.py:442
  83.4 27.7 %collective-permute-done.5.refs_3_.refs_5_.refs_2_.refs_4_ = bf16[2,512,768]{2,1,0:T(8,128)(2,1)S(1)} collective-permute-done((bf16[2,512,768]{2,1,0:T(8,128)(2,1)S(1)}, bf16[2,512,768]{2,1,0:T(8,128)(2,1)S(1)}, u32[]{:S(2)}, u32[]{:S(2)}) %collective-permute-start.5) | collective-permute-done | bytes 1572896 | tf_op jit(solution)/shard_map/ppermute | solution.py:448
  111.1 5.7 collective-permute-start.13
  117.8 5.2 collective-permute-done.8.refs_3_.refs_4_.refs_5_
  129.1 9.2 %joined.1 = (f32[512,1024]{1,0:T(8,128)}, bf16[512,1024]{1,0:T(8,128)(2,1)}, bf16[1024,512]{1,0:T(8,128)(2,1)}, f32[8,128]{1,0:T(8,128)}) custom-call(bf16[2,512,512]{2,1,0:T(8,128)(2,1)} %pad_maximum_fusion.9.refs_0_.refs_22_.refs_4_, bf16[2,512,512]{2,1,0:T(8,128)(2,1)} %pad_maximum_fusion.10.refs_1_.refs_23_.refs_4_, bf16[2,512,768]{2,1,0:T(8,128)(2,1)} %copy-done, ...), custom_call_target="tpu_custom_call" | custom-call | flops 1 | bytes 1 | tf_op jit(solution)/shard_map/joined/pallas_call | solution.py:36
  138.3 21.2 %collective-permute-done.12 = bf16[2,128,1024]{2,1,0:T(8,128)(2,1)} collective-permute-done((bf16[2,128,1024]{2,1,0:T(8,128)(2,1)}, bf16[2,128,1024]{2,1,0:T(8,128)(2,1)}, u32[]{:S(2)}, u32[]{:S(2)}) %collective-permute-start.12) | collective-permute-done | bytes 524320 | tf_op jit(solution)/shard_map/ppermute | solution.py:445
  166.5 7.7 %project.1 = (bf16[2,512,768]{2,1,0:T(8,128)(2,1)}, bf16[2,512,768]{2,1,0:T(8,128)(2,1)}, f32[8,128]{1,0:T(8,128)}) custom-call(bf16[512,1024]{1,0:T(8,128)(2,1)} %get-tuple-element.543.refs_0_, bf16[2,512,768]{2,1,0:T(8,128)(2,1)} %pad_maximum_fusion.5.refs_17_.refs_1_.refs_2_.refs_3_, ...), custom_call_target="tpu_custom_call" | custom-call | flops 1 | bytes 1 | tf_op jit(solution)/shard_map/project/pallas_call | solution.py:36
  176.1 8.6 %all-to-all-start.2 = ((bf16[16,32,1024]{2,1,0:T(8,128)(2,1)}), bf16[16,32,1024]{2,1,0:T(8,128)(2,1)}, u32[]{:S(2)}, u32[]{:S(2)}) async-start(bf16[16,32,1024]{2,1,0:T(8,128)(2,1)} %bitcast.45), calls=%async_computation.2 | async-start | bytes 2097152 | tf_op jit(solution)/shard_map/all_to_all | solution.py:439
  184.7 12.6 %attend_forward.2 = (bf16[2,4,1024,512]{3,2,1,0:T(8,128)(2,1)}, bf16[2,512,256]{2,1,0:T(8,128)(2,1)}, f32[8,128]{1,0:T(8,128)}) custom-call(bf16[2,512,768]{2,1,0:T(8,128)(2,1)} %get-tuple-element.731.refs_0_, bf16[2,512,768]{2,1,0:T(8,128)(2,1)} %collective-permute-done.14.refs_1_, f32[8,128]{1,0:T(8,128)} %get-tuple-element.561.refs_2_), custom_call_target="tpu_custom_call" | custom-call | flops 1 | bytes 1 | tf_op jit(solution)/shard_map/attend_forward/pallas_call | solution.py:36
  197.3 2.5 collective-permute-done.16
  199.8 9.6 %collective-permute-done.17 = bf16[512,1024]{1,0:T(8,128)(2,1)} collective-permute-done((bf16[512,1024]{1,0:T(8,128)(2,1)S(1)}, bf16[512,1024]{1,0:T(8,128)(2,1)}, u32[]{:S(2)}, u32[]{:S(2)}) %collective-permute-start.17) | collective-permute-done | bytes 1048608 | tf_op jit(solution)/shard_map/ppermute | solution.py:442
  209.5 2.7 pad_maximum_fusion.2.refs_4_.refs_1_.refs_3_.refs_2_
  213.6 2.7 pad_maximum_fusion.1.refs_3_.refs_1_.refs_2_
  218.2 2.2 fusion
  220.4 12.6 %attend_forward.3 = (bf16[2,4,1024,512]{3,2,1,0:T(8,128)(2,1)}, bf16[2,512,256]{2,1,0:T(8,128)(2,1)}, f32[8,128]{1,0:T(8,128)}) custom-call(bf16[2,512,768]{2,1,0:T(8,128)(2,1)} %get-tuple-element.720.refs_0_, bf16[2,512,768]{2,1,0:T(8,128)(2,1)} %collective-permute-done.15.refs_1_, f32[8,128]{1,0:T(8,128)} %get-tuple-element.573.refs_2_, ...), custom_call_target="tpu_custom_call" | custom-call | flops 1 | bytes 1 | tf_op jit(solution)/shard_map/attend_forward/pallas_call | solution.py:36
  233.6 9.0 %second.1 = (f32[512,1024]{1,0:T(8,128)}, bf16[512,1024]{1,0:T(8,128)(2,1)}, bf16[1024,512]{1,0:T(8,128)(2,1)}, f32[8,128]{1,0:T(8,128)}) custom-call(bf16[2,512,256]{2,1,0:T(8,128)(2,1)} %get-tuple-element.814.refs_0_.refs_3_.refs_5_, bf16[2,512,256]{2,1,0:T(8,128)(2,1)} %get-tuple-element.797.refs_1_.refs_3_.refs_5_, bf16[2,512,768]{2,1,0:T(8,128)(2,1)} %copy-done, ...), custom_call_target="tpu_custom_call" | custom-call | flops 1 | bytes 1 | tf_op jit(solution)/shard_map/second/pallas_call | solution.py:36
  242.6 3.2 multiply_convert_fusion.refs_7_.refs_0_.refs_11_
  245.8 12.4 %collective-permute-done.19.refs_2_.refs_4_.refs_3_.refs_5_ = bf16[2,512,1024]{2,1,0:T(8,128)(2,1)S(1)} collective-permute-done((bf16[2,512,1024]{2,1,0:T(8,128)(2,1)}, bf16[2,512,1024]{2,1,0:T(8,128)(2,1)S(1)}, u32[]{:S(2)}, u32[]{:S(2)}) %collective-permute-start.19) | collective-permute-done | bytes 2097184 | tf_op jit(solution)/shard_map/ppermute | solution.py:448
  258.2 4.3 collective-permute-done.18.refs_3_.refs_4_.refs_5_
  264.8 7.6 %hidden.2 = (bf16[2,512,1024]{2,1,0:T(8,128)(2,1)}, bf16[2,512,1024]{2,1,0:T(8,128)(2,1)}, f32[8,128]{1,0:T(8,128)}) custom-call(bf16[512,1024]{1,0:T(8,128)(2,1)} %get-tuple-element.616.refs_0_, bf16[2,512,1024]{2,1,0:T(8,128)(2,1)} %pad_maximum_fusion.1.refs_3_.refs_1_.refs_2_, bf16[2,512,1024]{2,1,0:T(8,128)(2,1)} %pad_maximum_fusion.1.refs_3_.refs_1_.refs_2_, ...), custom_call_target="tpu_custom_call" | custom-call | flops 1 | bytes 1 | tf_op jit(solution)/shard_map/hidden/pallas_call | solution.py:36
  273.0 7.7 %hidden.3 = (bf16[2,512,1024]{2,1,0:T(8,128)(2,1)}, bf16[2,512,1024]{2,1,0:T(8,128)(2,1)}, f32[8,128]{1,0:T(8,128)}) custom-call(bf16[512,1024]{1,0:T(8,128)(2,1)} %get-tuple-element.616.refs_0_, bf16[2,512,1024]{2,1,0:T(8,128)(2,1)} %collective-permute-done.20.refs_1_.refs_2_.refs_6_.refs_7_, ...), custom_call_target="tpu_custom_call" | custom-call | flops 1 | bytes 1 | tf_op jit(solution)/shard_map/hidden/pallas_call | solution.py:36
  282.1 5.7 weight_grad.8
  288.3 6.8 %hidden_back.2 = (bf16[2,512,1024]{2,1,0:T(8,128)(2,1)}, f32[2,1,1024]{2,1,0:T(1,128)}, f32[8,128]{1,0:T(8,128)}) custom-call(bf16[512,1024]{1,0:T(8,128)(2,1)} %copy-done.2, bf16[2,512,1024]{2,1,0:T(8,128)(2,1)} %collective-permute-done.24.refs_1_.refs_3_.refs_6_.refs_8_, bf16[2,512,1024]{2,1,0:T(8,128)(2,1)} %collective-permute-done.25.refs_2_.refs_4_.refs_7_.refs_9_, ...), custom_call_target="tpu_custom_call" | custom-call | flops 1 | bytes 1 | tf_op jit(solution)/shard_map/hidden_back/pallas_call | solution.py:36
  296.6 6.3 weight_grad.9
  302.9 6.7 %hidden_back.3 = (bf16[2,512,1024]{2,1,0:T(8,128)(2,1)}, f32[2,1,1024]{2,1,0:T(1,128)}, f32[8,128]{1,0:T(8,128)}) custom-call(bf16[512,1024]{1,0:T(8,128)(2,1)} %copy-done.2, bf16[2,512,1024]{2,1,0:T(8,128)(2,1)} %pad_maximum_fusion.2.refs_4_.refs_1_.refs_3_.refs_2_, bf16[2,512,1024]{2,1,0:T(8,128)(2,1)} %copy-done.5, ...), custom_call_target="tpu_custom_call" | custom-call | flops 1 | bytes 1 | tf_op jit(solution)/shard_map/hidden_back/pallas_call | solution.py:36
  309.6 5.7 weight_grad.10
  316.8 14.5 %second_back.1 = (f32[512,1024]{1,0:T(8,128)}, bf16[512,1024]{1,0:T(8,128)(2,1)}, bf16[1024,512]{1,0:T(8,128)(2,1)}, f32[4,1024]{1,0:T(4,128)}, f32[8,128]{1,0:T(8,128)}) custom-call(bf16[2,512,1024]{2,1,0:T(8,128)(2,1)} %get-tuple-element.681.refs_0_.refs_2_, bf16[2,512,1024]{2,1,0:T(8,128)(2,1)} %get-tuple-element.663.refs_2_.refs_1_, ...), custom_call_target="tpu_custom_call" | custom-call | flops 1 | bytes 1 | tf_op jit(solution)/shard_map/second_back/pallas_call | solution.py:36
  333.3 6.3 weight_grad.11
  340.0 5.2 attended_back.1
  345.7 10.9 %layer_out.1 = (bf16[512,1024]{1,0:T(8,128)(2,1)}, f32[8,128]{1,0:T(8,128)}) custom-call(bf16[2,512,1024]{2,1,0:T(8,128)(2,1)} %get-tuple-element.702.refs_2_.refs_0_, bf16[2,512,1024]{2,1,0:T(8,128)(2,1)} %get-tuple-element.703.refs_2_.refs_1_, bf16[2,512,1024]{2,1,0:T(8,128)(2,1)} %pad_maximum_fusion.2.refs_4_.refs_1_.refs_3_.refs_2_, ...), custom_call_target="tpu_custom_call" | custom-call | flops 1 | bytes 1 | tf_op jit(solution)/shard_map/layer_out/pallas_call | solution.py:36
  356.7 3.5 convolution_convert_fusion.refs_6_
  360.2 13.3 %attend_backward.2 = (bf16[2,512,768]{2,1,0:T(8,128)(2,1)}, bf16[2,512,512]{2,1,0:T(8,128)(2,1)}, f32[8,128]{1,0:T(8,128)}) custom-call(bf16[2,512,768]{2,1,0:T(8,128)(2,1)} %get-tuple-element.720.refs_0_, bf16[2,512,768]{2,1,0:T(8,128)(2,1)} %collective-permute-done.15.refs_1_, bf16[2,4,1024,512]{3,2,1,0:T(8,128)(2,1)} %get-tuple-element.722.refs_2_, ...), custom_call_target="tpu_custom_call" | custom-call | flops 1 | bytes 1 | tf_op jit(solution)/shard_map/attend_backward/pallas_call | solution.py:36
  373.5 2.3 fusion.2
  375.8 13.1 %attend_backward.3 = (bf16[2,512,768]{2,1,0:T(8,128)(2,1)}, bf16[2,512,512]{2,1,0:T(8,128)(2,1)}, f32[8,128]{1,0:T(8,128)}) custom-call(bf16[2,512,768]{2,1,0:T(8,128)(2,1)} %get-tuple-element.731.refs_0_, bf16[2,512,768]{2,1,0:T(8,128)(2,1)} %collective-permute-done.14.refs_1_, bf16[2,4,1024,512]{3,2,1,0:T(8,128)(2,1)} %get-tuple-element.733.refs_2_, ...), custom_call_target="tpu_custom_call" | custom-call | flops 1 | bytes 1 | tf_op jit(solution)/shard_map/attend_backward/pallas_call | solution.py:36
  389.5 1.7 collective-permute-start.36
  392.5 3.6 fusion.4
  399.5 4.9 weight_grad.12
  406.6 12.7 %first_back.1 = (bf16[512,1024]{1,0:T(8,128)(2,1)}, bf16[1024,512]{1,0:T(8,128)(2,1)}, f32[4,1024]{1,0:T(4,128)}, f32[8,128]{1,0:T(8,128)}) custom-call(bf16[2,512,768]{2,1,0:T(8,128)(2,1)} %pad_maximum_fusion.8.refs_0_.refs_14_.refs_2_, bf16[2,512,768]{2,1,0:T(8,128)(2,1)} %pad_maximum_fusion.7.refs_2_.refs_6_.refs_1_, ...), custom_call_target="tpu_custom_call" | custom-call | flops 1 | bytes 1 | tf_op jit(solution)/shard_map/first_back/pallas_call | solution.py:36
  422.4 5.0 weight_grad.13
  428.0 7.1 %all-to-all-start.4 = ((bf16[16,32,1024]{2,1,0:T(8,128)(2,1)}), bf16[16,32,1024]{2,1,0:T(8,128)(2,1)S(1)}, u32[]{:S(2)}, u32[]{:S(2)}) async-start(bf16[16,32,1024]{2,1,0:T(8,128)(2,1)} %bitcast.72), calls=%async_computation.4 | async-start | bytes 2097152 | tf_op jit(solution)/shard_map/all_to_all | solution.py:439
  441.0 5.3 weight_grad.14
  446.4 5.4 weight_grad.15
  451.8 2.0 collective-permute-start.41
  453.7 5.6 inputs_back.1
  462.8 3.6 all-to-all-start.5
  468.2 28.2 %all-to-all-done.5 = f32[32,1,352]{2,1,0:T(1,128)S(1)} async-done(((f32[32,1,352]{2,1,0:T(1,128)}), f32[32,1,352]{2,1,0:T(1,128)S(1)}, u32[]{:S(2)}, u32[]{:S(2)}) %all-to-all-start.5) | async-done | bytes 45088 | tf_op jit(solution)/shard_map/all_to_all | solution.py:673
  496.4 4.8 all-to-all-start.3
  503.8 1.9 fusion.6
  505.7 1.8 fusion.8
  507.5 2.1 collective-permute-start.44
  511.8 3.3 collective-permute-start.38
  516.1 27.6 %collective-permute-done.44 = bf16[512,768]{1,0:T(8,128)(2,1)S(1)} collective-permute-done((bf16[512,768]{1,0:T(8,128)(2,1)S(1)}, bf16[512,768]{1,0:T(8,128)(2,1)S(1)}, u32[]{:S(2)}, u32[]{:S(2)}) %collective-permute-start.44) | collective-permute-done | bytes 786464 | tf_op jit(solution)/shard_map/ppermute | solution.py:442
  547.1 2.7 collective-permute-done.38
  549.8 52.1 %collective-permute-start.47 = (bf16[2,128,768]{2,1,0:T(8,128)(2,1)}, bf16[2,128,768]{2,1,0:T(8,128)(2,1)}, u32[]{:S(2)}, u32[]{:S(2)}) collective-permute-start(bf16[2,128,768]{2,1,0:T(8,128)(2,1)} %pad_maximum_fusion.24), channel_id=1, source_target_pairs={{0,4},{4,8},{8,12},{12,0},{1,5},{5,9},{9,13},{13,1},{2,6},{6,10},{... | collective-permute-start | bytes 1179656 | tf_op jit(solution)/shard_map/ppermute | solution.py:445
  602.0 10.7 %collective-permute-done.39 = bf16[2,128,1024]{2,1,0:T(8,128)(2,1)S(1)} collective-permute-done((bf16[2,128,1024]{2,1,0:T(8,128)(2,1)S(1)}, bf16[2,128,1024]{2,1,0:T(8,128)(2,1)S(1)}, u32[]{:S(2)}, u32[]{:S(2)}) %collective-permute-start.39) | collective-permute-done | bytes 524320 | tf_op jit(solution)/shard_map/ppermute | solution.py:445
  614.0 2.6 convert_bitcast_fusion
  618.7 2.7 copy.84
  621.4 2.5 fusion.26
  623.9 5.3 collective-permute-done.46
  (313 shorter events, 85.0 us)
Async XLA Ops:
  0.7 15.9 %copy-start.30 = (bf16[4,2,256,256]{3,2,1,0:T(8,128)(2,1)S(1)}, bf16[4,2,256,256]{3,2,1,0:T(8,128)(2,1)}, u32[]{:S(2)}) copy-start(bf16[4,2,256,256]{3,2,1,0:T(8,128)(2,1)} %param.18) | copy-start | bytes 3145732
  0.7 15.8 %copy-start.31 = (bf16[4,2,256,256]{3,2,1,0:T(8,128)(2,1)S(1)}, bf16[4,2,256,256]{3,2,1,0:T(8,128)(2,1)}, u32[]{:S(2)}) copy-start(bf16[4,2,256,256]{3,2,1,0:T(8,128)(2,1)} %param.17) | copy-start | bytes 3145732
  4.0 41.4 %copy-start.18 = (bf16[2,128,768]{2,1,0:T(8,128)(2,1)}, bf16[2,128,768]{2,1,0:T(8,128)(2,1)S(1)}, u32[]{:S(2)}) copy-start(bf16[2,128,768]{2,1,0:T(8,128)(2,1)S(1)} %pad_maximum_fusion.20.refs_11_) | copy-start | bytes 1179652
  4.0 41.4 %collective-permute-start.2 = (bf16[2,128,768]{2,1,0:T(8,128)(2,1)S(1)}, bf16[2,128,768]{2,1,0:T(8,128)(2,1)S(1)}, u32[]{:S(2)}, u32[]{:S(2)}) collective-permute-start(bf16[2,128,768]{2,1,0:T(8,128)(2,1)S(1)} %pad_maximum_fusion.20.refs_11_), channel_id=1, source_target_pairs={{0,12},{4,0},{8,4},{12,8},{1,13},{5,1},{9,5},{13,9},{2,14},{6,2},{... | collective-permute-start | bytes 1179656 | tf_op jit(solution)/shard_map/ppermute | solution.py:445
  9.1 36.3 %collective-permute-start.1 = (bf16[2,128,768]{2,1,0:T(8,128)(2,1)S(1)}, bf16[2,128,768]{2,1,0:T(8,128)(2,1)S(1)}, u32[]{:S(2)}, u32[]{:S(2)}) collective-permute-start(bf16[2,128,768]{2,1,0:T(8,128)(2,1)S(1)} %pad_maximum_fusion.20.refs_11_), channel_id=1, source_target_pairs={{0,8},{4,12},{8,0},{12,4},{1,9},{5,13},{9,1},{13,5},{2,10},{6,14},... | collective-permute-start | bytes 1179656 | tf_op jit(solution)/shard_map/ppermute | solution.py:445
  9.1 36.3 %collective-permute-start = (bf16[2,128,768]{2,1,0:T(8,128)(2,1)S(1)}, bf16[2,128,768]{2,1,0:T(8,128)(2,1)}, u32[]{:S(2)}, u32[]{:S(2)}) collective-permute-start(bf16[2,128,768]{2,1,0:T(8,128)(2,1)S(1)} %pad_maximum_fusion.20.refs_11_), channel_id=1, source_target_pairs={{0,4},{4,8},{8,12},{12,0},{1,5},{5,9},{9,13},{13,1},{2,6},{6,10},{... | collective-permute-start | bytes 1179656 | tf_op jit(solution)/shard_map/ppermute | solution.py:445
  10.9 34.5 %all-to-all-start = ((f32[32,1,352]{2,1,0:T(1,128)}), f32[32,1,352]{2,1,0:T(1,128)S(1)}, u32[]{:S(2)}, u32[]{:S(2)}) async-start(f32[32,1,352]{2,1,0:T(1,128)} %broadcast_in_dim.8), calls=%async_computation | async-start | bytes 98304 | tf_op jit(solution)/shard_map/all_to_all | solution.py:531
  46.6 19.6 %collective-permute-start.3 = (bf16[512,768]{1,0:T(8,128)(2,1)S(1)}, bf16[512,768]{1,0:T(8,128)(2,1)S(1)}, u32[]{:S(2)}, u32[]{:S(2)}) collective-permute-start(bf16[512,768]{1,0:T(8,128)(2,1)S(1)} %pad_maximum_fusion.13.refs_15_), channel_id=1, source_target_pairs={{0,16},{16,0},{1,17},{17,1},{2,18},{18,2},{3,19},{19,3},{4,20},{20... | collective-permute-start | bytes 2359304 | tf_op jit(solution)/shard_map/ppermute | solution.py:448
  47.4 31.8 %copy-start.14 = (bf16[512,768]{1,0:T(8,128)(2,1)}, bf16[512,768]{1,0:T(8,128)(2,1)S(1)}, u32[]{:S(2)}) copy-start(bf16[512,768]{1,0:T(8,128)(2,1)S(1)} %pad_maximum_fusion.14.refs_16_) | copy-start | bytes 2359300
  47.4 30.9 %collective-permute-start.4 = (bf16[512,768]{1,0:T(8,128)(2,1)S(1)}, bf16[512,768]{1,0:T(8,128)(2,1)S(1)}, u32[]{:S(2)}, u32[]{:S(2)}) collective-permute-start(bf16[512,768]{1,0:T(8,128)(2,1)S(1)} %pad_maximum_fusion.14.refs_16_), channel_id=1, source_target_pairs={{0,2},{1,3},{2,0},{3,1},{4,6},{5,7},{6,4},{7,5},{8,10},{9,11},{10,... | collective-permute-start | bytes 2359304 | tf_op jit(solution)/shard_map/ppermute | solution.py:442
  48.1 76.0 %all-to-all-start.1 = ((bf16[16,128,512]{2,1,0:T(8,128)(2,1)}), bf16[16,128,512]{2,1,0:T(8,128)(2,1)}, u32[]{:S(2)}, u32[]{:S(2)}) async-start(bf16[16,128,512]{2,1,0:T(8,128)(2,1)} %bitcast.16), calls=%async_computation.1 | async-start | bytes 4194304 | tf_op jit(solution)/shard_map/all_to_all | solution.py:439
  54.0 28.0 %copy-start.13 = (bf16[512,768]{1,0:T(8,128)(2,1)S(1)}, bf16[512,768]{1,0:T(8,128)(2,1)}, u32[]{:S(2)}) copy-start(bf16[512,768]{1,0:T(8,128)(2,1)} %copy-done.12) | copy-start | bytes 2359300
  80.5 36.7 %copy-start = (bf16[2,512,768]{2,1,0:T(8,128)(2,1)}, bf16[2,512,768]{2,1,0:T(8,128)(2,1)S(1)}, u32[]{:S(2)}) copy-start(bf16[2,512,768]{2,1,0:T(8,128)(2,1)S(1)} %pad_maximum_fusion.6.refs_2_.refs_4_.refs_18_.refs_1_.refs_3_) | copy-start | bytes 4718596
  80.5 30.5 %collective-permute-start.5 = (bf16[2,512,768]{2,1,0:T(8,128)(2,1)S(1)}, bf16[2,512,768]{2,1,0:T(8,128)(2,1)S(1)}, u32[]{:S(2)}, u32[]{:S(2)}) collective-permute-start(bf16[2,512,768]{2,1,0:T(8,128)(2,1)S(1)} %pad_maximum_fusion.6.refs_2_.refs_4_.refs_18_.refs_1_.refs_3_), channel_id=1, source_target_pairs={{0,16},{16,0},{1,17},{17,1},{2,18},{18,2},{3,19},{19,3},{4,20},{20... | collective-permute-start | bytes 4718600 | tf_op jit(solution)/shard_map/ppermute | solution.py:448
  83.3 39.7 %collective-permute-start.8 = (bf16[2,512,768]{2,1,0:T(8,128)(2,1)}, bf16[2,512,768]{2,1,0:T(8,128)(2,1)}, u32[]{:S(2)}, u32[]{:S(2)}) collective-permute-start(bf16[2,512,768]{2,1,0:T(8,128)(2,1)} %pad_maximum_fusion.5.refs_17_.refs_1_.refs_2_.refs_3_), channel_id=1, source_target_pairs={{0,2},{1,3},{2,0},{3,1},{4,6},{5,7},{6,4},{7,5},{8,10},{9,11},{10,... | collective-permute-start | bytes 4718600 | tf_op jit(solution)/shard_map/ppermute | solution.py:442
  83.3 40.8 %collective-permute-start.6 = (bf16[2,512,768]{2,1,0:T(8,128)(2,1)S(1)}, bf16[2,512,768]{2,1,0:T(8,128)(2,1)}, u32[]{:S(2)}, u32[]{:S(2)}) collective-permute-start(bf16[2,512,768]{2,1,0:T(8,128)(2,1)S(1)} %pad_maximum_fusion.6.refs_2_.refs_4_.refs_18_.refs_1_.refs_3_), channel_id=1, source_target_pairs={{0,1},{1,0},{2,3},{3,2},{4,5},{5,4},{6,7},{7,6},{8,9},{9,8},{10,11... | collective-permute-start | bytes 4718600 | tf_op jit(solution)/shard_map/ppermute | solution.py:442
  111.1 15.3 %copy-start.1 = (bf16[2,512,768]{2,1,0:T(8,128)(2,1)}, bf16[2,512,768]{2,1,0:T(8,128)(2,1)S(1)}, u32[]{:S(2)}) copy-start(bf16[2,512,768]{2,1,0:T(8,128)(2,1)S(1)} %collective-permute-done.5.refs_3_.refs_5_.refs_2_.refs_4_) | copy-start | bytes 4718596
  111.1 13.1 %collective-permute-start.7 = (bf16[2,512,768]{2,1,0:T(8,128)(2,1)S(1)}, bf16[2,512,768]{2,1,0:T(8,128)(2,1)}, u32[]{:S(2)}, u32[]{:S(2)}) collective-permute-start(bf16[2,512,768]{2,1,0:T(8,128)(2,1)S(1)} %collective-permute-done.5.refs_3_.refs_5_.refs_2_.refs_4_), channel_id=1, source_target_pairs={{0,1},{1,0},{2,3},{3,2},{4,5},{5,4},{6,7},{7,6},{8,9},{9,8},{10,11... | collective-permute-start | bytes 4718600 | tf_op jit(solution)/shard_map/ppermute | solution.py:442
  111.1 27.2 %collective-permute-start.13 = (bf16[2,128,1024]{2,1,0:T(8,128)(2,1)}, bf16[2,128,1024]{2,1,0:T(8,128)(2,1)}, u32[]{:S(2)}, u32[]{:S(2)}) collective-permute-start(bf16[2,128,1024]{2,1,0:T(8,128)(2,1)} %pad_maximum_fusion.15.refs_14_), channel_id=1, source_target_pairs={{0,12},{4,0},{8,4},{12,8},{1,13},{5,1},{9,5},{13,9},{2,14},{6,2},{... | collective-permute-start | bytes 1572872 | tf_op jit(solution)/shard_map/ppermute | solution.py:445
  116.8 42.8 %collective-permute-start.12 = (bf16[2,128,1024]{2,1,0:T(8,128)(2,1)}, bf16[2,128,1024]{2,1,0:T(8,128)(2,1)}, u32[]{:S(2)}, u32[]{:S(2)}) collective-permute-start(bf16[2,128,1024]{2,1,0:T(8,128)(2,1)} %pad_maximum_fusion.15.refs_14_), channel_id=1, source_target_pairs={{0,8},{4,12},{8,0},{12,4},{1,9},{5,13},{9,1},{13,5},{2,10},{6,14},... | collective-permute-start | bytes 1572872 | tf_op jit(solution)/shard_map/ppermute | solution.py:445
  123.0 36.5 %collective-permute-start.11 = (bf16[2,128,1024]{2,1,0:T(8,128)(2,1)}, bf16[2,128,1024]{2,1,0:T(8,128)(2,1)}, u32[]{:S(2)}, u32[]{:S(2)}) collective-permute-start(bf16[2,128,1024]{2,1,0:T(8,128)(2,1)} %pad_maximum_fusion.15.refs_14_), channel_id=1, source_target_pairs={{0,4},{4,8},{8,12},{12,0},{1,5},{5,9},{9,13},{13,1},{2,6},{6,10},{... | collective-permute-start | bytes 1572872 | tf_op jit(solution)/shard_map/ppermute | solution.py:445
  124.1 40.7 %collective-permute-start.9 = (bf16[2,512,768]{2,1,0:T(8,128)(2,1)}, bf16[2,512,768]{2,1,0:T(8,128)(2,1)S(1)}, u32[]{:S(2)}, u32[]{:S(2)}) collective-permute-start(bf16[2,512,768]{2,1,0:T(8,128)(2,1)} %pad_maximum_fusion.5.refs_17_.refs_1_.refs_2_.refs_3_), channel_id=1, source_target_pairs={{0,1},{1,0},{2,3},{3,2},{4,5},{5,4},{6,7},{7,6},{8,9},{9,8},{10,11... | collective-permute-start | bytes 4718600 | tf_op jit(solution)/shard_map/ppermute | solution.py:442
  124.2 40.7 %collective-permute-start.10 = (bf16[2,512,768]{2,1,0:T(8,128)(2,1)}, bf16[2,512,768]{2,1,0:T(8,128)(2,1)S(1)}, u32[]{:S(2)}, u32[]{:S(2)}) collective-permute-start(bf16[2,512,768]{2,1,0:T(8,128)(2,1)} %collective-permute-done.8.refs_3_.refs_4_.refs_5_), channel_id=1, source_target_pairs={{0,1},{1,0},{2,3},{3,2},{4,5},{5,4},{6,7},{7,6},{8,9},{9,8},{10,11... | collective-permute-start | bytes 4718600 | tf_op jit(solution)/shard_map/ppermute | solution.py:442
  129.1 30.5 %copy-start.15 = (bf16[2,128,1024]{2,1,0:T(8,128)(2,1)S(1)}, bf16[2,128,1024]{2,1,0:T(8,128)(2,1)}, u32[]{:S(2)}) copy-start(bf16[2,128,1024]{2,1,0:T(8,128)(2,1)} %pad_maximum_fusion.15.refs_14_) | copy-start | bytes 1572868
  174.2 10.5 %collective-permute-start.14 = (bf16[2,512,768]{2,1,0:T(8,128)(2,1)}, bf16[2,512,768]{2,1,0:T(8,128)(2,1)}, u32[]{:S(2)}, u32[]{:S(2)}) collective-permute-start(bf16[2,512,768]{2,1,0:T(8,128)(2,1)} %get-tuple-element.720.refs_0_), channel_id=1, source_target_pairs={{0,1},{1,0},{2,3},{3,2},{4,5},{5,4},{6,7},{7,6},{8,9},{9,8},{10,11... | collective-permute-start | bytes 4718600 | tf_op jit(solution)/shard_map/ppermute | solution.py:442
  174.3 25.6 %collective-permute-start.16 = (bf16[512,1024]{1,0:T(8,128)(2,1)S(1)}, bf16[512,1024]{1,0:T(8,128)(2,1)S(1)}, u32[]{:S(2)}, u32[]{:S(2)}) collective-permute-start(bf16[512,1024]{1,0:T(8,128)(2,1)S(1)} %copy-done.10), channel_id=1, source_target_pairs={{0,16},{16,0},{1,17},{17,1},{2,18},{18,2},{3,19},{19,3},{4,20},{20... | collective-permute-start | bytes 3145736 | tf_op jit(solution)/shard_map/ppermute | solution.py:448
  174.9 34.5 %collective-permute-start.17 = (bf16[512,1024]{1,0:T(8,128)(2,1)S(1)}, bf16[512,1024]{1,0:T(8,128)(2,1)}, u32[]{:S(2)}, u32[]{:S(2)}) collective-permute-start(bf16[512,1024]{1,0:T(8,128)(2,1)S(1)} %copy-done.9), channel_id=1, source_target_pairs={{0,2},{1,3},{2,0},{3,1},{4,6},{5,7},{6,4},{7,5},{8,10},{9,11},{10,... | collective-permute-start | bytes 3145736 | tf_op jit(solution)/shard_map/ppermute | solution.py:442
  176.1 66.5 %all-to-all-start.2 = ((bf16[16,32,1024]{2,1,0:T(8,128)(2,1)}), bf16[16,32,1024]{2,1,0:T(8,128)(2,1)}, u32[]{:S(2)}, u32[]{:S(2)}) async-start(bf16[16,32,1024]{2,1,0:T(8,128)(2,1)} %bitcast.45), calls=%async_computation.2 | async-start | bytes 2097152 | tf_op jit(solution)/shard_map/all_to_all | solution.py:439
  212.2 46.0 %collective-permute-start.19 = (bf16[2,512,1024]{2,1,0:T(8,128)(2,1)}, bf16[2,512,1024]{2,1,0:T(8,128)(2,1)S(1)}, u32[]{:S(2)}, u32[]{:S(2)}) collective-permute-start(bf16[2,512,1024]{2,1,0:T(8,128)(2,1)} %pad_maximum_fusion.2.refs_4_.refs_1_.refs_3_.refs_2_), channel_id=1, source_target_pairs={{0,16},{16,0},{1,17},{17,1},{2,18},{18,2},{3,19},{19,3},{4,20},{20... | collective-permute-start | bytes 6291464 | tf_op jit(solution)/shard_map/ppermute | solution.py:448
  216.4 46.1 %collective-permute-start.18 = (bf16[2,512,1024]{2,1,0:T(8,128)(2,1)}, bf16[2,512,1024]{2,1,0:T(8,128)(2,1)}, u32[]{:S(2)}, u32[]{:S(2)}) collective-permute-start(bf16[2,512,1024]{2,1,0:T(8,128)(2,1)} %pad_maximum_fusion.1.refs_3_.refs_1_.refs_2_), channel_id=1, source_target_pairs={{0,2},{1,3},{2,0},{3,1},{4,6},{5,7},{6,4},{7,5},{8,10},{9,11},{10,... | collective-permute-start | bytes 6291464 | tf_op jit(solution)/shard_map/ppermute | solution.py:442
  216.6 3.8 collective-permute-start.15
  245.8 19.1 %copy-start.2 = (bf16[512,1024]{1,0:T(8,128)(2,1)}, bf16[512,1024]{1,0:T(8,128)(2,1)S(1)}, u32[]{:S(2)}) copy-start(bf16[512,1024]{1,0:T(8,128)(2,1)S(1)} %multiply_convert_fusion.refs_7_.refs_0_.refs_11_) | copy-start | bytes 3145732
  262.5 10.0 %collective-permute-start.20 = (bf16[2,512,1024]{2,1,0:T(8,128)(2,1)}, bf16[2,512,1024]{2,1,0:T(8,128)(2,1)}, u32[]{:S(2)}, u32[]{:S(2)}) collective-permute-start(bf16[2,512,1024]{2,1,0:T(8,128)(2,1)} %pad_maximum_fusion.1.refs_3_.refs_1_.refs_2_), channel_id=1, source_target_pairs={{0,1},{1,0},{2,3},{3,2},{4,5},{5,4},{6,7},{7,6},{8,9},{9,8},{10,11... | collective-permute-start | bytes 6291464 | tf_op jit(solution)/shard_map/ppermute | solution.py:442
  262.5 10.5 %collective-permute-start.21 = (bf16[2,512,1024]{2,1,0:T(8,128)(2,1)}, bf16[2,512,1024]{2,1,0:T(8,128)(2,1)}, u32[]{:S(2)}, u32[]{:S(2)}) collective-permute-start(bf16[2,512,1024]{2,1,0:T(8,128)(2,1)} %collective-permute-done.18.refs_3_.refs_4_.refs_5_), channel_id=1, source_target_pairs={{0,1},{1,0},{2,3},{3,2},{4,5},{5,4},{6,7},{7,6},{8,9},{9,8},{10,11... | collective-permute-start | bytes 6291464 | tf_op jit(solution)/shard_map/ppermute | solution.py:442
  264.3 24.0 %collective-permute-start.24 = (bf16[2,512,1024]{2,1,0:T(8,128)(2,1)}, bf16[2,512,1024]{2,1,0:T(8,128)(2,1)}, u32[]{:S(2)}, u32[]{:S(2)}) collective-permute-start(bf16[2,512,1024]{2,1,0:T(8,128)(2,1)} %pad_maximum_fusion.2.refs_4_.refs_1_.refs_3_.refs_2_), channel_id=1, source_target_pairs={{0,1},{1,0},{2,3},{3,2},{4,5},{5,4},{6,7},{7,6},{8,9},{9,8},{10,11... | collective-permute-start | bytes 6291464 | tf_op jit(solution)/shard_map/ppermute | solution.py:442
  264.3 24.0 %collective-permute-start.25 = (bf16[2,512,1024]{2,1,0:T(8,128)(2,1)S(1)}, bf16[2,512,1024]{2,1,0:T(8,128)(2,1)}, u32[]{:S(2)}, u32[]{:S(2)}) collective-permute-start(bf16[2,512,1024]{2,1,0:T(8,128)(2,1)S(1)} %collective-permute-done.19.refs_2_.refs_4_.refs_3_.refs_5_), channel_id=1, source_target_pairs={{0,1},{1,0},{2,3},{3,2},{4,5},{5,4},{6,7},{7,6},{8,9},{9,8},{10,11... | collective-permute-start | bytes 6291464 | tf_op jit(solution)/shard_map/ppermute | solution.py:442
  287.7 7.4 %collective-permute-start.22 = (bf16[2,512,1024]{2,1,0:T(8,128)(2,1)}, bf16[2,512,1024]{2,1,0:T(8,128)(2,1)}, u32[]{:S(2)}, u32[]{:S(2)}) collective-permute-start(bf16[2,512,1024]{2,1,0:T(8,128)(2,1)} %get-tuple-element.628), channel_id=1, source_target_pairs={{0,1},{1,0},{2,3},{3,2},{4,5},{5,4},{6,7},{7,6},{8,9},{9,8},{10,11... | collective-permute-start | bytes 6291464 | tf_op jit(solution)/shard_map/ppermute | solution.py:442
  287.9 7.4 %collective-permute-start.23 = (bf16[2,512,1024]{2,1,0:T(8,128)(2,1)}, bf16[2,512,1024]{2,1,0:T(8,128)(2,1)}, u32[]{:S(2)}, u32[]{:S(2)}) collective-permute-start(bf16[2,512,1024]{2,1,0:T(8,128)(2,1)} %get-tuple-element.629), channel_id=1, source_target_pairs={{0,1},{1,0},{2,3},{3,2},{4,5},{5,4},{6,7},{7,6},{8,9},{9,8},{10,11... | collective-permute-start | bytes 6291464 | tf_op jit(solution)/shard_map/ppermute | solution.py:442
  315.3 16.0 %collective-permute-start.26 = (bf16[2,512,1024]{2,1,0:T(8,128)(2,1)}, bf16[2,512,1024]{2,1,0:T(8,128)(2,1)S(1)}, u32[]{:S(2)}, u32[]{:S(2)}) collective-permute-start(bf16[2,512,1024]{2,1,0:T(8,128)(2,1)} %get-tuple-element.677), channel_id=1, source_target_pairs={{0,1},{1,0},{2,3},{3,2},{4,5},{5,4},{6,7},{7,6},{8,9},{9,8},{10,11... | collective-permute-start | bytes 6291464 | tf_op jit(solution)/shard_map/ppermute | solution.py:442
  315.5 15.8 %collective-permute-start.27 = (bf16[2,512,1024]{2,1,0:T(8,128)(2,1)}, bf16[2,512,1024]{2,1,0:T(8,128)(2,1)S(1)}, u32[]{:S(2)}, u32[]{:S(2)}) collective-permute-start(bf16[2,512,1024]{2,1,0:T(8,128)(2,1)} %get-tuple-element.678), channel_id=1, source_target_pairs={{0,1},{1,0},{2,3},{3,2},{4,5},{5,4},{6,7},{7,6},{8,9},{9,8},{10,11... | collective-permute-start | bytes 6291464 | tf_op jit(solution)/shard_map/ppermute | solution.py:442
  315.9 57.6 %collective-permute-start.28 = (bf16[2,512,1024]{2,1,0:T(8,128)(2,1)}, bf16[2,512,1024]{2,1,0:T(8,128)(2,1)S(1)}, u32[]{:S(2)}, u32[]{:S(2)}) collective-permute-start(bf16[2,512,1024]{2,1,0:T(8,128)(2,1)} %get-tuple-element.698), channel_id=1, source_target_pairs={{0,2},{1,3},{2,0},{3,1},{4,6},{5,7},{6,4},{7,5},{8,10},{9,11},{10,... | collective-permute-start | bytes 6291464 | tf_op jit(solution)/shard_map/ppermute | solution.py:442
  339.6 51.6 %collective-permute-start.31 = (bf16[2,512,1024]{2,1,0:T(8,128)(2,1)}, bf16[2,512,1024]{2,1,0:T(8,128)(2,1)S(1)}, u32[]{:S(2)}, u32[]{:S(2)}) collective-permute-start(bf16[2,512,1024]{2,1,0:T(8,128)(2,1)} %get-tuple-element.745), channel_id=1, source_target_pairs={{0,16},{16,0},{1,17},{17,1},{2,18},{18,2},{3,19},{19,3},{4,20},{20... | collective-permute-start | bytes 6291464 | tf_op jit(solution)/shard_map/ppermute | solution.py:448
  375.8 16.7 %copy-start.20 = (bf16[2,512,1024]{2,1,0:T(8,128)(2,1)S(1)}, bf16[2,512,1024]{2,1,0:T(8,128)(2,1)}, u32[]{:S(2)}) copy-start(bf16[2,512,1024]{2,1,0:T(8,128)(2,1)} %get-tuple-element.748) | copy-start | bytes 6291460
  388.9 9.0 %collective-permute-start.30 = (bf16[2,512,512]{2,1,0:T(8,128)(2,1)}, bf16[2,512,512]{2,1,0:T(8,128)(2,1)S(1)}, u32[]{:S(2)}, u32[]{:S(2)}) collective-permute-start(bf16[2,512,512]{2,1,0:T(8,128)(2,1)} %get-tuple-element.743), channel_id=1, source_target_pairs={{0,1},{1,0},{2,3},{3,2},{4,5},{5,4},{6,7},{7,6},{8,9},{9,8},{10,11... | collective-permute-start | bytes 3145736 | tf_op jit(solution)/shard_map/ppermute | solution.py:442
  388.9 15.5 %collective-permute-start.29 = (bf16[2,512,512]{2,1,0:T(8,128)(2,1)}, bf16[2,512,512]{2,1,0:T(8,128)(2,1)S(1)}, u32[]{:S(2)}, u32[]{:S(2)}) collective-permute-start(bf16[2,512,512]{2,1,0:T(8,128)(2,1)} %get-tuple-element.740), channel_id=1, source_target_pairs={{0,1},{1,0},{2,3},{3,2},{4,5},{5,4},{6,7},{7,6},{8,9},{9,8},{10,11... | collective-permute-start | bytes 3145736 | tf_op jit(solution)/shard_map/ppermute | solution.py:442
  389.5 38.0 %collective-permute-start.36 = (bf16[512,1024]{1,0:T(8,128)(2,1)S(1)}, bf16[512,1024]{1,0:T(8,128)(2,1)}, u32[]{:S(2)}, u32[]{:S(2)}) collective-permute-start(bf16[512,1024]{1,0:T(8,128)(2,1)S(1)} %copy-done.17), channel_id=1, source_target_pairs={{0,16},{16,0},{1,17},{17,1},{2,18},{18,2},{3,19},{19,3},{4,20},{20... | collective-permute-start | bytes 3145736 | tf_op jit(solution)/shard_map/ppermute | solution.py:448
  396.2 39.6 %collective-permute-start.37 = (bf16[512,1024]{1,0:T(8,128)(2,1)S(1)}, bf16[512,1024]{1,0:T(8,128)(2,1)}, u32[]{:S(2)}, u32[]{:S(2)}) collective-permute-start(bf16[512,1024]{1,0:T(8,128)(2,1)S(1)} %get-tuple-element.759.refs_5_), channel_id=1, source_target_pairs={{0,2},{1,3},{2,0},{3,1},{4,6},{5,7},{6,4},{7,5},{8,10},{9,11},{10,... | collective-permute-start | bytes 3145736 | tf_op jit(solution)/shard_map/ppermute | solution.py:442
  421.9 19.1 %collective-permute-start.34 = (bf16[2,512,768]{2,1,0:T(8,128)(2,1)}, bf16[2,512,768]{2,1,0:T(8,128)(2,1)}, u32[]{:S(2)}, u32[]{:S(2)}) collective-permute-start(bf16[2,512,768]{2,1,0:T(8,128)(2,1)} %get-tuple-element.802), channel_id=1, source_target_pairs={{0,1},{1,0},{2,3},{3,2},{4,5},{5,4},{6,7},{7,6},{8,9},{9,8},{10,11... | collective-permute-start | bytes 4718600 | tf_op jit(solution)/shard_map/ppermute | solution.py:442
  421.9 19.1 %collective-permute-start.35 = (bf16[2,512,768]{2,1,0:T(8,128)(2,1)}, bf16[2,512,768]{2,1,0:T(8,128)(2,1)}, u32[]{:S(2)}, u32[]{:S(2)}) collective-permute-start(bf16[2,512,768]{2,1,0:T(8,128)(2,1)} %get-tuple-element.803), channel_id=1, source_target_pairs={{0,1},{1,0},{2,3},{3,2},{4,5},{5,4},{6,7},{7,6},{8,9},{9,8},{10,11... | collective-permute-start | bytes 4718600 | tf_op jit(solution)/shard_map/ppermute | solution.py:442
  427.4 18.9 %collective-permute-start.32 = (bf16[2,512,768]{2,1,0:T(8,128)(2,1)}, bf16[2,512,768]{2,1,0:T(8,128)(2,1)}, u32[]{:S(2)}, u32[]{:S(2)}) collective-permute-start(bf16[2,512,768]{2,1,0:T(8,128)(2,1)} %get-tuple-element.800), channel_id=1, source_target_pairs={{0,1},{1,0},{2,3},{3,2},{4,5},{5,4},{6,7},{7,6},{8,9},{9,8},{10,11... | collective-permute-start | bytes 4718600 | tf_op jit(solution)/shard_map/ppermute | solution.py:442
  427.5 18.9 %collective-permute-start.33 = (bf16[2,512,768]{2,1,0:T(8,128)(2,1)}, bf16[2,512,768]{2,1,0:T(8,128)(2,1)}, u32[]{:S(2)}, u32[]{:S(2)}) collective-permute-start(bf16[2,512,768]{2,1,0:T(8,128)(2,1)} %get-tuple-element.801), channel_id=1, source_target_pairs={{0,1},{1,0},{2,3},{3,2},{4,5},{5,4},{6,7},{7,6},{8,9},{9,8},{10,11... | collective-permute-start | bytes 4718600 | tf_op jit(solution)/shard_map/ppermute | solution.py:442
  428.0 34.8 %all-to-all-start.4 = ((bf16[16,32,1024]{2,1,0:T(8,128)(2,1)}), bf16[16,32,1024]{2,1,0:T(8,128)(2,1)S(1)}, u32[]{:S(2)}, u32[]{:S(2)}) async-start(bf16[16,32,1024]{2,1,0:T(8,128)(2,1)} %bitcast.72), calls=%async_computation.4 | async-start | bytes 2097152 | tf_op jit(solution)/shard_map/all_to_all | solution.py:439
  451.8 52.0 %collective-permute-start.41 = (bf16[2,512,768]{2,1,0:T(8,128)(2,1)}, bf16[2,512,768]{2,1,0:T(8,128)(2,1)}, u32[]{:S(2)}, u32[]{:S(2)}) collective-permute-start(bf16[2,512,768]{2,1,0:T(8,128)(2,1)} %get-tuple-element.838), channel_id=1, source_target_pairs={{0,2},{1,3},{2,0},{3,1},{4,6},{5,7},{6,4},{7,5},{8,10},{9,11},{10,... | collective-permute-start | bytes 4718600 | tf_op jit(solution)/shard_map/ppermute | solution.py:442
  459.4 46.3 %collective-permute-start.43 = (bf16[2,512,768]{2,1,0:T(8,128)(2,1)}, bf16[2,512,768]{2,1,0:T(8,128)(2,1)}, u32[]{:S(2)}, u32[]{:S(2)}) collective-permute-start(bf16[2,512,768]{2,1,0:T(8,128)(2,1)} %get-tuple-element.842), channel_id=1, source_target_pairs={{0,16},{16,0},{1,17},{17,1},{2,18},{18,2},{3,19},{19,3},{4,20},{20... | collective-permute-start | bytes 4718600 | tf_op jit(solution)/shard_map/ppermute | solution.py:448
  462.8 33.6 %all-to-all-start.5 = ((f32[32,1,352]{2,1,0:T(1,128)}), f32[32,1,352]{2,1,0:T(1,128)S(1)}, u32[]{:S(2)}, u32[]{:S(2)}) async-start(f32[32,1,352]{2,1,0:T(1,128)} %copy.83), calls=%async_computation.5 | async-start | bytes 98304 | tf_op jit(solution)/shard_map/all_to_all | solution.py:673
  496.4 117.6 %all-to-all-start.3 = ((bf16[16,128,512]{2,1,0:T(8,128)(2,1)}), bf16[16,128,512]{2,1,0:T(8,128)(2,1)S(1)}, u32[]{:S(2)}, u32[]{:S(2)}) async-start(bf16[16,128,512]{2,1,0:T(8,128)(2,1)} %bitcast.191), calls=%async_computation.3 | async-start | bytes 4194304 | tf_op jit(solution)/shard_map/all_to_all | solution.py:439
  507.5 36.2 %collective-permute-start.44 = (bf16[512,768]{1,0:T(8,128)(2,1)S(1)}, bf16[512,768]{1,0:T(8,128)(2,1)S(1)}, u32[]{:S(2)}, u32[]{:S(2)}) collective-permute-start(bf16[512,768]{1,0:T(8,128)(2,1)S(1)} %get-tuple-element.938), channel_id=1, source_target_pairs={{0,2},{1,3},{2,0},{3,1},{4,6},{5,7},{6,4},{7,5},{8,10},{9,11},{10,... | collective-permute-start | bytes 2359304 | tf_op jit(solution)/shard_map/ppermute | solution.py:442
  509.6 34.1 %collective-permute-start.42 = (bf16[512,768]{1,0:T(8,128)(2,1)S(1)}, bf16[512,768]{1,0:T(8,128)(2,1)S(1)}, u32[]{:S(2)}, u32[]{:S(2)}) collective-permute-start(bf16[512,768]{1,0:T(8,128)(2,1)S(1)} %get-tuple-element.940), channel_id=1, source_target_pairs={{0,16},{16,0},{1,17},{17,1},{2,18},{18,2},{3,19},{19,3},{4,20},{20... | collective-permute-start | bytes 2359304 | tf_op jit(solution)/shard_map/ppermute | solution.py:448
  511.8 38.1 %collective-permute-start.38 = (bf16[2,128,1024]{2,1,0:T(8,128)(2,1)S(1)}, bf16[2,128,1024]{2,1,0:T(8,128)(2,1)S(1)}, u32[]{:S(2)}, u32[]{:S(2)}) collective-permute-start(bf16[2,128,1024]{2,1,0:T(8,128)(2,1)S(1)} %pad_maximum_fusion.17), channel_id=1, source_target_pairs={{0,12},{4,0},{8,4},{12,8},{1,13},{5,1},{9,5},{13,9},{2,14},{6,2},{... | collective-permute-start | bytes 1572872 | tf_op jit(solution)/shard_map/ppermute | solution.py:445
  515.0 97.6 %collective-permute-start.39 = (bf16[2,128,1024]{2,1,0:T(8,128)(2,1)S(1)}, bf16[2,128,1024]{2,1,0:T(8,128)(2,1)S(1)}, u32[]{:S(2)}, u32[]{:S(2)}) collective-permute-start(bf16[2,128,1024]{2,1,0:T(8,128)(2,1)S(1)} %pad_maximum_fusion.18), channel_id=1, source_target_pairs={{0,8},{4,12},{8,0},{12,4},{1,9},{5,13},{9,1},{13,5},{2,10},{6,14},... | collective-permute-start | bytes 1572872 | tf_op jit(solution)/shard_map/ppermute | solution.py:445
  515.0 97.6 %collective-permute-start.40 = (bf16[2,128,1024]{2,1,0:T(8,128)(2,1)S(1)}, bf16[2,128,1024]{2,1,0:T(8,128)(2,1)S(1)}, u32[]{:S(2)}, u32[]{:S(2)}) collective-permute-start(bf16[2,128,1024]{2,1,0:T(8,128)(2,1)S(1)} %pad_maximum_fusion.19), channel_id=1, source_target_pairs={{0,4},{4,8},{8,12},{12,0},{1,5},{5,9},{9,13},{13,1},{2,6},{6,10},{... | collective-permute-start | bytes 1572872 | tf_op jit(solution)/shard_map/ppermute | solution.py:445
  545.0 78.8 %collective-permute-start.45 = (bf16[2,128,768]{2,1,0:T(8,128)(2,1)}, bf16[2,128,768]{2,1,0:T(8,128)(2,1)}, u32[]{:S(2)}, u32[]{:S(2)}) collective-permute-start(bf16[2,128,768]{2,1,0:T(8,128)(2,1)} %pad_maximum_fusion.22), channel_id=1, source_target_pairs={{0,12},{4,0},{8,4},{12,8},{1,13},{5,1},{9,5},{13,9},{2,14},{6,2},{... | collective-permute-start | bytes 1179656 | tf_op jit(solution)/shard_map/ppermute | solution.py:445
  546.3 82.9 %collective-permute-start.46 = (bf16[2,128,768]{2,1,0:T(8,128)(2,1)}, bf16[2,128,768]{2,1,0:T(8,128)(2,1)}, u32[]{:S(2)}, u32[]{:S(2)}) collective-permute-start(bf16[2,128,768]{2,1,0:T(8,128)(2,1)} %pad_maximum_fusion.23), channel_id=1, source_target_pairs={{0,8},{4,12},{8,0},{12,4},{1,9},{5,13},{9,1},{13,5},{2,10},{6,14},... | collective-permute-start | bytes 1179656 | tf_op jit(solution)/shard_map/ppermute | solution.py:445
  549.8 79.3 %collective-permute-start.47 = (bf16[2,128,768]{2,1,0:T(8,128)(2,1)}, bf16[2,128,768]{2,1,0:T(8,128)(2,1)}, u32[]{:S(2)}, u32[]{:S(2)}) collective-permute-start(bf16[2,128,768]{2,1,0:T(8,128)(2,1)} %pad_maximum_fusion.24), channel_id=1, source_target_pairs={{0,4},{4,8},{8,12},{12,0},{1,5},{5,9},{9,13},{13,1},{2,6},{6,10},{... | collective-permute-start | bytes 1179656 | tf_op jit(solution)/shard_map/ppermute | solution.py:445
  (45 other events, 302.2 us)

commit v3 on v2

v3 whole, which is shorter than its diff:
```python
import functools

import jax
import jax.numpy as jnp
from jax import lax
from jax.experimental import pallas as pl
from jax.experimental.pallas import tpu as pltpu
from jax.sharding import PartitionSpec as P

HD = 64
EPSILON = 1e-05
F32 = jnp.float32
BF16 = jnp.bfloat16
ALL = ("fsdp", "ctx", "tp")
PARAMS = pltpu.CompilerParams(vmem_limit_bytes=56 * 1024 * 1024)
CHUNK = 128


def mxu(a, b, a_dim, b_dim):
    return lax.dot_general(a, b, (((a_dim,), (b_dim,)), ((), ())), preferred_element_type=F32)


def whole(shape):
    return pl.BlockSpec(shape, lambda *_: (0,) * len(shape))


def call(body, roles, after, *, in_specs, out_specs, out_shape, grid, name, scratch_shapes=()):
    n_in, n_after, n_out = len(in_specs), len(after), len(out_specs)

    def run(roles_ref, *refs):
        outs = refs[n_in + n_after :]
        outs[n_out][...] = jnp.zeros((8, 128), F32)
        body(roles_ref, *refs[:n_in], *outs[:n_out], *outs[n_out + 1 :])

    def apply(*args):
        outs = pl.pallas_call(
            run,
            grid_spec=pltpu.PrefetchScalarGridSpec(
                num_scalar_prefetch=1,
                grid=grid,
                in_specs=[*in_specs, *[pl.BlockSpec(memory_space=pl.ANY)] * n_after],
                out_specs=[*out_specs, whole((8, 128))],
                scratch_shapes=scratch_shapes,
            ),
            out_shape=[*out_shape, jax.ShapeDtypeStruct((8, 128), F32)],
            compiler_params=PARAMS,
            cost_estimate=pl.CostEstimate(flops=1, bytes_accessed=1, transcendentals=0),
            name=name,
        )(roles, *args, *after)
        return outs[:-1], outs[-1]

    return apply


def attend_forward_body(share, heads, roles, *refs):
    own, others = refs[0], refs[1:share]
    p_ref, o_ref = refs[share:]
    part = heads * HD
    rows = lax.broadcasted_iota(jnp.int32, (part, own.shape[1]), 0) // HD
    lanes = lax.broadcasted_iota(jnp.int32, (own.shape[1], part), 1) // HD
    q = own[0, :, :part] * jnp.asarray(HD**-0.5, BF16)
    k = jnp.concatenate([r[0, :, part : 2 * part] for r in (own, *others)], axis=0)
    v = jnp.concatenate([r[0, :, 2 * part :] for r in (own, *others)], axis=0)
    total = jnp.zeros((part, q.shape[0]), F32)
    for h in range(heads):
        s = mxu(k, jnp.where(lanes == h, q, jnp.zeros_like(q)), 1, 1)
        p = jnp.exp(s - jnp.max(s, axis=0, keepdims=True))
        low = (p * (1.0 / jnp.sum(p, axis=0, keepdims=True))).astype(BF16)
        p_ref[0, h] = low
        total = total + jnp.where(rows == h, mxu(v, low, 0, 0), 0.0)
    o_ref[0] = total.T.astype(BF16)


def other_specs(share, shape):
    return [pl.BlockSpec(shape, lambda x, _, d=d: (x ^ (d >> 1), 0, 0)) for d in range(1, share)]


def attend_forward(roles, after, own, others):
    blocks, count, cols = own.shape
    share = 1 + len(others)
    part = cols // 3
    heads = part // HD
    return call(
        functools.partial(attend_forward_body, share, heads),
        roles,
        after,
        grid=(blocks,),
        in_specs=[pl.BlockSpec((1, count, cols), lambda x, _: (x, 0, 0))] + other_specs(share, (1, count, cols)),
        out_specs=[
            pl.BlockSpec((1, heads, share * count, count), lambda x, _: (x, 0, 0, 0)),
            pl.BlockSpec((1, count, part), lambda x, _: (x, 0, 0)),
        ],
        out_shape=[
            jax.ShapeDtypeStruct((blocks, heads, share * count, count), BF16),
            jax.ShapeDtypeStruct((blocks, count, part), BF16),
        ],
        name="attend_forward",
    )(own, *others)


def attend_backward_body(share, heads, roles, *refs):
    own, others = refs[0], refs[1:share]
    p_ref, o_ref, g_ref = refs[share : share + 3]
    outs = refs[share + 3 :]
    part = heads * HD
    count = own.shape[1]
    q = own[0, :, :part] * jnp.asarray(HD**-0.5, BF16)
    k = jnp.concatenate([r[0, :, part : 2 * part] for r in (own, *others)], axis=0)
    v = jnp.concatenate([r[0, :, 2 * part :] for r in (own, *others)], axis=0)
    g = g_ref[0]
    rows = lax.broadcasted_iota(jnp.int32, (part, count), 0) // HD
    lanes = lax.broadcasted_iota(jnp.int32, (count, part), 1) // HD
    prod = (g.astype(F32) * o_ref[0].astype(F32)).T
    dq = jnp.zeros((part, count), F32)
    dk = jnp.zeros((share * count, part), F32)
    dv = jnp.zeros((share * count, part), F32)
    for h in range(heads):
        q_h = jnp.where(lanes == h, q, jnp.zeros_like(q))
        g_h = jnp.where(lanes == h, g, jnp.zeros_like(g))
        p = p_ref[0, h]
        delta = jnp.sum(prod[h * HD : (h + 1) * HD], axis=0, keepdims=True)
        ds = (p.astype(F32) * (mxu(v, g_h, 1, 1) - delta)).astype(BF16)
        dq = dq + jnp.where(rows == h, mxu(k, ds, 0, 0), 0.0)
        dk = dk + mxu(ds, q_h, 1, 0)
        dv = dv + mxu(p, g_h, 1, 0)
    outs[0][0, :, :part] = (dq.T * (HD**-0.5)).astype(BF16)
    outs[0][0, :, part : 2 * part] = dk[:count].astype(BF16)
    outs[0][0, :, 2 * part :] = dv[:count].astype(BF16)
    for d in range(1, share):
        outs[d][0, :, :part] = dk[d * count : (d + 1) * count].astype(BF16)
        outs[d][0, :, part:] = dv[d * count : (d + 1) * count].astype(BF16)


def attend_backward(roles, after, own, others, probs, attended, grad):
    blocks, count, cols = own.shape
    share = 1 + len(others)
    part = cols // 3
    heads = part // HD
    spec = pl.BlockSpec((1, count, cols), lambda x, _: (x, 0, 0))
    o_spec = pl.BlockSpec((1, count, part), lambda x, _: (x, 0, 0))
    p_spec = pl.BlockSpec((1, heads, share * count, count), lambda x, _: (x, 0, 0, 0))
    return call(
        functools.partial(attend_backward_body, share, heads),
        roles,
        after,
        grid=(blocks,),
        in_specs=[spec] + other_specs(share, (1, count, cols)) + [p_spec, o_spec, o_spec],
        out_specs=[spec] + other_specs(share, (1, count, 2 * part)),
        out_shape=[jax.ShapeDtypeStruct((blocks, count, cols), BF16)]
        + [jax.ShapeDtypeStruct((blocks, count, 2 * part), BF16)] * (share - 1),
        name="attend_backward",
    )(own, *others, probs, attended, grad)


def up_body(ks, parts, step, roles, *refs):
    left = refs[0]
    rest = refs[1 + 2 * len(ks) :]
    rows = left.shape[1] // parts
    for i, k in enumerate(ks):
        w = refs[1 + 2 * i : 3 + 2 * i]

        def term(x, h, at):
            return mxu(left[:, pl.ds(at * rows, rows)], w[x][h], 1, 0)

        if parts == 2:
            role = roles[k]
            one, two = term(0, 1, 1 - role), term(1, 0, role)
            step(i, 0, term(0, 0, 0) + jnp.where(role == 0, one, two), rest)
            step(i, 1, term(1, 1, 1) + jnp.where(role == 0, two, one), rest)
        else:
            for x in range(2):
                step(i, x, sum(term(x, h, h) for h in range(parts)), rest)


def up(roles, after, name, left, weights, ks, width, col, step, extras, outs, tile):
    parts, rows, _ = weights[0][0].shape
    per = width // tile
    count = left.shape[0]
    return call(
        functools.partial(up_body, ks, parts, step),
        roles,
        after,
        grid=(per,),
        in_specs=[whole((count, parts * rows))]
        + [pl.BlockSpec((parts, rows, tile), lambda n, _: (0, 0, col * per + n))] * (2 * len(ks))
        + [pl.BlockSpec((2, e.shape[1], tile), lambda n, _: (0, 0, n)) for e in extras],
        out_specs=[pl.BlockSpec((2, o[0], tile), lambda n, _: (0, 0, n)) for o in outs],
        out_shape=[jax.ShapeDtypeStruct((2, o[0], width), o[1]) for o in outs],
        name=name,
    )(left, *[a for w in weights for a in w], *extras)


def plain_step(i, x, total, refs):
    refs[i][x] = total.astype(BF16)


def gelu_step(i, x, total, refs):
    bias, act, slope = refs
    v = total + bias[x]
    half = 0.5 * (1.0 + lax.erf(v * (0.5**0.5)))
    act[x] = (v * half).astype(BF16)
    slope[x] = (half + v * jnp.exp(-0.5 * v * v) * 0.3989422804014327).astype(BF16)


def slope_step(i, x, total, refs):
    slope, grad, sums = refs
    low = (total * slope[x].astype(F32)).astype(BF16)
    grad[x] = low
    sums[x] = jnp.sum(low.astype(F32), axis=0, keepdims=True)


def down_body(parts, finish, roles, *refs):
    rest = refs[6:-1]
    acc = refs[-1]
    n = pl.program_id(0)
    per = pl.num_programs(0)
    total = [0] * parts
    for k in range(2):
        left, w = refs[k], refs[2 + 2 * k : 4 + 2 * k]

        def term(x, h, at):
            return mxu(left[at], w[x][h], 1, 1)

        if parts == 2:
            role = roles[k]
            one, two = term(0, 1, role), term(1, 0, 1 - role)
            total[0] = total[0] + term(0, 0, 0) + jnp.where(role == 0, two, one)
            total[1] = total[1] + term(1, 1, 1) + jnp.where(role == 0, one, two)
        else:
            for h in range(parts):
                total[h] = total[h] + term(0, h, 0) + term(1, h, 1)
    for h in range(parts):
        acc[h * per + n] = total[h]

    @pl.when(n == per - 1)
    def _():
        finish(acc, rest)


def down(roles, after, name, lefts, weights, width, col, finish, extras, outs):
    parts, rows, _ = weights[0][0].shape
    tile = min(256, rows)
    count = lefts[0].shape[1]
    return call(
        functools.partial(down_body, parts, finish),
        roles,
        after,
        grid=(rows // tile,),
        in_specs=[whole((2, count, width))] * 2
        + [pl.BlockSpec((parts, tile, width), lambda n, _: (0, n, col))] * 4
        + [whole(e.shape) for e in extras],
        out_specs=[whole(o[0]) for o in outs],
        out_shape=[jax.ShapeDtypeStruct(*o) for o in outs],
        scratch_shapes=[pltpu.VMEM((parts * rows // tile, count, tile), F32)],
        name=name,
    )(*lefts, *weights[0], *weights[1], *extras)


def row_mean(tiles):
    total = sum(jnp.sum(t, axis=-1, keepdims=True) for t in tiles)
    return total / sum(t.shape[-1] for t in tiles)


def norm_finish(has_residual, acc, refs):
    refs = list(refs)
    residual = refs.pop(0) if has_residual else None
    rows, total_ref, low_ref, low_t_ref = refs
    tiles, count, width = acc.shape
    for r in range(0, count, CHUNK):
        rr = pl.ds(r, CHUNK)
        total = []
        for i in range(tiles):
            cc = slice(i * width, (i + 1) * width)
            v = acc[i, rr, :] + rows[0:1, cc]
            if residual is not None:
                v = v + residual[rr, cc]
            total_ref[rr, cc] = v
            total.append(v)
        mean = row_mean(total)
        center = [t - mean for t in total]
        scale = lax.rsqrt(row_mean([c * c for c in center]) + EPSILON)
        for i in range(tiles):
            cc = slice(i * width, (i + 1) * width)
            v = center[i] * scale * rows[1:2, cc] + rows[2:3, cc]
            low_ref[rr, cc] = v.astype(BF16)
            low_t_ref[cc, rr] = v.T.astype(BF16)


def norm_back_finish(keep, acc, refs):
    total_ref, up_ref, rows, *outs = refs
    full_ref = outs.pop(0) if keep else None
    low_ref, low_t_ref, sums_ref = outs
    tiles, count, width = acc.shape
    zero = jnp.zeros((1, width), F32)
    sums = [[zero] * tiles for _ in range(4)]
    for r in range(0, count, CHUNK):
        rr = pl.ds(r, CHUNK)
        cuts = [slice(i * width, (i + 1) * width) for i in range(tiles)]
        total = [total_ref[rr, cc] for cc in cuts]
        mean = row_mean(total)
        center = [t - mean for t in total]
        scale = lax.rsqrt(row_mean([c * c for c in center]) + EPSILON)
        unit = [c * scale for c in center]
        grad = [acc[i, rr, :] for i in range(tiles)]
        z = [g * rows[0:1, cc] for g, cc in zip(grad, cuts)]
        z_mean = row_mean(z)
        zu_mean = row_mean([a * b for a, b in zip(z, unit)])
        for i, cc in enumerate(cuts):
            up_now = up_ref[rr, cc].astype(F32)
            v = up_now + scale * (z[i] - z_mean - unit[i] * zu_mean)
            if keep:
                full_ref[rr, cc] = v
            low_ref[rr, cc] = v.astype(BF16)
            low_t_ref[cc, rr] = v.T.astype(BF16)
            for j, s in enumerate((v, grad[i] * unit[i], grad[i], up_now)):
                sums[j][i] = sums[j][i] + jnp.sum(s, axis=0, keepdims=True)
    for j in range(4):
        for i in range(tiles):
            sums_ref[j : j + 1, i * width : (i + 1) * width] = sums[j][i]


def out_finish(acc, refs):
    total_ref, rows, low_ref = refs
    tiles, count, width = acc.shape
    for i in range(tiles):
        cc = slice(i * width, (i + 1) * width)
        v = (acc[i] + total_ref[:, cc] + rows[0:1, cc]) * rows[1:2, cc]
        low_ref[:, cc] = v.astype(BF16)


def weight_grad_body(n_parts, n_more, own, roles, *refs):
    ends = refs[4 * n_parts + n_more :]
    for a in range(2):
        at = 0
        more = [m[a].astype(F32) for m in refs[4 * n_parts : 4 * n_parts + n_more]]
        for p in range(n_parts):
            left, right = refs[4 * p + 2 * a : 4 * p + 2 * a + 2]
            total = mxu(left[...], right[...], 1, 0)
            cc = slice(at, at + total.shape[1])
            at = cc.stop
            if own:
                start = 0
                for m in more:
                    if start <= cc.start and cc.stop <= start + m.shape[1]:
                        total = total + m[:, cc.start - start : cc.stop - start]
                    start += m.shape[1]
                ends[a][:, cc] = total.astype(BF16)
            else:
                ends[0][a, :, cc] = total.astype(BF16)


def weight_grad(roles, after, lefts, rights, parts, k, more=()):
    depth, count = lefts[0].shape
    rows = depth // parts
    tile = min(256, rows)
    per = rows // tile
    cols = sum(r.shape[2] for r in rights)
    own = k == 0
    specs, args = [], []
    for left, right in zip(lefts, rights):
        for a in range(2):
            specs += [
                pl.BlockSpec((tile, count), lambda b, n, p, a=a: ((b + p[k] * (a - b)) * per + n, 0)),
                pl.BlockSpec((None, count, right.shape[2]), lambda b, n, p, a=a: (a + p[k] * (b - a), 0, 0)),
            ]
            args += [left, right]
    pair = lambda width: pl.BlockSpec((2, None, tile, width), lambda b, n, _: (0, b, n, 0))
    if own:
        out_specs = [pl.BlockSpec((None, tile, cols), lambda b, n, _: (b, n, 0))] * 2
        out_shape = [jax.ShapeDtypeStruct((parts, rows, cols), BF16)] * 2
    else:
        out_specs = [pair(cols)]
        out_shape = [jax.ShapeDtypeStruct((2, parts, rows, cols), BF16)]
    return call(
        functools.partial(weight_grad_body, len(lefts), len(more), own),
        roles,
        after,
        grid=(parts, per),
        in_specs=specs + [pair(m.shape[3]) for m in more],
        out_specs=out_specs,
        out_shape=out_shape,
        name="weight_grad",
    )(*args, *more)


def pick(array, index, axis=0):
    return lax.dynamic_index_in_dim(array, index, axis, keepdims=False)


def add(*terms):
    return sum(t.astype(F32) for t in terms).astype(BF16)


class Line:
    def __init__(self, roles):
        self.roles, self.marks = roles, []

    def gate(self, *arrays):
        leaves, form = jax.tree.flatten(arrays)
        places = [i for i, leaf in enumerate(leaves) if isinstance(leaf, jax.Array)]
        held, self.marks = lax.optimization_barrier(([leaves[i] for i in places], self.marks))
        for i, array in zip(places, held):
            leaves[i] = array
        arrays = jax.tree.unflatten(form, leaves)
        return arrays[0] if len(arrays) == 1 else arrays

    def plain(self, step, *args):
        out = step(*self.gate(args, ())[0])
        self.marks = self.marks + jax.tree.leaves(out)
        return out

    def __call__(self, step, *args):
        args = self.gate(args, ())[0]
        out, mark = step(self.roles, self.marks, *args)
        self.marks = [mark]
        return out


def on_device(
    sizes,
    tokens,
    skip_tokens,
    merger_weight,
    merger_bias,
    first_gain,
    first_shift,
    attend_weight,
    output_weight,
    output_bias,
    second_gain,
    second_shift,
    expand_weight,
    widen_bias,
    shrink_weight,
    shrink_bias,
    live_slots,
    cotangent,
):
    fs, cs, ts = sizes
    assert ts == 4
    f_rank, c_rank, t_rank = (lax.axis_index(a) for a in ALL)
    group = cs * ts
    devices = fs * group
    batches, local_seqs, local_len, part_width = tokens.shape
    slots = batches * local_seqs
    share = group // slots
    assert share in (1, 2, 4)
    fine = cotangent.shape[2] // share
    width = cotangent.shape[3]
    count = group * fine
    hidden = expand_weight.shape[1]
    rows = width // (fs * cs)
    role = t_rank % 2 if fs == 2 else 0 * t_rank
    line = Line(jnp.stack([role, (1 - role) if fs == 2 else role]).astype(jnp.int32))

    def to_group(array):
        return lax.all_to_all(array, ("ctx", "tp"), 0, 0, tiled=True)

    def over_tp(array, flip):
        return lax.ppermute(array, "tp", [(i, i ^ flip) for i in range(ts)])

    ring = list(range(0, cs, 2)) + list(range(cs - 1 - cs % 2, 0, -2))

    def over_ctx(array, d):
        return lax.ppermute(array, "ctx", [(ring[i], ring[(i + d) % cs]) for i in range(cs)])

    def ctx_behind(d):
        return jnp.asarray([ring[(ring.index(i) - d) % cs] for i in range(cs)], jnp.int32)[c_rank]

    def over_fsdp(array, d):
        return lax.ppermute(array, "fsdp", [(i, (i + d) % fs) for i in range(fs)])

    def first_pairs(i):
        f, c, t = i // (cs * ts), i // ts % cs, i % ts
        f, t = (f, t ^ 2) if t % 2 else (1 - f, t)
        return (f * cs + c) * ts + t

    def second_pairs(i):
        f, c, t = i // (cs * ts), i // ts % cs, i % ts
        f, t = (1 - f, t) if t % 2 else (f, t ^ 2)
        return (f * cs + c) * ts + t

    def over(array, target):
        return lax.ppermute(array, ALL, [(i, target(i)) for i in range(devices)])

    def gather_ctx(piece):
        return [piece] + [over_ctx(piece, d) for d in range(1, cs)]

    def ring_start(piece):
        return [piece, over_ctx(piece, 1)]

    def ring_step(moved):
        *kept, last = moved
        last = line.gate(last)
        return [*kept, last, over_ctx(last, 1)] if len(moved) < cs else [*kept, last]

    def gather_one(moved):
        own = line.plain(lambda *m: jnp.concatenate(m, axis=0), *moved)
        return own, [over(own, first_pairs)] if fs == 2 else [over_fsdp(own, h) for h in range(1, fs)]

    def gather_two(own, moved):
        first = line.plain(lambda a, m: jnp.stack([a, *m]), own, moved)
        return first, over(first, second_pairs) if fs == 2 else over_tp(first, 2), over_tp(first, 1)

    def gather_three(first, second, other):
        first, second, other = line.gate(first, second, other)
        return [[first, second], [other, over_tp(second, 1)]]

    def reduce_one(sums):
        keep, send = sums
        return keep, over(send, second_pairs) if fs == 2 else over_tp(send, 2)

    def reduce_two(keep, moved):
        sums = line.plain(lambda a, m: [add(a[h], m[h]) for h in range(fs)], keep, moved)
        if fs == 2:
            return sums[0], [over(sums[1], first_pairs)]
        return sums[0], [over_fsdp(sums[h], -h) for h in range(1, fs)]

    def reduce_three(own, moved):
        def pieces(own, moved):
            total = add(own, *moved).reshape(cs, rows, -1)
            return [total[d] for d in range(cs)]

        parts = line.plain(pieces, own, moved)
        return parts, over_ctx(parts[-1], -1)

    def reduce_step(parts, moving):
        *parts, last = line.plain(lambda p, m: [*p[:-2], add(p[-2], m)], parts, moving)
        return [*parts, last], over_ctx(last, -1)

    def reduce_last(parts, moving):
        while len(parts) > 2:
            parts, moving = reduce_step(parts, moving)
        return line.plain(lambda p, m: p.astype(F32) + m.astype(F32), parts[0], moving)

    spread = lambda blocks: [blocks[0][0], blocks[1][0], blocks[0][1], blocks[1][1]]
    owner = jnp.stack(
        [(f_rank - h) % fs * cs + ctx_behind(d) for h in range(fs) for d in range(cs)]
    )
    features = lax.broadcasted_iota(jnp.int32, (width, width), 0)
    places = (owner[:, None] * rows + jnp.arange(rows)[None, :]).reshape(1, width)
    permute = (features == places).astype(BF16)

    def relative(array, axis=0):
        return [
            jnp.stack([pick(array, t_rank ^ (2 * x + k), axis) for x in range(2)]) for k in range(2)
        ]

    def absolute(blocks):
        blocks = jnp.stack(spread(blocks))
        return jnp.stack([pick(blocks, t_rank ^ t) for t in range(ts)])

    flat = lambda w: w.reshape(w.shape[0], -1)
    side = merger_weight.shape[1] * merger_weight.shape[2]
    heads_width = output_weight.shape[1]

    def pack_att(m, o, a):
        return jnp.concatenate([flat(m), o, flat(a)], axis=1)

    def split_rows(one, two):
        array = jnp.concatenate([one, two], axis=-1)
        array = array.reshape(slots, ts, share, fine, -1).transpose(0, 2, 1, 3, 4)
        return array.reshape(group * ts * fine, -1)

    small = merger_bias.shape[0]
    att = gather_ctx(line.plain(pack_att, merger_weight, output_weight, attend_weight))
    packed = line.plain(
        lambda *v: jnp.broadcast_to(jnp.concatenate(v), (devices, sum(x.shape[0] for x in v))),
        merger_bias, first_gain, first_shift, output_bias, second_gain, second_shift, shrink_bias, widen_bias,
    )
    packed = lax.all_to_all(packed, ALL, 0, 0, tiled=True)
    both = line.plain(split_rows, tokens, skip_tokens)
    ffn = line.plain(lambda a, b: jnp.concatenate([a, b], axis=1), expand_weight, shrink_weight)
    packed = line.gate(packed)
    att = gather_one(att)
    ffn = ring_start(line.gate(ffn))
    ffn = ring_step(ffn)
    att = gather_two(*att)
    for _ in range(3, cs):
        ffn = ring_step(ffn)
    both = to_group(line.gate(both))
    ffn = gather_one(ring_step(ffn))

    def vectors_of(packed):
        vectors = packed[:, : 7 * small].reshape(fs * cs, ts, 7, small).transpose(0, 2, 1, 3)
        vectors = vectors.reshape(fs * cs, 7, rows)
        vectors = jnp.stack([pick(vectors, owner[i]) for i in range(fs * cs)], axis=1).reshape(7, width)
        return vectors, relative(packed[:, 7 * small :].reshape(ts, 1, hidden))

    def blocks_of(both):
        both = relative(both.reshape(cs, ts, ts * fine, side), 1)
        return [b.reshape(2, count, side) for b in both]

    vectors, widen = line.plain(vectors_of, packed)
    att = gather_three(*att)
    both = line.plain(blocks_of, both)
    act = (count, width)
    turned = (width, count)
    flows = [(count, BF16)] * 2

    joined, normed, normed_t = line(
        lambda *o: down(
            *o[:2], "joined", o[2], o[3], side, 0, functools.partial(norm_finish, False), [o[4][0:3]],
            [(act, F32), (act, BF16), (turned, BF16)],
        ),
        both, att, vectors,
    )
    ffn = gather_two(*ffn)
    project = line(
        lambda *o: up(*o[:2], "project", *o[2:], (0, 1), 3 * heads_width, 1, plain_step, [], flows, heads_width),
        normed, att,
    )
    cot = to_group(line.gate(cotangent).reshape(group * fine, width))
    others = [[over_tp(project[k ^ (d & 1)], d) for d in range(1, share)] for k in range(2)]
    inner = [line(attend_forward, project[k], others[k]) for k in range(2)]
    probs, attended = zip(*inner)
    second, normed_two, normed_two_t = line(
        lambda *o: down(
            *o[:2], "second", o[2], o[3], heads_width, side // heads_width, functools.partial(norm_finish, True),
            [o[4], o[5][3:6]], [(act, F32), (act, BF16), (turned, BF16)],
        ),
        attended, att, joined, vectors,
    )
    live = pick(live_slots.reshape(slots), (c_rank * ts + t_rank) // share).astype(F32)

    def arrived(cot, permute):
        ours = (mxu(cot.reshape(count, width), permute, 1, 0) * live).astype(BF16)
        return ours, ours.T

    branch_low, branch_low_t = line.plain(arrived, cot, permute)
    ffn = gather_three(*ffn)

    def hidden_step(k):
        return lambda *o: up(*o[:2], "hidden", *o[2:4], (k,), hidden, 0, gelu_step, [o[4]], flows, 256)

    activated, slope = [None, None], [None, None]
    for k in range(2):
        activated[k], slope[k] = line(hidden_step(k), normed_two, ffn[k : k + 1], widen[k])

    def grads(k):
        return lambda roles, after, lefts, rights, more=(): weight_grad(roles, after, lefts, rights, fs, k, more)

    def other_grads(lefts, rights):
        return over_tp(line(grads(1), lefts, rights)[0], 1)

    def hidden_back(k):
        return lambda *o: up(
            *o[:2], "hidden_back", *o[2:4], (k,), hidden, 1, slope_step, [o[4]], [(count, BF16), (1, F32)], 256
        )

    grad_expanded, wide = [None, None], [None, None]
    other = other_grads([branch_low_t], [activated[1]])
    grad_expanded[1], wide[1] = line(hidden_back(1), branch_low, ffn[1:], slope[1])
    shrink_sums = reduce_one(line(grads(0), [branch_low_t], [activated[0]], [other]))
    grad_expanded[0], wide[0] = line(hidden_back(0), branch_low, ffn[:1], slope[0])
    grad_second, attn_low, attn_low_t, sums_two = line(
        lambda *o: down(
            *o[:2], "second_back", o[2], o[3], hidden, 0, functools.partial(norm_back_finish, True),
            [o[4], o[5], o[6][4:5]], [(act, F32), (act, BF16), (turned, BF16), ((4, width), F32)],
        ),
        grad_expanded, ffn, second, branch_low, vectors,
    )
    shrink_sums = reduce_two(*shrink_sums)
    other = other_grads([normed_two_t], [grad_expanded[1]])
    grad_attended = line(
        lambda *o: up(
            *o[:2], "attended_back", *o[2:], (0, 1), heads_width, side // heads_width, plain_step, [], flows,
            heads_width // 2,
        ),
        attn_low, att,
    )
    shrink_sums = reduce_three(*shrink_sums)
    expand_sums = reduce_one(line(grads(0), [normed_two_t], [grad_expanded[0]], [other]))
    inner = [None, None]
    inner[1] = line(attend_backward, project[1], others[1], probs[1], attended[1], grad_attended[1])
    shrink_sums = reduce_step(*shrink_sums)
    inner[0] = line(attend_backward, project[0], others[0], probs[0], attended[0], grad_attended[0])
    shrink_sums = reduce_step(*shrink_sums)
    expand_sums = reduce_two(*expand_sums)

    def close(k):
        def total(own, *moves):
            third = own.shape[2] // 3
            return jnp.concatenate([own[:, :, :third], add(own[:, :, third:], *moves)], axis=-1)

        moves = [over_tp(inner[k ^ (d & 1)][d], d) for d in range(1, share)]
        return line.plain(total, inner[k][0], *moves)

    grad_project = [None, None]
    grad_project[1] = close(1)
    attend_other = other_grads([attn_low_t, normed_t], [attended[1], grad_project[1]])
    grad_project[0] = close(0)
    grad_shrink = reduce_last(*shrink_sums)
    expand_sums = reduce_three(*expand_sums)
    joined_low, joined_low_t, sums_one = line(
        lambda *o: down(
            *o[:2], "first_back", o[2], o[3], 3 * heads_width, 1, functools.partial(norm_back_finish, False),
            [o[4], o[5], o[6][1:2]], [(act, BF16), (turned, BF16), ((4, width), F32)],
        ),
        grad_project, att, joined, grad_second, vectors,
    )
    expand_sums = reduce_step(*expand_sums)
    merger_other = other_grads([joined_low_t], [both[1]])
    out = line(
        lambda *o: up(*o[:2], "inputs_back", *o[2:], (0, 1), side, 0, plain_step, [], flows, 256),
        joined_low, att,
    )
    expand_sums = reduce_step(*expand_sums)
    att_sums = reduce_one(
        line(
            grads(0), [joined_low_t, attn_low_t, normed_t], [both[0], attended[0], grad_project[0]],
            [merger_other, attend_other],
        )
    )

    def turn_back(out):
        out = absolute(out).reshape(ts, cs, ts * fine, side)
        return out.transpose(1, 0, 2, 3).reshape(group * ts * fine, side)

    out = to_group(line.plain(turn_back, out))
    grad_expand = reduce_last(*expand_sums)

    def vector_sums(one, two, wide):
        sums = jnp.concatenate([one[0:3], two]).reshape(7, fs * cs, rows)
        place = jnp.asarray([ring.index(i) for i in range(cs)], jnp.int32)[c_rank]
        places = [(f_rank - f) % fs * cs + (place - ring.index(c)) % cs for f in range(fs) for c in range(cs)]
        sums = jnp.stack([pick(sums, p, 1) for p in places])
        sums = sums.reshape(fs * cs, 7, ts, small).transpose(0, 2, 1, 3).reshape(devices, 7 * small)
        return jnp.concatenate([sums, absolute(wide).reshape(devices, -1)], axis=1)

    vec = line.plain(vector_sums, sums_one, sums_two, wide).reshape(fs, cs, 2, 2, -1)
    moved = over_tp(pick(vec, 1 - t_rank % 2, 3), 1)
    def layer_end(roles, after, a, w, t, v):
        ends = jnp.stack([v[6], jnp.full((width,), live)])
        return down(roles, after, "layer_out", a, w, hidden, 1, out_finish, [t, ends], [(act, BF16)])

    (layer_out,) = line(layer_end, activated, ffn, second, vectors)
    layer_out = line.plain(lambda a, p: mxu(a, p, 1, 1).astype(BF16), layer_out, permute)
    vec = line.plain(lambda v, m: pick(v, t_rank % 2, 3) + m, vec, moved)
    moved = over_tp(pick(vec, 1 - t_rank // 2, 2), 2)
    att_sums = reduce_two(*att_sums)
    vec = line.plain(lambda v, m: pick(v, t_rank // 2, 2) + m, vec, moved)
    moved = [over_fsdp(pick(vec, (f_rank - h) % fs), -h) for h in range(1, fs)]
    att_sums = reduce_three(*att_sums)
    vec = line.plain(lambda v, m: sum(m, pick(v, f_rank)), vec, moved)
    moved = [over_ctx(pick(vec, ctx_behind(d)), -d) for d in range(1, cs)]
    att_sums = reduce_step(*att_sums)
    vec = line.plain(lambda v, m: sum(m, pick(v, c_rank)), vec, moved)
    out = line.gate(out)
    layer_out = to_group(line.gate(layer_out).reshape(group * fine, width))
    grad_att = reduce_last(*att_sums)

    def unpack(out, layer_out):
        out = out.reshape(slots, share, ts, fine, side).transpose(0, 2, 1, 3, 4)
        out = out.reshape(batches, local_seqs, local_len, side).astype(F32)
        layer_out = layer_out.reshape(batches, local_seqs, share * fine, width)
        return out[..., :part_width], out[..., part_width:], layer_out

    grad_tokens, grad_skip, layer_out = line.plain(unpack, out, layer_out)
    cut = side + heads_width
    vec_out = [vec[i * small : (i + 1) * small] for i in range(7)] + [vec[7 * small :]]
    return (
        layer_out,
        grad_tokens,
        grad_skip,
        grad_att[:, :side].reshape(merger_weight.shape),
        vec_out[0],
        vec_out[1],
        vec_out[2],
        grad_att[:, cut:].reshape(attend_weight.shape),
        grad_att[:, side:cut],
        vec_out[3],
        vec_out[4],
        vec_out[5],
        grad_expand,
        vec_out[7],
        grad_shrink,
        vec_out[6],
    )


def solution(mesh):
    sizes = tuple(mesh.shape[a] for a in ALL)
    act = P(None, "fsdp", "ctx", "tp")
    vec = P(ALL)
    flat = P(None, "fsdp", ("ctx", "tp"), None)
    w_three = P(("fsdp", "ctx"), None, "tp")
    w_two = P(("fsdp", "ctx"), "tp")
    return jax.shard_map(
        functools.partial(on_device, sizes),
        mesh=mesh,
        in_specs=(
            act, act, w_three, vec, vec, vec, w_three, w_two, vec, vec, vec, w_two, vec, w_two, vec,
            P(None, "fsdp"), flat,
        ),
        out_specs=(
            flat, act, act, w_three, vec, vec, vec, w_three, w_two, vec, vec, vec, w_two, vec, w_two, vec,
        ),
        check_vma=False,
    )
```

time: 642 us -> 611 us (0.952)
  starting transfers between devices: 126 us -> 76 us
  Pallas kernels: 200 us -> 220 us
  between operations: 2.59 us -> 16.5 us
  waiting for transfers between devices: 209 us -> 198 us
  other arithmetic: 46.3 us -> 37.1 us
    ppermute x12 -> x28, waiting for transfers between devices: 39.9 us -> 145 us  [the longest x18 77.4 us: over_ctx(): lax.ppermute(array, 'ctx', [(ring[i], ring[(i + d) % cs]) for i in range(...]
    ppermute x28 -> x14, waiting for transfers between devices: 59.5 us -> 3.21 us  [over_tp(): return lax.ppermute(array, 'tp', [(i, i ^ flip) for i in range(ts)])]
    ppermute x8 -> x1, waiting for transfers between devices: 54.9 us -> 2.14 us  [over_fsdp(): return lax.ppermute(array, 'fsdp', [(i, (i + d) % fs) for i in range(fs)])]
    all_to_all x1 -> x0, waiting for transfers between devices: 28.2 us -> none  [on_device(): lax.all_to_all(line.plain(vector_sums, sums_one, sums_two, wide), ALL, 0,...]
    ppermute x12 -> x28, starting transfers between devices: 69.3 us -> 41.2 us  [the longest x18 29.3 us: over_ctx(): lax.ppermute(array, 'ctx', [(ring[i], ring[(i + d) % cs]) for i in range(...]
    all_to_all x4, waiting for transfers between devices: 0.01 us -> 20.6 us  [to_group(): return lax.all_to_all(array, ('ctx', 'tp'), 0, 0, tiled=True)]
    pallas_call x24 -> x23, Pallas kernels: 200 us -> 220 us  [apply(): pl.pallas_call(run, grid_spec=pltpu.PrefetchScalarGridSpec(num_scalar_pre...]
    another operation x15 -> x3, other arithmetic: 14.7 us -> 5.5 us  [the longest x2 4.92 us: gather_two(): first = line.plain(lambda a, m: jnp.stack([a, *m]), own, moved)]
  transfers between devices with their start and end apart: 54 -> 48, of which waited for: 17 -> 19; matrix products, arithmetic and copies ran while one was open for 13% -> 11% of each run, Pallas kernels for 27% -> 30%
where the time goes in v3:
time: 611 us; the launch traced here: 603 us
  Pallas kernels  220 us (36%)
  waiting for transfers between devices  198 us (32%)
  starting transfers between devices  76 us (12%)
  local copies, waits for them, and re-layouts  48.5 us (8%)
  other arithmetic  37.1 us (6%)
  between operations  16.5 us (3%)
  matrix products  6.48 us (1%)
    pallas_call x23, Pallas kernels, apply(): pl.pallas_call(run, grid_spec=pltpu.PrefetchScalarGridSpec(num_scalar_pre...  220 us
    ppermute x18, waiting for transfers between devices, over_ctx(): lax.ppermute(array, 'ctx', [(ring[i], ring[(i + d) % cs]) for i in range(...  77.4 us
    ppermute x10, waiting for transfers between devices, over(): return lax.ppermute(array, ALL, [(i, target(i)) for i in range(devices)])  67.9 us
    ppermute x18, starting transfers between devices, over_ctx(): lax.ppermute(array, 'ctx', [(ring[i], ring[(i + d) % cs]) for i in range(...  29.3 us
    all_to_all x1, waiting for transfers between devices, on_device(): packed = lax.all_to_all(packed, ALL, 0, 0, tiled=True)  26.5 us
    all_to_all x4, starting transfers between devices, to_group(): return lax.all_to_all(array, ('ctx', 'tp'), 0, 0, tiled=True)  23.8 us
    all_to_all x4, waiting for transfers between devices, to_group(): return lax.all_to_all(array, ('ctx', 'tp'), 0, 0, tiled=True)  20.6 us
    convert_element_type x14, other arithmetic, add(): return sum((t.astype(F32) for t in terms)).astype(BF16)  17.9 us
  transfers between devices with their start and end apart: 48, of which 19 were waited for; matrix products, arithmetic and copies ran while one was open for 11% of the time, Pallas kernels for 30%

profile of v3, /device:TPU:0, one launch (start us, length us, event | category | flops | bytes accessed | tf_op | source)
XLA Modules:
  0.0 602.9 jit_solution(13266617764222629470)
XLA Ops:
  3.8 4.1 collective-permute-start
  11.5 4.5 all-to-all-start
  19.6 26.5 %all-to-all-done = f32[32,1,352]{2,1,0:T(1,128)S(1)} async-done(((f32[32,1,352]{2,1,0:T(1,128)}), f32[32,1,352]{2,1,0:T(1,128)S(1)}, u32[]{:S(2)}, u32[]{:S(2)}) %all-to-all-start) | async-done | bytes 45088 | tf_op jit(solution)/shard_map/all_to_all | solution.py:571
  48.6 12.1 %collective-permute-done.3 = bf16[128,2048]{1,0:T(8,128)(2,1)S(1)} collective-permute-done((bf16[128,2048]{1,0:T(8,128)(2,1)S(1)}, bf16[128,2048]{1,0:T(8,128)(2,1)S(1)}, u32[]{:S(2)}, u32[]{:S(2)}) %collective-permute-start.3) | collective-permute-done | bytes 524320 | tf_op jit(solution)/shard_map/ppermute | solution.py:465
  60.6 6.1 %collective-permute-done.5 = bf16[512,1536]{1,0:T(8,128)(2,1)S(1)} collective-permute-done((bf16[512,1536]{1,0:T(8,128)(2,1)S(1)}, bf16[512,1536]{1,0:T(8,128)(2,1)S(1)}, u32[]{:S(2)}, u32[]{:S(2)}) %collective-permute-start.5) | collective-permute-done | bytes 1572896 | tf_op jit(solution)/shard_map/ppermute | solution.py:484
  69.4 13.0 %collective-permute-done.4 = bf16[128,2048]{1,0:T(8,128)(2,1)} collective-permute-done((bf16[128,2048]{1,0:T(8,128)(2,1)S(1)}, bf16[128,2048]{1,0:T(8,128)(2,1)}, u32[]{:S(2)}, u32[]{:S(2)}) %collective-permute-start.4) | collective-permute-done | bytes 524320 | tf_op jit(solution)/shard_map/ppermute | solution.py:465
  82.4 2.3 collective-permute-start.8
  90.5 4.5 all-to-all-start.1
  104.8 9.5 %collective-permute-done.6.refs_3_.refs_2_ = bf16[2,512,1536]{2,1,0:T(8,128)(2,1)} collective-permute-done((bf16[2,512,1536]{2,1,0:T(8,128)(2,1)S(1)}, bf16[2,512,1536]{2,1,0:T(8,128)(2,1)}, u32[]{:S(2)}, u32[]{:S(2)}) %collective-permute-start.6) | collective-permute-done | bytes 3145760 | tf_op jit(solution)/shard_map/ppermute | solution.py:484
  115.6 20.6 %all-to-all-done.1 = bf16[16,128,512]{2,1,0:T(8,128)(2,1)} async-done(((bf16[16,128,512]{2,1,0:T(8,128)(2,1)}), bf16[16,128,512]{2,1,0:T(8,128)(2,1)}, u32[]{:S(2)}, u32[]{:S(2)}) %all-to-all-start.1) | async-done | bytes 2097184 | tf_op jit(solution)/shard_map/all_to_all | solution.py:457
  141.8 8.8 %joined.1 = (f32[512,1024]{1,0:T(8,128)}, bf16[512,1024]{1,0:T(8,128)(2,1)}, bf16[1024,512]{1,0:T(8,128)(2,1)}, f32[8,128]{1,0:T(8,128)}) custom-call(s32[2]{0:T(128)} %pad_add_fusion.roles_ref, bf16[2,512,512]{2,1,0:T(8,128)(2,1)} %pad_maximum_fusion.7.refs_0_.refs_17_.refs_1_.refs_3_, bf16[2,512,512]{2,1,0:T(8,128)(2,1)} %pad_maximum_fusion.8.refs_1_.refs_18_.refs_3_, ...), custom_call_target="tpu_custom_call" | custom-call | flops 1 | bytes 1 | tf_op jit(solution)/shard_map/joined/pallas_call | solution.py:36
  150.7 4.6 pad_maximum_fusion.refs_6_.refs_1_.refs_2_
  155.3 3.3 collective-permute-start.13
  158.6 7.9 %project.1 = (bf16[2,512,768]{2,1,0:T(8,128)(2,1)}, bf16[2,512,768]{2,1,0:T(8,128)(2,1)}, f32[8,128]{1,0:T(8,128)}) custom-call(s32[2]{0:T(128)} %pad_add_fusion.roles_ref, bf16[512,1024]{1,0:T(8,128)(2,1)} %get-tuple-element.619.refs_0_, bf16[2,512,1536]{2,1,0:T(8,128)(2,1)} %copy-done, bf16[2,512,1536]{2,1,0:T(8,128)(2,1)} %collective-permute-done.6.refs_3_.refs_2_, ...), custom_call_target="tpu_custom_call" | custom-call | flops 1 | bytes 1 | tf_op jit(solution)/shard_map/project/pallas_call | solution.py:36
  166.5 9.4 %all-to-all-start.2 = ((bf16[16,32,1024]{2,1,0:T(8,128)(2,1)}), bf16[16,32,1024]{2,1,0:T(8,128)(2,1)}, u32[]{:S(2)}, u32[]{:S(2)}) async-start(bf16[16,32,1024]{2,1,0:T(8,128)(2,1)} %bitcast.31), calls=%async_computation.2 | async-start | bytes 2097152 | tf_op jit(solution)/shard_map/all_to_all | solution.py:457
  178.2 2.2 fusion
  181.3 13.3 %attend_forward.2 = (bf16[2,4,1024,512]{3,2,1,0:T(8,128)(2,1)}, bf16[2,512,256]{2,1,0:T(8,128)(2,1)}, f32[8,128]{1,0:T(8,128)}) custom-call(s32[2]{0:T(128)} %pad_add_fusion.roles_ref, bf16[2,512,768]{2,1,0:T(8,128)(2,1)} %get-tuple-element.765.refs_0_, bf16[2,512,768]{2,1,0:T(8,128)(2,1)} %collective-permute-done.11.refs_1_, ...), custom_call_target="tpu_custom_call" | custom-call | flops 1 | bytes 1 | tf_op jit(solution)/shard_map/attend_forward/pallas_call | solution.py:36
  195.7 13.3 %attend_forward.3 = (bf16[2,4,1024,512]{3,2,1,0:T(8,128)(2,1)}, bf16[2,512,256]{2,1,0:T(8,128)(2,1)}, f32[8,128]{1,0:T(8,128)}) custom-call(s32[2]{0:T(128)} %pad_add_fusion.roles_ref, bf16[2,512,768]{2,1,0:T(8,128)(2,1)} %get-tuple-element.753.refs_0_, bf16[2,512,768]{2,1,0:T(8,128)(2,1)} %copy-done.11, f32[8,128]{1,0:T(8,128)} %get-tuple-element.639.refs_2_), custom_call_target="tpu_custom_call" | custom-call | flops 1 | bytes 1 | tf_op jit(solution)/shard_map/attend_forward/pallas_call | solution.py:36
  209.6 8.2 %second.1 = (f32[512,1024]{1,0:T(8,128)}, bf16[512,1024]{1,0:T(8,128)(2,1)}, bf16[1024,512]{1,0:T(8,128)(2,1)}, f32[8,128]{1,0:T(8,128)}) custom-call(s32[2]{0:T(128)} %pad_add_fusion.roles_ref, bf16[2,512,256]{2,1,0:T(8,128)(2,1)} %get-tuple-element.872.refs_0_.refs_3_.refs_5_.refs_7_, bf16[2,512,256]{2,1,0:T(8,128)(2,1)} %get-tuple-element.800.refs_1_.refs_3_, ...), custom_call_target="tpu_custom_call" | custom-call | flops 1 | bytes 1 | tf_op jit(solution)/shard_map/second/pallas_call | solution.py:36
  217.8 2.5 multiply_convert_fusion.refs_5_.refs_0_.refs_7_
  222.1 8.5 %hidden.2 = (bf16[2,512,1024]{2,1,0:T(8,128)(2,1)}, bf16[2,512,1024]{2,1,0:T(8,128)(2,1)}, f32[8,128]{1,0:T(8,128)}) custom-call(s32[2]{0:T(128)} %pad_add_fusion.roles_ref, bf16[512,1024]{1,0:T(8,128)(2,1)} %get-tuple-element.673.refs_0_, bf16[2,512,2048]{2,1,0:T(8,128)(2,1)} %pad_maximum_fusion.refs_6_.refs_1_.refs_2_, ...), custom_call_target="tpu_custom_call" | custom-call | flops 1 | bytes 1 | tf_op jit(solution)/shard_map/hidden/pallas_call | solution.py:36
  230.6 8.6 %hidden.3 = (bf16[2,512,1024]{2,1,0:T(8,128)(2,1)}, bf16[2,512,1024]{2,1,0:T(8,128)(2,1)}, f32[8,128]{1,0:T(8,128)}) custom-call(s32[2]{0:T(128)} %pad_add_fusion.roles_ref, bf16[512,1024]{1,0:T(8,128)(2,1)} %get-tuple-element.673.refs_0_, bf16[2,512,2048]{2,1,0:T(8,128)(2,1)} %collective-permute-done.14.refs_1_.refs_4_, ...), custom_call_target="tpu_custom_call" | custom-call | flops 1 | bytes 1 | tf_op jit(solution)/shard_map/hidden/pallas_call | solution.py:36
  240.5 8.2 %weight_grad.7 = (bf16[2,2,512,1024]{3,2,1,0:T(8,128)(2,1)}, f32[8,128]{1,0:T(8,128)}) custom-call(s32[2]{0:T(128)} %pad_add_fusion.roles_ref, bf16[1024,512]{1,0:T(8,128)(2,1)} %copy.92.refs_0_.refs_2_, bf16[2,512,1024]{2,1,0:T(8,128)(2,1)} %get-tuple-element.900.refs_1_.refs_3_, bf16[1024,512]{1,0:T(8,128)(2,1)} %copy.92.refs_0_.refs_2_, ...), custom_call_target="tpu_custom_call" | custom-call | flops 1 | bytes 1 | tf_op jit(solution)/shard_map/weight_grad/pallas_call | solution.py:36
  248.8 7.8 %hidden_back.2 = (bf16[2,512,1024]{2,1,0:T(8,128)(2,1)}, f32[2,1,1024]{2,1,0:T(1,128)}, f32[8,128]{1,0:T(8,128)}) custom-call(s32[2]{0:T(128)} %pad_add_fusion.roles_ref, bf16[512,1024]{1,0:T(8,128)(2,1)} %copy-done.2, bf16[2,512,2048]{2,1,0:T(8,128)(2,1)} %collective-permute-done.14.refs_1_.refs_4_, ...), custom_call_target="tpu_custom_call" | custom-call | flops 1 | bytes 1 | tf_op jit(solution)/shard_map/hidden_back/pallas_call | solution.py:36
  257.9 7.6 %weight_grad.8 = (bf16[2,512,1024]{2,1,0:T(8,128)(2,1)}, bf16[2,512,1024]{2,1,0:T(8,128)(2,1)}, f32[8,128]{1,0:T(8,128)}) custom-call(s32[2]{0:T(128)} %pad_add_fusion.roles_ref, bf16[1024,512]{1,0:T(8,128)(2,1)} %copy.94.refs_0_.refs_2_, bf16[2,512,1024]{2,1,0:T(8,128)(2,1)} %get-tuple-element.899.refs_1_.refs_3_.refs_0_, ...), custom_call_target="tpu_custom_call" | custom-call | flops 1 | bytes 1 | tf_op jit(solution)/shard_map/weight_grad/pallas_call | solution.py:36
  266.6 7.6 %hidden_back.3 = (bf16[2,512,1024]{2,1,0:T(8,128)(2,1)}, f32[2,1,1024]{2,1,0:T(1,128)}, f32[8,128]{1,0:T(8,128)}) custom-call(s32[2]{0:T(128)} %pad_add_fusion.roles_ref, bf16[512,1024]{1,0:T(8,128)(2,1)} %copy-done.2, bf16[2,512,2048]{2,1,0:T(8,128)(2,1)} %pad_maximum_fusion.refs_6_.refs_1_.refs_2_, ...), custom_call_target="tpu_custom_call" | custom-call | flops 1 | bytes 1 | tf_op jit(solution)/shard_map/hidden_back/pallas_call | solution.py:36
  274.8 14.9 %second_back.1 = (f32[512,1024]{1,0:T(8,128)}, bf16[512,1024]{1,0:T(8,128)(2,1)}, bf16[1024,512]{1,0:T(8,128)(2,1)}, f32[4,1024]{1,0:T(4,128)}, f32[8,128]{1,0:T(8,128)}) custom-call(s32[2]{0:T(128)} %pad_add_fusion.roles_ref, bf16[2,512,1024]{2,1,0:T(8,128)(2,1)} %get-tuple-element.745.refs_0_.refs_1_.refs_3_, ...), custom_call_target="tpu_custom_call" | custom-call | flops 1 | bytes 1 | tf_op jit(solution)/shard_map/second_back/pallas_call | solution.py:36
  289.7 2.1 collective-permute-done.17
  291.8 2.3 fusion.4
  294.1 8.3 %weight_grad.9 = (bf16[2,2,512,1024]{3,2,1,0:T(8,128)(2,1)}, f32[8,128]{1,0:T(8,128)}) custom-call(s32[2]{0:T(128)} %pad_add_fusion.roles_ref, bf16[1024,512]{1,0:T(8,128)(2,1)} %get-tuple-element.744.refs_0_.refs_2_, bf16[2,512,1024]{2,1,0:T(8,128)(2,1)} %get-tuple-element.725.refs_1_.refs_3_, bf16[1024,512]{1,0:T(8,128)(2,1)} %get-tuple-element.744.refs_0_.refs_2_, ...), custom_call_target="tpu_custom_call" | custom-call | flops 1 | bytes 1 | tf_op jit(solution)/shard_map/weight_grad/pallas_call | solution.py:36
  303.5 5.8 attended_back.1
  309.3 8.0 %collective-permute-done.18 = bf16[512,1024]{1,0:T(8,128)(2,1)S(1)} collective-permute-done((bf16[512,1024]{1,0:T(8,128)(2,1)S(1)}, bf16[512,1024]{1,0:T(8,128)(2,1)S(1)}, u32[]{:S(2)}, u32[]{:S(2)}) %collective-permute-start.18) | collective-permute-done | bytes 1048608 | tf_op jit(solution)/shard_map/ppermute | solution.py:484
  318.7 2.0 copy-done.15
  320.7 7.8 %weight_grad.10 = (bf16[2,512,1024]{2,1,0:T(8,128)(2,1)}, bf16[2,512,1024]{2,1,0:T(8,128)(2,1)}, f32[8,128]{1,0:T(8,128)}) custom-call(s32[2]{0:T(128)} %pad_add_fusion.roles_ref, bf16[1024,512]{1,0:T(8,128)(2,1)} %get-tuple-element.744.refs_0_.refs_2_, bf16[2,512,1024]{2,1,0:T(8,128)(2,1)} %get-tuple-element.745.refs_0_.refs_1_.refs_3_, ...), custom_call_target="tpu_custom_call" | custom-call | flops 1 | bytes 1 | tf_op jit(solution)/shard_map/weight_grad/pallas_call | solution.py:36
  329.5 5.7 collective-permute-start.19
  335.2 14.0 %attend_backward.2 = (bf16[2,512,768]{2,1,0:T(8,128)(2,1)}, bf16[2,512,512]{2,1,0:T(8,128)(2,1)}, f32[8,128]{1,0:T(8,128)}) custom-call(s32[2]{0:T(128)} %pad_add_fusion.roles_ref, bf16[2,512,768]{2,1,0:T(8,128)(2,1)} %get-tuple-element.753.refs_0_, bf16[2,512,768]{2,1,0:T(8,128)(2,1)} %copy-done.11, bf16[2,4,1024,512]{3,2,1,0:T(8,128)(2,1)} %get-tuple-element.755.refs_2_, ...), custom_call_target="tpu_custom_call" | custom-call | flops 1 | bytes 1 | tf_op jit(solution)/shard_map/attend_backward/pallas_call | solution.py:36
  349.9 14.0 %attend_backward.3 = (bf16[2,512,768]{2,1,0:T(8,128)(2,1)}, bf16[2,512,512]{2,1,0:T(8,128)(2,1)}, f32[8,128]{1,0:T(8,128)}) custom-call(s32[2]{0:T(128)} %pad_add_fusion.roles_ref, bf16[2,512,768]{2,1,0:T(8,128)(2,1)} %get-tuple-element.765.refs_0_, bf16[2,512,768]{2,1,0:T(8,128)(2,1)} %collective-permute-done.11.refs_1_, ...), custom_call_target="tpu_custom_call" | custom-call | flops 1 | bytes 1 | tf_op jit(solution)/shard_map/attend_backward/pallas_call | solution.py:36
  365.8 7.8 %collective-permute-done.24 = bf16[128,1024]{1,0:T(8,128)(2,1)S(1)} collective-permute-done((bf16[128,1024]{1,0:T(8,128)(2,1)S(1)}, bf16[128,1024]{1,0:T(8,128)(2,1)S(1)}, u32[]{:S(2)}, u32[]{:S(2)}) %collective-permute-start.24) | collective-permute-done | bytes 262176 | tf_op jit(solution)/shard_map/ppermute | solution.py:465
  374.4 2.0 fusion.6
  378.6 8.8 %weight_grad.11 = (bf16[2,2,512,1024]{3,2,1,0:T(8,128)(2,1)}, f32[8,128]{1,0:T(8,128)}) custom-call(s32[2]{0:T(128)} %pad_add_fusion.roles_ref, bf16[1024,512]{1,0:T(8,128)(2,1)} %get-tuple-element.871.refs_0_.refs_2_.refs_4_.refs_6_, bf16[2,512,256]{2,1,0:T(8,128)(2,1)} %get-tuple-element.800.refs_1_.refs_3_, ...), custom_call_target="tpu_custom_call" | custom-call | flops 1 | bytes 1 | tf_op jit(solution)/shard_map/weight_grad/pallas_call | solution.py:36
  389.8 7.3 %collective-permute-done.26 = bf16[128,1024]{1,0:T(8,128)(2,1)S(1)} collective-permute-done((bf16[128,1024]{1,0:T(8,128)(2,1)S(1)}, bf16[128,1024]{1,0:T(8,128)(2,1)S(1)}, u32[]{:S(2)}, u32[]{:S(2)}) %collective-permute-start.26) | collective-permute-done | bytes 262176 | tf_op jit(solution)/shard_map/ppermute | solution.py:465
  400.0 12.5 %first_back.1 = (bf16[512,1024]{1,0:T(8,128)(2,1)}, bf16[1024,512]{1,0:T(8,128)(2,1)}, f32[4,1024]{1,0:T(4,128)}, f32[8,128]{1,0:T(8,128)}) custom-call(s32[2]{0:T(128)} %pad_add_fusion.roles_ref, bf16[2,512,768]{2,1,0:T(8,128)(2,1)} %pad_maximum_fusion.6.refs_0_.refs_10_.refs_9_.refs_11_, ...), custom_call_target="tpu_custom_call" | custom-call | flops 1 | bytes 1 | tf_op jit(solution)/shard_map/first_back/pallas_call | solution.py:36
  413.3 6.2 %weight_grad.12 = (bf16[2,2,512,512]{3,2,1,0:T(8,128)(2,1)}, f32[8,128]{1,0:T(8,128)}) custom-call(s32[2]{0:T(128)} %pad_add_fusion.roles_ref, bf16[1024,512]{1,0:T(8,128)(2,1)} %get-tuple-element.869.refs_0_.refs_2_, bf16[2,512,512]{2,1,0:T(8,128)(2,1)} %pad_maximum_fusion.8.refs_1_.refs_18_.refs_3_, bf16[1024,512]{1,0:T(8,128)(2,1)} %get-tuple-element.869.refs_0_.refs_2_, ...), custom_call_target="tpu_custom_call" | custom-call | flops 1 | bytes 1 | tf_op jit(solution)/shard_map/weight_grad/pallas_call | solution.py:36
  419.5 2.7 collective-permute-start.30
  426.7 6.5 %inputs_back.1 = (bf16[2,512,512]{2,1,0:T(8,128)(2,1)}, bf16[2,512,512]{2,1,0:T(8,128)(2,1)}, f32[8,128]{1,0:T(8,128)}) custom-call(s32[2]{0:T(128)} %pad_add_fusion.roles_ref, bf16[512,1024]{1,0:T(8,128)(2,1)} %get-tuple-element.854.refs_0_, bf16[2,512,1536]{2,1,0:T(8,128)(2,1)} %copy-done, bf16[2,512,1536]{2,1,0:T(8,128)(2,1)} %collective-permute-done.6.refs_3_.refs_2_, ...), custom_call_target="tpu_custom_call" | custom-call | flops 1 | bytes 1 | tf_op jit(solution)/shard_map/inputs_back/pallas_call | solution.py:36
  434.8 11.1 %weight_grad.13 = (bf16[2,512,1536]{2,1,0:T(8,128)(2,1)}, bf16[2,512,1536]{2,1,0:T(8,128)(2,1)}, f32[8,128]{1,0:T(8,128)}) custom-call(s32[2]{0:T(128)} %pad_add_fusion.roles_ref, bf16[1024,512]{1,0:T(8,128)(2,1)} %get-tuple-element.869.refs_0_.refs_2_, bf16[2,512,512]{2,1,0:T(8,128)(2,1)} %pad_maximum_fusion.7.refs_0_.refs_17_.refs_1_.refs_3_, ...), custom_call_target="tpu_custom_call" | custom-call | flops 1 | bytes 1 | tf_op jit(solution)/shard_map/weight_grad/pallas_call | solution.py:36
  453.9 10.8 %layer_out.1 = (bf16[512,1024]{1,0:T(8,128)(2,1)}, f32[8,128]{1,0:T(8,128)}) custom-call(s32[2]{0:T(128)} %pad_add_fusion.roles_ref, bf16[2,512,1024]{2,1,0:T(8,128)(2,1)} %get-tuple-element.899.refs_1_.refs_3_.refs_0_, bf16[2,512,1024]{2,1,0:T(8,128)(2,1)} %get-tuple-element.900.refs_1_.refs_3_, ...), custom_call_target="tpu_custom_call" | custom-call | flops 1 | bytes 1 | tf_op jit(solution)/shard_map/layer_out/pallas_call | solution.py:36
  465.9 5.6 all-to-all-start.3
  471.5 4.0 convolution_convert_fusion
  475.7 27.9 %collective-permute-done.34 = bf16[2,512,1536]{2,1,0:T(8,128)(2,1)} collective-permute-done((bf16[2,512,1536]{2,1,0:T(8,128)(2,1)}, bf16[2,512,1536]{2,1,0:T(8,128)(2,1)}, u32[]{:S(2)}, u32[]{:S(2)}) %collective-permute-start.34) | collective-permute-done | bytes 3145760 | tf_op jit(solution)/shard_map/ppermute | solution.py:484
  503.6 4.4 fusion.2
  509.6 2.5 collective-permute-start.33
  512.1 2.3 collective-permute-done.33
  514.5 14.3 %collective-permute-done.36 = bf16[512,1536]{1,0:T(8,128)(2,1)} collective-permute-done((bf16[512,1536]{1,0:T(8,128)(2,1)}, bf16[512,1536]{1,0:T(8,128)(2,1)}, u32[]{:S(2)}, u32[]{:S(2)}) %collective-permute-start.36) | collective-permute-done | bytes 1572896 | tf_op jit(solution)/shard_map/ppermute | solution.py:484
  528.8 2.3 add_convert_fusion
  533.6 2.1 collective-permute-done.35
  535.7 5.0 collective-permute-done.40
  541.5 4.4 all-to-all-start.4
  545.9 2.0 add_convert_fusion.12
  555.6 2.4 collective-permute-start.37
  558.1 1.9 collective-permute-start.39
  560.0 21.0 %collective-permute-done.37 = f32[352]{0:T(512)S(1)} collective-permute-done((f32[352]{0:T(512)S(1)}, f32[352]{0:T(512)S(1)}, u32[]{:S(2)}, u32[]{:S(2)}) %collective-permute-start.37) | collective-permute-done | bytes 1440 | tf_op jit(solution)/shard_map/ppermute | solution.py:465
  584.1 9.9 %collective-permute-done.42 = bf16[128,1536]{1,0:T(8,128)(2,1)S(1)} collective-permute-done((bf16[128,1536]{1,0:T(8,128)(2,1)S(1)}, bf16[128,1536]{1,0:T(8,128)(2,1)S(1)}, u32[]{:S(2)}, u32[]{:S(2)}) %collective-permute-start.42) | collective-permute-done | bytes 393248 | tf_op jit(solution)/shard_map/ppermute | solution.py:465
  597.0 2.5 fusion.31
  (309 shorter events, 86.3 us)
Async XLA Ops:
  0.6 16.0 %copy-start.36 = (bf16[4,2,256,256]{3,2,1,0:T(8,128)(2,1)S(1)}, bf16[4,2,256,256]{3,2,1,0:T(8,128)(2,1)}, u32[]{:S(2)}) copy-start(bf16[4,2,256,256]{3,2,1,0:T(8,128)(2,1)} %param.30) | copy-start | bytes 3145732
  3.8 42.3 %copy-start.17 = (bf16[128,1536]{1,0:T(8,128)(2,1)}, bf16[128,1536]{1,0:T(8,128)(2,1)S(1)}, u32[]{:S(2)}) copy-start(bf16[128,1536]{1,0:T(8,128)(2,1)S(1)} %pad_maximum_fusion.9.refs_7_) | copy-start | bytes 1179652
  3.8 42.3 %collective-permute-start = (bf16[128,1536]{1,0:T(8,128)(2,1)S(1)}, bf16[128,1536]{1,0:T(8,128)(2,1)S(1)}, u32[]{:S(2)}, u32[]{:S(2)}) collective-permute-start(bf16[128,1536]{1,0:T(8,128)(2,1)S(1)} %pad_maximum_fusion.9.refs_7_), channel_id=1, source_target_pairs={{0,8},{8,12},{12,4},{4,0},{1,9},{9,13},{13,5},{5,1},{2,10},{10,14}... | collective-permute-start | bytes 1179656 | tf_op jit(solution)/shard_map/ppermute | solution.py:465
  7.9 38.2 %collective-permute-start.1 = (bf16[128,1536]{1,0:T(8,128)(2,1)S(1)}, bf16[128,1536]{1,0:T(8,128)(2,1)S(1)}, u32[]{:S(2)}, u32[]{:S(2)}) collective-permute-start(bf16[128,1536]{1,0:T(8,128)(2,1)S(1)} %pad_maximum_fusion.9.refs_7_), channel_id=1, source_target_pairs={{0,12},{8,4},{12,0},{4,8},{1,13},{9,5},{13,1},{5,9},{2,14},{10,6},... | collective-permute-start | bytes 1179656 | tf_op jit(solution)/shard_map/ppermute | solution.py:465
  9.2 36.9 %collective-permute-start.2 = (bf16[128,1536]{1,0:T(8,128)(2,1)S(1)}, bf16[128,1536]{1,0:T(8,128)(2,1)S(1)}, u32[]{:S(2)}, u32[]{:S(2)}) collective-permute-start(bf16[128,1536]{1,0:T(8,128)(2,1)S(1)} %pad_maximum_fusion.9.refs_7_), channel_id=1, source_target_pairs={{0,4},{8,0},{12,8},{4,12},{1,5},{9,1},{13,9},{5,13},{2,6},{10,2},{... | collective-permute-start | bytes 1179656 | tf_op jit(solution)/shard_map/ppermute | solution.py:465
  11.5 34.6 %all-to-all-start = ((f32[32,1,352]{2,1,0:T(1,128)}), f32[32,1,352]{2,1,0:T(1,128)S(1)}, u32[]{:S(2)}, u32[]{:S(2)}) async-start(f32[32,1,352]{2,1,0:T(1,128)} %broadcast_in_dim.8), calls=%async_computation | async-start | bytes 98304 | tf_op jit(solution)/shard_map/all_to_all | solution.py:571
  19.6 47.2 %copy-start.18 = (bf16[128,2048]{1,0:T(8,128)(2,1)}, bf16[128,2048]{1,0:T(8,128)(2,1)S(1)}, u32[]{:S(2)}) copy-start(bf16[128,2048]{1,0:T(8,128)(2,1)S(1)} %constant_dynamic-update-slice_fusion.refs_10_) | copy-start | bytes 1572868
  46.3 20.8 %copy-start.7 = (bf16[512,1536]{1,0:T(8,128)(2,1)}, bf16[512,1536]{1,0:T(8,128)(2,1)S(1)}, u32[]{:S(2)}) copy-start(bf16[512,1536]{1,0:T(8,128)(2,1)S(1)} %constant_dynamic-update-slice_fusion.2.refs_11_) | copy-start | bytes 4718596
  46.3 20.5 %collective-permute-start.5 = (bf16[512,1536]{1,0:T(8,128)(2,1)S(1)}, bf16[512,1536]{1,0:T(8,128)(2,1)S(1)}, u32[]{:S(2)}, u32[]{:S(2)}) collective-permute-start(bf16[512,1536]{1,0:T(8,128)(2,1)S(1)} %constant_dynamic-update-slice_fusion.2.refs_11_), channel_id=1, source_target_pairs={{0,16},{1,3},{2,18},{3,1},{4,20},{5,7},{6,22},{7,5},{8,24},{9,11},... | collective-permute-start | bytes 4718600 | tf_op jit(solution)/shard_map/ppermute | solution.py:484
  47.0 13.6 %collective-permute-start.3 = (bf16[128,2048]{1,0:T(8,128)(2,1)S(1)}, bf16[128,2048]{1,0:T(8,128)(2,1)S(1)}, u32[]{:S(2)}, u32[]{:S(2)}) collective-permute-start(bf16[128,2048]{1,0:T(8,128)(2,1)S(1)} %constant_dynamic-update-slice_fusion.refs_10_), channel_id=1, source_target_pairs={{0,8},{8,12},{12,4},{4,0},{1,9},{9,13},{13,5},{5,1},{2,10},{10,14}... | collective-permute-start | bytes 1572872 | tf_op jit(solution)/shard_map/ppermute | solution.py:465
  66.8 17.9 %copy-start.54 = (s32[4]{0:T(128)S(1)}, s32[4]{0:T(128)}, u32[]{:S(2)}) copy-start(s32[4]{0:T(128)} %constant.248.clone) | copy-start | bytes 52
  66.8 19.2 %copy-start.53 = (s32[4]{0:T(128)S(1)}, s32[4]{0:T(128)}, u32[]{:S(2)}) copy-start(s32[4]{0:T(128)} %constant.249.clone) | copy-start | bytes 52
  66.8 20.4 %copy-start.52 = (s32[4]{0:T(128)S(1)}, s32[4]{0:T(128)}, u32[]{:S(2)}) copy-start(s32[4]{0:T(128)} %constant.250.clone) | copy-start | bytes 52
  67.1 23.4 %copy-start = (bf16[2,512,1536]{2,1,0:T(8,128)(2,1)}, bf16[2,512,1536]{2,1,0:T(8,128)(2,1)S(1)}, u32[]{:S(2)}) copy-start(bf16[2,512,1536]{2,1,0:T(8,128)(2,1)S(1)} %pad_maximum_fusion.1.refs_2_.refs_12_.refs_1_) | copy-start | bytes 9437188
  67.1 47.2 %collective-permute-start.6 = (bf16[2,512,1536]{2,1,0:T(8,128)(2,1)S(1)}, bf16[2,512,1536]{2,1,0:T(8,128)(2,1)}, u32[]{:S(2)}, u32[]{:S(2)}) collective-permute-start(bf16[2,512,1536]{2,1,0:T(8,128)(2,1)S(1)} %pad_maximum_fusion.1.refs_2_.refs_12_.refs_1_), channel_id=1, source_target_pairs={{0,2},{1,17},{2,0},{3,19},{4,6},{5,21},{6,4},{7,23},{8,10},{9,25},... | collective-permute-start | bytes 9437192 | tf_op jit(solution)/shard_map/ppermute | solution.py:484
  67.9 46.4 %collective-permute-start.7 = (bf16[2,512,1536]{2,1,0:T(8,128)(2,1)S(1)}, bf16[2,512,1536]{2,1,0:T(8,128)(2,1)}, u32[]{:S(2)}, u32[]{:S(2)}) collective-permute-start(bf16[2,512,1536]{2,1,0:T(8,128)(2,1)S(1)} %pad_maximum_fusion.1.refs_2_.refs_12_.refs_1_), channel_id=1, source_target_pairs={{0,1},{1,0},{2,3},{3,2},{4,5},{5,4},{6,7},{7,6},{8,9},{9,8},{10,11... | collective-permute-start | bytes 9437192 | tf_op jit(solution)/shard_map/ppermute | solution.py:460
  67.9 14.4 %collective-permute-start.4 = (bf16[128,2048]{1,0:T(8,128)(2,1)S(1)}, bf16[128,2048]{1,0:T(8,128)(2,1)}, u32[]{:S(2)}, u32[]{:S(2)}) collective-permute-start(bf16[128,2048]{1,0:T(8,128)(2,1)S(1)} %collective-permute-done.3), channel_id=1, source_target_pairs={{0,8},{8,12},{12,4},{4,0},{1,9},{9,13},{13,5},{5,1},{2,10},{10,14}... | collective-permute-start | bytes 1572872 | tf_op jit(solution)/shard_map/ppermute | solution.py:465
  82.4 13.9 %collective-permute-start.8 = (bf16[128,2048]{1,0:T(8,128)(2,1)}, bf16[128,2048]{1,0:T(8,128)(2,1)}, u32[]{:S(2)}, u32[]{:S(2)}) collective-permute-start(bf16[128,2048]{1,0:T(8,128)(2,1)} %collective-permute-done.4), channel_id=1, source_target_pairs={{0,8},{8,12},{12,4},{4,0},{1,9},{9,13},{13,5},{5,1},{2,10},{10,14}... | collective-permute-start | bytes 1572872 | tf_op jit(solution)/shard_map/ppermute | solution.py:465
  90.5 45.8 %all-to-all-start.1 = ((bf16[16,128,512]{2,1,0:T(8,128)(2,1)}), bf16[16,128,512]{2,1,0:T(8,128)(2,1)}, u32[]{:S(2)}, u32[]{:S(2)}) async-start(bf16[16,128,512]{2,1,0:T(8,128)(2,1)} %bitcast.125), calls=%async_computation.1 | async-start | bytes 4194304 | tf_op jit(solution)/shard_map/all_to_all | solution.py:457
  104.2 35.9 %copy-start.40 = (f32[1,7,8,128]{3,1,2,0:T(8,128)}, f32[1,7,8,128]{3,1,2,0:T(8,128)S(1)}, u32[]{:S(2)}) copy-start(f32[1,7,8,128]{3,1,2,0:T(8,128)S(1)} %copy.118) | copy-start | bytes 86020
  114.3 25.7 %collective-permute-start.9 = (bf16[2,512,1536]{2,1,0:T(8,128)(2,1)}, bf16[2,512,1536]{2,1,0:T(8,128)(2,1)S(1)}, u32[]{:S(2)}, u32[]{:S(2)}) collective-permute-start(bf16[2,512,1536]{2,1,0:T(8,128)(2,1)} %collective-permute-done.6.refs_3_.refs_2_), channel_id=1, source_target_pairs={{0,1},{1,0},{2,3},{3,2},{4,5},{5,4},{6,7},{7,6},{8,9},{9,8},{10,11... | collective-permute-start | bytes 9437192 | tf_op jit(solution)/shard_map/ppermute | solution.py:460
  114.3 36.3 %collective-permute-start.10 = (bf16[512,2048]{1,0:T(8,128)(2,1)}, bf16[512,2048]{1,0:T(8,128)(2,1)}, u32[]{:S(2)}, u32[]{:S(2)}) collective-permute-start(bf16[512,2048]{1,0:T(8,128)(2,1)} %constant_dynamic-update-slice_fusion.6.refs_13_), channel_id=1, source_target_pairs={{0,16},{1,3},{2,18},{3,1},{4,20},{5,7},{6,22},{7,5},{8,24},{9,11},... | collective-permute-start | bytes 6291464 | tf_op jit(solution)/shard_map/ppermute | solution.py:484
  155.3 65.0 %collective-permute-start.13 = (bf16[2,512,2048]{2,1,0:T(8,128)(2,1)}, bf16[2,512,2048]{2,1,0:T(8,128)(2,1)}, u32[]{:S(2)}, u32[]{:S(2)}) collective-permute-start(bf16[2,512,2048]{2,1,0:T(8,128)(2,1)} %pad_maximum_fusion.refs_6_.refs_1_.refs_2_), channel_id=1, source_target_pairs={{0,2},{1,17},{2,0},{3,19},{4,6},{5,21},{6,4},{7,23},{8,10},{9,25},... | collective-permute-start | bytes 12582920 | tf_op jit(solution)/shard_map/ppermute | solution.py:484
  158.6 61.7 %collective-permute-start.14 = (bf16[2,512,2048]{2,1,0:T(8,128)(2,1)}, bf16[2,512,2048]{2,1,0:T(8,128)(2,1)}, u32[]{:S(2)}, u32[]{:S(2)}) collective-permute-start(bf16[2,512,2048]{2,1,0:T(8,128)(2,1)} %pad_maximum_fusion.refs_6_.refs_1_.refs_2_), channel_id=1, source_target_pairs={{0,1},{1,0},{2,3},{3,2},{4,5},{5,4},{6,7},{7,6},{8,9},{9,8},{10,11... | collective-permute-start | bytes 12582920 | tf_op jit(solution)/shard_map/ppermute | solution.py:460
  166.5 51.2 %all-to-all-start.2 = ((bf16[16,32,1024]{2,1,0:T(8,128)(2,1)}), bf16[16,32,1024]{2,1,0:T(8,128)(2,1)}, u32[]{:S(2)}, u32[]{:S(2)}) async-start(bf16[16,32,1024]{2,1,0:T(8,128)(2,1)} %bitcast.31), calls=%async_computation.2 | async-start | bytes 2097152 | tf_op jit(solution)/shard_map/all_to_all | solution.py:457
  176.0 5.3 collective-permute-start.11
  176.5 18.0 %collective-permute-start.12 = (bf16[2,512,768]{2,1,0:T(8,128)(2,1)S(1)}, bf16[2,512,768]{2,1,0:T(8,128)(2,1)S(1)}, u32[]{:S(2)}, u32[]{:S(2)}) collective-permute-start(bf16[2,512,768]{2,1,0:T(8,128)(2,1)S(1)} %copy-done.10), channel_id=1, source_target_pairs={{0,1},{1,0},{2,3},{3,2},{4,5},{5,4},{6,7},{7,6},{8,9},{9,8},{10,11... | collective-permute-start | bytes 4718600 | tf_op jit(solution)/shard_map/ppermute | solution.py:460
  194.5 14.4 %copy-start.41 = (f32[1,7,8,128]{3,1,2,0:T(8,128)S(1)}, f32[1,7,8,128]{3,1,2,0:T(8,128)}, u32[]{:S(2)}) copy-start(f32[1,7,8,128]{3,1,2,0:T(8,128)} %copy-done.40) | copy-start | bytes 86020
  220.3 10.2 %collective-permute-start.15 = (bf16[2,512,2048]{2,1,0:T(8,128)(2,1)}, bf16[2,512,2048]{2,1,0:T(8,128)(2,1)}, u32[]{:S(2)}, u32[]{:S(2)}) collective-permute-start(bf16[2,512,2048]{2,1,0:T(8,128)(2,1)} %collective-permute-done.13.refs_2_.refs_3_), channel_id=1, source_target_pairs={{0,1},{1,0},{2,3},{3,2},{4,5},{5,4},{6,7},{7,6},{8,9},{9,8},{10,11... | collective-permute-start | bytes 12582920 | tf_op jit(solution)/shard_map/ppermute | solution.py:460
  248.8 7.8 %collective-permute-start.16 = (bf16[2,2,512,1024]{3,2,1,0:T(8,128)(2,1)}, bf16[2,2,512,1024]{3,2,1,0:T(8,128)(2,1)}, u32[]{:S(2)}, u32[]{:S(2)}) collective-permute-start(bf16[2,2,512,1024]{3,2,1,0:T(8,128)(2,1)} %get-tuple-element.683), channel_id=1, source_target_pairs={{0,1},{1,0},{2,3},{3,2},{4,5},{5,4},{6,7},{7,6},{8,9},{9,8},{10,11... | collective-permute-start | bytes 12582920 | tf_op jit(solution)/shard_map/ppermute | solution.py:460
  265.6 26.2 %collective-permute-start.17 = (bf16[2,512,1024]{2,1,0:T(8,128)(2,1)}, bf16[2,512,1024]{2,1,0:T(8,128)(2,1)S(1)}, u32[]{:S(2)}, u32[]{:S(2)}) collective-permute-start(bf16[2,512,1024]{2,1,0:T(8,128)(2,1)} %get-tuple-element.719), channel_id=1, source_target_pairs={{0,2},{1,17},{2,0},{3,19},{4,6},{5,21},{6,4},{7,23},{8,10},{9,25},... | collective-permute-start | bytes 6291464 | tf_op jit(solution)/shard_map/ppermute | solution.py:484
  274.8 17.0 %copy-start.25 = (bf16[2,512,1024]{2,1,0:T(8,128)(2,1)S(1)}, bf16[2,512,1024]{2,1,0:T(8,128)(2,1)}, u32[]{:S(2)}) copy-start(bf16[2,512,1024]{2,1,0:T(8,128)(2,1)} %get-tuple-element.722) | copy-start | bytes 6291460
  302.4 16.3 %collective-permute-start.20 = (bf16[2,2,512,1024]{3,2,1,0:T(8,128)(2,1)}, bf16[2,2,512,1024]{3,2,1,0:T(8,128)(2,1)S(1)}, u32[]{:S(2)}, u32[]{:S(2)}) collective-permute-start(bf16[2,2,512,1024]{3,2,1,0:T(8,128)(2,1)} %get-tuple-element.742), channel_id=1, source_target_pairs={{0,1},{1,0},{2,3},{3,2},{4,5},{5,4},{6,7},{7,6},{8,9},{9,8},{10,11... | collective-permute-start | bytes 12582920 | tf_op jit(solution)/shard_map/ppermute | solution.py:460
  302.5 14.9 %collective-permute-start.18 = (bf16[512,1024]{1,0:T(8,128)(2,1)S(1)}, bf16[512,1024]{1,0:T(8,128)(2,1)S(1)}, u32[]{:S(2)}, u32[]{:S(2)}) collective-permute-start(bf16[512,1024]{1,0:T(8,128)(2,1)S(1)} %copy-done.16), channel_id=1, source_target_pairs={{0,16},{1,3},{2,18},{3,1},{4,20},{5,7},{6,22},{7,5},{8,24},{9,11},... | collective-permute-start | bytes 3145736 | tf_op jit(solution)/shard_map/ppermute | solution.py:484
  328.4 45.9 %collective-permute-start.23 = (bf16[2,512,1024]{2,1,0:T(8,128)(2,1)}, bf16[2,512,1024]{2,1,0:T(8,128)(2,1)S(1)}, u32[]{:S(2)}, u32[]{:S(2)}) collective-permute-start(bf16[2,512,1024]{2,1,0:T(8,128)(2,1)} %get-tuple-element.781), channel_id=1, source_target_pairs={{0,2},{1,17},{2,0},{3,19},{4,6},{5,21},{6,4},{7,23},{8,10},{9,25},... | collective-permute-start | bytes 6291464 | tf_op jit(solution)/shard_map/ppermute | solution.py:484
  329.5 19.6 %collective-permute-start.19 = (bf16[128,1024]{1,0:T(8,128)(2,1)S(1)}, bf16[128,1024]{1,0:T(8,128)(2,1)S(1)}, u32[]{:S(2)}, u32[]{:S(2)}) collective-permute-start(bf16[128,1024]{1,0:T(8,128)(2,1)S(1)} %copy-done.37), channel_id=1, source_target_pairs={{0,4},{8,0},{12,8},{4,12},{1,5},{9,1},{13,9},{5,13},{2,6},{10,2},{... | collective-permute-start | bytes 786440 | tf_op jit(solution)/shard_map/ppermute | solution.py:465
  349.9 14.1 %copy-start.33 = (bf16[128,1024]{1,0:T(8,128)(2,1)S(1)}, bf16[128,1024]{1,0:T(8,128)(2,1)}, u32[]{:S(2)}) copy-start(bf16[128,1024]{1,0:T(8,128)(2,1)} %add_convert_fusion.16.refs_8_) | copy-start | bytes 786436
  349.9 15.7 %copy-start.49 = (bf16[2,512,512]{2,1,0:T(8,128)(2,1)S(1)}, bf16[2,512,512]{2,1,0:T(8,128)(2,1)}, u32[]{:S(2)}) copy-start(bf16[2,512,512]{2,1,0:T(8,128)(2,1)} %get-tuple-element.775) | copy-start | bytes 3145732
  349.9 23.7 %copy-start.14 = (bf16[128,1024]{1,0:T(8,128)(2,1)S(1)}, bf16[128,1024]{1,0:T(8,128)(2,1)}, u32[]{:S(2)}) copy-start(bf16[128,1024]{1,0:T(8,128)(2,1)} %get-tuple-element.785.refs_7_) | copy-start | bytes 786436
  349.9 24.4 %copy-start.24 = (bf16[2,512,1024]{2,1,0:T(8,128)(2,1)S(1)}, bf16[2,512,1024]{2,1,0:T(8,128)(2,1)}, u32[]{:S(2)}) copy-start(bf16[2,512,1024]{2,1,0:T(8,128)(2,1)} %get-tuple-element.790) | copy-start | bytes 6291460
  363.9 13.0 %collective-permute-start.22 = (bf16[2,512,512]{2,1,0:T(8,128)(2,1)}, bf16[2,512,512]{2,1,0:T(8,128)(2,1)S(1)}, u32[]{:S(2)}, u32[]{:S(2)}) collective-permute-start(bf16[2,512,512]{2,1,0:T(8,128)(2,1)} %get-tuple-element.779), channel_id=1, source_target_pairs={{0,1},{1,0},{2,3},{3,2},{4,5},{5,4},{6,7},{7,6},{8,9},{9,8},{10,11... | collective-permute-start | bytes 3145736 | tf_op jit(solution)/shard_map/ppermute | solution.py:460
  364.0 9.6 %collective-permute-start.24 = (bf16[128,1024]{1,0:T(8,128)(2,1)S(1)}, bf16[128,1024]{1,0:T(8,128)(2,1)S(1)}, u32[]{:S(2)}, u32[]{:S(2)}) collective-permute-start(bf16[128,1024]{1,0:T(8,128)(2,1)S(1)} %copy-done.33), channel_id=1, source_target_pairs={{0,4},{8,0},{12,8},{4,12},{1,5},{9,1},{13,9},{5,13},{2,6},{10,2},{... | collective-permute-start | bytes 786440 | tf_op jit(solution)/shard_map/ppermute | solution.py:465
  365.6 22.7 %collective-permute-start.21 = (bf16[2,512,512]{2,1,0:T(8,128)(2,1)S(1)}, bf16[2,512,512]{2,1,0:T(8,128)(2,1)S(1)}, u32[]{:S(2)}, u32[]{:S(2)}) collective-permute-start(bf16[2,512,512]{2,1,0:T(8,128)(2,1)S(1)} %copy-done.49), channel_id=1, source_target_pairs={{0,1},{1,0},{2,3},{3,2},{4,5},{5,4},{6,7},{7,6},{8,9},{9,8},{10,11... | collective-permute-start | bytes 3145736 | tf_op jit(solution)/shard_map/ppermute | solution.py:460
  376.4 21.6 %collective-permute-start.25 = (bf16[512,1024]{1,0:T(8,128)(2,1)S(1)}, bf16[512,1024]{1,0:T(8,128)(2,1)S(1)}, u32[]{:S(2)}, u32[]{:S(2)}) collective-permute-start(bf16[512,1024]{1,0:T(8,128)(2,1)S(1)} %get-tuple-element.807.refs_12_), channel_id=1, source_target_pairs={{0,16},{1,3},{2,18},{3,1},{4,20},{5,7},{6,22},{7,5},{8,24},{9,11},... | collective-permute-start | bytes 3145736 | tf_op jit(solution)/shard_map/ppermute | solution.py:484
  387.4 46.1 %collective-permute-start.29 = (bf16[2,2,512,1024]{3,2,1,0:T(8,128)(2,1)}, bf16[2,2,512,1024]{3,2,1,0:T(8,128)(2,1)}, u32[]{:S(2)}, u32[]{:S(2)}) collective-permute-start(bf16[2,2,512,1024]{3,2,1,0:T(8,128)(2,1)} %get-tuple-element.863), channel_id=1, source_target_pairs={{0,1},{1,0},{2,3},{3,2},{4,5},{5,4},{6,7},{7,6},{8,9},{9,8},{10,11... | collective-permute-start | bytes 12582920 | tf_op jit(solution)/shard_map/ppermute | solution.py:460
  387.5 9.6 %collective-permute-start.26 = (bf16[128,1024]{1,0:T(8,128)(2,1)S(1)}, bf16[128,1024]{1,0:T(8,128)(2,1)S(1)}, u32[]{:S(2)}, u32[]{:S(2)}) collective-permute-start(bf16[128,1024]{1,0:T(8,128)(2,1)S(1)} %copy-done.32), channel_id=1, source_target_pairs={{0,4},{8,0},{12,8},{4,12},{1,5},{9,1},{13,9},{5,13},{2,6},{10,2},{... | collective-permute-start | bytes 786440 | tf_op jit(solution)/shard_map/ppermute | solution.py:465
  399.3 13.2 %collective-permute-start.27 = (bf16[128,1024]{1,0:T(8,128)(2,1)S(1)}, bf16[128,1024]{1,0:T(8,128)(2,1)S(1)}, u32[]{:S(2)}, u32[]{:S(2)}) collective-permute-start(bf16[128,1024]{1,0:T(8,128)(2,1)S(1)} %get-tuple-element.838.refs_15_), channel_id=1, source_target_pairs={{0,4},{8,0},{12,8},{4,12},{1,5},{9,1},{13,9},{5,13},{2,6},{10,2},{... | collective-permute-start | bytes 786440 | tf_op jit(solution)/shard_map/ppermute | solution.py:465
  419.5 14.0 %collective-permute-start.28 = (bf16[2,2,512,512]{3,2,1,0:T(8,128)(2,1)}, bf16[2,2,512,512]{3,2,1,0:T(8,128)(2,1)S(1)}, u32[]{:S(2)}, u32[]{:S(2)}) collective-permute-start(bf16[2,2,512,512]{3,2,1,0:T(8,128)(2,1)} %get-tuple-element.862), channel_id=1, source_target_pairs={{0,1},{1,0},{2,3},{3,2},{4,5},{5,4},{6,7},{7,6},{8,9},{9,8},{10,11... | collective-permute-start | bytes 6291464 | tf_op jit(solution)/shard_map/ppermute | solution.py:460
  419.5 13.8 %collective-permute-start.30 = (bf16[128,1024]{1,0:T(8,128)(2,1)S(1)}, bf16[128,1024]{1,0:T(8,128)(2,1)S(1)}, u32[]{:S(2)}, u32[]{:S(2)}) collective-permute-start(bf16[128,1024]{1,0:T(8,128)(2,1)S(1)} %copy-done.31), channel_id=1, source_target_pairs={{0,4},{8,0},{12,8},{4,12},{1,5},{9,1},{13,9},{5,13},{2,6},{10,2},{... | collective-permute-start | bytes 786440 | tf_op jit(solution)/shard_map/ppermute | solution.py:465
  433.3 17.2 %collective-permute-start.31 = (bf16[128,1024]{1,0:T(8,128)(2,1)S(1)}, bf16[128,1024]{1,0:T(8,128)(2,1)S(1)}, u32[]{:S(2)}, u32[]{:S(2)}) collective-permute-start(bf16[128,1024]{1,0:T(8,128)(2,1)S(1)} %add_convert_fusion.13.refs_16_), channel_id=1, source_target_pairs={{0,4},{8,0},{12,8},{4,12},{1,5},{9,1},{13,9},{5,13},{2,6},{10,2},{... | collective-permute-start | bytes 786440 | tf_op jit(solution)/shard_map/ppermute | solution.py:465
  447.6 56.0 %collective-permute-start.34 = (bf16[2,512,1536]{2,1,0:T(8,128)(2,1)}, bf16[2,512,1536]{2,1,0:T(8,128)(2,1)}, u32[]{:S(2)}, u32[]{:S(2)}) collective-permute-start(bf16[2,512,1536]{2,1,0:T(8,128)(2,1)} %get-tuple-element.917), channel_id=1, source_target_pairs={{0,2},{1,17},{2,0},{3,19},{4,6},{5,21},{6,4},{7,23},{8,10},{9,25},... | collective-permute-start | bytes 9437192 | tf_op jit(solution)/shard_map/ppermute | solution.py:484
  464.9 10.8 %collective-permute-start.32 = (f32[2,4,2,352]{3,2,1,0:T(2,128)S(1)}, f32[2,4,2,352]{3,2,1,0:T(2,128)S(1)}, u32[]{:S(2)}, u32[]{:S(2)}) collective-permute-start(f32[2,4,2,352]{3,2,1,0:T(2,128)S(1)} %bitcast.159), channel_id=1, source_target_pairs={{0,1},{1,0},{2,3},{3,2},{4,5},{5,4},{6,7},{7,6},{8,9},{9,8},{10,11... | collective-permute-start | bytes 67592 | tf_op jit(solution)/shard_map/ppermute | solution.py:460
  465.9 74.8 %all-to-all-start.3 = ((bf16[16,128,512]{2,1,0:T(8,128)(2,1)}), bf16[16,128,512]{2,1,0:T(8,128)(2,1)S(1)}, u32[]{:S(2)}, u32[]{:S(2)}) async-start(bf16[16,128,512]{2,1,0:T(8,128)(2,1)} %bitcast.50), calls=%async_computation.3 | async-start | bytes 4194304 | tf_op jit(solution)/shard_map/all_to_all | solution.py:457
  471.5 32.1 %copy-start.20 = (bf16[2,512,1536]{2,1,0:T(8,128)(2,1)S(1)}, bf16[2,512,1536]{2,1,0:T(8,128)(2,1)}, u32[]{:S(2)}) copy-start(bf16[2,512,1536]{2,1,0:T(8,128)(2,1)} %get-tuple-element.918) | copy-start | bytes 9437188
  508.0 20.7 %collective-permute-start.36 = (bf16[512,1536]{1,0:T(8,128)(2,1)}, bf16[512,1536]{1,0:T(8,128)(2,1)}, u32[]{:S(2)}, u32[]{:S(2)}) collective-permute-start(bf16[512,1536]{1,0:T(8,128)(2,1)} %get-tuple-element.1017), channel_id=1, source_target_pairs={{0,16},{1,3},{2,18},{3,1},{4,20},{5,7},{6,22},{7,5},{8,24},{9,11},... | collective-permute-start | bytes 4718600 | tf_op jit(solution)/shard_map/ppermute | solution.py:484
  509.6 4.9 collective-permute-start.33
  532.1 8.7 %collective-permute-start.40 = (bf16[128,1536]{1,0:T(8,128)(2,1)S(1)}, bf16[128,1536]{1,0:T(8,128)(2,1)S(1)}, u32[]{:S(2)}, u32[]{:S(2)}) collective-permute-start(bf16[128,1536]{1,0:T(8,128)(2,1)S(1)} %get-tuple-element.1033), channel_id=1, source_target_pairs={{0,4},{8,0},{12,8},{4,12},{1,5},{9,1},{13,9},{5,13},{2,6},{10,2},{... | collective-permute-start | bytes 1179656 | tf_op jit(solution)/shard_map/ppermute | solution.py:465
  532.1 3.6 collective-permute-start.35
  541.5 54.1 %all-to-all-start.4 = ((bf16[16,32,1024]{2,1,0:T(8,128)(2,1)}), bf16[16,32,1024]{2,1,0:T(8,128)(2,1)S(1)}, u32[]{:S(2)}, u32[]{:S(2)}) async-start(bf16[16,32,1024]{2,1,0:T(8,128)(2,1)} %bitcast.139), calls=%async_computation.4 | async-start | bytes 2097152 | tf_op jit(solution)/shard_map/all_to_all | solution.py:457
  547.8 33.3 %collective-permute-start.41 = (bf16[128,1536]{1,0:T(8,128)(2,1)}, bf16[128,1536]{1,0:T(8,128)(2,1)}, u32[]{:S(2)}, u32[]{:S(2)}) collective-permute-start(bf16[128,1536]{1,0:T(8,128)(2,1)} %add_convert_fusion.12), channel_id=1, source_target_pairs={{0,4},{8,0},{12,8},{4,12},{1,5},{9,1},{13,9},{5,13},{2,6},{10,2},{... | collective-permute-start | bytes 1179656 | tf_op jit(solution)/shard_map/ppermute | solution.py:465
  555.6 25.5 %collective-permute-start.37 = (f32[352]{0:T(512)S(1)}, f32[352]{0:T(512)S(1)}, u32[]{:S(2)}, u32[]{:S(2)}) collective-permute-start(f32[352]{0:T(512)S(1)} %get-tuple-element.1016), channel_id=1, source_target_pairs={{0,4},{8,0},{12,8},{4,12},{1,5},{9,1},{13,9},{5,13},{2,6},{10,2},{... | collective-permute-start | bytes 4232 | tf_op jit(solution)/shard_map/ppermute | solution.py:465
  558.0 23.1 %collective-permute-start.38 = (f32[352]{0:T(512)S(1)}, f32[352]{0:T(512)S(1)}, u32[]{:S(2)}, u32[]{:S(2)}) collective-permute-start(f32[352]{0:T(512)S(1)} %get-tuple-element.1015), channel_id=1, source_target_pairs={{0,12},{8,4},{12,0},{4,8},{1,13},{9,5},{13,1},{5,9},{2,14},{10,6},... | collective-permute-start | bytes 4232 | tf_op jit(solution)/shard_map/ppermute | solution.py:465
  558.1 23.0 %collective-permute-start.39 = (f32[352]{0:T(512)S(1)}, f32[352]{0:T(512)S(1)}, u32[]{:S(2)}, u32[]{:S(2)}) collective-permute-start(f32[352]{0:T(512)S(1)} %get-tuple-element.1014), channel_id=1, source_target_pairs={{0,8},{8,12},{12,4},{4,0},{1,9},{9,13},{13,5},{5,1},{2,10},{10,14}... | collective-permute-start | bytes 4232 | tf_op jit(solution)/shard_map/ppermute | solution.py:465
  582.3 11.6 %collective-permute-start.42 = (bf16[128,1536]{1,0:T(8,128)(2,1)S(1)}, bf16[128,1536]{1,0:T(8,128)(2,1)S(1)}, u32[]{:S(2)}, u32[]{:S(2)}) collective-permute-start(bf16[128,1536]{1,0:T(8,128)(2,1)S(1)} %add_convert_fusion.11), channel_id=1, source_target_pairs={{0,4},{8,0},{12,8},{4,12},{1,5},{9,1},{13,9},{5,13},{2,6},{10,2},{... | collective-permute-start | bytes 1179656 | tf_op jit(solution)/shard_map/ppermute | solution.py:465
  (41 other events, 224.2 us)

commit v4 on v3

--- a/solution.py
+++ b/solution.py
@@ -152,27 +152,30 @@
     )(own, *others, probs, attended, grad)
 
 
+def up_tiles(left, w, k, parts, roles):
+    rows = left.shape[1] // parts
+
+    def term(x, h, at):
+        return mxu(left[:, pl.ds(at * rows, rows)], w[x][h], 1, 0)
+
+    if parts != 2:
+        return [sum(term(x, h, h) for h in range(parts)) for x in range(2)]
+    role = roles[k]
+    one, two = term(0, 1, 1 - role), term(1, 0, role)
+    return [
+        term(0, 0, 0) + jnp.where(role == 0, one, two),
+        term(1, 1, 1) + jnp.where(role == 0, two, one),
+    ]
+
+
 def up_body(ks, parts, step, roles, *refs):
     left = refs[0]
-    rest = refs[1 + 2 * len(ks) :]
-    rows = left.shape[1] // parts
     for i, k in enumerate(ks):
-        w = refs[1 + 2 * i : 3 + 2 * i]
-
-        def term(x, h, at):
-            return mxu(left[:, pl.ds(at * rows, rows)], w[x][h], 1, 0)
-
-        if parts == 2:
-            role = roles[k]
-            one, two = term(0, 1, 1 - role), term(1, 0, role)
-            step(i, 0, term(0, 0, 0) + jnp.where(role == 0, one, two), rest)
-            step(i, 1, term(1, 1, 1) + jnp.where(role == 0, two, one), rest)
-        else:
-            for x in range(2):
-                step(i, x, sum(term(x, h, h) for h in range(parts)), rest)
-
-
-def up(roles, after, name, left, weights, ks, width, col, step, extras, outs, tile):
+        for x, tile in enumerate(up_tiles(left, refs[1 + 2 * i : 3 + 2 * i], k, parts, roles)):
+            step(i, x, tile, refs[1 + 2 * len(ks) :])
+
+
+def up(roles, after, name, left, weights, ks, width, col, step, outs, tile):
     parts, rows, _ = weights[0][0].shape
     per = width // tile
     count = left.shape[0]
@@ -182,78 +185,183 @@
         after,
         grid=(per,),
         in_specs=[whole((count, parts * rows))]
-        + [pl.BlockSpec((parts, rows, tile), lambda n, _: (0, 0, col * per + n))] * (2 * len(ks))
-        + [pl.BlockSpec((2, e.shape[1], tile), lambda n, _: (0, 0, n)) for e in extras],
+        + [pl.BlockSpec((parts, rows, tile), lambda n, _: (0, 0, col * per + n))] * (2 * len(ks)),
         out_specs=[pl.BlockSpec((2, o[0], tile), lambda n, _: (0, 0, n)) for o in outs],
         out_shape=[jax.ShapeDtypeStruct((2, o[0], width), o[1]) for o in outs],
         name=name,
-    )(left, *[a for w in weights for a in w], *extras)
+    )(left, *[a for w in weights for a in w])
+
+
+def up_grad_body(k, parts, step, n_extra, n_out, n_more, roles, left, left_t, *refs):
+    w, extras, more = refs[:2], refs[2 : 2 + n_extra], refs[2 + n_extra : 2 + n_extra + n_more]
+    outs = refs[2 + n_extra + n_more : 2 + n_extra + n_more + n_out]
+    ends, kept = refs[2 + n_extra + n_more + n_out : -1], refs[-1]
+    for x, tile in enumerate(up_tiles(left, w, k, parts, roles)):
+        kept[x] = step(x, tile, extras, outs)
+    rows = left_t.shape[0] // parts
+    role = roles[k]
+    for a in range(2):
+        for b in range(parts):
+            total = mxu(left_t[pl.ds((b + role * (a - b)) * rows, rows), :], kept[a + role * (b - a)], 1, 0)
+            if n_more:
+                ends[a][b] = (total + more[0][a, b].astype(F32)).astype(BF16)
+            else:
+                ends[0][a, b] = total.astype(BF16)
+
+
+def up_grad(roles, after, name, left, left_t, weights, k, col, step, extras, outs, more=()):
+    parts, rows, _ = weights[0].shape
+    tile = 256
+    width = extras[0].shape[2]
+    per = width // tile
+    count = left.shape[0]
+    thin = lambda r: pl.BlockSpec((2, r, tile), lambda n, _: (0, 0, n))
+    pair = pl.BlockSpec((2, parts, rows, tile), lambda n, _: (0, 0, 0, n))
+    single = pl.BlockSpec((parts, rows, tile), lambda n, _: (0, 0, n))
+    ends = [(single, (parts, rows, width))] * 2 if more else [(pair, (2, parts, rows, width))]
+    return call(
+        functools.partial(up_grad_body, k, parts, step, len(extras), len(outs), len(more)),
+        roles,
+        after,
+        grid=(per,),
+        in_specs=[whole(left.shape), whole(left_t.shape)]
+        + [pl.BlockSpec((parts, rows, tile), lambda n, _: (0, 0, col * per + n))] * 2
+        + [thin(e.shape[1]) for e in extras]
+        + [pair] * len(more),
+        out_specs=[thin(o[0]) for o in outs] + [e[0] for e in ends],
+        out_shape=[jax.ShapeDtypeStruct((2, o[0], width), o[1]) for o in outs]
+        + [jax.ShapeDtypeStruct(e[1], BF16) for e in ends],
+        scratch_shapes=[pltpu.VMEM((2, count, tile), BF16)],
+        name=name,
+    )(left, left_t, *weights, *extras, *more)
 
 
 def plain_step(i, x, total, refs):
     refs[i][x] = total.astype(BF16)
 
 
-def gelu_step(i, x, total, refs):
-    bias, act, slope = refs
-    v = total + bias[x]
+def gelu_step(x, total, extras, outs):
+    act, slope = outs
+    v = total + extras[0][x]
     half = 0.5 * (1.0 + lax.erf(v * (0.5**0.5)))
-    act[x] = (v * half).astype(BF16)
+    low = (v * half).astype(BF16)
+    act[x] = low
     slope[x] = (half + v * jnp.exp(-0.5 * v * v) * 0.3989422804014327).astype(BF16)
-
-
-def slope_step(i, x, total, refs):
-    slope, grad, sums = refs
-    low = (total * slope[x].astype(F32)).astype(BF16)
+    return low
+
+
+def slope_step(x, total, extras, outs):
+    grad, sums = outs
+    low = (total * extras[0][x].astype(F32)).astype(BF16)
     grad[x] = low
     sums[x] = jnp.sum(low.astype(F32), axis=0, keepdims=True)
-
-
-def down_body(parts, finish, roles, *refs):
-    rest = refs[6:-1]
+    return low
+
+
+def down_body(parts, per, finish, n_extra, n_out, n_in, body, roles, *refs):
+    extras = refs[6 : 6 + n_extra]
+    outs = refs[6 + n_extra + n_in : 6 + n_extra + n_in + n_out]
     acc = refs[-1]
     n = pl.program_id(0)
-    per = pl.num_programs(0)
-    total = [0] * parts
-    for k in range(2):
-        left, w = refs[k], refs[2 + 2 * k : 4 + 2 * k]
-
-        def term(x, h, at):
-            return mxu(left[at], w[x][h], 1, 1)
-
-        if parts == 2:
-            role = roles[k]
-            one, two = term(0, 1, role), term(1, 0, 1 - role)
-            total[0] = total[0] + term(0, 0, 0) + jnp.where(role == 0, two, one)
-            total[1] = total[1] + term(1, 1, 1) + jnp.where(role == 0, one, two)
-        else:
-            for h in range(parts):
-                total[h] = total[h] + term(0, h, 0) + term(1, h, 1)
-    for h in range(parts):
-        acc[h * per + n] = total[h]
+
+    @pl.when(n < per)
+    def _():
+        total = [0] * parts
+        for k in range(2):
+            left, w = refs[k], refs[2 + 2 * k : 4 + 2 * k]
+
+            def term(x, h, at):
+                return mxu(left[at], w[x][h], 1, 1)
+
+            if parts == 2:
+                role = roles[k]
+                one, two = term(0, 1, role), term(1, 0, 1 - role)
+                total[0] = total[0] + term(0, 0, 0) + jnp.where(role == 0, two, one)
+                total[1] = total[1] + term(1, 1, 1) + jnp.where(role == 0, one, two)
+            else:
+                for h in range(parts):
+                    total[h] = total[h] + term(0, h, 0) + term(1, h, 1)
+        for h in range(parts):
+            acc[h * per + n] = total[h]
 
     @pl.when(n == per - 1)
     def _():
-        finish(acc, rest)
-
-
-def down(roles, after, name, lefts, weights, width, col, finish, extras, outs):
+        finish(acc, [*extras, *outs])
+
+    if body is not None:
+
+        @pl.when(n >= per)
+        def _():
+            body(roles, outs, refs[6 + n_extra : 6 + n_extra + n_in], refs[6 + n_extra + n_in + n_out : -1])
+
+
+def down(roles, after, name, lefts, weights, width, col, finish, extras, outs, then=(0, None, [], [])):
     parts, rows, _ = weights[0][0].shape
     tile = min(256, rows)
+    per = rows // tile
     count = lefts[0].shape[1]
+    steps, body, ins, more = then
+
+    def late(block, index):
+        return pl.BlockSpec(block, lambda n, _: index(jnp.maximum(n - per, 0)))
+
     return call(
-        functools.partial(down_body, parts, finish),
+        functools.partial(down_body, parts, per, finish, len(extras), len(outs), len(ins), body),
         roles,
         after,
-        grid=(rows // tile,),
+        grid=(per + steps,),
         in_specs=[whole((2, count, width))] * 2
-        + [pl.BlockSpec((parts, tile, width), lambda n, _: (0, n, col))] * 4
-        + [whole(e.shape) for e in extras],
-        out_specs=[whole(o[0]) for o in outs],
-        out_shape=[jax.ShapeDtypeStruct(*o) for o in outs],
+        + [pl.BlockSpec((parts, tile, width), lambda n, _: (0, jnp.minimum(n, per - 1), col))] * 4
+        + [whole(e.shape) for e in extras]
+        + [late(*i[1:]) for i in ins],
+        out_specs=[whole(o[0]) for o in outs] + [late(*m[2:]) for m in more],
+        out_shape=[jax.ShapeDtypeStruct(*o) for o in outs] + [jax.ShapeDtypeStruct(*m[:2]) for m in more],
         scratch_shapes=[pltpu.VMEM((parts * rows // tile, count, tile), F32)],
         name=name,
-    )(*lefts, *weights[0], *weights[1], *extras)
+    )(*lefts, *weights[0], *weights[1], *extras, *[i[0] for i in ins])
+
+
+def then_up(place, weights, width, col, tile):
+    parts, rows, _ = weights[0][0].shape
+    per = width // tile
+
+    def body(roles, outs, ins, ends):
+        for k in range(2):
+            for x, total in enumerate(up_tiles(outs[place], ins[2 * k : 2 * k + 2], k, parts, roles)):
+                ends[k][x] = total.astype(BF16)
+
+    def of(count):
+        return (
+            per,
+            body,
+            [(a, (parts, rows, tile), lambda m: (0, 0, col * per + m)) for w in weights for a in w],
+            [((2, count, width), BF16, (2, count, tile), lambda m: (0, 0, m))] * 2,
+        )
+
+    return of
+
+
+def then_grad(place, right, parts):
+    _, count, cols = right.shape
+
+    def body(roles, outs, ins, ends):
+        b = pl.program_id(0) - pl.num_programs(0) + parts
+        rows = outs[place].shape[0] // parts
+        role = roles[1]
+        for a in range(2):
+            left = outs[place][pl.ds((b + role * (a - b)) * rows, rows), :]
+            ends[0][a] = mxu(left, ins[0][a + role * (b - a)], 1, 0).astype(BF16)
+
+    def of(depth):
+        rows = depth // parts
+        return (
+            parts,
+            body,
+            [(right, right.shape, lambda m: (0, 0, 0))],
+            [((2, parts, rows, cols), BF16, (2, None, rows, cols), lambda m: (0, m, 0, 0))],
+        )
+
+    return of
 
 
 def row_mean(tiles):
@@ -326,6 +434,27 @@
         cc = slice(i * width, (i + 1) * width)
         v = (acc[i] + total_ref[:, cc] + rows[0:1, cc]) * rows[1:2, cc]
         low_ref[:, cc] = v.astype(BF16)
+
+
+def arrived_body(roles, cot, permute, live, low_ref, low_t_ref):
+    low = mxu(cot[...], permute[...], 1, 0) * live[...]
+    low_ref[...] = low.astype(BF16)
+    low_t_ref[...] = low.T.astype(BF16)
+
+
+def arrived(roles, after, cot, permute, live):
+    count, width = cot.shape
+    tile = min(256, width)
+    return call(
+        arrived_body,
+        roles,
+        after,
+        grid=(width // tile,),
+        in_specs=[whole(cot.shape), pl.BlockSpec((width, tile), lambda n, _: (0, n)), whole((1, 1))],
+        out_specs=[pl.BlockSpec((count, tile), lambda n, _: (0, n)), pl.BlockSpec((tile, count), lambda n, _: (n, 0))],
+        out_shape=[jax.ShapeDtypeStruct((count, width), BF16), jax.ShapeDtypeStruct((width, count), BF16)],
+        name="arrived",
+    )(cot, permute, live.reshape(1, 1))
 
 
 def weight_grad_body(n_parts, n_more, own, roles, *refs):
@@ -500,7 +629,11 @@
 
     def gather_two(own, moved):
         first = line.plain(lambda a, m: jnp.stack([a, *m]), own, moved)
-        return first, over(first, second_pairs) if fs == 2 else over_tp(first, 2), over_tp(first, 1)
+        return first, over(first, second_pairs) if fs == 2 else over_tp(first, 2)
+
+    def gather_near(first, second):
+        first = line.gate(first)
+        return first, second, over_tp(first, 1)
 
     def gather_three(first, second, other):
         first, second, other = line.gate(first, second, other)
@@ -516,12 +649,12 @@
             return sums[0], [over(sums[1], first_pairs)]
         return sums[0], [over_fsdp(sums[h], -h) for h in range(1, fs)]
 
-    def reduce_three(own, moved):
-        def pieces(own, moved):
-            total = add(own, *moved).reshape(cs, rows, -1)
+    def reduce_three(*sums):
+        def pieces(*sums):
+            total = jnp.concatenate([add(own, *moved) for own, moved in sums], axis=1).reshape(cs, rows, -1)
             return [total[d] for d in range(cs)]
 
-        parts = line.plain(pieces, own, moved)
+        parts = line.plain(pieces, *sums)
         return parts, over_ctx(parts[-1], -1)
 
     def reduce_step(parts, moving):
@@ -572,14 +705,19 @@
     both = line.plain(split_rows, tokens, skip_tokens)
     ffn = line.plain(lambda a, b: jnp.concatenate([a, b], axis=1), expand_weight, shrink_weight)
     packed = line.gate(packed)
+    cot = to_group(line.gate(cotangent).reshape(group * fine, width))
     att = gather_one(att)
     ffn = ring_start(line.gate(ffn))
     ffn = ring_step(ffn)
-    att = gather_two(*att)
+    att = gather_near(*gather_two(*att))
     for _ in range(3, cs):
         ffn = ring_step(ffn)
+    cot = line.gate(cot)
     both = to_group(line.gate(both))
     ffn = gather_one(ring_step(ffn))
+
+    live = pick(live_slots.reshape(slots), (c_rank * ts + t_rank) // share).astype(F32)
+    branch_low, branch_low_t = line(arrived, cot.reshape(count, width), permute, live)
 
     def vectors_of(packed):
         vectors = packed[:, : 7 * small].reshape(fs * cs, ts, 7, small).transpose(0, 2, 1, 3)
@@ -598,22 +736,22 @@
     turned = (width, count)
     flows = [(count, BF16)] * 2
 
-    joined, normed, normed_t = line(
+    joined, normed, normed_t, *project = line(
         lambda *o: down(
             *o[:2], "joined", o[2], o[3], side, 0, functools.partial(norm_finish, False), [o[4][0:3]],
             [(act, F32), (act, BF16), (turned, BF16)],
+            then_up(1, o[3], 3 * heads_width, 1, heads_width)(count),
         ),
         both, att, vectors,
     )
     ffn = gather_two(*ffn)
-    project = line(
-        lambda *o: up(*o[:2], "project", *o[2:], (0, 1), 3 * heads_width, 1, plain_step, [], flows, heads_width),
-        normed, att,
-    )
-    cot = to_group(line.gate(cotangent).reshape(group * fine, width))
     others = [[over_tp(project[k ^ (d & 1)], d) for d in range(1, share)] for k in range(2)]
-    inner = [line(attend_forward, project[k], others[k]) for k in range(2)]
+    inner = [line(attend_forward, project[0], others[0])]
+    ffn = gather_near(*ffn)
+    inner.append(line(attend_forward, project[1], others[1]))
     probs, attended = zip(*inner)
+
+    ffn = gather_three(*ffn)
     second, normed_two, normed_two_t = line(
         lambda *o: down(
             *o[:2], "second", o[2], o[3], heads_width, side // heads_width, functools.partial(norm_finish, True),
@@ -621,21 +759,6 @@
         ),
         attended, att, joined, vectors,
     )
-    live = pick(live_slots.reshape(slots), (c_rank * ts + t_rank) // share).astype(F32)
-
-    def arrived(cot, permute):
-        ours = (mxu(cot.reshape(count, width), permute, 1, 0) * live).astype(BF16)
-        return ours, ours.T
-
-    branch_low, branch_low_t = line.plain(arrived, cot, permute)
-    ffn = gather_three(*ffn)
-
-    def hidden_step(k):
-        return lambda *o: up(*o[:2], "hidden", *o[2:4], (k,), hidden, 0, gelu_step, [o[4]], flows, 256)
-
-    activated, slope = [None, None], [None, None]
-    for k in range(2):
-        activated[k], slope[k] = line(hidden_step(k), normed_two, ffn[k : k + 1], widen[k])
 
     def grads(k):
         return lambda roles, after, lefts, rights, more=(): weight_grad(roles, after, lefts, rights, fs, k, more)
@@ -643,40 +766,45 @@
     def other_grads(lefts, rights):
         return over_tp(line(grads(1), lefts, rights)[0], 1)
 
+    def hidden_step(k):
+        return lambda *o: up_grad(*o[:2], "hidden", *o[2:5], k, 0, gelu_step, [o[5]], flows, *o[6:])
+
     def hidden_back(k):
-        return lambda *o: up(
-            *o[:2], "hidden_back", *o[2:4], (k,), hidden, 1, slope_step, [o[4]], [(count, BF16), (1, F32)], 256
+        return lambda *o: up_grad(
+            *o[:2], "hidden_back", *o[2:5], k, 1, slope_step, [o[5]], [(count, BF16), (1, F32)], *o[6:]
         )
 
-    grad_expanded, wide = [None, None], [None, None]
-    other = other_grads([branch_low_t], [activated[1]])
-    grad_expanded[1], wide[1] = line(hidden_back(1), branch_low, ffn[1:], slope[1])
-    shrink_sums = reduce_one(line(grads(0), [branch_low_t], [activated[0]], [other]))
-    grad_expanded[0], wide[0] = line(hidden_back(0), branch_low, ffn[:1], slope[0])
-    grad_second, attn_low, attn_low_t, sums_two = line(
+    activated, slope, grad_expanded, wide = ([None, None] for _ in range(4))
+    activated[1], slope[1], other = line(hidden_step(1), normed_two, branch_low_t, ffn[1], widen[1])
+    other = over_tp(other, 1)
+    grad_expanded[1], wide[1], other_two = line(hidden_back(1), branch_low, normed_two_t, ffn[1], slope[1])
+    other_two = over_tp(other_two, 1)
+    activated[0], slope[0], *sums = line(hidden_step(0), normed_two, branch_low_t, ffn[0], widen[0], [other])
+    shrink_sums = reduce_one(sums)
+    grad_expanded[0], wide[0], *sums = line(hidden_back(0), branch_low, normed_two_t, ffn[0], slope[0], [other_two])
+    expand_sums = reduce_one(sums)
+    grad_second, attn_low, attn_low_t, sums_two, *grad_attended = line(
         lambda *o: down(
             *o[:2], "second_back", o[2], o[3], hidden, 0, functools.partial(norm_back_finish, True),
             [o[4], o[5], o[6][4:5]], [(act, F32), (act, BF16), (turned, BF16), ((4, width), F32)],
+            then_up(1, o[7], heads_width, side // heads_width, heads_width // 2)(count),
         ),
-        grad_expanded, ffn, second, branch_low, vectors,
+        grad_expanded, ffn, second, branch_low, vectors, att,
     )
     shrink_sums = reduce_two(*shrink_sums)
-    other = other_grads([normed_two_t], [grad_expanded[1]])
-    grad_attended = line(
-        lambda *o: up(
-            *o[:2], "attended_back", *o[2:], (0, 1), heads_width, side // heads_width, plain_step, [], flows,
-            heads_width // 2,
-        ),
-        attn_low, att,
-    )
-    shrink_sums = reduce_three(*shrink_sums)
-    expand_sums = reduce_one(line(grads(0), [normed_two_t], [grad_expanded[0]], [other]))
     inner = [None, None]
     inner[1] = line(attend_backward, project[1], others[1], probs[1], attended[1], grad_attended[1])
-    shrink_sums = reduce_step(*shrink_sums)
+
+    def layer_end(roles, after, a, w, t, v):
+        ends = jnp.stack([v[6], jnp.full((width,), live)])
+        return down(roles, after, "layer_out", a, w, hidden, 1, out_finish, [t, ends], [(act, BF16)])
+
+    (layer_out,) = line(layer_end, activated, ffn, second, vectors)
+    layer_out = line.plain(lambda a, p: mxu(a, p, 1, 1).astype(BF16), layer_out, permute)
+    layer_out = to_group(layer_out.reshape(group * fine, width))
+    expand_sums = reduce_two(*expand_sums)
     inner[0] = line(attend_backward, project[0], others[0], probs[0], attended[0], grad_attended[0])
-    shrink_sums = reduce_step(*shrink_sums)
-    expand_sums = reduce_two(*expand_sums)
+    ffn_sums = reduce_three(shrink_sums, expand_sums)
 
     def close(k):
         def total(own, *moves):
@@ -690,35 +818,34 @@
     grad_project[1] = close(1)
     attend_other = other_grads([attn_low_t, normed_t], [attended[1], grad_project[1]])
     grad_project[0] = close(0)
-    grad_shrink = reduce_last(*shrink_sums)
-    expand_sums = reduce_three(*expand_sums)
-    joined_low, joined_low_t, sums_one = line(
+    joined_low, joined_low_t, sums_one, merger_other = line(
         lambda *o: down(
             *o[:2], "first_back", o[2], o[3], 3 * heads_width, 1, functools.partial(norm_back_finish, False),
             [o[4], o[5], o[6][1:2]], [(act, BF16), (turned, BF16), ((4, width), F32)],
+            then_grad(1, o[7], fs)(width),
         ),
-        grad_project, att, joined, grad_second, vectors,
+        grad_project, att, joined, grad_second, vectors, both[1],
     )
-    expand_sums = reduce_step(*expand_sums)
-    merger_other = other_grads([joined_low_t], [both[1]])
+    merger_other = over_tp(merger_other, 1)
+    layer_out = line.gate(layer_out)
+    ffn_sums = reduce_step(*ffn_sums)
     out = line(
-        lambda *o: up(*o[:2], "inputs_back", *o[2:], (0, 1), side, 0, plain_step, [], flows, 256),
+        lambda *o: up(*o[:2], "inputs_back", *o[2:], (0, 1), side, 0, plain_step, flows, 256),
         joined_low, att,
     )
-    expand_sums = reduce_step(*expand_sums)
+    def turn_back(out):
+        out = absolute(out).reshape(ts, cs, ts * fine, side)
+        return out.transpose(1, 0, 2, 3).reshape(group * ts * fine, side)
+
+    out = to_group(line.plain(turn_back, out))
+    ffn_sums = reduce_step(*ffn_sums)
     att_sums = reduce_one(
         line(
             grads(0), [joined_low_t, attn_low_t, normed_t], [both[0], attended[0], grad_project[0]],
             [merger_other, attend_other],
         )
     )
-
-    def turn_back(out):
-        out = absolute(out).reshape(ts, cs, ts * fine, side)
-        return out.transpose(1, 0, 2, 3).reshape(group * ts * fine, side)
-
-    out = to_group(line.plain(turn_back, out))
-    grad_expand = reduce_last(*expand_sums)
+    grad_ffn = reduce_last(*ffn_sums)
 
     def vector_sums(one, two, wide):
         sums = jnp.concatenate([one[0:3], two]).reshape(7, fs * cs, rows)
@@ -730,24 +857,17 @@
 
     vec = line.plain(vector_sums, sums_one, sums_two, wide).reshape(fs, cs, 2, 2, -1)
     moved = over_tp(pick(vec, 1 - t_rank % 2, 3), 1)
-    def layer_end(roles, after, a, w, t, v):
-        ends = jnp.stack([v[6], jnp.full((width,), live)])
-        return down(roles, after, "layer_out", a, w, hidden, 1, out_finish, [t, ends], [(act, BF16)])
-
-    (layer_out,) = line(layer_end, activated, ffn, second, vectors)
-    layer_out = line.plain(lambda a, p: mxu(a, p, 1, 1).astype(BF16), layer_out, permute)
     vec = line.plain(lambda v, m: pick(v, t_rank % 2, 3) + m, vec, moved)
     moved = over_tp(pick(vec, 1 - t_rank // 2, 2), 2)
+    out = line.gate(out)
     att_sums = reduce_two(*att_sums)
     vec = line.plain(lambda v, m: pick(v, t_rank // 2, 2) + m, vec, moved)
     moved = [over_fsdp(pick(vec, (f_rank - h) % fs), -h) for h in range(1, fs)]
-    att_sums = reduce_three(*att_sums)
+    att_sums = reduce_three(att_sums)
     vec = line.plain(lambda v, m: sum(m, pick(v, f_rank)), vec, moved)
     moved = [over_ctx(pick(vec, ctx_behind(d)), -d) for d in range(1, cs)]
     att_sums = reduce_step(*att_sums)
     vec = line.plain(lambda v, m: sum(m, pick(v, c_rank)), vec, moved)
-    out = line.gate(out)
-    layer_out = to_group(line.gate(layer_out).reshape(group * fine, width))
     grad_att = reduce_last(*att_sums)
 
     def unpack(out, layer_out):
@@ -772,9 +892,9 @@
         vec_out[3],
         vec_out[4],
         vec_out[5],
-        grad_expand,
+        grad_ffn[:, hidden:],
         vec_out[7],
-        grad_shrink,
+        grad_ffn[:, :hidden],
         vec_out[6],
     )
 

time: 611 us -> 590 us (0.966)
  Pallas kernels: 220 us -> 196 us
    pallas_call x23 -> x17, Pallas kernels: 220 us -> 196 us  [apply(): pl.pallas_call(run, grid_spec=pltpu.PrefetchScalarGridSpec(num_scalar_pre...]
    ppermute x18 -> x15, starting transfers between devices: 29.3 us -> 15.6 us  [over_ctx(): lax.ppermute(array, 'ctx', [(ring[i], ring[(i + d) % cs]) for i in range(...]
    all_to_all x4, starting transfers between devices: 23.8 us -> 34.7 us  [to_group(): return lax.all_to_all(array, ('ctx', 'tp'), 0, 0, tiled=True)]
    ppermute x14, waiting for transfers between devices: 3.21 us -> 12.3 us  [over_tp(): return lax.ppermute(array, 'tp', [(i, i ^ flip) for i in range(ts)])]
    ppermute x10, waiting for transfers between devices: 67.9 us -> 59.4 us  [over(): return lax.ppermute(array, ALL, [(i, target(i)) for i in range(devices)])]
    ppermute x18 -> x15, waiting for transfers between devices: 77.4 us -> 69.1 us  [over_ctx(): lax.ppermute(array, 'ctx', [(ring[i], ring[(i + d) % cs]) for i in range(...]
    all_to_all x4, waiting for transfers between devices: 20.6 us -> 28.3 us  [to_group(): return lax.all_to_all(array, ('ctx', 'tp'), 0, 0, tiled=True)]
    ppermute x14, starting transfers between devices: 4.93 us -> 11.7 us  [over_tp(): return lax.ppermute(array, 'tp', [(i, i ^ flip) for i in range(ts)])]
  transfers between devices with their start and end apart: 48 -> 45, of which waited for: 19 -> 22; matrix products, arithmetic and copies ran while one was open for 11% -> 12% of each run, Pallas kernels for 30% -> 28%
where the time goes in v4:
time: 590 us; the launch traced here: 585 us
  waiting for transfers between devices  199 us (34%)
  Pallas kernels  196 us (33%)
  starting transfers between devices  79.5 us (13%)
  local copies, waits for them, and re-layouts  48.7 us (8%)
  other arithmetic  41.6 us (7%)
  between operations  16.1 us (3%)
    pallas_call x17, Pallas kernels, apply(): pl.pallas_call(run, grid_spec=pltpu.PrefetchScalarGridSpec(num_scalar_pre...  196 us
    ppermute x15, waiting for transfers between devices, over_ctx(): lax.ppermute(array, 'ctx', [(ring[i], ring[(i + d) % cs]) for i in range(...  69.1 us
    ppermute x10, waiting for transfers between devices, over(): return lax.ppermute(array, ALL, [(i, target(i)) for i in range(devices)])  59.4 us
    all_to_all x4, starting transfers between devices, to_group(): return lax.all_to_all(array, ('ctx', 'tp'), 0, 0, tiled=True)  34.7 us
    all_to_all x4, waiting for transfers between devices, to_group(): return lax.all_to_all(array, ('ctx', 'tp'), 0, 0, tiled=True)  28.3 us
    all_to_all x1, waiting for transfers between devices, on_device(): packed = lax.all_to_all(packed, ALL, 0, 0, tiled=True)  26.5 us
    convert_element_type x12, other arithmetic, add(): return sum((t.astype(F32) for t in terms)).astype(BF16)  19.1 us
    unnamed x115, local copies, waits for them, and re-layouts  17.8 us
  transfers between devices with their start and end apart: 45, of which 22 were waited for; matrix products, arithmetic and copies ran while one was open for 12% of the time, Pallas kernels for 28%

profile of v4, /device:TPU:0, one launch (start us, length us, event | category | flops | bytes accessed | tf_op | source)
XLA Modules:
  0.0 584.5 jit_solution(6140491686529653676)
XLA Ops:
  3.8 4.1 collective-permute-start
  11.5 4.5 all-to-all-start
  19.6 26.5 %all-to-all-done = f32[32,1,352]{2,1,0:T(1,128)S(1)} async-done(((f32[32,1,352]{2,1,0:T(1,128)}), f32[32,1,352]{2,1,0:T(1,128)S(1)}, u32[]{:S(2)}, u32[]{:S(2)}) %all-to-all-start) | async-done | bytes 45088 | tf_op jit(solution)/shard_map/all_to_all | solution.py:704
  48.6 1.6 collective-permute-start.3
  50.2 4.3 all-to-all-start.1
  54.5 10.9 %collective-permute-done.3 = bf16[128,2048]{1,0:T(8,128)(2,1)} collective-permute-done((bf16[128,2048]{1,0:T(8,128)(2,1)S(1)}, bf16[128,2048]{1,0:T(8,128)(2,1)}, u32[]{:S(2)}, u32[]{:S(2)}) %collective-permute-start.3) | collective-permute-done | bytes 524320 | tf_op jit(solution)/shard_map/ppermute | solution.py:594
  65.4 3.0 collective-permute-done.5
  68.5 2.2 pad_maximum_fusion.1.refs_8_.refs_2_.refs_7_.refs_9_.refs_1_
  71.5 5.2 collective-permute-start.7
  82.5 9.5 %collective-permute-done.4 = bf16[128,2048]{1,0:T(8,128)(2,1)} collective-permute-done((bf16[128,2048]{1,0:T(8,128)(2,1)}, bf16[128,2048]{1,0:T(8,128)(2,1)}, u32[]{:S(2)}, u32[]{:S(2)}) %collective-permute-start.4) | collective-permute-done | bytes 524320 | tf_op jit(solution)/shard_map/ppermute | solution.py:594
  95.1 2.2 fusion.refs_1_
  97.3 16.3 %all-to-all-start.2 = ((bf16[16,128,512]{2,1,0:T(8,128)(2,1)}), bf16[16,128,512]{2,1,0:T(8,128)(2,1)}, u32[]{:S(2)}, u32[]{:S(2)}) async-start(bf16[16,128,512]{2,1,0:T(8,128)(2,1)} %bitcast.119), calls=%async_computation.2 | async-start | bytes 4194304 | tf_op jit(solution)/shard_map/all_to_all | solution.py:586
  119.3 5.8 arrived.1
  127.3 27.5 %all-to-all-done.2 = bf16[16,128,512]{2,1,0:T(8,128)(2,1)} async-done(((bf16[16,128,512]{2,1,0:T(8,128)(2,1)}), bf16[16,128,512]{2,1,0:T(8,128)(2,1)}, u32[]{:S(2)}, u32[]{:S(2)}) %all-to-all-start.2) | async-done | bytes 2097184 | tf_op jit(solution)/shard_map/all_to_all | solution.py:586
  154.8 1.7 constant_dynamic-slice_fusion.26
  160.3 14.6 %joined.1 = (f32[512,1024]{1,0:T(8,128)}, bf16[512,1024]{1,0:T(8,128)(2,1)}, bf16[1024,512]{1,0:T(8,128)(2,1)}, bf16[2,512,768]{2,1,0:T(8,128)(2,1)}, bf16[2,512,768]{2,1,0:T(8,128)(2,1)}, /*index=5*/f32[8,128]{1,0:T(8,128)}) custom-call(s32[2]{0:T(128)} %pad_add_fusion.roles_ref, bf16[2,512,512]{2,1,0:T(8,128)(2,1)} %pad_maximum_fusion.7.refs_0_.refs_15_.refs_1_.refs_3_, ...), custom_call_target="tpu_custom_call" | custom-call | flops 1 | bytes 1 | tf_op jit(solution)/shard_map/joined/pallas_call | solution.py:36
  175.7 2.6 pad_maximum_fusion.refs_3_.refs_2_
  178.3 3.4 collective-permute-start.13
  182.9 13.4 %attend_forward.2 = (bf16[2,4,1024,512]{3,2,1,0:T(8,128)(2,1)}, bf16[2,512,256]{2,1,0:T(8,128)(2,1)}, f32[8,128]{1,0:T(8,128)}) custom-call(s32[2]{0:T(128)} %pad_add_fusion.roles_ref, bf16[2,512,768]{2,1,0:T(8,128)(2,1)} %get-tuple-element.692.refs_0_, bf16[2,512,768]{2,1,0:T(8,128)(2,1)} %copy-done.13, f32[8,128]{1,0:T(8,128)} %get-tuple-element.570.refs_2_, ...), custom_call_target="tpu_custom_call" | custom-call | flops 1 | bytes 1 | tf_op jit(solution)/shard_map/attend_forward/pallas_call | solution.py:36
  196.8 8.5 %collective-permute-done.12.refs_1_ = bf16[2,512,768]{2,1,0:T(8,128)(2,1)S(1)} collective-permute-done((bf16[2,512,768]{2,1,0:T(8,128)(2,1)S(1)}, bf16[2,512,768]{2,1,0:T(8,128)(2,1)S(1)}, u32[]{:S(2)}, u32[]{:S(2)}) %collective-permute-start.12) | collective-permute-done | bytes 1572896 | tf_op jit(solution)/shard_map/ppermute | solution.py:589
  206.6 13.4 %attend_forward.3 = (bf16[2,4,1024,512]{3,2,1,0:T(8,128)(2,1)}, bf16[2,512,256]{2,1,0:T(8,128)(2,1)}, f32[8,128]{1,0:T(8,128)}) custom-call(s32[2]{0:T(128)} %pad_add_fusion.roles_ref, bf16[2,512,768]{2,1,0:T(8,128)(2,1)} %get-tuple-element.665.refs_0_, bf16[2,512,768]{2,1,0:T(8,128)(2,1)} %copy-done.11, f32[8,128]{1,0:T(8,128)} %get-tuple-element.579.refs_2_), custom_call_target="tpu_custom_call" | custom-call | flops 1 | bytes 1 | tf_op jit(solution)/shard_map/attend_forward/pallas_call | solution.py:36
  220.0 8.3 %collective-permute-done.13.refs_3_ = bf16[2,512,2048]{2,1,0:T(8,128)(2,1)} collective-permute-done((bf16[2,512,2048]{2,1,0:T(8,128)(2,1)S(1)}, bf16[2,512,2048]{2,1,0:T(8,128)(2,1)}, u32[]{:S(2)}, u32[]{:S(2)}) %collective-permute-start.13) | collective-permute-done | bytes 4194336 | tf_op jit(solution)/shard_map/ppermute | solution.py:613
  229.0 7.8 %second.1 = (f32[512,1024]{1,0:T(8,128)}, bf16[512,1024]{1,0:T(8,128)(2,1)}, bf16[1024,512]{1,0:T(8,128)(2,1)}, f32[8,128]{1,0:T(8,128)}) custom-call(s32[2]{0:T(128)} %pad_add_fusion.roles_ref, bf16[2,512,256]{2,1,0:T(8,128)(2,1)} %get-tuple-element.792.refs_0_.refs_3_.refs_5_.refs_7_, bf16[2,512,256]{2,1,0:T(8,128)(2,1)} %get-tuple-element.721.refs_1_.refs_3_, ...), custom_call_target="tpu_custom_call" | custom-call | flops 1 | bytes 1 | tf_op jit(solution)/shard_map/second/pallas_call | solution.py:36
  236.8 1.9 copy-done.3
  238.7 11.3 %hidden.2 = (bf16[2,512,1024]{2,1,0:T(8,128)(2,1)}, bf16[2,512,1024]{2,1,0:T(8,128)(2,1)}, bf16[2,2,512,1024]{3,2,1,0:T(8,128)(2,1)}, f32[8,128]{1,0:T(8,128)}) custom-call(s32[2]{0:T(128)} %pad_add_fusion.roles_ref, bf16[512,1024]{1,0:T(8,128)(2,1)} %get-tuple-element.617.refs_0_, bf16[1024,512]{1,0:T(8,128)(2,1)} %get-tuple-element.618.refs_1_, ...), custom_call_target="tpu_custom_call" | custom-call | flops 1 | bytes 1 | tf_op jit(solution)/shard_map/hidden/pallas_call | solution.py:36
  250.5 10.3 %hidden_back.2 = (bf16[2,512,1024]{2,1,0:T(8,128)(2,1)}, f32[2,1,1024]{2,1,0:T(1,128)}, bf16[2,2,512,1024]{3,2,1,0:T(8,128)(2,1)}, f32[8,128]{1,0:T(8,128)}) custom-call(s32[2]{0:T(128)} %pad_add_fusion.roles_ref, bf16[512,1024]{1,0:T(8,128)(2,1)} %get-tuple-element.645.refs_0_.refs_7_, bf16[1024,512]{1,0:T(8,128)(2,1)} %get-tuple-element.628.refs_1_, ...), custom_call_target="tpu_custom_call" | custom-call | flops 1 | bytes 1 | tf_op jit(solution)/shard_map/hidden_back/pallas_call | solution.py:36
  260.8 2.1 copy-done.15
  262.9 11.6 %hidden.3 = (bf16[2,512,1024]{2,1,0:T(8,128)(2,1)}, bf16[2,512,1024]{2,1,0:T(8,128)(2,1)}, bf16[2,512,1024]{2,1,0:T(8,128)(2,1)}, bf16[2,512,1024]{2,1,0:T(8,128)(2,1)}, f32[8,128]{1,0:T(8,128)}) custom-call(s32[2]{0:T(128)} %pad_add_fusion.roles_ref, bf16[512,1024]{1,0:T(8,128)(2,1)} %get-tuple-element.617.refs_0_, ...), custom_call_target="tpu_custom_call" | custom-call | flops 1 | bytes 1 | tf_op jit(solution)/shard_map/hidden/pallas_call | solution.py:36
  274.5 2.1 collective-permute-start.19
  276.5 10.8 %hidden_back.3 = (bf16[2,512,1024]{2,1,0:T(8,128)(2,1)}, f32[2,1,1024]{2,1,0:T(1,128)}, bf16[2,512,1024]{2,1,0:T(8,128)(2,1)}, bf16[2,512,1024]{2,1,0:T(8,128)(2,1)}, f32[8,128]{1,0:T(8,128)}) custom-call(s32[2]{0:T(128)} %pad_add_fusion.roles_ref, bf16[512,1024]{1,0:T(8,128)(2,1)} %get-tuple-element.645.refs_0_.refs_7_, ...), custom_call_target="tpu_custom_call" | custom-call | flops 1 | bytes 1 | tf_op jit(solution)/shard_map/hidden_back/pallas_call | solution.py:36
  288.0 17.8 %second_back.1 = (f32[512,1024]{1,0:T(8,128)}, bf16[512,1024]{1,0:T(8,128)(2,1)}, bf16[1024,512]{1,0:T(8,128)(2,1)}, f32[4,1024]{1,0:T(4,128)}, bf16[2,512,256]{...) custom-call(s32[2]{0:T(128)} %pad_add_fusion.roles_ref, ...), custom_call_target="tpu_custom_call" | custom-call | flops 1 | bytes 1 | tf_op jit(solution)/shard_map/second_back/pallas_call | solution.py:36
  305.8 2.0 fusion.4
  308.8 13.7 %attend_backward.2 = (bf16[2,512,768]{2,1,0:T(8,128)(2,1)}, bf16[2,512,512]{2,1,0:T(8,128)(2,1)}, f32[8,128]{1,0:T(8,128)}) custom-call(s32[2]{0:T(128)} %pad_add_fusion.roles_ref, bf16[2,512,768]{2,1,0:T(8,128)(2,1)} %get-tuple-element.665.refs_0_, bf16[2,512,768]{2,1,0:T(8,128)(2,1)} %copy-done.11, bf16[2,4,1024,512]{3,2,1,0:T(8,128)(2,1)} %get-tuple-element.667.refs_2_, ...), custom_call_target="tpu_custom_call" | custom-call | flops 1 | bytes 1 | tf_op jit(solution)/shard_map/attend_backward/pallas_call | solution.py:36
  323.1 11.4 %layer_out.1 = (bf16[512,1024]{1,0:T(8,128)(2,1)}, f32[8,128]{1,0:T(8,128)}) custom-call(s32[2]{0:T(128)} %pad_add_fusion.roles_ref, bf16[2,512,1024]{2,1,0:T(8,128)(2,1)} %get-tuple-element.674.refs_0_, bf16[2,512,1024]{2,1,0:T(8,128)(2,1)} %get-tuple-element.675.refs_1_, bf16[2,512,2048]{2,1,0:T(8,128)(2,1)} %copy-done.1, ...), custom_call_target="tpu_custom_call" | custom-call | flops 1 | bytes 1 | tf_op jit(solution)/shard_map/layer_out/pallas_call | solution.py:36
  334.5 3.6 convolution_convert_fusion.refs_6_
  338.1 2.0 fusion.6
  341.2 13.8 %attend_backward.3 = (bf16[2,512,768]{2,1,0:T(8,128)(2,1)}, bf16[2,512,512]{2,1,0:T(8,128)(2,1)}, f32[8,128]{1,0:T(8,128)}) custom-call(s32[2]{0:T(128)} %pad_add_fusion.roles_ref, bf16[2,512,768]{2,1,0:T(8,128)(2,1)} %get-tuple-element.692.refs_0_, bf16[2,512,768]{2,1,0:T(8,128)(2,1)} %copy-done.13, bf16[2,4,1024,512]{3,2,1,0:T(8,128)(2,1)} %get-tuple-element.694.refs_2_, ...), custom_call_target="tpu_custom_call" | custom-call | flops 1 | bytes 1 | tf_op jit(solution)/shard_map/attend_backward/pallas_call | solution.py:36
  360.3 8.6 %weight_grad.2 = (bf16[2,2,512,1024]{3,2,1,0:T(8,128)(2,1)}, f32[8,128]{1,0:T(8,128)}) custom-call(s32[2]{0:T(128)} %pad_add_fusion.roles_ref, bf16[1024,512]{1,0:T(8,128)(2,1)} %get-tuple-element.791.refs_0_.refs_2_.refs_4_.refs_6_, bf16[2,512,256]{2,1,0:T(8,128)(2,1)} %get-tuple-element.721.refs_1_.refs_3_, ...), custom_call_target="tpu_custom_call" | custom-call | flops 1 | bytes 1 | tf_op jit(solution)/shard_map/weight_grad/pallas_call | solution.py:36
  369.0 9.6 %all-to-all-start.3 = ((bf16[16,32,1024]{2,1,0:T(8,128)(2,1)}), bf16[16,32,1024]{2,1,0:T(8,128)(2,1)S(1)}, u32[]{:S(2)}, u32[]{:S(2)}) async-start(bf16[16,32,1024]{2,1,0:T(8,128)(2,1)} %bitcast.48), calls=%async_computation.3 | async-start | bytes 2097152 | tf_op jit(solution)/shard_map/all_to_all | solution.py:586
  379.0 1.7 collective-permute-start.24
  382.6 1.5 add_convert_fusion.3
  386.0 14.7 %first_back.1 = (bf16[512,1024]{1,0:T(8,128)(2,1)}, bf16[1024,512]{1,0:T(8,128)(2,1)}, f32[4,1024]{1,0:T(4,128)}, bf16[2,2,512,512]{3,2,1,0:T(8,128)(2,1)}, f32[8,128]{1,0:T(8,128)}) custom-call(s32[2]{0:T(128)} %pad_add_fusion.roles_ref, bf16[2,512,768]{2,1,0:T(8,128)(2,1)} %pad_maximum_fusion.6.refs_0_.refs_11_.refs_9_, ...), custom_call_target="tpu_custom_call" | custom-call | flops 1 | bytes 1 | tf_op jit(solution)/shard_map/first_back/pallas_call | solution.py:36
  401.9 14.5 %collective-permute-done.24 = bf16[128,2048]{1,0:T(8,128)(2,1)S(1)} collective-permute-done((bf16[128,2048]{1,0:T(8,128)(2,1)S(1)}, bf16[128,2048]{1,0:T(8,128)(2,1)S(1)}, u32[]{:S(2)}, u32[]{:S(2)}) %collective-permute-start.24) | collective-permute-done | bytes 524320 | tf_op jit(solution)/shard_map/ppermute | solution.py:594
  417.3 6.3 %inputs_back.1 = (bf16[2,512,512]{2,1,0:T(8,128)(2,1)}, bf16[2,512,512]{2,1,0:T(8,128)(2,1)}, f32[8,128]{1,0:T(8,128)}) custom-call(s32[2]{0:T(128)} %pad_add_fusion.roles_ref, bf16[512,1024]{1,0:T(8,128)(2,1)} %get-tuple-element.755.refs_0_, bf16[2,512,1536]{2,1,0:T(8,128)(2,1)} %copy-done, ...), custom_call_target="tpu_custom_call" | custom-call | flops 1 | bytes 1 | tf_op jit(solution)/shard_map/inputs_back/pallas_call | solution.py:36
  427.5 3.4 collective-permute-done.25
  431.9 11.1 %weight_grad.3 = (bf16[2,512,1536]{2,1,0:T(8,128)(2,1)}, bf16[2,512,1536]{2,1,0:T(8,128)(2,1)}, f32[8,128]{1,0:T(8,128)}) custom-call(s32[2]{0:T(128)} %pad_add_fusion.roles_ref, bf16[1024,512]{1,0:T(8,128)(2,1)} %get-tuple-element.789.refs_0_.refs_2_, bf16[2,512,512]{2,1,0:T(8,128)(2,1)} %pad_maximum_fusion.7.refs_0_.refs_15_.refs_1_.refs_3_, ...), custom_call_target="tpu_custom_call" | custom-call | flops 1 | bytes 1 | tf_op jit(solution)/shard_map/weight_grad/pallas_call | solution.py:36
  442.9 1.5 collective-permute-start.30
  449.1 4.4 all-to-all-start.4
  453.6 17.6 %collective-permute-done.26 = bf16[128,2048]{1,0:T(8,128)(2,1)} collective-permute-done((bf16[128,2048]{1,0:T(8,128)(2,1)S(1)}, bf16[128,2048]{1,0:T(8,128)(2,1)}, u32[]{:S(2)}, u32[]{:S(2)}) %collective-permute-start.26) | collective-permute-done | bytes 524320 | tf_op jit(solution)/shard_map/ppermute | solution.py:594
  471.2 2.1 convert_add_fusion
  474.4 34.0 %collective-permute-done.30 = bf16[2,512,1536]{2,1,0:T(8,128)(2,1)} collective-permute-done((bf16[2,512,1536]{2,1,0:T(8,128)(2,1)}, bf16[2,512,1536]{2,1,0:T(8,128)(2,1)}, u32[]{:S(2)}, u32[]{:S(2)}) %collective-permute-start.30) | collective-permute-done | bytes 3145760 | tf_op jit(solution)/shard_map/ppermute | solution.py:613
  508.4 5.4 fusion.2
  516.4 2.5 collective-permute-start.32
  518.9 1.7 collective-permute-done.32
  520.6 14.0 %collective-permute-done.31 = bf16[512,1536]{1,0:T(8,128)(2,1)} collective-permute-done((bf16[512,1536]{1,0:T(8,128)(2,1)}, bf16[512,1536]{1,0:T(8,128)(2,1)}, u32[]{:S(2)}, u32[]{:S(2)}) %collective-permute-start.31) | collective-permute-done | bytes 1572896 | tf_op jit(solution)/shard_map/ppermute | solution.py:613
  534.6 2.3 add_convert_fusion
  539.5 2.9 collective-permute-done.34
  543.7 3.2 collective-permute-done.33
  547.0 2.0 add_convert_fusion.14
  555.6 3.0 collective-permute-start.36
  561.5 2.5 collective-permute-done.37
  564.7 2.0 add_convert_fusion.13
  569.5 6.2 %collective-permute-done.39 = bf16[128,1536]{1,0:T(8,128)(2,1)} collective-permute-done((bf16[128,1536]{1,0:T(8,128)(2,1)}, bf16[128,1536]{1,0:T(8,128)(2,1)}, u32[]{:S(2)}, u32[]{:S(2)}) %collective-permute-start.39) | collective-permute-done | bytes 393248 | tf_op jit(solution)/shard_map/ppermute | solution.py:594
  578.9 2.5 fusion.34
  (270 shorter events, 75.5 us)
Async XLA Ops:
  0.6 16.0 %copy-start.31 = (bf16[4,2,256,256]{3,2,1,0:T(8,128)(2,1)S(1)}, bf16[4,2,256,256]{3,2,1,0:T(8,128)(2,1)}, u32[]{:S(2)}) copy-start(bf16[4,2,256,256]{3,2,1,0:T(8,128)(2,1)} %param.30) | copy-start | bytes 3145732
  3.8 42.9 %copy-start.21 = (bf16[128,1536]{1,0:T(8,128)(2,1)}, bf16[128,1536]{1,0:T(8,128)(2,1)S(1)}, u32[]{:S(2)}) copy-start(bf16[128,1536]{1,0:T(8,128)(2,1)S(1)} %pad_maximum_fusion.10.refs_3_) | copy-start | bytes 1179652
  3.8 42.9 %collective-permute-start = (bf16[128,1536]{1,0:T(8,128)(2,1)S(1)}, bf16[128,1536]{1,0:T(8,128)(2,1)S(1)}, u32[]{:S(2)}, u32[]{:S(2)}) collective-permute-start(bf16[128,1536]{1,0:T(8,128)(2,1)S(1)} %pad_maximum_fusion.10.refs_3_), channel_id=1, source_target_pairs={{0,8},{8,12},{12,4},{4,0},{1,9},{9,13},{13,5},{5,1},{2,10},{10,14}... | collective-permute-start | bytes 1179656 | tf_op jit(solution)/shard_map/ppermute | solution.py:594
  7.9 38.8 %collective-permute-start.1 = (bf16[128,1536]{1,0:T(8,128)(2,1)S(1)}, bf16[128,1536]{1,0:T(8,128)(2,1)S(1)}, u32[]{:S(2)}, u32[]{:S(2)}) collective-permute-start(bf16[128,1536]{1,0:T(8,128)(2,1)S(1)} %pad_maximum_fusion.10.refs_3_), channel_id=1, source_target_pairs={{0,12},{8,4},{12,0},{4,8},{1,13},{9,5},{13,1},{5,9},{2,14},{10,6},... | collective-permute-start | bytes 1179656 | tf_op jit(solution)/shard_map/ppermute | solution.py:594
  9.2 37.5 %collective-permute-start.2 = (bf16[128,1536]{1,0:T(8,128)(2,1)S(1)}, bf16[128,1536]{1,0:T(8,128)(2,1)}, u32[]{:S(2)}, u32[]{:S(2)}) collective-permute-start(bf16[128,1536]{1,0:T(8,128)(2,1)S(1)} %pad_maximum_fusion.10.refs_3_), channel_id=1, source_target_pairs={{0,4},{8,0},{12,8},{4,12},{1,5},{9,1},{13,9},{5,13},{2,6},{10,2},{... | collective-permute-start | bytes 1179656 | tf_op jit(solution)/shard_map/ppermute | solution.py:594
  11.5 34.6 %all-to-all-start = ((f32[32,1,352]{2,1,0:T(1,128)}), f32[32,1,352]{2,1,0:T(1,128)S(1)}, u32[]{:S(2)}, u32[]{:S(2)}) async-start(f32[32,1,352]{2,1,0:T(1,128)} %broadcast_in_dim.8), calls=%async_computation | async-start | bytes 98304 | tf_op jit(solution)/shard_map/all_to_all | solution.py:704
  19.6 30.6 %copy-start.22 = (bf16[128,2048]{1,0:T(8,128)(2,1)}, bf16[128,2048]{1,0:T(8,128)(2,1)S(1)}, u32[]{:S(2)}) copy-start(bf16[128,2048]{1,0:T(8,128)(2,1)S(1)} %constant_dynamic-update-slice_fusion.refs_6_) | copy-start | bytes 1572868
  47.9 20.6 %copy-start.10 = (bf16[512,1536]{1,0:T(8,128)(2,1)}, bf16[512,1536]{1,0:T(8,128)(2,1)S(1)}, u32[]{:S(2)}) copy-start(bf16[512,1536]{1,0:T(8,128)(2,1)S(1)} %constant_dynamic-update-slice_fusion.2.refs_7_) | copy-start | bytes 4718596
  47.9 20.6 %collective-permute-start.5 = (bf16[512,1536]{1,0:T(8,128)(2,1)S(1)}, bf16[512,1536]{1,0:T(8,128)(2,1)}, u32[]{:S(2)}, u32[]{:S(2)}) collective-permute-start(bf16[512,1536]{1,0:T(8,128)(2,1)S(1)} %constant_dynamic-update-slice_fusion.2.refs_7_), channel_id=1, source_target_pairs={{0,16},{1,3},{2,18},{3,1},{4,20},{5,7},{6,22},{7,5},{8,24},{9,11},... | collective-permute-start | bytes 4718600 | tf_op jit(solution)/shard_map/ppermute | solution.py:613
  48.6 16.8 %collective-permute-start.3 = (bf16[128,2048]{1,0:T(8,128)(2,1)S(1)}, bf16[128,2048]{1,0:T(8,128)(2,1)}, u32[]{:S(2)}, u32[]{:S(2)}) collective-permute-start(bf16[128,2048]{1,0:T(8,128)(2,1)S(1)} %constant_dynamic-update-slice_fusion.refs_6_), channel_id=1, source_target_pairs={{0,8},{8,12},{12,4},{4,0},{1,9},{9,13},{13,5},{5,1},{2,10},{10,14}... | collective-permute-start | bytes 1572872 | tf_op jit(solution)/shard_map/ppermute | solution.py:594
  50.2 47.1 %all-to-all-start.1 = ((bf16[16,32,1024]{2,1,0:T(8,128)(2,1)}), bf16[16,32,1024]{2,1,0:T(8,128)(2,1)}, u32[]{:S(2)}, u32[]{:S(2)}) async-start(bf16[16,32,1024]{2,1,0:T(8,128)(2,1)} %bitcast.7), calls=%async_computation.1 | async-start | bytes 2097152 | tf_op jit(solution)/shard_map/all_to_all | solution.py:586
  68.5 25.1 %copy-start.41 = (s32[4,2]{0,1:T(2,128)S(1)}, s32[4,2]{0,1:T(2,128)}, u32[]{:S(2)}) copy-start(s32[4,2]{0,1:T(2,128)} %param.44) | copy-start | bytes 100
  70.7 26.6 %copy-start = (bf16[2,512,1536]{2,1,0:T(8,128)(2,1)}, bf16[2,512,1536]{2,1,0:T(8,128)(2,1)S(1)}, u32[]{:S(2)}) copy-start(bf16[2,512,1536]{2,1,0:T(8,128)(2,1)S(1)} %pad_maximum_fusion.1.refs_8_.refs_2_.refs_7_.refs_9_.refs_1_) | copy-start | bytes 9437188
  70.7 55.4 %collective-permute-start.6 = (bf16[2,512,1536]{2,1,0:T(8,128)(2,1)S(1)}, bf16[2,512,1536]{2,1,0:T(8,128)(2,1)}, u32[]{:S(2)}, u32[]{:S(2)}) collective-permute-start(bf16[2,512,1536]{2,1,0:T(8,128)(2,1)S(1)} %pad_maximum_fusion.1.refs_8_.refs_2_.refs_7_.refs_9_.refs_1_), channel_id=1, source_target_pairs={{0,2},{1,17},{2,0},{3,19},{4,6},{5,21},{6,4},{7,23},{8,10},{9,25},... | collective-permute-start | bytes 9437192 | tf_op jit(solution)/shard_map/ppermute | solution.py:613
  71.5 54.6 %collective-permute-start.7 = (bf16[2,512,1536]{2,1,0:T(8,128)(2,1)S(1)}, bf16[2,512,1536]{2,1,0:T(8,128)(2,1)}, u32[]{:S(2)}, u32[]{:S(2)}) collective-permute-start(bf16[2,512,1536]{2,1,0:T(8,128)(2,1)S(1)} %pad_maximum_fusion.1.refs_8_.refs_2_.refs_7_.refs_9_.refs_1_), channel_id=1, source_target_pairs={{0,1},{1,0},{2,3},{3,2},{4,5},{5,4},{6,7},{7,6},{8,9},{9,8},{10,11... | collective-permute-start | bytes 9437192 | tf_op jit(solution)/shard_map/ppermute | solution.py:589
  76.7 15.3 %collective-permute-start.4 = (bf16[128,2048]{1,0:T(8,128)(2,1)}, bf16[128,2048]{1,0:T(8,128)(2,1)}, u32[]{:S(2)}, u32[]{:S(2)}) collective-permute-start(bf16[128,2048]{1,0:T(8,128)(2,1)} %collective-permute-done.3), channel_id=1, source_target_pairs={{0,8},{8,12},{12,4},{4,0},{1,9},{9,13},{13,5},{5,1},{2,10},{10,14}... | collective-permute-start | bytes 1572872 | tf_op jit(solution)/shard_map/ppermute | solution.py:594
  92.0 21.5 %collective-permute-start.8 = (bf16[128,2048]{1,0:T(8,128)(2,1)}, bf16[128,2048]{1,0:T(8,128)(2,1)}, u32[]{:S(2)}, u32[]{:S(2)}) collective-permute-start(bf16[128,2048]{1,0:T(8,128)(2,1)} %collective-permute-done.4), channel_id=1, source_target_pairs={{0,8},{8,12},{12,4},{4,0},{1,9},{9,13},{13,5},{5,1},{2,10},{10,14}... | collective-permute-start | bytes 1572872 | tf_op jit(solution)/shard_map/ppermute | solution.py:594
  97.3 57.6 %all-to-all-start.2 = ((bf16[16,128,512]{2,1,0:T(8,128)(2,1)}), bf16[16,128,512]{2,1,0:T(8,128)(2,1)}, u32[]{:S(2)}, u32[]{:S(2)}) async-start(bf16[16,128,512]{2,1,0:T(8,128)(2,1)} %bitcast.119), calls=%async_computation.2 | async-start | bytes 4194304 | tf_op jit(solution)/shard_map/all_to_all | solution.py:586
  125.5 33.2 %copy-start.32 = (f32[1,7,8,128]{3,1,2,0:T(8,128)}, f32[1,7,8,128]{3,1,2,0:T(8,128)S(1)}, u32[]{:S(2)}) copy-start(f32[1,7,8,128]{3,1,2,0:T(8,128)S(1)} %copy.94) | copy-start | bytes 86020
  126.1 32.5 %collective-permute-start.9 = (bf16[2,512,1536]{2,1,0:T(8,128)(2,1)}, bf16[2,512,1536]{2,1,0:T(8,128)(2,1)S(1)}, u32[]{:S(2)}, u32[]{:S(2)}) collective-permute-start(bf16[2,512,1536]{2,1,0:T(8,128)(2,1)} %collective-permute-done.6.refs_3_.refs_8_.refs_10_.refs_2_), channel_id=1, source_target_pairs={{0,1},{1,0},{2,3},{3,2},{4,5},{5,4},{6,7},{7,6},{8,9},{9,8},{10,11... | collective-permute-start | bytes 9437192 | tf_op jit(solution)/shard_map/ppermute | solution.py:589
  126.7 49.0 %collective-permute-start.11 = (bf16[512,2048]{1,0:T(8,128)(2,1)}, bf16[512,2048]{1,0:T(8,128)(2,1)}, u32[]{:S(2)}, u32[]{:S(2)}) collective-permute-start(bf16[512,2048]{1,0:T(8,128)(2,1)} %copy-done.5), channel_id=1, source_target_pairs={{0,16},{1,3},{2,18},{3,1},{4,20},{5,7},{6,22},{7,5},{8,24},{9,11},... | collective-permute-start | bytes 6291464 | tf_op jit(solution)/shard_map/ppermute | solution.py:613
  175.0 6.8 %collective-permute-start.10 = (bf16[2,512,768]{2,1,0:T(8,128)(2,1)}, bf16[2,512,768]{2,1,0:T(8,128)(2,1)S(1)}, u32[]{:S(2)}, u32[]{:S(2)}) collective-permute-start(bf16[2,512,768]{2,1,0:T(8,128)(2,1)} %get-tuple-element.665.refs_0_), channel_id=1, source_target_pairs={{0,1},{1,0},{2,3},{3,2},{4,5},{5,4},{6,7},{7,6},{8,9},{9,8},{10,11... | collective-permute-start | bytes 4718600 | tf_op jit(solution)/shard_map/ppermute | solution.py:589
  178.3 50.0 %collective-permute-start.13 = (bf16[2,512,2048]{2,1,0:T(8,128)(2,1)S(1)}, bf16[2,512,2048]{2,1,0:T(8,128)(2,1)}, u32[]{:S(2)}, u32[]{:S(2)}) collective-permute-start(bf16[2,512,2048]{2,1,0:T(8,128)(2,1)S(1)} %pad_maximum_fusion.refs_3_.refs_2_), channel_id=1, source_target_pairs={{0,2},{1,17},{2,0},{3,19},{4,6},{5,21},{6,4},{7,23},{8,10},{9,25},... | collective-permute-start | bytes 12582920 | tf_op jit(solution)/shard_map/ppermute | solution.py:613
  182.9 13.4 %copy-start.12 = (bf16[2,512,768]{2,1,0:T(8,128)(2,1)S(1)}, bf16[2,512,768]{2,1,0:T(8,128)(2,1)}, u32[]{:S(2)}) copy-start(bf16[2,512,768]{2,1,0:T(8,128)(2,1)} %get-tuple-element.692.refs_0_) | copy-start | bytes 4718596
  196.3 32.0 %copy-start.33 = (f32[1,7,8,128]{3,1,2,0:T(8,128)S(1)}, f32[1,7,8,128]{3,1,2,0:T(8,128)}, u32[]{:S(2)}) copy-start(f32[1,7,8,128]{3,1,2,0:T(8,128)} %copy-done.32) | copy-start | bytes 86020
  196.3 32.0 %collective-permute-start.14 = (bf16[2,512,2048]{2,1,0:T(8,128)(2,1)}, bf16[2,512,2048]{2,1,0:T(8,128)(2,1)}, u32[]{:S(2)}, u32[]{:S(2)}) collective-permute-start(bf16[2,512,2048]{2,1,0:T(8,128)(2,1)} %copy-done.1), channel_id=1, source_target_pairs={{0,1},{1,0},{2,3},{3,2},{4,5},{5,4},{6,7},{7,6},{8,9},{9,8},{10,11... | collective-permute-start | bytes 12582920 | tf_op jit(solution)/shard_map/ppermute | solution.py:589
  196.4 9.0 %collective-permute-start.12 = (bf16[2,512,768]{2,1,0:T(8,128)(2,1)S(1)}, bf16[2,512,768]{2,1,0:T(8,128)(2,1)S(1)}, u32[]{:S(2)}, u32[]{:S(2)}) collective-permute-start(bf16[2,512,768]{2,1,0:T(8,128)(2,1)S(1)} %copy-done.12), channel_id=1, source_target_pairs={{0,1},{1,0},{2,3},{3,2},{4,5},{5,4},{6,7},{7,6},{8,9},{9,8},{10,11... | collective-permute-start | bytes 4718600 | tf_op jit(solution)/shard_map/ppermute | solution.py:589
  228.3 8.4 %collective-permute-start.15 = (bf16[2,512,2048]{2,1,0:T(8,128)(2,1)}, bf16[2,512,2048]{2,1,0:T(8,128)(2,1)S(1)}, u32[]{:S(2)}, u32[]{:S(2)}) collective-permute-start(bf16[2,512,2048]{2,1,0:T(8,128)(2,1)} %collective-permute-done.13.refs_3_), channel_id=1, source_target_pairs={{0,1},{1,0},{2,3},{3,2},{4,5},{5,4},{6,7},{7,6},{8,9},{9,8},{10,11... | collective-permute-start | bytes 12582920 | tf_op jit(solution)/shard_map/ppermute | solution.py:589
  250.0 10.8 %collective-permute-start.16 = (bf16[2,2,512,1024]{3,2,1,0:T(8,128)(2,1)}, bf16[2,2,512,1024]{3,2,1,0:T(8,128)(2,1)S(1)}, u32[]{:S(2)}, u32[]{:S(2)}) collective-permute-start(bf16[2,2,512,1024]{3,2,1,0:T(8,128)(2,1)} %get-tuple-element.607), channel_id=1, source_target_pairs={{0,1},{1,0},{2,3},{3,2},{4,5},{5,4},{6,7},{7,6},{8,9},{9,8},{10,11... | collective-permute-start | bytes 12582920 | tf_op jit(solution)/shard_map/ppermute | solution.py:589
  260.8 15.7 %collective-permute-start.17 = (bf16[2,2,512,1024]{3,2,1,0:T(8,128)(2,1)}, bf16[2,2,512,1024]{3,2,1,0:T(8,128)(2,1)}, u32[]{:S(2)}, u32[]{:S(2)}) collective-permute-start(bf16[2,2,512,1024]{3,2,1,0:T(8,128)(2,1)} %get-tuple-element.625), channel_id=1, source_target_pairs={{0,1},{1,0},{2,3},{3,2},{4,5},{5,4},{6,7},{7,6},{8,9},{9,8},{10,11... | collective-permute-start | bytes 12582920 | tf_op jit(solution)/shard_map/ppermute | solution.py:589
  274.5 31.4 %collective-permute-start.19 = (bf16[2,512,1024]{2,1,0:T(8,128)(2,1)}, bf16[2,512,1024]{2,1,0:T(8,128)(2,1)S(1)}, u32[]{:S(2)}, u32[]{:S(2)}) collective-permute-start(bf16[2,512,1024]{2,1,0:T(8,128)(2,1)} %get-tuple-element.660), channel_id=1, source_target_pairs={{0,2},{1,17},{2,0},{3,19},{4,6},{5,21},{6,4},{7,23},{8,10},{9,25},... | collective-permute-start | bytes 6291464 | tf_op jit(solution)/shard_map/ppermute | solution.py:613
  287.4 50.7 %collective-permute-start.18 = (bf16[2,512,1024]{2,1,0:T(8,128)(2,1)}, bf16[2,512,1024]{2,1,0:T(8,128)(2,1)S(1)}, u32[]{:S(2)}, u32[]{:S(2)}) collective-permute-start(bf16[2,512,1024]{2,1,0:T(8,128)(2,1)} %get-tuple-element.654), channel_id=1, source_target_pairs={{0,2},{1,17},{2,0},{3,19},{4,6},{5,21},{6,4},{7,23},{8,10},{9,25},... | collective-permute-start | bytes 6291464 | tf_op jit(solution)/shard_map/ppermute | solution.py:613
  288.0 17.8 %copy-start.25 = (bf16[2,512,1024]{2,1,0:T(8,128)(2,1)S(1)}, bf16[2,512,1024]{2,1,0:T(8,128)(2,1)}, u32[]{:S(2)}) copy-start(bf16[2,512,1024]{2,1,0:T(8,128)(2,1)} %get-tuple-element.663) | copy-start | bytes 6291460
  307.8 47.8 %collective-permute-start.22 = (bf16[512,1024]{1,0:T(8,128)(2,1)S(1)}, bf16[512,1024]{1,0:T(8,128)(2,1)S(1)}, u32[]{:S(2)}, u32[]{:S(2)}) collective-permute-start(bf16[512,1024]{1,0:T(8,128)(2,1)S(1)} %get-tuple-element.672.refs_7_), channel_id=1, source_target_pairs={{0,16},{1,3},{2,18},{3,1},{4,20},{5,7},{6,22},{7,5},{8,24},{9,11},... | collective-permute-start | bytes 3145736 | tf_op jit(solution)/shard_map/ppermute | solution.py:613
  340.1 15.5 %collective-permute-start.23 = (bf16[512,1024]{1,0:T(8,128)(2,1)S(1)}, bf16[512,1024]{1,0:T(8,128)(2,1)S(1)}, u32[]{:S(2)}, u32[]{:S(2)}) collective-permute-start(bf16[512,1024]{1,0:T(8,128)(2,1)S(1)} %get-tuple-element.700.refs_8_), channel_id=1, source_target_pairs={{0,16},{1,3},{2,18},{3,1},{4,20},{5,7},{6,22},{7,5},{8,24},{9,11},... | collective-permute-start | bytes 3145736 | tf_op jit(solution)/shard_map/ppermute | solution.py:613
  341.2 14.4 %copy-start.7 = (bf16[512,1024]{1,0:T(8,128)(2,1)S(1)}, bf16[512,1024]{1,0:T(8,128)(2,1)}, u32[]{:S(2)}) copy-start(bf16[512,1024]{1,0:T(8,128)(2,1)} %get-tuple-element.711.refs_7_) | copy-start | bytes 3145732
  354.9 3.2 collective-permute-start.21
  368.9 63.0 %collective-permute-start.29 = (bf16[2,2,512,1024]{3,2,1,0:T(8,128)(2,1)}, bf16[2,2,512,1024]{3,2,1,0:T(8,128)(2,1)}, u32[]{:S(2)}, u32[]{:S(2)}) collective-permute-start(bf16[2,2,512,1024]{3,2,1,0:T(8,128)(2,1)} %get-tuple-element.786), channel_id=1, source_target_pairs={{0,1},{1,0},{2,3},{3,2},{4,5},{5,4},{6,7},{7,6},{8,9},{9,8},{10,11... | collective-permute-start | bytes 12582920 | tf_op jit(solution)/shard_map/ppermute | solution.py:589
  369.0 32.9 %all-to-all-start.3 = ((bf16[16,32,1024]{2,1,0:T(8,128)(2,1)}), bf16[16,32,1024]{2,1,0:T(8,128)(2,1)S(1)}, u32[]{:S(2)}, u32[]{:S(2)}) async-start(bf16[16,32,1024]{2,1,0:T(8,128)(2,1)} %bitcast.48), calls=%async_computation.3 | async-start | bytes 2097152 | tf_op jit(solution)/shard_map/all_to_all | solution.py:586
  378.6 2.9 collective-permute-start.20
  379.0 37.4 %collective-permute-start.24 = (bf16[128,2048]{1,0:T(8,128)(2,1)S(1)}, bf16[128,2048]{1,0:T(8,128)(2,1)S(1)}, u32[]{:S(2)}, u32[]{:S(2)}) collective-permute-start(bf16[128,2048]{1,0:T(8,128)(2,1)S(1)} %copy-done.27), channel_id=1, source_target_pairs={{0,4},{8,0},{12,8},{4,12},{1,5},{9,1},{13,9},{5,13},{2,6},{10,2},{... | collective-permute-start | bytes 1572872 | tf_op jit(solution)/shard_map/ppermute | solution.py:594
  386.0 30.4 %copy-start.14 = (bf16[128,2048]{1,0:T(8,128)(2,1)S(1)}, bf16[128,2048]{1,0:T(8,128)(2,1)}, u32[]{:S(2)}) copy-start(bf16[128,2048]{1,0:T(8,128)(2,1)} %get-tuple-element.753.refs_11_) | copy-start | bytes 1572868
  400.7 31.2 %collective-permute-start.28 = (bf16[2,2,512,512]{3,2,1,0:T(8,128)(2,1)}, bf16[2,2,512,512]{3,2,1,0:T(8,128)(2,1)}, u32[]{:S(2)}, u32[]{:S(2)}) collective-permute-start(bf16[2,2,512,512]{3,2,1,0:T(8,128)(2,1)} %get-tuple-element.785), channel_id=1, source_target_pairs={{0,1},{1,0},{2,3},{3,2},{4,5},{5,4},{6,7},{7,6},{8,9},{9,8},{10,11... | collective-permute-start | bytes 6291464 | tf_op jit(solution)/shard_map/ppermute | solution.py:589
  401.9 21.8 %copy-start.16 = (bf16[16,32,1024]{2,1,0:T(8,128)(2,1)}, bf16[16,32,1024]{2,1,0:T(8,128)(2,1)S(1)}, u32[]{:S(2)}) copy-start(bf16[16,32,1024]{2,1,0:T(8,128)(2,1)S(1)} %all-to-all-done.3) | copy-start | bytes 3145732
  416.5 14.4 %collective-permute-start.25 = (bf16[128,2048]{1,0:T(8,128)(2,1)S(1)}, bf16[128,2048]{1,0:T(8,128)(2,1)S(1)}, u32[]{:S(2)}, u32[]{:S(2)}) collective-permute-start(bf16[128,2048]{1,0:T(8,128)(2,1)S(1)} %add_convert_fusion.12.refs_8_), channel_id=1, source_target_pairs={{0,4},{8,0},{12,8},{4,12},{1,5},{9,1},{13,9},{5,13},{2,6},{10,2},{... | collective-permute-start | bytes 1572872 | tf_op jit(solution)/shard_map/ppermute | solution.py:594
  431.9 12.6 %copy-start.42 = (s32[4]{0:T(128)S(1)}, s32[4]{0:T(128)}, u32[]{:S(2)}) copy-start(s32[4]{0:T(128)} %constant.251.clone) | copy-start | bytes 52
  442.9 65.5 %collective-permute-start.30 = (bf16[2,512,1536]{2,1,0:T(8,128)(2,1)}, bf16[2,512,1536]{2,1,0:T(8,128)(2,1)}, u32[]{:S(2)}, u32[]{:S(2)}) collective-permute-start(bf16[2,512,1536]{2,1,0:T(8,128)(2,1)} %get-tuple-element.802), channel_id=1, source_target_pairs={{0,2},{1,17},{2,0},{3,19},{4,6},{5,21},{6,4},{7,23},{8,10},{9,25},... | collective-permute-start | bytes 9437192 | tf_op jit(solution)/shard_map/ppermute | solution.py:613
  444.5 26.7 %collective-permute-start.26 = (bf16[128,2048]{1,0:T(8,128)(2,1)S(1)}, bf16[128,2048]{1,0:T(8,128)(2,1)}, u32[]{:S(2)}, u32[]{:S(2)}) collective-permute-start(bf16[128,2048]{1,0:T(8,128)(2,1)S(1)} %copy-done.28), channel_id=1, source_target_pairs={{0,4},{8,0},{12,8},{4,12},{1,5},{9,1},{13,9},{5,13},{2,6},{10,2},{... | collective-permute-start | bytes 1572872 | tf_op jit(solution)/shard_map/ppermute | solution.py:594
  449.1 22.1 %copy-start.4 = (bf16[128,2048]{1,0:T(8,128)(2,1)S(1)}, bf16[128,2048]{1,0:T(8,128)(2,1)}, u32[]{:S(2)}) copy-start(bf16[128,2048]{1,0:T(8,128)(2,1)} %get-tuple-element.799.refs_9_.refs_6_.refs_16_) | copy-start | bytes 1572868
  449.1 119.2 %all-to-all-start.4 = ((bf16[16,128,512]{2,1,0:T(8,128)(2,1)}), bf16[16,128,512]{2,1,0:T(8,128)(2,1)S(1)}, u32[]{:S(2)}, u32[]{:S(2)}) async-start(bf16[16,128,512]{2,1,0:T(8,128)(2,1)} %bitcast.52), calls=%async_computation.4 | async-start | bytes 4194304 | tf_op jit(solution)/shard_map/all_to_all | solution.py:586
  453.6 19.7 %copy-start.37 = (f32[4,1024]{1,0:T(4,128)S(1)}, f32[4,1024]{1,0:T(4,128)}, u32[]{:S(2)}) copy-start(f32[4,1024]{1,0:T(4,128)} %get-tuple-element.777) | copy-start | bytes 49156
  453.6 19.7 %copy-start.38 = (f32[4,1024]{1,0:T(4,128)S(1)}, f32[4,1024]{1,0:T(4,128)}, u32[]{:S(2)}) copy-start(f32[4,1024]{1,0:T(4,128)} %get-tuple-element.776) | copy-start | bytes 49156
  453.6 20.8 %copy-start.39 = (f32[2,1,1024]{2,1,0:T(1,128)S(1)}, f32[2,1,1024]{2,1,0:T(1,128)}, u32[]{:S(2)}) copy-start(f32[2,1,1024]{2,1,0:T(1,128)} %get-tuple-element.779) | copy-start | bytes 24580
  513.8 20.8 %collective-permute-start.31 = (bf16[512,1536]{1,0:T(8,128)(2,1)}, bf16[512,1536]{1,0:T(8,128)(2,1)}, u32[]{:S(2)}, u32[]{:S(2)}) collective-permute-start(bf16[512,1536]{1,0:T(8,128)(2,1)} %get-tuple-element.901), channel_id=1, source_target_pairs={{0,16},{1,3},{2,18},{3,1},{4,20},{5,7},{6,22},{7,5},{8,24},{9,11},... | collective-permute-start | bytes 4718600 | tf_op jit(solution)/shard_map/ppermute | solution.py:613
  515.0 1.3 collective-permute-start.27
  516.4 4.2 collective-permute-start.32
  536.9 30.4 %copy-start.18 = (f32[128,2048]{1,0:T(8,128)S(1)}, f32[128,2048]{1,0:T(8,128)}, u32[]{:S(2)}) copy-start(f32[128,2048]{1,0:T(8,128)} %convert_add_fusion) | copy-start | bytes 3145732
  537.9 9.1 %collective-permute-start.33 = (bf16[128,1536]{1,0:T(8,128)(2,1)}, bf16[128,1536]{1,0:T(8,128)(2,1)}, u32[]{:S(2)}, u32[]{:S(2)}) collective-permute-start(bf16[128,1536]{1,0:T(8,128)(2,1)} %get-tuple-element.921), channel_id=1, source_target_pairs={{0,4},{8,0},{12,8},{4,12},{1,5},{9,1},{13,9},{5,13},{2,6},{10,2},{... | collective-permute-start | bytes 1179656 | tf_op jit(solution)/shard_map/ppermute | solution.py:594
  538.5 3.9 collective-permute-start.34
  548.9 15.8 %collective-permute-start.35 = (bf16[128,1536]{1,0:T(8,128)(2,1)}, bf16[128,1536]{1,0:T(8,128)(2,1)}, u32[]{:S(2)}, u32[]{:S(2)}) collective-permute-start(bf16[128,1536]{1,0:T(8,128)(2,1)} %add_convert_fusion.14), channel_id=1, source_target_pairs={{0,4},{8,0},{12,8},{4,12},{1,5},{9,1},{13,9},{5,13},{2,6},{10,2},{... | collective-permute-start | bytes 1179656 | tf_op jit(solution)/shard_map/ppermute | solution.py:594
  555.6 5.9 %collective-permute-start.36 = (f32[352]{0:T(512)S(1)}, f32[352]{0:T(512)S(1)}, u32[]{:S(2)}, u32[]{:S(2)}) collective-permute-start(f32[352]{0:T(512)S(1)} %get-tuple-element.900), channel_id=1, source_target_pairs={{0,4},{8,0},{12,8},{4,12},{1,5},{9,1},{13,9},{5,13},{2,6},{10,2},{... | collective-permute-start | bytes 4232 | tf_op jit(solution)/shard_map/ppermute | solution.py:594
  558.6 5.4 collective-permute-start.37
  560.0 4.0 collective-permute-start.38
  566.7 9.0 %collective-permute-start.39 = (bf16[128,1536]{1,0:T(8,128)(2,1)}, bf16[128,1536]{1,0:T(8,128)(2,1)}, u32[]{:S(2)}, u32[]{:S(2)}) collective-permute-start(bf16[128,1536]{1,0:T(8,128)(2,1)} %add_convert_fusion.13), channel_id=1, source_target_pairs={{0,4},{8,0},{12,8},{4,12},{1,5},{9,1},{13,9},{5,13},{2,6},{10,2},{... | collective-permute-start | bytes 1179656 | tf_op jit(solution)/shard_map/ppermute | solution.py:594
  (29 other events, 118.1 us)

commit v5 on v4

--- a/solution.py
+++ b/solution.py
@@ -746,6 +746,7 @@
     )
     ffn = gather_two(*ffn)
     others = [[over_tp(project[k ^ (d & 1)], d) for d in range(1, share)] for k in range(2)]
+    others = line.gate(others)
     inner = [line(attend_forward, project[0], others[0])]
     ffn = gather_near(*ffn)
     inner.append(line(attend_forward, project[1], others[1]))
@@ -827,26 +828,23 @@
         grad_project, att, joined, grad_second, vectors, both[1],
     )
     merger_other = over_tp(merger_other, 1)
-    layer_out = line.gate(layer_out)
-    ffn_sums = reduce_step(*ffn_sums)
     out = line(
         lambda *o: up(*o[:2], "inputs_back", *o[2:], (0, 1), side, 0, plain_step, flows, 256),
         joined_low, att,
     )
-    def turn_back(out):
-        out = absolute(out).reshape(ts, cs, ts * fine, side)
-        return out.transpose(1, 0, 2, 3).reshape(group * ts * fine, side)
-
-    out = to_group(line.plain(turn_back, out))
-    ffn_sums = reduce_step(*ffn_sums)
     att_sums = reduce_one(
         line(
             grads(0), [joined_low_t, attn_low_t, normed_t], [both[0], attended[0], grad_project[0]],
             [merger_other, attend_other],
         )
     )
-    grad_ffn = reduce_last(*ffn_sums)
-
+    layer_out = line.gate(layer_out)
+    def turn_back(out):
+        out = absolute(out).reshape(ts, cs, ts * fine, side)
+        return out.transpose(1, 0, 2, 3).reshape(group * ts * fine, side)
+
+    out = to_group(line.plain(turn_back, out))
+    ffn_sums = reduce_step(*ffn_sums)
     def vector_sums(one, two, wide):
         sums = jnp.concatenate([one[0:3], two]).reshape(7, fs * cs, rows)
         place = jnp.asarray([ring.index(i) for i in range(cs)], jnp.int32)[c_rank]
@@ -857,26 +855,28 @@
 
     vec = line.plain(vector_sums, sums_one, sums_two, wide).reshape(fs, cs, 2, 2, -1)
     moved = over_tp(pick(vec, 1 - t_rank % 2, 3), 1)
+    ffn_sums = reduce_step(*ffn_sums)
     vec = line.plain(lambda v, m: pick(v, t_rank % 2, 3) + m, vec, moved)
     moved = over_tp(pick(vec, 1 - t_rank // 2, 2), 2)
     out = line.gate(out)
     att_sums = reduce_two(*att_sums)
     vec = line.plain(lambda v, m: pick(v, t_rank // 2, 2) + m, vec, moved)
     moved = [over_fsdp(pick(vec, (f_rank - h) % fs), -h) for h in range(1, fs)]
+    grad_ffn = reduce_last(*ffn_sums)
+
+    def unpack(out, layer_out):
+        out = out.reshape(slots, share, ts, fine, side).transpose(0, 2, 1, 3, 4)
+        out = out.reshape(batches, local_seqs, local_len, side).astype(F32)
+        layer_out = layer_out.reshape(batches, local_seqs, share * fine, width)
+        return out[..., :part_width], out[..., part_width:], layer_out
+
+    grad_tokens, grad_skip, layer_out = line.plain(unpack, out, layer_out)
     att_sums = reduce_three(att_sums)
     vec = line.plain(lambda v, m: sum(m, pick(v, f_rank)), vec, moved)
     moved = [over_ctx(pick(vec, ctx_behind(d)), -d) for d in range(1, cs)]
     att_sums = reduce_step(*att_sums)
     vec = line.plain(lambda v, m: sum(m, pick(v, c_rank)), vec, moved)
     grad_att = reduce_last(*att_sums)
-
-    def unpack(out, layer_out):
-        out = out.reshape(slots, share, ts, fine, side).transpose(0, 2, 1, 3, 4)
-        out = out.reshape(batches, local_seqs, local_len, side).astype(F32)
-        layer_out = layer_out.reshape(batches, local_seqs, share * fine, width)
-        return out[..., :part_width], out[..., part_width:], layer_out
-
-    grad_tokens, grad_skip, layer_out = line.plain(unpack, out, layer_out)
     cut = side + heads_width
     vec_out = [vec[i * small : (i + 1) * small] for i in range(7)] + [vec[7 * small :]]
     return (

time: 590 us -> 550 us (0.932)
  waiting for transfers between devices: 199 us -> 162 us
  starting transfers between devices: 79.5 us -> 90.4 us
  other arithmetic: 41.6 us -> 31.9 us
    ppermute x10, waiting for transfers between devices: 59.4 us -> 27.5 us  [over(): return lax.ppermute(array, ALL, [(i, target(i)) for i in range(devices)])]
    ppermute x14, waiting for transfers between devices: 12.3 us -> 0.22 us  [over_tp(): return lax.ppermute(array, 'tp', [(i, i ^ flip) for i in range(ts)])]
    ppermute x15, starting transfers between devices: 15.6 us -> 26.4 us  [over_ctx(): lax.ppermute(array, 'ctx', [(ring[i], ring[(i + d) % cs]) for i in range(...]
    ppermute x15, waiting for transfers between devices: 69.1 us -> 77.5 us  [over_ctx(): lax.ppermute(array, 'ctx', [(ring[i], ring[(i + d) % cs]) for i in range(...]
    convert_element_type x12, other arithmetic: 19.1 us -> 12.6 us  [add(): return sum((t.astype(F32) for t in terms)).astype(BF16)]
    unnamed x115 -> x107, local copies, waits for them, and re-layouts: 17.8 us -> 16.7 us
  transfers between devices with their start and end apart: 45 -> 45, of which waited for: 22 -> 15; matrix products, arithmetic and copies ran while one was open for 12% -> 11% of each run, Pallas kernels for 28% -> 32%
where the time goes in v5:
time: 550 us; the launch traced here: 544 us
  Pallas kernels  197 us (36%)
  waiting for transfers between devices  162 us (29%)
  starting transfers between devices  90.4 us (16%)
  local copies, waits for them, and re-layouts  43.6 us (8%)
  other arithmetic  31.9 us (6%)
  between operations  16.3 us (3%)
    pallas_call x17, Pallas kernels, apply(): pl.pallas_call(run, grid_spec=pltpu.PrefetchScalarGridSpec(num_scalar_pre...  197 us
    ppermute x15, waiting for transfers between devices, over_ctx(): lax.ppermute(array, 'ctx', [(ring[i], ring[(i + d) % cs]) for i in range(...  77.5 us
    all_to_all x4, starting transfers between devices, to_group(): return lax.all_to_all(array, ('ctx', 'tp'), 0, 0, tiled=True)  35.1 us
    all_to_all x4, waiting for transfers between devices, to_group(): return lax.all_to_all(array, ('ctx', 'tp'), 0, 0, tiled=True)  27.5 us
    ppermute x10, waiting for transfers between devices, over(): return lax.ppermute(array, ALL, [(i, target(i)) for i in range(devices)])  27.5 us
    all_to_all x1, waiting for transfers between devices, on_device(): packed = lax.all_to_all(packed, ALL, 0, 0, tiled=True)  26.5 us
    ppermute x15, starting transfers between devices, over_ctx(): lax.ppermute(array, 'ctx', [(ring[i], ring[(i + d) % cs]) for i in range(...  26.4 us
    unnamed x107, local copies, waits for them, and re-layouts  16.7 us
  transfers between devices with their start and end apart: 45, of which 15 were waited for; matrix products, arithmetic and copies ran while one was open for 11% of the time, Pallas kernels for 32%

profile of v5, /device:TPU:0, one launch (start us, length us, event | category | flops | bytes accessed | tf_op | source)
XLA Modules:
  0.0 544.3 jit_solution(523517614267897254)
XLA Ops:
  3.8 4.1 collective-permute-start
  11.5 4.5 all-to-all-start
  16.7 1.4 pad_maximum_fusion.2
  18.1 1.5 copy.69
  19.6 26.5 %all-to-all-done = f32[32,1,352]{2,1,0:T(1,128)S(1)} async-done(((f32[32,1,352]{2,1,0:T(1,128)}), f32[32,1,352]{2,1,0:T(1,128)S(1)}, u32[]{:S(2)}, u32[]{:S(2)}) %all-to-all-start) | async-done | bytes 45088 | tf_op jit(solution)/shard_map/all_to_all | solution.py:704
  48.6 1.6 collective-permute-start.3
  50.2 4.3 all-to-all-start.1
  54.5 10.9 %collective-permute-done.3 = bf16[128,2048]{1,0:T(8,128)(2,1)} collective-permute-done((bf16[128,2048]{1,0:T(8,128)(2,1)S(1)}, bf16[128,2048]{1,0:T(8,128)(2,1)}, u32[]{:S(2)}, u32[]{:S(2)}) %collective-permute-start.3) | collective-permute-done | bytes 524320 | tf_op jit(solution)/shard_map/ppermute | solution.py:594
  65.4 3.0 collective-permute-done.5
  68.5 2.2 pad_maximum_fusion.1.refs_8_.refs_2_.refs_7_.refs_9_.refs_1_
  71.5 5.2 collective-permute-start.7
  82.5 9.5 %collective-permute-done.4 = bf16[128,2048]{1,0:T(8,128)(2,1)} collective-permute-done((bf16[128,2048]{1,0:T(8,128)(2,1)}, bf16[128,2048]{1,0:T(8,128)(2,1)}, u32[]{:S(2)}, u32[]{:S(2)}) %collective-permute-start.4) | collective-permute-done | bytes 524320 | tf_op jit(solution)/shard_map/ppermute | solution.py:594
  95.2 2.2 fusion.refs_1_
  97.4 16.0 %all-to-all-start.2 = ((bf16[16,128,512]{2,1,0:T(8,128)(2,1)}), bf16[16,128,512]{2,1,0:T(8,128)(2,1)}, u32[]{:S(2)}, u32[]{:S(2)}) async-start(bf16[16,128,512]{2,1,0:T(8,128)(2,1)} %bitcast.117), calls=%async_computation.2 | async-start | bytes 4194304 | tf_op jit(solution)/shard_map/all_to_all | solution.py:586
  119.1 5.8 %arrived.1 = (bf16[512,1024]{1,0:T(8,128)(2,1)}, bf16[1024,512]{1,0:T(8,128)(2,1)}, f32[8,128]{1,0:T(8,128)}) custom-call(s32[2]{0:T(128)} %pad_add_fusion.roles_ref, bf16[512,1024]{1,0:T(8,128)(2,1)} %bitcast.8.refs_0_, bf16[1024,1024]{1,0:T(8,128)(2,1)} %fusion.refs_1_, f32[1,1]{1,0:T(1,128)} %bitcast.26.refs_2_, bf16[128,1536]{1,0:T(8,128)(2,1)} %copy-done.19, ...), custom_call_target="tpu_custom_call" | custom-call | flops 1 | bytes 1 | tf_op jit(solution)/shard_map/arrived/pallas_call | solution.py:36
  127.2 27.5 %all-to-all-done.2 = bf16[16,128,512]{2,1,0:T(8,128)(2,1)} async-done(((bf16[16,128,512]{2,1,0:T(8,128)(2,1)}), bf16[16,128,512]{2,1,0:T(8,128)(2,1)}, u32[]{:S(2)}, u32[]{:S(2)}) %all-to-all-start.2) | async-done | bytes 2097184 | tf_op jit(solution)/shard_map/all_to_all | solution.py:586
  154.7 1.7 constant_dynamic-slice_fusion.26
  160.1 14.7 %joined.1 = (f32[512,1024]{1,0:T(8,128)}, bf16[512,1024]{1,0:T(8,128)(2,1)}, bf16[1024,512]{1,0:T(8,128)(2,1)}, bf16[2,512,768]{2,1,0:T(8,128)(2,1)}, bf16[2,512,768]{2,1,0:T(8,128)(2,1)}, /*index=5*/f32[8,128]{1,0:T(8,128)}) custom-call(s32[2]{0:T(128)} %pad_add_fusion.roles_ref, bf16[2,512,512]{2,1,0:T(8,128)(2,1)} %pad_maximum_fusion.7.refs_0_.refs_15_.refs_1_.refs_3_, ...), custom_call_target="tpu_custom_call" | custom-call | flops 1 | bytes 1 | tf_op jit(solution)/shard_map/joined/pallas_call | solution.py:36
  175.7 2.6 pad_maximum_fusion.refs_3_.refs_2_
  178.3 3.4 collective-permute-start.13
  182.9 13.3 %attend_forward.2 = (bf16[2,4,1024,512]{3,2,1,0:T(8,128)(2,1)}, bf16[2,512,256]{2,1,0:T(8,128)(2,1)}, f32[8,128]{1,0:T(8,128)}) custom-call(s32[2]{0:T(128)} %pad_add_fusion.roles_ref, bf16[2,512,768]{2,1,0:T(8,128)(2,1)} %get-tuple-element.695.refs_0_, bf16[2,512,768]{2,1,0:T(8,128)(2,1)} %copy-done.10, f32[8,128]{1,0:T(8,128)} %get-tuple-element.572.refs_2_, ...), custom_call_target="tpu_custom_call" | custom-call | flops 1 | bytes 1 | tf_op jit(solution)/shard_map/attend_forward/pallas_call | solution.py:36
  196.2 13.8 %attend_forward.3 = (bf16[2,4,1024,512]{3,2,1,0:T(8,128)(2,1)}, bf16[2,512,256]{2,1,0:T(8,128)(2,1)}, f32[8,128]{1,0:T(8,128)}) custom-call(s32[2]{0:T(128)} %pad_add_fusion.roles_ref, bf16[2,512,768]{2,1,0:T(8,128)(2,1)} %get-tuple-element.668.refs_0_, bf16[2,512,768]{2,1,0:T(8,128)(2,1)} %copy-done.9, f32[8,128]{1,0:T(8,128)} %get-tuple-element.582.refs_2_), custom_call_target="tpu_custom_call" | custom-call | flops 1 | bytes 1 | tf_op jit(solution)/shard_map/attend_forward/pallas_call | solution.py:36
  210.0 18.3 %collective-permute-done.13.refs_3_ = bf16[2,512,2048]{2,1,0:T(8,128)(2,1)} collective-permute-done((bf16[2,512,2048]{2,1,0:T(8,128)(2,1)S(1)}, bf16[2,512,2048]{2,1,0:T(8,128)(2,1)}, u32[]{:S(2)}, u32[]{:S(2)}) %collective-permute-start.13) | collective-permute-done | bytes 4194336 | tf_op jit(solution)/shard_map/ppermute | solution.py:613
  228.9 7.8 %second.1 = (f32[512,1024]{1,0:T(8,128)}, bf16[512,1024]{1,0:T(8,128)(2,1)}, bf16[1024,512]{1,0:T(8,128)(2,1)}, f32[8,128]{1,0:T(8,128)}) custom-call(s32[2]{0:T(128)} %pad_add_fusion.roles_ref, bf16[2,512,256]{2,1,0:T(8,128)(2,1)} %get-tuple-element.767.refs_0_.refs_3_.refs_5_.refs_7_, bf16[2,512,256]{2,1,0:T(8,128)(2,1)} %get-tuple-element.724.refs_1_.refs_3_, ...), custom_call_target="tpu_custom_call" | custom-call | flops 1 | bytes 1 | tf_op jit(solution)/shard_map/second/pallas_call | solution.py:36
  236.7 1.9 copy-done.3
  238.7 11.3 %hidden.2 = (bf16[2,512,1024]{2,1,0:T(8,128)(2,1)}, bf16[2,512,1024]{2,1,0:T(8,128)(2,1)}, bf16[2,2,512,1024]{3,2,1,0:T(8,128)(2,1)}, f32[8,128]{1,0:T(8,128)}) custom-call(s32[2]{0:T(128)} %pad_add_fusion.roles_ref, bf16[512,1024]{1,0:T(8,128)(2,1)} %get-tuple-element.620.refs_0_, bf16[1024,512]{1,0:T(8,128)(2,1)} %get-tuple-element.621.refs_1_, ...), custom_call_target="tpu_custom_call" | custom-call | flops 1 | bytes 1 | tf_op jit(solution)/shard_map/hidden/pallas_call | solution.py:36
  250.5 10.3 %hidden_back.2 = (bf16[2,512,1024]{2,1,0:T(8,128)(2,1)}, f32[2,1,1024]{2,1,0:T(1,128)}, bf16[2,2,512,1024]{3,2,1,0:T(8,128)(2,1)}, f32[8,128]{1,0:T(8,128)}) custom-call(s32[2]{0:T(128)} %pad_add_fusion.roles_ref, bf16[512,1024]{1,0:T(8,128)(2,1)} %get-tuple-element.648.refs_0_.refs_7_, bf16[1024,512]{1,0:T(8,128)(2,1)} %get-tuple-element.631.refs_1_, ...), custom_call_target="tpu_custom_call" | custom-call | flops 1 | bytes 1 | tf_op jit(solution)/shard_map/hidden_back/pallas_call | solution.py:36
  260.8 2.1 copy-done.14
  262.8 11.6 %hidden.3 = (bf16[2,512,1024]{2,1,0:T(8,128)(2,1)}, bf16[2,512,1024]{2,1,0:T(8,128)(2,1)}, bf16[2,512,1024]{2,1,0:T(8,128)(2,1)}, bf16[2,512,1024]{2,1,0:T(8,128)(2,1)}, f32[8,128]{1,0:T(8,128)}) custom-call(s32[2]{0:T(128)} %pad_add_fusion.roles_ref, bf16[512,1024]{1,0:T(8,128)(2,1)} %get-tuple-element.620.refs_0_, ...), custom_call_target="tpu_custom_call" | custom-call | flops 1 | bytes 1 | tf_op jit(solution)/shard_map/hidden/pallas_call | solution.py:36
  274.4 2.1 collective-permute-start.19
  276.5 10.8 %hidden_back.3 = (bf16[2,512,1024]{2,1,0:T(8,128)(2,1)}, f32[2,1,1024]{2,1,0:T(1,128)}, bf16[2,512,1024]{2,1,0:T(8,128)(2,1)}, bf16[2,512,1024]{2,1,0:T(8,128)(2,1)}, f32[8,128]{1,0:T(8,128)}) custom-call(s32[2]{0:T(128)} %pad_add_fusion.roles_ref, bf16[512,1024]{1,0:T(8,128)(2,1)} %get-tuple-element.648.refs_0_.refs_7_, ...), custom_call_target="tpu_custom_call" | custom-call | flops 1 | bytes 1 | tf_op jit(solution)/shard_map/hidden_back/pallas_call | solution.py:36
  288.0 17.8 %second_back.1 = (f32[512,1024]{1,0:T(8,128)}, bf16[512,1024]{1,0:T(8,128)(2,1)}, bf16[1024,512]{1,0:T(8,128)(2,1)}, f32[4,1024]{1,0:T(4,128)}, bf16[2,512,256]{...) custom-call(s32[2]{0:T(128)} %pad_add_fusion.roles_ref, ...), custom_call_target="tpu_custom_call" | custom-call | flops 1 | bytes 1 | tf_op jit(solution)/shard_map/second_back/pallas_call | solution.py:36
  305.8 1.9 fusion.4
  308.7 13.6 %attend_backward.2 = (bf16[2,512,768]{2,1,0:T(8,128)(2,1)}, bf16[2,512,512]{2,1,0:T(8,128)(2,1)}, f32[8,128]{1,0:T(8,128)}) custom-call(s32[2]{0:T(128)} %pad_add_fusion.roles_ref, bf16[2,512,768]{2,1,0:T(8,128)(2,1)} %get-tuple-element.668.refs_0_, bf16[2,512,768]{2,1,0:T(8,128)(2,1)} %copy-done.9, bf16[2,4,1024,512]{3,2,1,0:T(8,128)(2,1)} %get-tuple-element.670.refs_2_, ...), custom_call_target="tpu_custom_call" | custom-call | flops 1 | bytes 1 | tf_op jit(solution)/shard_map/attend_backward/pallas_call | solution.py:36
  323.0 11.2 %layer_out.1 = (bf16[512,1024]{1,0:T(8,128)(2,1)}, f32[8,128]{1,0:T(8,128)}) custom-call(s32[2]{0:T(128)} %pad_add_fusion.roles_ref, bf16[2,512,1024]{2,1,0:T(8,128)(2,1)} %get-tuple-element.677.refs_0_, bf16[2,512,1024]{2,1,0:T(8,128)(2,1)} %get-tuple-element.678.refs_1_, bf16[2,512,2048]{2,1,0:T(8,128)(2,1)} %copy-done.1, ...), custom_call_target="tpu_custom_call" | custom-call | flops 1 | bytes 1 | tf_op jit(solution)/shard_map/layer_out/pallas_call | solution.py:36
  334.2 3.6 convolution_convert_fusion.refs_6_
  337.8 2.0 fusion.6
  340.9 13.8 %attend_backward.3 = (bf16[2,512,768]{2,1,0:T(8,128)(2,1)}, bf16[2,512,512]{2,1,0:T(8,128)(2,1)}, f32[8,128]{1,0:T(8,128)}) custom-call(s32[2]{0:T(128)} %pad_add_fusion.roles_ref, bf16[2,512,768]{2,1,0:T(8,128)(2,1)} %get-tuple-element.695.refs_0_, bf16[2,512,768]{2,1,0:T(8,128)(2,1)} %copy-done.10, bf16[2,4,1024,512]{3,2,1,0:T(8,128)(2,1)} %get-tuple-element.697.refs_2_, ...), custom_call_target="tpu_custom_call" | custom-call | flops 1 | bytes 1 | tf_op jit(solution)/shard_map/attend_backward/pallas_call | solution.py:36
  360.0 8.7 %weight_grad.2 = (bf16[2,2,512,1024]{3,2,1,0:T(8,128)(2,1)}, f32[8,128]{1,0:T(8,128)}) custom-call(s32[2]{0:T(128)} %pad_add_fusion.roles_ref, bf16[1024,512]{1,0:T(8,128)(2,1)} %get-tuple-element.766.refs_0_.refs_2_.refs_4_.refs_6_, bf16[2,512,256]{2,1,0:T(8,128)(2,1)} %get-tuple-element.724.refs_1_.refs_3_, ...), custom_call_target="tpu_custom_call" | custom-call | flops 1 | bytes 1 | tf_op jit(solution)/shard_map/weight_grad/pallas_call | solution.py:36
  369.2 10.0 %all-to-all-start.3 = ((bf16[16,32,1024]{2,1,0:T(8,128)(2,1)}), bf16[16,32,1024]{2,1,0:T(8,128)(2,1)S(1)}, u32[]{:S(2)}, u32[]{:S(2)}) async-start(bf16[16,32,1024]{2,1,0:T(8,128)(2,1)} %bitcast.55), calls=%async_computation.3 | async-start | bytes 2097152 | tf_op jit(solution)/shard_map/all_to_all | solution.py:586
  379.3 1.5 add_convert_fusion.3
  382.7 14.5 %first_back.1 = (bf16[512,1024]{1,0:T(8,128)(2,1)}, bf16[1024,512]{1,0:T(8,128)(2,1)}, f32[4,1024]{1,0:T(4,128)}, bf16[2,2,512,512]{3,2,1,0:T(8,128)(2,1)}, f32[8,128]{1,0:T(8,128)}) custom-call(s32[2]{0:T(128)} %pad_add_fusion.roles_ref, bf16[2,512,768]{2,1,0:T(8,128)(2,1)} %pad_maximum_fusion.6.refs_0_.refs_11_.refs_9_, ...), custom_call_target="tpu_custom_call" | custom-call | flops 1 | bytes 1 | tf_op jit(solution)/shard_map/first_back/pallas_call | solution.py:36
  397.8 4.0 collective-permute-start.26
  401.8 6.3 %inputs_back.1 = (bf16[2,512,512]{2,1,0:T(8,128)(2,1)}, bf16[2,512,512]{2,1,0:T(8,128)(2,1)}, f32[8,128]{1,0:T(8,128)}) custom-call(s32[2]{0:T(128)} %pad_add_fusion.roles_ref, bf16[512,1024]{1,0:T(8,128)(2,1)} %get-tuple-element.752.refs_0_, bf16[2,512,1536]{2,1,0:T(8,128)(2,1)} %copy-done, ...), custom_call_target="tpu_custom_call" | custom-call | flops 1 | bytes 1 | tf_op jit(solution)/shard_map/inputs_back/pallas_call | solution.py:36
  410.5 1.5 copy.72
  413.0 4.8 all-to-all-start.4
  422.5 11.3 %weight_grad.3 = (bf16[2,512,1536]{2,1,0:T(8,128)(2,1)}, bf16[2,512,1536]{2,1,0:T(8,128)(2,1)}, f32[8,128]{1,0:T(8,128)}) custom-call(s32[2]{0:T(128)} %pad_add_fusion.roles_ref, bf16[1024,512]{1,0:T(8,128)(2,1)} %get-tuple-element.764.refs_0_.refs_2_, bf16[2,512,512]{2,1,0:T(8,128)(2,1)} %pad_maximum_fusion.7.refs_0_.refs_15_.refs_1_.refs_3_, ...), custom_call_target="tpu_custom_call" | custom-call | flops 1 | bytes 1 | tf_op jit(solution)/shard_map/weight_grad/pallas_call | solution.py:36
  433.8 2.0 collective-permute-start.31
  436.7 1.5 collective-permute-start.28
  439.9 38.3 %collective-permute-done.28 = bf16[128,2048]{1,0:T(8,128)(2,1)S(1)} collective-permute-done((bf16[128,2048]{1,0:T(8,128)(2,1)}, bf16[128,2048]{1,0:T(8,128)(2,1)S(1)}, u32[]{:S(2)}, u32[]{:S(2)}) %collective-permute-start.28) | collective-permute-done | bytes 524320 | tf_op jit(solution)/shard_map/ppermute | solution.py:594
  479.4 1.6 collective-permute-start.30
  480.9 3.7 fusion.2
  485.8 8.1 %collective-permute-done.29 = bf16[128,2048]{1,0:T(8,128)(2,1)} collective-permute-done((bf16[128,2048]{1,0:T(8,128)(2,1)}, bf16[128,2048]{1,0:T(8,128)(2,1)}, u32[]{:S(2)}, u32[]{:S(2)}) %collective-permute-start.29) | collective-permute-done | bytes 524320 | tf_op jit(solution)/shard_map/ppermute | solution.py:594
  496.5 2.5 fusion.34
  499.0 6.2 %collective-permute-done.32 = bf16[512,1536]{1,0:T(8,128)(2,1)S(1)} collective-permute-done((bf16[512,1536]{1,0:T(8,128)(2,1)S(1)}, bf16[512,1536]{1,0:T(8,128)(2,1)S(1)}, u32[]{:S(2)}, u32[]{:S(2)}) %collective-permute-start.32) | collective-permute-done | bytes 1572896 | tf_op jit(solution)/shard_map/ppermute | solution.py:613
  505.7 3.7 collective-permute-start.33
  510.4 2.6 collective-permute-done.34
  513.0 4.1 collective-permute-done.33
  517.1 2.0 collective-permute-start.35
  525.9 2.0 collective-permute-start.37
  527.9 1.9 collective-permute-start.38
  529.8 1.5 collective-permute-done.37
  531.6 1.6 collective-permute-start.39
  535.4 4.9 collective-permute-done.39
  (260 shorter events, 61.5 us)
Async XLA Ops:
  0.6 16.0 %copy-start.27 = (bf16[4,2,256,256]{3,2,1,0:T(8,128)(2,1)S(1)}, bf16[4,2,256,256]{3,2,1,0:T(8,128)(2,1)}, u32[]{:S(2)}) copy-start(bf16[4,2,256,256]{3,2,1,0:T(8,128)(2,1)} %param.30) | copy-start | bytes 3145732
  3.8 42.9 %copy-start.19 = (bf16[128,1536]{1,0:T(8,128)(2,1)}, bf16[128,1536]{1,0:T(8,128)(2,1)S(1)}, u32[]{:S(2)}) copy-start(bf16[128,1536]{1,0:T(8,128)(2,1)S(1)} %pad_maximum_fusion.10.refs_3_) | copy-start | bytes 1179652
  3.8 42.9 %collective-permute-start = (bf16[128,1536]{1,0:T(8,128)(2,1)S(1)}, bf16[128,1536]{1,0:T(8,128)(2,1)S(1)}, u32[]{:S(2)}, u32[]{:S(2)}) collective-permute-start(bf16[128,1536]{1,0:T(8,128)(2,1)S(1)} %pad_maximum_fusion.10.refs_3_), channel_id=1, source_target_pairs={{0,8},{8,12},{12,4},{4,0},{1,9},{9,13},{13,5},{5,1},{2,10},{10,14}... | collective-permute-start | bytes 1179656 | tf_op jit(solution)/shard_map/ppermute | solution.py:594
  7.9 38.8 %collective-permute-start.1 = (bf16[128,1536]{1,0:T(8,128)(2,1)S(1)}, bf16[128,1536]{1,0:T(8,128)(2,1)S(1)}, u32[]{:S(2)}, u32[]{:S(2)}) collective-permute-start(bf16[128,1536]{1,0:T(8,128)(2,1)S(1)} %pad_maximum_fusion.10.refs_3_), channel_id=1, source_target_pairs={{0,12},{8,4},{12,0},{4,8},{1,13},{9,5},{13,1},{5,9},{2,14},{10,6},... | collective-permute-start | bytes 1179656 | tf_op jit(solution)/shard_map/ppermute | solution.py:594
  9.2 37.5 %collective-permute-start.2 = (bf16[128,1536]{1,0:T(8,128)(2,1)S(1)}, bf16[128,1536]{1,0:T(8,128)(2,1)}, u32[]{:S(2)}, u32[]{:S(2)}) collective-permute-start(bf16[128,1536]{1,0:T(8,128)(2,1)S(1)} %pad_maximum_fusion.10.refs_3_), channel_id=1, source_target_pairs={{0,4},{8,0},{12,8},{4,12},{1,5},{9,1},{13,9},{5,13},{2,6},{10,2},{... | collective-permute-start | bytes 1179656 | tf_op jit(solution)/shard_map/ppermute | solution.py:594
  11.5 34.6 %all-to-all-start = ((f32[32,1,352]{2,1,0:T(1,128)}), f32[32,1,352]{2,1,0:T(1,128)S(1)}, u32[]{:S(2)}, u32[]{:S(2)}) async-start(f32[32,1,352]{2,1,0:T(1,128)} %broadcast_in_dim.8), calls=%async_computation | async-start | bytes 98304 | tf_op jit(solution)/shard_map/all_to_all | solution.py:704
  19.6 30.6 %copy-start.20 = (bf16[128,2048]{1,0:T(8,128)(2,1)}, bf16[128,2048]{1,0:T(8,128)(2,1)S(1)}, u32[]{:S(2)}) copy-start(bf16[128,2048]{1,0:T(8,128)(2,1)S(1)} %constant_dynamic-update-slice_fusion.refs_6_) | copy-start | bytes 1572868
  47.9 20.6 %copy-start.8 = (bf16[512,1536]{1,0:T(8,128)(2,1)}, bf16[512,1536]{1,0:T(8,128)(2,1)S(1)}, u32[]{:S(2)}) copy-start(bf16[512,1536]{1,0:T(8,128)(2,1)S(1)} %constant_dynamic-update-slice_fusion.2.refs_7_) | copy-start | bytes 4718596
  47.9 20.6 %collective-permute-start.5 = (bf16[512,1536]{1,0:T(8,128)(2,1)S(1)}, bf16[512,1536]{1,0:T(8,128)(2,1)}, u32[]{:S(2)}, u32[]{:S(2)}) collective-permute-start(bf16[512,1536]{1,0:T(8,128)(2,1)S(1)} %constant_dynamic-update-slice_fusion.2.refs_7_), channel_id=1, source_target_pairs={{0,16},{1,3},{2,18},{3,1},{4,20},{5,7},{6,22},{7,5},{8,24},{9,11},... | collective-permute-start | bytes 4718600 | tf_op jit(solution)/shard_map/ppermute | solution.py:613
  48.6 16.8 %collective-permute-start.3 = (bf16[128,2048]{1,0:T(8,128)(2,1)S(1)}, bf16[128,2048]{1,0:T(8,128)(2,1)}, u32[]{:S(2)}, u32[]{:S(2)}) collective-permute-start(bf16[128,2048]{1,0:T(8,128)(2,1)S(1)} %constant_dynamic-update-slice_fusion.refs_6_), channel_id=1, source_target_pairs={{0,8},{8,12},{12,4},{4,0},{1,9},{9,13},{13,5},{5,1},{2,10},{10,14}... | collective-permute-start | bytes 1572872 | tf_op jit(solution)/shard_map/ppermute | solution.py:594
  50.2 47.2 %all-to-all-start.1 = ((bf16[16,32,1024]{2,1,0:T(8,128)(2,1)}), bf16[16,32,1024]{2,1,0:T(8,128)(2,1)}, u32[]{:S(2)}, u32[]{:S(2)}) async-start(bf16[16,32,1024]{2,1,0:T(8,128)(2,1)} %bitcast.7), calls=%async_computation.1 | async-start | bytes 2097152 | tf_op jit(solution)/shard_map/all_to_all | solution.py:586
  68.5 12.0 %copy-start.39 = (s32[4]{0:T(128)S(1)}, s32[4]{0:T(128)}, u32[]{:S(2)}) copy-start(s32[4]{0:T(128)} %constant.250.clone) | copy-start | bytes 52
  68.5 25.1 %copy-start.37 = (s32[4,2]{0,1:T(2,128)S(1)}, s32[4,2]{0,1:T(2,128)}, u32[]{:S(2)}) copy-start(s32[4,2]{0,1:T(2,128)} %param.44) | copy-start | bytes 100
  70.7 26.7 %copy-start = (bf16[2,512,1536]{2,1,0:T(8,128)(2,1)}, bf16[2,512,1536]{2,1,0:T(8,128)(2,1)S(1)}, u32[]{:S(2)}) copy-start(bf16[2,512,1536]{2,1,0:T(8,128)(2,1)S(1)} %pad_maximum_fusion.1.refs_8_.refs_2_.refs_7_.refs_9_.refs_1_) | copy-start | bytes 9437188
  70.7 55.3 %collective-permute-start.6 = (bf16[2,512,1536]{2,1,0:T(8,128)(2,1)S(1)}, bf16[2,512,1536]{2,1,0:T(8,128)(2,1)}, u32[]{:S(2)}, u32[]{:S(2)}) collective-permute-start(bf16[2,512,1536]{2,1,0:T(8,128)(2,1)S(1)} %pad_maximum_fusion.1.refs_8_.refs_2_.refs_7_.refs_9_.refs_1_), channel_id=1, source_target_pairs={{0,2},{1,17},{2,0},{3,19},{4,6},{5,21},{6,4},{7,23},{8,10},{9,25},... | collective-permute-start | bytes 9437192 | tf_op jit(solution)/shard_map/ppermute | solution.py:613
  71.5 54.4 %collective-permute-start.7 = (bf16[2,512,1536]{2,1,0:T(8,128)(2,1)S(1)}, bf16[2,512,1536]{2,1,0:T(8,128)(2,1)}, u32[]{:S(2)}, u32[]{:S(2)}) collective-permute-start(bf16[2,512,1536]{2,1,0:T(8,128)(2,1)S(1)} %pad_maximum_fusion.1.refs_8_.refs_2_.refs_7_.refs_9_.refs_1_), channel_id=1, source_target_pairs={{0,1},{1,0},{2,3},{3,2},{4,5},{5,4},{6,7},{7,6},{8,9},{9,8},{10,11... | collective-permute-start | bytes 9437192 | tf_op jit(solution)/shard_map/ppermute | solution.py:589
  76.7 15.3 %collective-permute-start.4 = (bf16[128,2048]{1,0:T(8,128)(2,1)}, bf16[128,2048]{1,0:T(8,128)(2,1)}, u32[]{:S(2)}, u32[]{:S(2)}) collective-permute-start(bf16[128,2048]{1,0:T(8,128)(2,1)} %collective-permute-done.3), channel_id=1, source_target_pairs={{0,8},{8,12},{12,4},{4,0},{1,9},{9,13},{13,5},{5,1},{2,10},{10,14}... | collective-permute-start | bytes 1572872 | tf_op jit(solution)/shard_map/ppermute | solution.py:594
  92.0 21.4 %collective-permute-start.8 = (bf16[128,2048]{1,0:T(8,128)(2,1)}, bf16[128,2048]{1,0:T(8,128)(2,1)}, u32[]{:S(2)}, u32[]{:S(2)}) collective-permute-start(bf16[128,2048]{1,0:T(8,128)(2,1)} %collective-permute-done.4), channel_id=1, source_target_pairs={{0,8},{8,12},{12,4},{4,0},{1,9},{9,13},{13,5},{5,1},{2,10},{10,14}... | collective-permute-start | bytes 1572872 | tf_op jit(solution)/shard_map/ppermute | solution.py:594
  97.4 57.3 %all-to-all-start.2 = ((bf16[16,128,512]{2,1,0:T(8,128)(2,1)}), bf16[16,128,512]{2,1,0:T(8,128)(2,1)}, u32[]{:S(2)}, u32[]{:S(2)}) async-start(bf16[16,128,512]{2,1,0:T(8,128)(2,1)} %bitcast.117), calls=%async_computation.2 | async-start | bytes 4194304 | tf_op jit(solution)/shard_map/all_to_all | solution.py:586
  125.3 33.2 %copy-start.28 = (f32[1,7,8,128]{3,1,2,0:T(8,128)}, f32[1,7,8,128]{3,1,2,0:T(8,128)S(1)}, u32[]{:S(2)}) copy-start(f32[1,7,8,128]{3,1,2,0:T(8,128)S(1)} %copy.93) | copy-start | bytes 86020
  126.0 32.5 %collective-permute-start.9 = (bf16[2,512,1536]{2,1,0:T(8,128)(2,1)}, bf16[2,512,1536]{2,1,0:T(8,128)(2,1)S(1)}, u32[]{:S(2)}, u32[]{:S(2)}) collective-permute-start(bf16[2,512,1536]{2,1,0:T(8,128)(2,1)} %collective-permute-done.6.refs_3_.refs_8_.refs_10_.refs_2_), channel_id=1, source_target_pairs={{0,1},{1,0},{2,3},{3,2},{4,5},{5,4},{6,7},{7,6},{8,9},{9,8},{10,11... | collective-permute-start | bytes 9437192 | tf_op jit(solution)/shard_map/ppermute | solution.py:589
  126.5 49.2 %collective-permute-start.12 = (bf16[512,2048]{1,0:T(8,128)(2,1)}, bf16[512,2048]{1,0:T(8,128)(2,1)}, u32[]{:S(2)}, u32[]{:S(2)}) collective-permute-start(bf16[512,2048]{1,0:T(8,128)(2,1)} %copy-done.4), channel_id=1, source_target_pairs={{0,16},{1,3},{2,18},{3,1},{4,20},{5,7},{6,22},{7,5},{8,24},{9,11},... | collective-permute-start | bytes 6291464 | tf_op jit(solution)/shard_map/ppermute | solution.py:613
  174.9 6.9 %collective-permute-start.10 = (bf16[2,512,768]{2,1,0:T(8,128)(2,1)}, bf16[2,512,768]{2,1,0:T(8,128)(2,1)S(1)}, u32[]{:S(2)}, u32[]{:S(2)}) collective-permute-start(bf16[2,512,768]{2,1,0:T(8,128)(2,1)} %get-tuple-element.668.refs_0_), channel_id=1, source_target_pairs={{0,1},{1,0},{2,3},{3,2},{4,5},{5,4},{6,7},{7,6},{8,9},{9,8},{10,11... | collective-permute-start | bytes 4718600 | tf_op jit(solution)/shard_map/ppermute | solution.py:589
  175.6 6.1 %collective-permute-start.11 = (bf16[2,512,768]{2,1,0:T(8,128)(2,1)}, bf16[2,512,768]{2,1,0:T(8,128)(2,1)S(1)}, u32[]{:S(2)}, u32[]{:S(2)}) collective-permute-start(bf16[2,512,768]{2,1,0:T(8,128)(2,1)} %get-tuple-element.695.refs_0_), channel_id=1, source_target_pairs={{0,1},{1,0},{2,3},{3,2},{4,5},{5,4},{6,7},{7,6},{8,9},{9,8},{10,11... | collective-permute-start | bytes 4718600 | tf_op jit(solution)/shard_map/ppermute | solution.py:589
  178.3 50.0 %collective-permute-start.13 = (bf16[2,512,2048]{2,1,0:T(8,128)(2,1)S(1)}, bf16[2,512,2048]{2,1,0:T(8,128)(2,1)}, u32[]{:S(2)}, u32[]{:S(2)}) collective-permute-start(bf16[2,512,2048]{2,1,0:T(8,128)(2,1)S(1)} %pad_maximum_fusion.refs_3_.refs_2_), channel_id=1, source_target_pairs={{0,2},{1,17},{2,0},{3,19},{4,6},{5,21},{6,4},{7,23},{8,10},{9,25},... | collective-permute-start | bytes 12582920 | tf_op jit(solution)/shard_map/ppermute | solution.py:613
  182.9 13.3 %copy-start.9 = (bf16[2,512,768]{2,1,0:T(8,128)(2,1)}, bf16[2,512,768]{2,1,0:T(8,128)(2,1)S(1)}, u32[]{:S(2)}) copy-start(bf16[2,512,768]{2,1,0:T(8,128)(2,1)S(1)} %collective-permute-done.11.refs_1_) | copy-start | bytes 4718596
  196.2 32.2 %copy-start.29 = (f32[1,7,8,128]{3,1,2,0:T(8,128)S(1)}, f32[1,7,8,128]{3,1,2,0:T(8,128)}, u32[]{:S(2)}) copy-start(f32[1,7,8,128]{3,1,2,0:T(8,128)} %copy-done.28) | copy-start | bytes 86020
  196.2 32.2 %collective-permute-start.14 = (bf16[2,512,2048]{2,1,0:T(8,128)(2,1)}, bf16[2,512,2048]{2,1,0:T(8,128)(2,1)}, u32[]{:S(2)}, u32[]{:S(2)}) collective-permute-start(bf16[2,512,2048]{2,1,0:T(8,128)(2,1)} %copy-done.1), channel_id=1, source_target_pairs={{0,1},{1,0},{2,3},{3,2},{4,5},{5,4},{6,7},{7,6},{8,9},{9,8},{10,11... | collective-permute-start | bytes 12582920 | tf_op jit(solution)/shard_map/ppermute | solution.py:589
  228.3 8.4 %collective-permute-start.15 = (bf16[2,512,2048]{2,1,0:T(8,128)(2,1)}, bf16[2,512,2048]{2,1,0:T(8,128)(2,1)S(1)}, u32[]{:S(2)}, u32[]{:S(2)}) collective-permute-start(bf16[2,512,2048]{2,1,0:T(8,128)(2,1)} %collective-permute-done.13.refs_3_), channel_id=1, source_target_pairs={{0,1},{1,0},{2,3},{3,2},{4,5},{5,4},{6,7},{7,6},{8,9},{9,8},{10,11... | collective-permute-start | bytes 12582920 | tf_op jit(solution)/shard_map/ppermute | solution.py:589
  250.0 10.8 %collective-permute-start.16 = (bf16[2,2,512,1024]{3,2,1,0:T(8,128)(2,1)}, bf16[2,2,512,1024]{3,2,1,0:T(8,128)(2,1)S(1)}, u32[]{:S(2)}, u32[]{:S(2)}) collective-permute-start(bf16[2,2,512,1024]{3,2,1,0:T(8,128)(2,1)} %get-tuple-element.610), channel_id=1, source_target_pairs={{0,1},{1,0},{2,3},{3,2},{4,5},{5,4},{6,7},{7,6},{8,9},{9,8},{10,11... | collective-permute-start | bytes 12582920 | tf_op jit(solution)/shard_map/ppermute | solution.py:589
  260.8 15.8 %collective-permute-start.17 = (bf16[2,2,512,1024]{3,2,1,0:T(8,128)(2,1)}, bf16[2,2,512,1024]{3,2,1,0:T(8,128)(2,1)}, u32[]{:S(2)}, u32[]{:S(2)}) collective-permute-start(bf16[2,2,512,1024]{3,2,1,0:T(8,128)(2,1)} %get-tuple-element.628), channel_id=1, source_target_pairs={{0,1},{1,0},{2,3},{3,2},{4,5},{5,4},{6,7},{7,6},{8,9},{9,8},{10,11... | collective-permute-start | bytes 12582920 | tf_op jit(solution)/shard_map/ppermute | solution.py:589
  274.4 31.3 %collective-permute-start.19 = (bf16[2,512,1024]{2,1,0:T(8,128)(2,1)}, bf16[2,512,1024]{2,1,0:T(8,128)(2,1)S(1)}, u32[]{:S(2)}, u32[]{:S(2)}) collective-permute-start(bf16[2,512,1024]{2,1,0:T(8,128)(2,1)} %get-tuple-element.663), channel_id=1, source_target_pairs={{0,2},{1,17},{2,0},{3,19},{4,6},{5,21},{6,4},{7,23},{8,10},{9,25},... | collective-permute-start | bytes 6291464 | tf_op jit(solution)/shard_map/ppermute | solution.py:613
  287.3 50.5 %collective-permute-start.18 = (bf16[2,512,1024]{2,1,0:T(8,128)(2,1)}, bf16[2,512,1024]{2,1,0:T(8,128)(2,1)S(1)}, u32[]{:S(2)}, u32[]{:S(2)}) collective-permute-start(bf16[2,512,1024]{2,1,0:T(8,128)(2,1)} %get-tuple-element.657), channel_id=1, source_target_pairs={{0,2},{1,17},{2,0},{3,19},{4,6},{5,21},{6,4},{7,23},{8,10},{9,25},... | collective-permute-start | bytes 6291464 | tf_op jit(solution)/shard_map/ppermute | solution.py:613
  288.0 17.8 %copy-start.22 = (bf16[2,512,1024]{2,1,0:T(8,128)(2,1)S(1)}, bf16[2,512,1024]{2,1,0:T(8,128)(2,1)}, u32[]{:S(2)}) copy-start(bf16[2,512,1024]{2,1,0:T(8,128)(2,1)} %get-tuple-element.666) | copy-start | bytes 6291460
  307.7 47.6 %collective-permute-start.22 = (bf16[512,1024]{1,0:T(8,128)(2,1)S(1)}, bf16[512,1024]{1,0:T(8,128)(2,1)S(1)}, u32[]{:S(2)}, u32[]{:S(2)}) collective-permute-start(bf16[512,1024]{1,0:T(8,128)(2,1)S(1)} %get-tuple-element.675.refs_7_), channel_id=1, source_target_pairs={{0,16},{1,3},{2,18},{3,1},{4,20},{5,7},{6,22},{7,5},{8,24},{9,11},... | collective-permute-start | bytes 3145736 | tf_op jit(solution)/shard_map/ppermute | solution.py:613
  323.0 11.2 %copy-start.7 = (bf16[1024,1024]{1,0:T(8,128)(2,1)S(1)}, bf16[1024,1024]{1,0:T(8,128)(2,1)}, u32[]{:S(2)}) copy-start(bf16[1024,1024]{1,0:T(8,128)(2,1)} %fusion.refs_1_) | copy-start | bytes 6291460
  339.8 15.5 %collective-permute-start.23 = (bf16[512,1024]{1,0:T(8,128)(2,1)S(1)}, bf16[512,1024]{1,0:T(8,128)(2,1)S(1)}, u32[]{:S(2)}, u32[]{:S(2)}) collective-permute-start(bf16[512,1024]{1,0:T(8,128)(2,1)S(1)} %get-tuple-element.703.refs_8_), channel_id=1, source_target_pairs={{0,16},{1,3},{2,18},{3,1},{4,20},{5,7},{6,22},{7,5},{8,24},{9,11},... | collective-permute-start | bytes 3145736 | tf_op jit(solution)/shard_map/ppermute | solution.py:613
  340.9 14.5 %copy-start.6 = (bf16[512,1024]{1,0:T(8,128)(2,1)S(1)}, bf16[512,1024]{1,0:T(8,128)(2,1)}, u32[]{:S(2)}) copy-start(bf16[512,1024]{1,0:T(8,128)(2,1)} %get-tuple-element.714.refs_7_) | copy-start | bytes 3145732
  354.6 3.2 collective-permute-start.21
  368.7 53.7 %collective-permute-start.25 = (bf16[2,2,512,1024]{3,2,1,0:T(8,128)(2,1)}, bf16[2,2,512,1024]{3,2,1,0:T(8,128)(2,1)}, u32[]{:S(2)}, u32[]{:S(2)}) collective-permute-start(bf16[2,2,512,1024]{3,2,1,0:T(8,128)(2,1)} %get-tuple-element.762), channel_id=1, source_target_pairs={{0,1},{1,0},{2,3},{3,2},{4,5},{5,4},{6,7},{7,6},{8,9},{9,8},{10,11... | collective-permute-start | bytes 12582920 | tf_op jit(solution)/shard_map/ppermute | solution.py:589
  368.8 10.5 %collective-permute-start.20 = (bf16[2,512,512]{2,1,0:T(8,128)(2,1)}, bf16[2,512,512]{2,1,0:T(8,128)(2,1)}, u32[]{:S(2)}, u32[]{:S(2)}) collective-permute-start(bf16[2,512,512]{2,1,0:T(8,128)(2,1)} %get-tuple-element.705), channel_id=1, source_target_pairs={{0,1},{1,0},{2,3},{3,2},{4,5},{5,4},{6,7},{7,6},{8,9},{9,8},{10,11... | collective-permute-start | bytes 3145736 | tf_op jit(solution)/shard_map/ppermute | solution.py:589
  369.2 42.7 %all-to-all-start.3 = ((bf16[16,32,1024]{2,1,0:T(8,128)(2,1)}), bf16[16,32,1024]{2,1,0:T(8,128)(2,1)S(1)}, u32[]{:S(2)}, u32[]{:S(2)}) async-start(bf16[16,32,1024]{2,1,0:T(8,128)(2,1)} %bitcast.55), calls=%async_computation.3 | async-start | bytes 2097152 | tf_op jit(solution)/shard_map/all_to_all | solution.py:586
  382.7 15.1 %copy-start.23 = (bf16[128,2048]{1,0:T(8,128)(2,1)S(1)}, bf16[128,2048]{1,0:T(8,128)(2,1)}, u32[]{:S(2)}) copy-start(bf16[128,2048]{1,0:T(8,128)(2,1)} %get-tuple-element.731.refs_12_) | copy-start | bytes 1572868
  397.2 25.2 %collective-permute-start.24 = (bf16[2,2,512,512]{3,2,1,0:T(8,128)(2,1)}, bf16[2,2,512,512]{3,2,1,0:T(8,128)(2,1)}, u32[]{:S(2)}, u32[]{:S(2)}) collective-permute-start(bf16[2,2,512,512]{3,2,1,0:T(8,128)(2,1)} %get-tuple-element.761), channel_id=1, source_target_pairs={{0,1},{1,0},{2,3},{3,2},{4,5},{5,4},{6,7},{7,6},{8,9},{9,8},{10,11... | collective-permute-start | bytes 6291464 | tf_op jit(solution)/shard_map/ppermute | solution.py:589
  397.8 24.6 %collective-permute-start.26 = (bf16[128,2048]{1,0:T(8,128)(2,1)S(1)}, bf16[128,2048]{1,0:T(8,128)(2,1)S(1)}, u32[]{:S(2)}, u32[]{:S(2)}) collective-permute-start(bf16[128,2048]{1,0:T(8,128)(2,1)S(1)} %copy-done.23), channel_id=1, source_target_pairs={{0,4},{8,0},{12,8},{4,12},{1,5},{9,1},{13,9},{5,13},{2,6},{10,2},{... | collective-permute-start | bytes 1572872 | tf_op jit(solution)/shard_map/ppermute | solution.py:594
  413.0 68.0 %all-to-all-start.4 = ((bf16[16,128,512]{2,1,0:T(8,128)(2,1)}), bf16[16,128,512]{2,1,0:T(8,128)(2,1)S(1)}, u32[]{:S(2)}, u32[]{:S(2)}) async-start(bf16[16,128,512]{2,1,0:T(8,128)(2,1)} %bitcast.122), calls=%async_computation.4 | async-start | bytes 4194304 | tf_op jit(solution)/shard_map/all_to_all | solution.py:586
  422.4 13.4 %copy-start.12 = (bf16[128,2048]{1,0:T(8,128)(2,1)S(1)}, bf16[128,2048]{1,0:T(8,128)(2,1)}, u32[]{:S(2)}) copy-start(bf16[128,2048]{1,0:T(8,128)(2,1)} %get-tuple-element.784.refs_11_) | copy-start | bytes 1572868
  422.4 15.8 %copy-start.33 = (f32[4,1024]{1,0:T(4,128)S(1)}, f32[4,1024]{1,0:T(4,128)}, u32[]{:S(2)}) copy-start(f32[4,1024]{1,0:T(4,128)} %get-tuple-element.787) | copy-start | bytes 49156
  422.4 15.8 %copy-start.34 = (f32[4,1024]{1,0:T(4,128)S(1)}, f32[4,1024]{1,0:T(4,128)}, u32[]{:S(2)}) copy-start(f32[4,1024]{1,0:T(4,128)} %get-tuple-element.786) | copy-start | bytes 49156
  433.8 44.4 %copy-start.11 = (bf16[128,2048]{1,0:T(8,128)(2,1)S(1)}, bf16[128,2048]{1,0:T(8,128)(2,1)}, u32[]{:S(2)}) copy-start(bf16[128,2048]{1,0:T(8,128)(2,1)} %get-tuple-element.791.refs_10_) | copy-start | bytes 1572868
  433.8 47.1 %collective-permute-start.31 = (bf16[2,512,1536]{2,1,0:T(8,128)(2,1)}, bf16[2,512,1536]{2,1,0:T(8,128)(2,1)}, u32[]{:S(2)}, u32[]{:S(2)}) collective-permute-start(bf16[2,512,1536]{2,1,0:T(8,128)(2,1)} %get-tuple-element.798), channel_id=1, source_target_pairs={{0,2},{1,17},{2,0},{3,19},{4,6},{5,21},{6,4},{7,23},{8,10},{9,25},... | collective-permute-start | bytes 9437192 | tf_op jit(solution)/shard_map/ppermute | solution.py:613
  436.7 41.4 %collective-permute-start.28 = (bf16[128,2048]{1,0:T(8,128)(2,1)}, bf16[128,2048]{1,0:T(8,128)(2,1)S(1)}, u32[]{:S(2)}, u32[]{:S(2)}) collective-permute-start(bf16[128,2048]{1,0:T(8,128)(2,1)} %add_convert_fusion.12), channel_id=1, source_target_pairs={{0,4},{8,0},{12,8},{4,12},{1,5},{9,1},{13,9},{5,13},{2,6},{10,2},{... | collective-permute-start | bytes 1572872 | tf_op jit(solution)/shard_map/ppermute | solution.py:594
  439.5 39.8 %collective-permute-start.27 = (f32[2,4,2,352]{3,2,1,0:T(2,128)S(1)}, f32[2,4,2,352]{3,2,1,0:T(2,128)S(1)}, u32[]{:S(2)}, u32[]{:S(2)}) collective-permute-start(f32[2,4,2,352]{3,2,1,0:T(2,128)S(1)} %bitcast.150), channel_id=1, source_target_pairs={{0,1},{1,0},{2,3},{3,2},{4,5},{5,4},{6,7},{7,6},{8,9},{9,8},{10,11... | collective-permute-start | bytes 67592 | tf_op jit(solution)/shard_map/ppermute | solution.py:589
  479.1 14.8 %collective-permute-start.29 = (bf16[128,2048]{1,0:T(8,128)(2,1)}, bf16[128,2048]{1,0:T(8,128)(2,1)}, u32[]{:S(2)}, u32[]{:S(2)}) collective-permute-start(bf16[128,2048]{1,0:T(8,128)(2,1)} %add_convert_fusion.11), channel_id=1, source_target_pairs={{0,4},{8,0},{12,8},{4,12},{1,5},{9,1},{13,9},{5,13},{2,6},{10,2},{... | collective-permute-start | bytes 1572872 | tf_op jit(solution)/shard_map/ppermute | solution.py:594
  479.4 6.4 %collective-permute-start.30 = (f32[2,4,352]{2,1,0:T(4,128)S(1)}, f32[2,4,352]{2,1,0:T(4,128)S(1)}, u32[]{:S(2)}, u32[]{:S(2)}) collective-permute-start(f32[2,4,352]{2,1,0:T(4,128)S(1)} %bitcast.152), channel_id=1, source_target_pairs={{0,2},{1,3},{2,0},{3,1},{4,6},{5,7},{6,4},{7,5},{8,10},{9,11},{10,... | collective-permute-start | bytes 33800 | tf_op jit(solution)/shard_map/ppermute | solution.py:589
  480.9 13.0 %copy-start.13 = (bf16[128,2048]{1,0:T(8,128)(2,1)S(1)}, bf16[128,2048]{1,0:T(8,128)(2,1)}, u32[]{:S(2)}) copy-start(bf16[128,2048]{1,0:T(8,128)(2,1)} %get-tuple-element.803.refs_9_) | copy-start | bytes 1572868
  484.7 20.5 %collective-permute-start.32 = (bf16[512,1536]{1,0:T(8,128)(2,1)S(1)}, bf16[512,1536]{1,0:T(8,128)(2,1)S(1)}, u32[]{:S(2)}, u32[]{:S(2)}) collective-permute-start(bf16[512,1536]{1,0:T(8,128)(2,1)S(1)} %get-tuple-element.899), channel_id=1, source_target_pairs={{0,16},{1,3},{2,18},{3,1},{4,20},{5,7},{6,22},{7,5},{8,24},{9,11},... | collective-permute-start | bytes 4718600 | tf_op jit(solution)/shard_map/ppermute | solution.py:613
  505.7 11.4 %collective-permute-start.33 = (bf16[128,1536]{1,0:T(8,128)(2,1)S(1)}, bf16[128,1536]{1,0:T(8,128)(2,1)S(1)}, u32[]{:S(2)}, u32[]{:S(2)}) collective-permute-start(bf16[128,1536]{1,0:T(8,128)(2,1)S(1)} %get-tuple-element.919), channel_id=1, source_target_pairs={{0,4},{8,0},{12,8},{4,12},{1,5},{9,1},{13,9},{5,13},{2,6},{10,2},{... | collective-permute-start | bytes 1179656 | tf_op jit(solution)/shard_map/ppermute | solution.py:594
  509.3 3.6 collective-permute-start.34
  517.1 14.4 %collective-permute-start.35 = (bf16[128,1536]{1,0:T(8,128)(2,1)S(1)}, bf16[128,1536]{1,0:T(8,128)(2,1)S(1)}, u32[]{:S(2)}, u32[]{:S(2)}) collective-permute-start(bf16[128,1536]{1,0:T(8,128)(2,1)S(1)} %add_convert_fusion.14), channel_id=1, source_target_pairs={{0,4},{8,0},{12,8},{4,12},{1,5},{9,1},{13,9},{5,13},{2,6},{10,2},{... | collective-permute-start | bytes 1179656 | tf_op jit(solution)/shard_map/ppermute | solution.py:594
  524.9 4.9 collective-permute-start.36
  525.9 5.5 %collective-permute-start.37 = (f32[352]{0:T(512)S(1)}, f32[352]{0:T(512)S(1)}, u32[]{:S(2)}, u32[]{:S(2)}) collective-permute-start(f32[352]{0:T(512)S(1)} %get-tuple-element.897), channel_id=1, source_target_pairs={{0,12},{8,4},{12,0},{4,8},{1,13},{9,5},{13,1},{5,9},{2,14},{10,6},... | collective-permute-start | bytes 4232 | tf_op jit(solution)/shard_map/ppermute | solution.py:594
  527.9 3.6 collective-permute-start.38
  531.6 8.7 %collective-permute-start.39 = (bf16[128,1536]{1,0:T(8,128)(2,1)S(1)}, bf16[128,1536]{1,0:T(8,128)(2,1)S(1)}, u32[]{:S(2)}, u32[]{:S(2)}) collective-permute-start(bf16[128,1536]{1,0:T(8,128)(2,1)S(1)} %add_convert_fusion.13), channel_id=1, source_target_pairs={{0,4},{8,0},{12,8},{4,12},{1,5},{9,1},{13,9},{5,13},{2,6},{10,2},{... | collective-permute-start | bytes 1179656 | tf_op jit(solution)/shard_map/ppermute | solution.py:594
  (23 other events, 80.3 us)

commit v6 on v5

--- a/solution.py
+++ b/solution.py
@@ -629,7 +629,10 @@
 
     def gather_two(own, moved):
         first = line.plain(lambda a, m: jnp.stack([a, *m]), own, moved)
-        return first, over(first, second_pairs) if fs == 2 else over_tp(first, 2)
+        return first, second_move(first)
+
+    def second_move(first):
+        return over(first, second_pairs) if fs == 2 else over_tp(first, 2)
 
     def gather_near(first, second):
         first = line.gate(first)
@@ -744,15 +747,20 @@
         ),
         both, att, vectors,
     )
-    ffn = gather_two(*ffn)
+    def halves(own, moved):
+        cuts = [slice(0, hidden), slice(hidden, None)]
+        return [jnp.stack([p[:, cc] for p in (own, *moved)]) for cc in cuts]
+
+    expand, shrink = [(p, second_move(p)) for p in line.plain(halves, *ffn)]
     others = [[over_tp(project[k ^ (d & 1)], d) for d in range(1, share)] for k in range(2)]
     others = line.gate(others)
     inner = [line(attend_forward, project[0], others[0])]
-    ffn = gather_near(*ffn)
+    expand = gather_near(*expand)
     inner.append(line(attend_forward, project[1], others[1]))
+    shrink = gather_near(*shrink)
     probs, attended = zip(*inner)
 
-    ffn = gather_three(*ffn)
+    expand = gather_three(*expand)
     second, normed_two, normed_two_t = line(
         lambda *o: down(
             *o[:2], "second", o[2], o[3], heads_width, side // heads_width, functools.partial(norm_finish, True),
@@ -772,17 +780,18 @@
 
     def hidden_back(k):
         return lambda *o: up_grad(
-            *o[:2], "hidden_back", *o[2:5], k, 1, slope_step, [o[5]], [(count, BF16), (1, F32)], *o[6:]
+            *o[:2], "hidden_back", *o[2:5], k, 0, slope_step, [o[5]], [(count, BF16), (1, F32)], *o[6:]
         )
 
+    shrink = gather_three(*shrink)
     activated, slope, grad_expanded, wide = ([None, None] for _ in range(4))
-    activated[1], slope[1], other = line(hidden_step(1), normed_two, branch_low_t, ffn[1], widen[1])
+    activated[1], slope[1], other = line(hidden_step(1), normed_two, branch_low_t, expand[1], widen[1])
     other = over_tp(other, 1)
-    grad_expanded[1], wide[1], other_two = line(hidden_back(1), branch_low, normed_two_t, ffn[1], slope[1])
+    grad_expanded[1], wide[1], other_two = line(hidden_back(1), branch_low, normed_two_t, shrink[1], slope[1])
     other_two = over_tp(other_two, 1)
-    activated[0], slope[0], *sums = line(hidden_step(0), normed_two, branch_low_t, ffn[0], widen[0], [other])
+    activated[0], slope[0], *sums = line(hidden_step(0), normed_two, branch_low_t, expand[0], widen[0], [other])
     shrink_sums = reduce_one(sums)
-    grad_expanded[0], wide[0], *sums = line(hidden_back(0), branch_low, normed_two_t, ffn[0], slope[0], [other_two])
+    grad_expanded[0], wide[0], *sums = line(hidden_back(0), branch_low, normed_two_t, shrink[0], slope[0], [other_two])
     expand_sums = reduce_one(sums)
     grad_second, attn_low, attn_low_t, sums_two, *grad_attended = line(
         lambda *o: down(
@@ -790,7 +799,7 @@
             [o[4], o[5], o[6][4:5]], [(act, F32), (act, BF16), (turned, BF16), ((4, width), F32)],
             then_up(1, o[7], heads_width, side // heads_width, heads_width // 2)(count),
         ),
-        grad_expanded, ffn, second, branch_low, vectors, att,
+        grad_expanded, expand, second, branch_low, vectors, att,
     )
     shrink_sums = reduce_two(*shrink_sums)
     inner = [None, None]
@@ -798,9 +807,9 @@
 
     def layer_end(roles, after, a, w, t, v):
         ends = jnp.stack([v[6], jnp.full((width,), live)])
-        return down(roles, after, "layer_out", a, w, hidden, 1, out_finish, [t, ends], [(act, BF16)])
-
-    (layer_out,) = line(layer_end, activated, ffn, second, vectors)
+        return down(roles, after, "layer_out", a, w, hidden, 0, out_finish, [t, ends], [(act, BF16)])
+
+    (layer_out,) = line(layer_end, activated, shrink, second, vectors)
     layer_out = line.plain(lambda a, p: mxu(a, p, 1, 1).astype(BF16), layer_out, permute)
     layer_out = to_group(layer_out.reshape(group * fine, width))
     expand_sums = reduce_two(*expand_sums)

time: 550 us -> 541 us (0.984)
  waiting for transfers between devices: 162 us -> 148 us
    ppermute x10 -> x11, waiting for transfers between devices: 27.5 us -> 16 us  [over(): return lax.ppermute(array, ALL, [(i, target(i)) for i in range(devices)])]
    unnamed x107 -> x115, local copies, waits for them, and re-layouts: 16.7 us -> 18 us
    ppermute x14 -> x16, starting transfers between devices: 10.8 us -> 12 us  [over_tp(): return lax.ppermute(array, 'tp', [(i, i ^ flip) for i in range(ts)])]
    ppermute x10 -> x11, starting transfers between devices: 12.5 us -> 13.2 us  [over(): return lax.ppermute(array, ALL, [(i, target(i)) for i in range(devices)])]
  transfers between devices with their start and end apart: 45 -> 48, of which waited for: 15 -> 15; matrix products, arithmetic and copies ran while one was open for 11% -> 11% of each run, Pallas kernels for 32% -> 35%
where the time goes in v6:
time: 541 us; the launch traced here: 536 us
  Pallas kernels  196 us (36%)
  waiting for transfers between devices  148 us (27%)
  starting transfers between devices  92.8 us (17%)
  local copies, waits for them, and re-layouts  47.1 us (9%)
  other arithmetic  31 us (6%)
  between operations  16.3 us (3%)
    pallas_call x17, Pallas kernels, apply(): pl.pallas_call(run, grid_spec=pltpu.PrefetchScalarGridSpec(num_scalar_pre...  196 us
    ppermute x15, waiting for transfers between devices, over_ctx(): lax.ppermute(array, 'ctx', [(ring[i], ring[(i + d) % cs]) for i in range(...  75.6 us
    all_to_all x4, starting transfers between devices, to_group(): return lax.all_to_all(array, ('ctx', 'tp'), 0, 0, tiled=True)  35.1 us
    all_to_all x4, waiting for transfers between devices, to_group(): return lax.all_to_all(array, ('ctx', 'tp'), 0, 0, tiled=True)  27.5 us
    ppermute x15, starting transfers between devices, over_ctx(): lax.ppermute(array, 'ctx', [(ring[i], ring[(i + d) % cs]) for i in range(...  27.1 us
    all_to_all x1, waiting for transfers between devices, on_device(): packed = lax.all_to_all(packed, ALL, 0, 0, tiled=True)  26.5 us
    unnamed x115, local copies, waits for them, and re-layouts  18 us
    ppermute x11, waiting for transfers between devices, over(): return lax.ppermute(array, ALL, [(i, target(i)) for i in range(devices)])  16 us
  transfers between devices with their start and end apart: 48, of which 15 were waited for; matrix products, arithmetic and copies ran while one was open for 11% of the time, Pallas kernels for 35%

profile of v6, /device:TPU:0, one launch (start us, length us, event | category | flops | bytes accessed | tf_op | source)
XLA Modules:
  0.0 535.5 jit_solution(9479232695165172634)
XLA Ops:
  3.8 4.1 collective-permute-start
  11.5 4.5 all-to-all-start
  16.7 1.4 pad_maximum_fusion.1
  18.1 1.5 copy.69
  19.6 26.5 %all-to-all-done = f32[32,1,352]{2,1,0:T(1,128)S(1)} async-done(((f32[32,1,352]{2,1,0:T(1,128)}), f32[32,1,352]{2,1,0:T(1,128)S(1)}, u32[]{:S(2)}, u32[]{:S(2)}) %all-to-all-start) | async-done | bytes 45088 | tf_op jit(solution)/shard_map/all_to_all | solution.py:707
  48.6 1.6 collective-permute-start.3
  50.2 4.3 all-to-all-start.1
  54.5 10.9 %collective-permute-done.3 = bf16[128,2048]{1,0:T(8,128)(2,1)} collective-permute-done((bf16[128,2048]{1,0:T(8,128)(2,1)S(1)}, bf16[128,2048]{1,0:T(8,128)(2,1)}, u32[]{:S(2)}, u32[]{:S(2)}) %collective-permute-start.3) | collective-permute-done | bytes 524320 | tf_op jit(solution)/shard_map/ppermute | solution.py:594
  65.4 3.0 collective-permute-done.5
  68.5 2.2 pad_maximum_fusion.refs_8_.refs_2_.refs_7_.refs_9_.refs_1_
  71.5 5.2 collective-permute-start.7
  82.5 9.5 %collective-permute-done.4 = bf16[128,2048]{1,0:T(8,128)(2,1)} collective-permute-done((bf16[128,2048]{1,0:T(8,128)(2,1)}, bf16[128,2048]{1,0:T(8,128)(2,1)}, u32[]{:S(2)}, u32[]{:S(2)}) %collective-permute-start.4) | collective-permute-done | bytes 524320 | tf_op jit(solution)/shard_map/ppermute | solution.py:594
  95.3 2.2 fusion.refs_1_
  97.5 15.9 %all-to-all-start.2 = ((bf16[16,128,512]{2,1,0:T(8,128)(2,1)}), bf16[16,128,512]{2,1,0:T(8,128)(2,1)}, u32[]{:S(2)}, u32[]{:S(2)}) async-start(bf16[16,128,512]{2,1,0:T(8,128)(2,1)} %bitcast.123), calls=%async_computation.2 | async-start | bytes 4194304 | tf_op jit(solution)/shard_map/all_to_all | solution.py:586
  119.1 5.8 %arrived.1 = (bf16[512,1024]{1,0:T(8,128)(2,1)}, bf16[1024,512]{1,0:T(8,128)(2,1)}, f32[8,128]{1,0:T(8,128)}) custom-call(s32[2]{0:T(128)} %pad_add_fusion.roles_ref, bf16[512,1024]{1,0:T(8,128)(2,1)} %bitcast.8.refs_0_, bf16[1024,1024]{1,0:T(8,128)(2,1)} %fusion.refs_1_, f32[1,1]{1,0:T(1,128)} %bitcast.26.refs_2_, bf16[128,1536]{1,0:T(8,128)(2,1)} %copy-done.23, ...), custom_call_target="tpu_custom_call" | custom-call | flops 1 | bytes 1 | tf_op jit(solution)/shard_map/arrived/pallas_call | solution.py:36
  127.2 27.5 %all-to-all-done.2 = bf16[16,128,512]{2,1,0:T(8,128)(2,1)} async-done(((bf16[16,128,512]{2,1,0:T(8,128)(2,1)}), bf16[16,128,512]{2,1,0:T(8,128)(2,1)}, u32[]{:S(2)}, u32[]{:S(2)}) %all-to-all-start.2) | async-done | bytes 2097184 | tf_op jit(solution)/shard_map/all_to_all | solution.py:586
  154.7 1.7 constant_dynamic-slice_fusion.26
  160.2 14.7 %joined.1 = (f32[512,1024]{1,0:T(8,128)}, bf16[512,1024]{1,0:T(8,128)(2,1)}, bf16[1024,512]{1,0:T(8,128)(2,1)}, bf16[2,512,768]{2,1,0:T(8,128)(2,1)}, bf16[2,512,768]{2,1,0:T(8,128)(2,1)}, /*index=5*/f32[8,128]{1,0:T(8,128)}) custom-call(s32[2]{0:T(128)} %pad_add_fusion.roles_ref, bf16[2,512,512]{2,1,0:T(8,128)(2,1)} %pad_maximum_fusion.8.refs_0_.refs_15_.refs_1_.refs_3_, ...), custom_call_target="tpu_custom_call" | custom-call | flops 1 | bytes 1 | tf_op jit(solution)/shard_map/joined/pallas_call | solution.py:36
  175.7 1.9 slice_bitcast_fusion
  178.3 3.4 collective-permute-start.13
  181.7 1.5 pad_maximum_fusion.3.refs_4_.refs_2_
  184.4 13.3 %attend_forward.2 = (bf16[2,4,1024,512]{3,2,1,0:T(8,128)(2,1)}, bf16[2,512,256]{2,1,0:T(8,128)(2,1)}, f32[8,128]{1,0:T(8,128)}) custom-call(s32[2]{0:T(128)} %pad_add_fusion.roles_ref, bf16[2,512,768]{2,1,0:T(8,128)(2,1)} %get-tuple-element.711.refs_0_, bf16[2,512,768]{2,1,0:T(8,128)(2,1)} %copy-done.14, f32[8,128]{1,0:T(8,128)} %get-tuple-element.581.refs_2_, ...), custom_call_target="tpu_custom_call" | custom-call | flops 1 | bytes 1 | tf_op jit(solution)/shard_map/attend_forward/pallas_call | solution.py:36
  198.6 13.8 %attend_forward.3 = (bf16[2,4,1024,512]{3,2,1,0:T(8,128)(2,1)}, bf16[2,512,256]{2,1,0:T(8,128)(2,1)}, f32[8,128]{1,0:T(8,128)}) custom-call(s32[2]{0:T(128)} %pad_add_fusion.roles_ref, bf16[2,512,768]{2,1,0:T(8,128)(2,1)} %get-tuple-element.684.refs_0_, bf16[2,512,768]{2,1,0:T(8,128)(2,1)} %copy-done.13, f32[8,128]{1,0:T(8,128)} %get-tuple-element.592.refs_2_), custom_call_target="tpu_custom_call" | custom-call | flops 1 | bytes 1 | tf_op jit(solution)/shard_map/attend_forward/pallas_call | solution.py:36
  213.7 7.9 %second.1 = (f32[512,1024]{1,0:T(8,128)}, bf16[512,1024]{1,0:T(8,128)(2,1)}, bf16[1024,512]{1,0:T(8,128)(2,1)}, f32[8,128]{1,0:T(8,128)}) custom-call(s32[2]{0:T(128)} %pad_add_fusion.roles_ref, bf16[2,512,256]{2,1,0:T(8,128)(2,1)} %get-tuple-element.783.refs_0_.refs_3_.refs_5_.refs_7_, bf16[2,512,256]{2,1,0:T(8,128)(2,1)} %get-tuple-element.740.refs_1_.refs_3_, ...), custom_call_target="tpu_custom_call" | custom-call | flops 1 | bytes 1 | tf_op jit(solution)/shard_map/second/pallas_call | solution.py:36
  221.6 6.8 %collective-permute-done.15.refs_3_ = bf16[2,512,1024]{2,1,0:T(8,128)(2,1)} collective-permute-done((bf16[2,512,1024]{2,1,0:T(8,128)(2,1)S(1)}, bf16[2,512,1024]{2,1,0:T(8,128)(2,1)}, u32[]{:S(2)}, u32[]{:S(2)}) %collective-permute-start.15) | collective-permute-done | bytes 2097184 | tf_op jit(solution)/shard_map/ppermute | solution.py:613
  229.7 11.3 %hidden.2 = (bf16[2,512,1024]{2,1,0:T(8,128)(2,1)}, bf16[2,512,1024]{2,1,0:T(8,128)(2,1)}, bf16[2,2,512,1024]{3,2,1,0:T(8,128)(2,1)}, f32[8,128]{1,0:T(8,128)}) custom-call(s32[2]{0:T(128)} %pad_add_fusion.roles_ref, bf16[512,1024]{1,0:T(8,128)(2,1)} %get-tuple-element.636.refs_0_, bf16[1024,512]{1,0:T(8,128)(2,1)} %get-tuple-element.637.refs_1_, ...), custom_call_target="tpu_custom_call" | custom-call | flops 1 | bytes 1 | tf_op jit(solution)/shard_map/hidden/pallas_call | solution.py:36
  242.8 10.3 %hidden_back.2 = (bf16[2,512,1024]{2,1,0:T(8,128)(2,1)}, f32[2,1,1024]{2,1,0:T(1,128)}, bf16[2,2,512,1024]{3,2,1,0:T(8,128)(2,1)}, f32[8,128]{1,0:T(8,128)}) custom-call(s32[2]{0:T(128)} %pad_add_fusion.roles_ref, bf16[512,1024]{1,0:T(8,128)(2,1)} %get-tuple-element.664.refs_0_.refs_7_, bf16[1024,512]{1,0:T(8,128)(2,1)} %get-tuple-element.647.refs_1_, ...), custom_call_target="tpu_custom_call" | custom-call | flops 1 | bytes 1 | tf_op jit(solution)/shard_map/hidden_back/pallas_call | solution.py:36
  253.2 11.6 %hidden.3 = (bf16[2,512,1024]{2,1,0:T(8,128)(2,1)}, bf16[2,512,1024]{2,1,0:T(8,128)(2,1)}, bf16[2,512,1024]{2,1,0:T(8,128)(2,1)}, bf16[2,512,1024]{2,1,0:T(8,128)(2,1)}, f32[8,128]{1,0:T(8,128)}) custom-call(s32[2]{0:T(128)} %pad_add_fusion.roles_ref, bf16[512,1024]{1,0:T(8,128)(2,1)} %get-tuple-element.636.refs_0_, ...), custom_call_target="tpu_custom_call" | custom-call | flops 1 | bytes 1 | tf_op jit(solution)/shard_map/hidden/pallas_call | solution.py:36
  264.8 2.0 collective-permute-start.22
  266.8 2.0 copy-done.18
  268.8 10.8 %hidden_back.3 = (bf16[2,512,1024]{2,1,0:T(8,128)(2,1)}, f32[2,1,1024]{2,1,0:T(1,128)}, bf16[2,512,1024]{2,1,0:T(8,128)(2,1)}, bf16[2,512,1024]{2,1,0:T(8,128)(2,1)}, f32[8,128]{1,0:T(8,128)}) custom-call(s32[2]{0:T(128)} %pad_add_fusion.roles_ref, bf16[512,1024]{1,0:T(8,128)(2,1)} %get-tuple-element.664.refs_0_.refs_7_, ...), custom_call_target="tpu_custom_call" | custom-call | flops 1 | bytes 1 | tf_op jit(solution)/shard_map/hidden_back/pallas_call | solution.py:36
  280.3 17.8 %second_back.1 = (f32[512,1024]{1,0:T(8,128)}, bf16[512,1024]{1,0:T(8,128)(2,1)}, bf16[1024,512]{1,0:T(8,128)(2,1)}, f32[4,1024]{1,0:T(4,128)}, bf16[2,512,256]{...) custom-call(s32[2]{0:T(128)} %pad_add_fusion.roles_ref, ...), custom_call_target="tpu_custom_call" | custom-call | flops 1 | bytes 1 | tf_op jit(solution)/shard_map/second_back/pallas_call | solution.py:36
  298.1 2.1 fusion.4
  301.2 13.7 %attend_backward.2 = (bf16[2,512,768]{2,1,0:T(8,128)(2,1)}, bf16[2,512,512]{2,1,0:T(8,128)(2,1)}, f32[8,128]{1,0:T(8,128)}) custom-call(s32[2]{0:T(128)} %pad_add_fusion.roles_ref, bf16[2,512,768]{2,1,0:T(8,128)(2,1)} %get-tuple-element.684.refs_0_, bf16[2,512,768]{2,1,0:T(8,128)(2,1)} %copy-done.13, bf16[2,4,1024,512]{3,2,1,0:T(8,128)(2,1)} %get-tuple-element.686.refs_2_, ...), custom_call_target="tpu_custom_call" | custom-call | flops 1 | bytes 1 | tf_op jit(solution)/shard_map/attend_backward/pallas_call | solution.py:36
  315.5 11.2 %layer_out.1 = (bf16[512,1024]{1,0:T(8,128)(2,1)}, f32[8,128]{1,0:T(8,128)}) custom-call(s32[2]{0:T(128)} %pad_add_fusion.roles_ref, bf16[2,512,1024]{2,1,0:T(8,128)(2,1)} %get-tuple-element.693.refs_0_, bf16[2,512,1024]{2,1,0:T(8,128)(2,1)} %get-tuple-element.694.refs_1_, bf16[2,512,1024]{2,1,0:T(8,128)(2,1)} %pad_maximum_fusion.3.refs_4_.refs_2_, ...), custom_call_target="tpu_custom_call" | custom-call | flops 1 | bytes 1 | tf_op jit(solution)/shard_map/layer_out/pallas_call | solution.py:36
  326.7 3.6 convolution_convert_fusion.refs_6_
  330.3 2.0 fusion.6
  333.3 13.8 %attend_backward.3 = (bf16[2,512,768]{2,1,0:T(8,128)(2,1)}, bf16[2,512,512]{2,1,0:T(8,128)(2,1)}, f32[8,128]{1,0:T(8,128)}) custom-call(s32[2]{0:T(128)} %pad_add_fusion.roles_ref, bf16[2,512,768]{2,1,0:T(8,128)(2,1)} %get-tuple-element.711.refs_0_, bf16[2,512,768]{2,1,0:T(8,128)(2,1)} %copy-done.14, bf16[2,4,1024,512]{3,2,1,0:T(8,128)(2,1)} %get-tuple-element.713.refs_2_, ...), custom_call_target="tpu_custom_call" | custom-call | flops 1 | bytes 1 | tf_op jit(solution)/shard_map/attend_backward/pallas_call | solution.py:36
  348.7 1.4 pad_maximum_fusion.10
  352.4 8.6 %weight_grad.2 = (bf16[2,2,512,1024]{3,2,1,0:T(8,128)(2,1)}, f32[8,128]{1,0:T(8,128)}) custom-call(s32[2]{0:T(128)} %pad_add_fusion.roles_ref, bf16[1024,512]{1,0:T(8,128)(2,1)} %get-tuple-element.782.refs_0_.refs_2_.refs_4_.refs_6_, bf16[2,512,256]{2,1,0:T(8,128)(2,1)} %get-tuple-element.740.refs_1_.refs_3_, ...), custom_call_target="tpu_custom_call" | custom-call | flops 1 | bytes 1 | tf_op jit(solution)/shard_map/weight_grad/pallas_call | solution.py:36
  361.7 10.0 %all-to-all-start.3 = ((bf16[16,32,1024]{2,1,0:T(8,128)(2,1)}), bf16[16,32,1024]{2,1,0:T(8,128)(2,1)S(1)}, u32[]{:S(2)}, u32[]{:S(2)}) async-start(bf16[16,32,1024]{2,1,0:T(8,128)(2,1)} %bitcast.57), calls=%async_computation.3 | async-start | bytes 2097152 | tf_op jit(solution)/shard_map/all_to_all | solution.py:586
  371.8 1.5 add_convert_fusion.3
  375.1 14.5 %first_back.1 = (bf16[512,1024]{1,0:T(8,128)(2,1)}, bf16[1024,512]{1,0:T(8,128)(2,1)}, f32[4,1024]{1,0:T(4,128)}, bf16[2,2,512,512]{3,2,1,0:T(8,128)(2,1)}, f32[8,128]{1,0:T(8,128)}) custom-call(s32[2]{0:T(128)} %pad_add_fusion.roles_ref, bf16[2,512,768]{2,1,0:T(8,128)(2,1)} %pad_maximum_fusion.7.refs_0_.refs_11_.refs_9_, ...), custom_call_target="tpu_custom_call" | custom-call | flops 1 | bytes 1 | tf_op jit(solution)/shard_map/first_back/pallas_call | solution.py:36
  390.2 4.0 collective-permute-start.29
  394.2 6.3 %inputs_back.1 = (bf16[2,512,512]{2,1,0:T(8,128)(2,1)}, bf16[2,512,512]{2,1,0:T(8,128)(2,1)}, f32[8,128]{1,0:T(8,128)}) custom-call(s32[2]{0:T(128)} %pad_add_fusion.roles_ref, bf16[512,1024]{1,0:T(8,128)(2,1)} %get-tuple-element.768.refs_0_, bf16[2,512,1536]{2,1,0:T(8,128)(2,1)} %copy-done, ...), custom_call_target="tpu_custom_call" | custom-call | flops 1 | bytes 1 | tf_op jit(solution)/shard_map/inputs_back/pallas_call | solution.py:36
  402.9 1.5 copy.72
  405.4 4.8 all-to-all-start.4
  414.9 10.8 %weight_grad.3 = (bf16[2,512,1536]{2,1,0:T(8,128)(2,1)}, bf16[2,512,1536]{2,1,0:T(8,128)(2,1)}, f32[8,128]{1,0:T(8,128)}) custom-call(s32[2]{0:T(128)} %pad_add_fusion.roles_ref, bf16[1024,512]{1,0:T(8,128)(2,1)} %get-tuple-element.780.refs_0_.refs_2_, bf16[2,512,512]{2,1,0:T(8,128)(2,1)} %pad_maximum_fusion.8.refs_0_.refs_15_.refs_1_.refs_3_, ...), custom_call_target="tpu_custom_call" | custom-call | flops 1 | bytes 1 | tf_op jit(solution)/shard_map/weight_grad/pallas_call | solution.py:36
  425.7 2.0 collective-permute-start.34
  428.6 1.5 collective-permute-start.31
  432.4 38.2 %collective-permute-done.31 = bf16[128,2048]{1,0:T(8,128)(2,1)S(1)} collective-permute-done((bf16[128,2048]{1,0:T(8,128)(2,1)}, bf16[128,2048]{1,0:T(8,128)(2,1)S(1)}, u32[]{:S(2)}, u32[]{:S(2)}) %collective-permute-start.31) | collective-permute-done | bytes 524320 | tf_op jit(solution)/shard_map/ppermute | solution.py:594
  471.8 1.6 collective-permute-start.33
  473.4 3.7 fusion.2
  478.2 8.1 %collective-permute-done.32 = bf16[128,2048]{1,0:T(8,128)(2,1)} collective-permute-done((bf16[128,2048]{1,0:T(8,128)(2,1)}, bf16[128,2048]{1,0:T(8,128)(2,1)}, u32[]{:S(2)}, u32[]{:S(2)}) %collective-permute-start.32) | collective-permute-done | bytes 524320 | tf_op jit(solution)/shard_map/ppermute | solution.py:594
  488.9 2.5 fusion.34
  491.4 6.2 %collective-permute-done.35 = bf16[512,1536]{1,0:T(8,128)(2,1)S(1)} collective-permute-done((bf16[512,1536]{1,0:T(8,128)(2,1)S(1)}, bf16[512,1536]{1,0:T(8,128)(2,1)S(1)}, u32[]{:S(2)}, u32[]{:S(2)}) %collective-permute-start.35) | collective-permute-done | bytes 1572896 | tf_op jit(solution)/shard_map/ppermute | solution.py:613
  498.1 3.7 collective-permute-start.36
  502.7 2.6 collective-permute-done.37
  505.4 3.2 collective-permute-done.36
  508.7 2.5 collective-permute-start.38
  517.2 1.9 collective-permute-start.40
  519.1 1.9 collective-permute-start.41
  522.8 2.5 collective-permute-start.42
  527.6 4.0 collective-permute-done.42
  (277 shorter events, 66.5 us)
Async XLA Ops:
  0.6 16.0 %copy-start.31 = (bf16[4,2,256,256]{3,2,1,0:T(8,128)(2,1)S(1)}, bf16[4,2,256,256]{3,2,1,0:T(8,128)(2,1)}, u32[]{:S(2)}) copy-start(bf16[4,2,256,256]{3,2,1,0:T(8,128)(2,1)} %param.30) | copy-start | bytes 3145732
  3.8 42.9 %copy-start.23 = (bf16[128,1536]{1,0:T(8,128)(2,1)}, bf16[128,1536]{1,0:T(8,128)(2,1)S(1)}, u32[]{:S(2)}) copy-start(bf16[128,1536]{1,0:T(8,128)(2,1)S(1)} %pad_maximum_fusion.11.refs_3_) | copy-start | bytes 1179652
  3.8 42.9 %collective-permute-start = (bf16[128,1536]{1,0:T(8,128)(2,1)S(1)}, bf16[128,1536]{1,0:T(8,128)(2,1)S(1)}, u32[]{:S(2)}, u32[]{:S(2)}) collective-permute-start(bf16[128,1536]{1,0:T(8,128)(2,1)S(1)} %pad_maximum_fusion.11.refs_3_), channel_id=1, source_target_pairs={{0,8},{8,12},{12,4},{4,0},{1,9},{9,13},{13,5},{5,1},{2,10},{10,14}... | collective-permute-start | bytes 1179656 | tf_op jit(solution)/shard_map/ppermute | solution.py:594
  7.9 38.8 %collective-permute-start.1 = (bf16[128,1536]{1,0:T(8,128)(2,1)S(1)}, bf16[128,1536]{1,0:T(8,128)(2,1)S(1)}, u32[]{:S(2)}, u32[]{:S(2)}) collective-permute-start(bf16[128,1536]{1,0:T(8,128)(2,1)S(1)} %pad_maximum_fusion.11.refs_3_), channel_id=1, source_target_pairs={{0,12},{8,4},{12,0},{4,8},{1,13},{9,5},{13,1},{5,9},{2,14},{10,6},... | collective-permute-start | bytes 1179656 | tf_op jit(solution)/shard_map/ppermute | solution.py:594
  9.2 37.5 %collective-permute-start.2 = (bf16[128,1536]{1,0:T(8,128)(2,1)S(1)}, bf16[128,1536]{1,0:T(8,128)(2,1)}, u32[]{:S(2)}, u32[]{:S(2)}) collective-permute-start(bf16[128,1536]{1,0:T(8,128)(2,1)S(1)} %pad_maximum_fusion.11.refs_3_), channel_id=1, source_target_pairs={{0,4},{8,0},{12,8},{4,12},{1,5},{9,1},{13,9},{5,13},{2,6},{10,2},{... | collective-permute-start | bytes 1179656 | tf_op jit(solution)/shard_map/ppermute | solution.py:594
  11.5 34.6 %all-to-all-start = ((f32[32,1,352]{2,1,0:T(1,128)}), f32[32,1,352]{2,1,0:T(1,128)S(1)}, u32[]{:S(2)}, u32[]{:S(2)}) async-start(f32[32,1,352]{2,1,0:T(1,128)} %broadcast_in_dim.8), calls=%async_computation | async-start | bytes 98304 | tf_op jit(solution)/shard_map/all_to_all | solution.py:707
  19.6 30.6 %copy-start.24 = (bf16[128,2048]{1,0:T(8,128)(2,1)}, bf16[128,2048]{1,0:T(8,128)(2,1)S(1)}, u32[]{:S(2)}) copy-start(bf16[128,2048]{1,0:T(8,128)(2,1)S(1)} %constant_dynamic-update-slice_fusion.refs_6_) | copy-start | bytes 1572868
  47.9 20.6 %copy-start.12 = (bf16[512,1536]{1,0:T(8,128)(2,1)}, bf16[512,1536]{1,0:T(8,128)(2,1)S(1)}, u32[]{:S(2)}) copy-start(bf16[512,1536]{1,0:T(8,128)(2,1)S(1)} %constant_dynamic-update-slice_fusion.2.refs_7_) | copy-start | bytes 4718596
  47.9 20.6 %collective-permute-start.5 = (bf16[512,1536]{1,0:T(8,128)(2,1)S(1)}, bf16[512,1536]{1,0:T(8,128)(2,1)}, u32[]{:S(2)}, u32[]{:S(2)}) collective-permute-start(bf16[512,1536]{1,0:T(8,128)(2,1)S(1)} %constant_dynamic-update-slice_fusion.2.refs_7_), channel_id=1, source_target_pairs={{0,16},{1,3},{2,18},{3,1},{4,20},{5,7},{6,22},{7,5},{8,24},{9,11},... | collective-permute-start | bytes 4718600 | tf_op jit(solution)/shard_map/ppermute | solution.py:613
  48.6 16.8 %collective-permute-start.3 = (bf16[128,2048]{1,0:T(8,128)(2,1)S(1)}, bf16[128,2048]{1,0:T(8,128)(2,1)}, u32[]{:S(2)}, u32[]{:S(2)}) collective-permute-start(bf16[128,2048]{1,0:T(8,128)(2,1)S(1)} %constant_dynamic-update-slice_fusion.refs_6_), channel_id=1, source_target_pairs={{0,8},{8,12},{12,4},{4,0},{1,9},{9,13},{13,5},{5,1},{2,10},{10,14}... | collective-permute-start | bytes 1572872 | tf_op jit(solution)/shard_map/ppermute | solution.py:594
  50.2 47.3 %all-to-all-start.1 = ((bf16[16,32,1024]{2,1,0:T(8,128)(2,1)}), bf16[16,32,1024]{2,1,0:T(8,128)(2,1)}, u32[]{:S(2)}, u32[]{:S(2)}) async-start(bf16[16,32,1024]{2,1,0:T(8,128)(2,1)} %bitcast.7), calls=%async_computation.1 | async-start | bytes 2097152 | tf_op jit(solution)/shard_map/all_to_all | solution.py:586
  68.5 25.1 %copy-start.41 = (s32[4,2]{0,1:T(2,128)S(1)}, s32[4,2]{0,1:T(2,128)}, u32[]{:S(2)}) copy-start(s32[4,2]{0,1:T(2,128)} %param.44) | copy-start | bytes 100
  70.7 26.8 %copy-start = (bf16[2,512,1536]{2,1,0:T(8,128)(2,1)}, bf16[2,512,1536]{2,1,0:T(8,128)(2,1)S(1)}, u32[]{:S(2)}) copy-start(bf16[2,512,1536]{2,1,0:T(8,128)(2,1)S(1)} %pad_maximum_fusion.refs_8_.refs_2_.refs_7_.refs_9_.refs_1_) | copy-start | bytes 9437188
  70.7 55.2 %collective-permute-start.6 = (bf16[2,512,1536]{2,1,0:T(8,128)(2,1)S(1)}, bf16[2,512,1536]{2,1,0:T(8,128)(2,1)}, u32[]{:S(2)}, u32[]{:S(2)}) collective-permute-start(bf16[2,512,1536]{2,1,0:T(8,128)(2,1)S(1)} %pad_maximum_fusion.refs_8_.refs_2_.refs_7_.refs_9_.refs_1_), channel_id=1, source_target_pairs={{0,2},{1,17},{2,0},{3,19},{4,6},{5,21},{6,4},{7,23},{8,10},{9,25},... | collective-permute-start | bytes 9437192 | tf_op jit(solution)/shard_map/ppermute | solution.py:613
  71.5 54.4 %collective-permute-start.7 = (bf16[2,512,1536]{2,1,0:T(8,128)(2,1)S(1)}, bf16[2,512,1536]{2,1,0:T(8,128)(2,1)}, u32[]{:S(2)}, u32[]{:S(2)}) collective-permute-start(bf16[2,512,1536]{2,1,0:T(8,128)(2,1)S(1)} %pad_maximum_fusion.refs_8_.refs_2_.refs_7_.refs_9_.refs_1_), channel_id=1, source_target_pairs={{0,1},{1,0},{2,3},{3,2},{4,5},{5,4},{6,7},{7,6},{8,9},{9,8},{10,11... | collective-permute-start | bytes 9437192 | tf_op jit(solution)/shard_map/ppermute | solution.py:589
  76.7 15.3 %collective-permute-start.4 = (bf16[128,2048]{1,0:T(8,128)(2,1)}, bf16[128,2048]{1,0:T(8,128)(2,1)}, u32[]{:S(2)}, u32[]{:S(2)}) collective-permute-start(bf16[128,2048]{1,0:T(8,128)(2,1)} %collective-permute-done.3), channel_id=1, source_target_pairs={{0,8},{8,12},{12,4},{4,0},{1,9},{9,13},{13,5},{5,1},{2,10},{10,14}... | collective-permute-start | bytes 1572872 | tf_op jit(solution)/shard_map/ppermute | solution.py:594
  92.0 21.4 %collective-permute-start.8 = (bf16[128,2048]{1,0:T(8,128)(2,1)}, bf16[128,2048]{1,0:T(8,128)(2,1)}, u32[]{:S(2)}, u32[]{:S(2)}) collective-permute-start(bf16[128,2048]{1,0:T(8,128)(2,1)} %collective-permute-done.4), channel_id=1, source_target_pairs={{0,8},{8,12},{12,4},{4,0},{1,9},{9,13},{13,5},{5,1},{2,10},{10,14}... | collective-permute-start | bytes 1572872 | tf_op jit(solution)/shard_map/ppermute | solution.py:594
  97.5 57.2 %all-to-all-start.2 = ((bf16[16,128,512]{2,1,0:T(8,128)(2,1)}), bf16[16,128,512]{2,1,0:T(8,128)(2,1)}, u32[]{:S(2)}, u32[]{:S(2)}) async-start(bf16[16,128,512]{2,1,0:T(8,128)(2,1)} %bitcast.123), calls=%async_computation.2 | async-start | bytes 4194304 | tf_op jit(solution)/shard_map/all_to_all | solution.py:586
  125.3 33.2 %copy-start.32 = (f32[1,7,8,128]{3,1,2,0:T(8,128)}, f32[1,7,8,128]{3,1,2,0:T(8,128)S(1)}, u32[]{:S(2)}) copy-start(f32[1,7,8,128]{3,1,2,0:T(8,128)S(1)} %copy.93) | copy-start | bytes 86020
  125.9 32.6 %collective-permute-start.9 = (bf16[2,512,1536]{2,1,0:T(8,128)(2,1)}, bf16[2,512,1536]{2,1,0:T(8,128)(2,1)S(1)}, u32[]{:S(2)}, u32[]{:S(2)}) collective-permute-start(bf16[2,512,1536]{2,1,0:T(8,128)(2,1)} %collective-permute-done.6.refs_3_.refs_8_.refs_10_.refs_2_), channel_id=1, source_target_pairs={{0,1},{1,0},{2,3},{3,2},{4,5},{5,4},{6,7},{7,6},{8,9},{9,8},{10,11... | collective-permute-start | bytes 9437192 | tf_op jit(solution)/shard_map/ppermute | solution.py:589
  126.5 49.2 %collective-permute-start.12 = (bf16[512,2048]{1,0:T(8,128)(2,1)}, bf16[512,2048]{1,0:T(8,128)(2,1)}, u32[]{:S(2)}, u32[]{:S(2)}) collective-permute-start(bf16[512,2048]{1,0:T(8,128)(2,1)} %copy-done.4), channel_id=1, source_target_pairs={{0,16},{1,3},{2,18},{3,1},{4,20},{5,7},{6,22},{7,5},{8,24},{9,11},... | collective-permute-start | bytes 6291464 | tf_op jit(solution)/shard_map/ppermute | solution.py:613
  174.9 8.4 %collective-permute-start.10 = (bf16[2,512,768]{2,1,0:T(8,128)(2,1)}, bf16[2,512,768]{2,1,0:T(8,128)(2,1)S(1)}, u32[]{:S(2)}, u32[]{:S(2)}) collective-permute-start(bf16[2,512,768]{2,1,0:T(8,128)(2,1)} %get-tuple-element.684.refs_0_), channel_id=1, source_target_pairs={{0,1},{1,0},{2,3},{3,2},{4,5},{5,4},{6,7},{7,6},{8,9},{9,8},{10,11... | collective-permute-start | bytes 4718600 | tf_op jit(solution)/shard_map/ppermute | solution.py:589
  175.6 7.6 %collective-permute-start.11 = (bf16[2,512,768]{2,1,0:T(8,128)(2,1)}, bf16[2,512,768]{2,1,0:T(8,128)(2,1)S(1)}, u32[]{:S(2)}, u32[]{:S(2)}) collective-permute-start(bf16[2,512,768]{2,1,0:T(8,128)(2,1)} %get-tuple-element.711.refs_0_), channel_id=1, source_target_pairs={{0,1},{1,0},{2,3},{3,2},{4,5},{5,4},{6,7},{7,6},{8,9},{9,8},{10,11... | collective-permute-start | bytes 4718600 | tf_op jit(solution)/shard_map/ppermute | solution.py:589
  178.3 34.1 %collective-permute-start.13 = (bf16[2,512,1024]{2,1,0:T(8,128)(2,1)S(1)}, bf16[2,512,1024]{2,1,0:T(8,128)(2,1)}, u32[]{:S(2)}, u32[]{:S(2)}) collective-permute-start(bf16[2,512,1024]{2,1,0:T(8,128)(2,1)S(1)} %pad_maximum_fusion.2.refs_3_.refs_2_), channel_id=1, source_target_pairs={{0,2},{1,17},{2,0},{3,19},{4,6},{5,21},{6,4},{7,23},{8,10},{9,25},... | collective-permute-start | bytes 6291464 | tf_op jit(solution)/shard_map/ppermute | solution.py:613
  183.2 14.6 %copy-start.2 = (bf16[2,512,1024]{2,1,0:T(8,128)(2,1)S(1)}, bf16[2,512,1024]{2,1,0:T(8,128)(2,1)}, u32[]{:S(2)}) copy-start(bf16[2,512,1024]{2,1,0:T(8,128)(2,1)} %pad_maximum_fusion.3.refs_4_.refs_2_) | copy-start | bytes 6291460
  184.4 13.3 %copy-start.13 = (bf16[2,512,768]{2,1,0:T(8,128)(2,1)}, bf16[2,512,768]{2,1,0:T(8,128)(2,1)S(1)}, u32[]{:S(2)}) copy-start(bf16[2,512,768]{2,1,0:T(8,128)(2,1)S(1)} %collective-permute-done.11.refs_1_) | copy-start | bytes 4718596
  197.7 15.3 %copy-start.33 = (f32[1,7,8,128]{3,1,2,0:T(8,128)S(1)}, f32[1,7,8,128]{3,1,2,0:T(8,128)}, u32[]{:S(2)}) copy-start(f32[1,7,8,128]{3,1,2,0:T(8,128)} %copy-done.32) | copy-start | bytes 86020
  197.7 14.7 %collective-permute-start.14 = (bf16[2,512,1024]{2,1,0:T(8,128)(2,1)}, bf16[2,512,1024]{2,1,0:T(8,128)(2,1)S(1)}, u32[]{:S(2)}, u32[]{:S(2)}) collective-permute-start(bf16[2,512,1024]{2,1,0:T(8,128)(2,1)} %copy-done.3), channel_id=1, source_target_pairs={{0,1},{1,0},{2,3},{3,2},{4,5},{5,4},{6,7},{7,6},{8,9},{9,8},{10,11... | collective-permute-start | bytes 6291464 | tf_op jit(solution)/shard_map/ppermute | solution.py:589
  197.8 30.6 %collective-permute-start.15 = (bf16[2,512,1024]{2,1,0:T(8,128)(2,1)S(1)}, bf16[2,512,1024]{2,1,0:T(8,128)(2,1)}, u32[]{:S(2)}, u32[]{:S(2)}) collective-permute-start(bf16[2,512,1024]{2,1,0:T(8,128)(2,1)S(1)} %copy-done.2), channel_id=1, source_target_pairs={{0,2},{1,17},{2,0},{3,19},{4,6},{5,21},{6,4},{7,23},{8,10},{9,25},... | collective-permute-start | bytes 6291464 | tf_op jit(solution)/shard_map/ppermute | solution.py:613
  212.4 16.0 %collective-permute-start.16 = (bf16[2,512,1024]{2,1,0:T(8,128)(2,1)S(1)}, bf16[2,512,1024]{2,1,0:T(8,128)(2,1)}, u32[]{:S(2)}, u32[]{:S(2)}) collective-permute-start(bf16[2,512,1024]{2,1,0:T(8,128)(2,1)S(1)} %copy-done.2), channel_id=1, source_target_pairs={{0,1},{1,0},{2,3},{3,2},{4,5},{5,4},{6,7},{7,6},{8,9},{9,8},{10,11... | collective-permute-start | bytes 6291464 | tf_op jit(solution)/shard_map/ppermute | solution.py:589
  212.4 15.9 %collective-permute-start.17 = (bf16[2,512,1024]{2,1,0:T(8,128)(2,1)}, bf16[2,512,1024]{2,1,0:T(8,128)(2,1)S(1)}, u32[]{:S(2)}, u32[]{:S(2)}) collective-permute-start(bf16[2,512,1024]{2,1,0:T(8,128)(2,1)} %collective-permute-done.13.refs_3_), channel_id=1, source_target_pairs={{0,1},{1,0},{2,3},{3,2},{4,5},{5,4},{6,7},{7,6},{8,9},{9,8},{10,11... | collective-permute-start | bytes 6291464 | tf_op jit(solution)/shard_map/ppermute | solution.py:589
  228.3 13.2 %collective-permute-start.19 = (bf16[2,512,1024]{2,1,0:T(8,128)(2,1)}, bf16[2,512,1024]{2,1,0:T(8,128)(2,1)S(1)}, u32[]{:S(2)}, u32[]{:S(2)}) collective-permute-start(bf16[2,512,1024]{2,1,0:T(8,128)(2,1)} %collective-permute-done.15.refs_3_), channel_id=1, source_target_pairs={{0,1},{1,0},{2,3},{3,2},{4,5},{5,4},{6,7},{7,6},{8,9},{9,8},{10,11... | collective-permute-start | bytes 6291464 | tf_op jit(solution)/shard_map/ppermute | solution.py:589
  241.0 12.1 %collective-permute-start.18 = (bf16[2,2,512,1024]{3,2,1,0:T(8,128)(2,1)}, bf16[2,2,512,1024]{3,2,1,0:T(8,128)(2,1)}, u32[]{:S(2)}, u32[]{:S(2)}) collective-permute-start(bf16[2,2,512,1024]{3,2,1,0:T(8,128)(2,1)} %get-tuple-element.625), channel_id=1, source_target_pairs={{0,1},{1,0},{2,3},{3,2},{4,5},{5,4},{6,7},{7,6},{8,9},{9,8},{10,11... | collective-permute-start | bytes 12582920 | tf_op jit(solution)/shard_map/ppermute | solution.py:589
  253.1 13.7 %collective-permute-start.20 = (bf16[2,2,512,1024]{3,2,1,0:T(8,128)(2,1)}, bf16[2,2,512,1024]{3,2,1,0:T(8,128)(2,1)S(1)}, u32[]{:S(2)}, u32[]{:S(2)}) collective-permute-start(bf16[2,2,512,1024]{3,2,1,0:T(8,128)(2,1)} %get-tuple-element.644), channel_id=1, source_target_pairs={{0,1},{1,0},{2,3},{3,2},{4,5},{5,4},{6,7},{7,6},{8,9},{9,8},{10,11... | collective-permute-start | bytes 12582920 | tf_op jit(solution)/shard_map/ppermute | solution.py:589
  264.8 33.3 %collective-permute-start.22 = (bf16[2,512,1024]{2,1,0:T(8,128)(2,1)}, bf16[2,512,1024]{2,1,0:T(8,128)(2,1)S(1)}, u32[]{:S(2)}, u32[]{:S(2)}) collective-permute-start(bf16[2,512,1024]{2,1,0:T(8,128)(2,1)} %get-tuple-element.679), channel_id=1, source_target_pairs={{0,2},{1,17},{2,0},{3,19},{4,6},{5,21},{6,4},{7,23},{8,10},{9,25},... | collective-permute-start | bytes 6291464 | tf_op jit(solution)/shard_map/ppermute | solution.py:613
  279.7 50.6 %collective-permute-start.21 = (bf16[2,512,1024]{2,1,0:T(8,128)(2,1)}, bf16[2,512,1024]{2,1,0:T(8,128)(2,1)S(1)}, u32[]{:S(2)}, u32[]{:S(2)}) collective-permute-start(bf16[2,512,1024]{2,1,0:T(8,128)(2,1)} %get-tuple-element.673), channel_id=1, source_target_pairs={{0,2},{1,17},{2,0},{3,19},{4,6},{5,21},{6,4},{7,23},{8,10},{9,25},... | collective-permute-start | bytes 6291464 | tf_op jit(solution)/shard_map/ppermute | solution.py:613
  280.3 17.8 %copy-start.26 = (bf16[2,512,1024]{2,1,0:T(8,128)(2,1)S(1)}, bf16[2,512,1024]{2,1,0:T(8,128)(2,1)}, u32[]{:S(2)}) copy-start(bf16[2,512,1024]{2,1,0:T(8,128)(2,1)} %get-tuple-element.682) | copy-start | bytes 6291460
  300.1 47.6 %collective-permute-start.25 = (bf16[512,1024]{1,0:T(8,128)(2,1)S(1)}, bf16[512,1024]{1,0:T(8,128)(2,1)S(1)}, u32[]{:S(2)}, u32[]{:S(2)}) collective-permute-start(bf16[512,1024]{1,0:T(8,128)(2,1)S(1)} %get-tuple-element.691.refs_7_), channel_id=1, source_target_pairs={{0,16},{1,3},{2,18},{3,1},{4,20},{5,7},{6,22},{7,5},{8,24},{9,11},... | collective-permute-start | bytes 3145736 | tf_op jit(solution)/shard_map/ppermute | solution.py:613
  332.3 15.5 %collective-permute-start.26 = (bf16[512,1024]{1,0:T(8,128)(2,1)S(1)}, bf16[512,1024]{1,0:T(8,128)(2,1)S(1)}, u32[]{:S(2)}, u32[]{:S(2)}) collective-permute-start(bf16[512,1024]{1,0:T(8,128)(2,1)S(1)} %get-tuple-element.719.refs_8_), channel_id=1, source_target_pairs={{0,16},{1,3},{2,18},{3,1},{4,20},{5,7},{6,22},{7,5},{8,24},{9,11},... | collective-permute-start | bytes 3145736 | tf_op jit(solution)/shard_map/ppermute | solution.py:613
  333.3 14.5 %copy-start.7 = (bf16[512,1024]{1,0:T(8,128)(2,1)S(1)}, bf16[512,1024]{1,0:T(8,128)(2,1)}, u32[]{:S(2)}) copy-start(bf16[512,1024]{1,0:T(8,128)(2,1)} %get-tuple-element.730.refs_7_) | copy-start | bytes 3145732
  347.1 3.2 collective-permute-start.24
  361.1 53.7 %collective-permute-start.28 = (bf16[2,2,512,1024]{3,2,1,0:T(8,128)(2,1)}, bf16[2,2,512,1024]{3,2,1,0:T(8,128)(2,1)}, u32[]{:S(2)}, u32[]{:S(2)}) collective-permute-start(bf16[2,2,512,1024]{3,2,1,0:T(8,128)(2,1)} %get-tuple-element.778), channel_id=1, source_target_pairs={{0,1},{1,0},{2,3},{3,2},{4,5},{5,4},{6,7},{7,6},{8,9},{9,8},{10,11... | collective-permute-start | bytes 12582920 | tf_op jit(solution)/shard_map/ppermute | solution.py:589
  361.2 10.5 %collective-permute-start.23 = (bf16[2,512,512]{2,1,0:T(8,128)(2,1)}, bf16[2,512,512]{2,1,0:T(8,128)(2,1)}, u32[]{:S(2)}, u32[]{:S(2)}) collective-permute-start(bf16[2,512,512]{2,1,0:T(8,128)(2,1)} %get-tuple-element.721), channel_id=1, source_target_pairs={{0,1},{1,0},{2,3},{3,2},{4,5},{5,4},{6,7},{7,6},{8,9},{9,8},{10,11... | collective-permute-start | bytes 3145736 | tf_op jit(solution)/shard_map/ppermute | solution.py:589
  361.7 42.7 %all-to-all-start.3 = ((bf16[16,32,1024]{2,1,0:T(8,128)(2,1)}), bf16[16,32,1024]{2,1,0:T(8,128)(2,1)S(1)}, u32[]{:S(2)}, u32[]{:S(2)}) async-start(bf16[16,32,1024]{2,1,0:T(8,128)(2,1)} %bitcast.57), calls=%async_computation.3 | async-start | bytes 2097152 | tf_op jit(solution)/shard_map/all_to_all | solution.py:586
  375.1 15.1 %copy-start.27 = (bf16[128,2048]{1,0:T(8,128)(2,1)S(1)}, bf16[128,2048]{1,0:T(8,128)(2,1)}, u32[]{:S(2)}) copy-start(bf16[128,2048]{1,0:T(8,128)(2,1)} %get-tuple-element.747.refs_12_) | copy-start | bytes 1572868
  389.7 25.2 %collective-permute-start.27 = (bf16[2,2,512,512]{3,2,1,0:T(8,128)(2,1)}, bf16[2,2,512,512]{3,2,1,0:T(8,128)(2,1)}, u32[]{:S(2)}, u32[]{:S(2)}) collective-permute-start(bf16[2,2,512,512]{3,2,1,0:T(8,128)(2,1)} %get-tuple-element.777), channel_id=1, source_target_pairs={{0,1},{1,0},{2,3},{3,2},{4,5},{5,4},{6,7},{7,6},{8,9},{9,8},{10,11... | collective-permute-start | bytes 6291464 | tf_op jit(solution)/shard_map/ppermute | solution.py:589
  390.2 24.6 %collective-permute-start.29 = (bf16[128,2048]{1,0:T(8,128)(2,1)S(1)}, bf16[128,2048]{1,0:T(8,128)(2,1)S(1)}, u32[]{:S(2)}, u32[]{:S(2)}) collective-permute-start(bf16[128,2048]{1,0:T(8,128)(2,1)S(1)} %copy-done.27), channel_id=1, source_target_pairs={{0,4},{8,0},{12,8},{4,12},{1,5},{9,1},{13,9},{5,13},{2,6},{10,2},{... | collective-permute-start | bytes 1572872 | tf_op jit(solution)/shard_map/ppermute | solution.py:594
  405.4 68.0 %all-to-all-start.4 = ((bf16[16,128,512]{2,1,0:T(8,128)(2,1)}), bf16[16,128,512]{2,1,0:T(8,128)(2,1)S(1)}, u32[]{:S(2)}, u32[]{:S(2)}) async-start(bf16[16,128,512]{2,1,0:T(8,128)(2,1)} %bitcast.127), calls=%async_computation.4 | async-start | bytes 4194304 | tf_op jit(solution)/shard_map/all_to_all | solution.py:586
  414.8 15.3 %copy-start.37 = (f32[4,1024]{1,0:T(4,128)S(1)}, f32[4,1024]{1,0:T(4,128)}, u32[]{:S(2)}) copy-start(f32[4,1024]{1,0:T(4,128)} %get-tuple-element.803) | copy-start | bytes 49156
  414.9 15.3 %copy-start.38 = (f32[4,1024]{1,0:T(4,128)S(1)}, f32[4,1024]{1,0:T(4,128)}, u32[]{:S(2)}) copy-start(f32[4,1024]{1,0:T(4,128)} %get-tuple-element.802) | copy-start | bytes 49156
  425.7 44.9 %copy-start.15 = (bf16[128,2048]{1,0:T(8,128)(2,1)S(1)}, bf16[128,2048]{1,0:T(8,128)(2,1)}, u32[]{:S(2)}) copy-start(bf16[128,2048]{1,0:T(8,128)(2,1)} %get-tuple-element.807.refs_10_) | copy-start | bytes 1572868
  425.7 47.6 %collective-permute-start.34 = (bf16[2,512,1536]{2,1,0:T(8,128)(2,1)}, bf16[2,512,1536]{2,1,0:T(8,128)(2,1)}, u32[]{:S(2)}, u32[]{:S(2)}) collective-permute-start(bf16[2,512,1536]{2,1,0:T(8,128)(2,1)} %get-tuple-element.814), channel_id=1, source_target_pairs={{0,2},{1,17},{2,0},{3,19},{4,6},{5,21},{6,4},{7,23},{8,10},{9,25},... | collective-permute-start | bytes 9437192 | tf_op jit(solution)/shard_map/ppermute | solution.py:613
  428.6 41.9 %collective-permute-start.31 = (bf16[128,2048]{1,0:T(8,128)(2,1)}, bf16[128,2048]{1,0:T(8,128)(2,1)S(1)}, u32[]{:S(2)}, u32[]{:S(2)}) collective-permute-start(bf16[128,2048]{1,0:T(8,128)(2,1)} %add_convert_fusion.12), channel_id=1, source_target_pairs={{0,4},{8,0},{12,8},{4,12},{1,5},{9,1},{13,9},{5,13},{2,6},{10,2},{... | collective-permute-start | bytes 1572872 | tf_op jit(solution)/shard_map/ppermute | solution.py:594
  431.4 40.3 %collective-permute-start.30 = (f32[2,4,2,352]{3,2,1,0:T(2,128)S(1)}, f32[2,4,2,352]{3,2,1,0:T(2,128)S(1)}, u32[]{:S(2)}, u32[]{:S(2)}) collective-permute-start(f32[2,4,2,352]{3,2,1,0:T(2,128)S(1)} %bitcast.155), channel_id=1, source_target_pairs={{0,1},{1,0},{2,3},{3,2},{4,5},{5,4},{6,7},{7,6},{8,9},{9,8},{10,11... | collective-permute-start | bytes 67592 | tf_op jit(solution)/shard_map/ppermute | solution.py:589
  471.5 14.8 %collective-permute-start.32 = (bf16[128,2048]{1,0:T(8,128)(2,1)}, bf16[128,2048]{1,0:T(8,128)(2,1)}, u32[]{:S(2)}, u32[]{:S(2)}) collective-permute-start(bf16[128,2048]{1,0:T(8,128)(2,1)} %add_convert_fusion.11), channel_id=1, source_target_pairs={{0,4},{8,0},{12,8},{4,12},{1,5},{9,1},{13,9},{5,13},{2,6},{10,2},{... | collective-permute-start | bytes 1572872 | tf_op jit(solution)/shard_map/ppermute | solution.py:594
  471.8 6.4 %collective-permute-start.33 = (f32[2,4,352]{2,1,0:T(4,128)S(1)}, f32[2,4,352]{2,1,0:T(4,128)S(1)}, u32[]{:S(2)}, u32[]{:S(2)}) collective-permute-start(f32[2,4,352]{2,1,0:T(4,128)S(1)} %bitcast.157), channel_id=1, source_target_pairs={{0,2},{1,3},{2,0},{3,1},{4,6},{5,7},{6,4},{7,5},{8,10},{9,11},{10,... | collective-permute-start | bytes 33800 | tf_op jit(solution)/shard_map/ppermute | solution.py:589
  477.1 20.5 %collective-permute-start.35 = (bf16[512,1536]{1,0:T(8,128)(2,1)S(1)}, bf16[512,1536]{1,0:T(8,128)(2,1)S(1)}, u32[]{:S(2)}, u32[]{:S(2)}) collective-permute-start(bf16[512,1536]{1,0:T(8,128)(2,1)S(1)} %get-tuple-element.915), channel_id=1, source_target_pairs={{0,16},{1,3},{2,18},{3,1},{4,20},{5,7},{6,22},{7,5},{8,24},{9,11},... | collective-permute-start | bytes 4718600 | tf_op jit(solution)/shard_map/ppermute | solution.py:613
  498.1 10.5 %collective-permute-start.36 = (bf16[128,1536]{1,0:T(8,128)(2,1)S(1)}, bf16[128,1536]{1,0:T(8,128)(2,1)S(1)}, u32[]{:S(2)}, u32[]{:S(2)}) collective-permute-start(bf16[128,1536]{1,0:T(8,128)(2,1)S(1)} %get-tuple-element.939), channel_id=1, source_target_pairs={{0,4},{8,0},{12,8},{4,12},{1,5},{9,1},{13,9},{5,13},{2,6},{10,2},{... | collective-permute-start | bytes 1179656 | tf_op jit(solution)/shard_map/ppermute | solution.py:594
  501.7 3.6 collective-permute-start.37
  508.7 14.0 %collective-permute-start.38 = (bf16[128,1536]{1,0:T(8,128)(2,1)S(1)}, bf16[128,1536]{1,0:T(8,128)(2,1)S(1)}, u32[]{:S(2)}, u32[]{:S(2)}) collective-permute-start(bf16[128,1536]{1,0:T(8,128)(2,1)S(1)} %add_convert_fusion.14), channel_id=1, source_target_pairs={{0,4},{8,0},{12,8},{4,12},{1,5},{9,1},{13,9},{5,13},{2,6},{10,2},{... | collective-permute-start | bytes 1179656 | tf_op jit(solution)/shard_map/ppermute | solution.py:594
  517.1 4.5 collective-permute-start.39
  517.2 5.5 %collective-permute-start.40 = (f32[352]{0:T(512)S(1)}, f32[352]{0:T(512)S(1)}, u32[]{:S(2)}, u32[]{:S(2)}) collective-permute-start(f32[352]{0:T(512)S(1)} %get-tuple-element.913), channel_id=1, source_target_pairs={{0,12},{8,4},{12,0},{4,8},{1,13},{9,5},{13,1},{5,9},{2,14},{10,6},... | collective-permute-start | bytes 4232 | tf_op jit(solution)/shard_map/ppermute | solution.py:594
  519.1 3.6 collective-permute-start.41
  522.8 8.7 %collective-permute-start.42 = (bf16[128,1536]{1,0:T(8,128)(2,1)S(1)}, bf16[128,1536]{1,0:T(8,128)(2,1)S(1)}, u32[]{:S(2)}, u32[]{:S(2)}) collective-permute-start(bf16[128,1536]{1,0:T(8,128)(2,1)S(1)} %add_convert_fusion.13), channel_id=1, source_target_pairs={{0,4},{8,0},{12,8},{4,12},{1,5},{9,1},{13,9},{5,13},{2,6},{10,2},{... | collective-permute-start | bytes 1179656 | tf_op jit(solution)/shard_map/ppermute | solution.py:594
  (30 other events, 143.0 us)

commit v7 on v6

--- a/solution.py
+++ b/solution.py
@@ -211,7 +211,7 @@
 
 def up_grad(roles, after, name, left, left_t, weights, k, col, step, extras, outs, more=()):
     parts, rows, _ = weights[0].shape
-    tile = 256
+    tile = 512
     width = extras[0].shape[2]
     per = width // tile
     count = left.shape[0]
@@ -481,7 +481,7 @@
 def weight_grad(roles, after, lefts, rights, parts, k, more=()):
     depth, count = lefts[0].shape
     rows = depth // parts
-    tile = min(256, rows)
+    tile = rows
     per = rows // tile
     cols = sum(r.shape[2] for r in rights)
     own = k == 0

time: 541 us -> 539 us (level)
  no operation moved by 1% of the time
where the time goes in v7:
time: 539 us; the launch traced here: 534 us
  Pallas kernels  194 us (36%)
  waiting for transfers between devices  150 us (28%)
  starting transfers between devices  91.4 us (17%)
  local copies, waits for them, and re-layouts  47.1 us (9%)
  other arithmetic  31 us (6%)
  between operations  16.4 us (3%)
    pallas_call x17, Pallas kernels, apply(): pl.pallas_call(run, grid_spec=pltpu.PrefetchScalarGridSpec(num_scalar_pre...  194 us
    ppermute x15, waiting for transfers between devices, over_ctx(): lax.ppermute(array, 'ctx', [(ring[i], ring[(i + d) % cs]) for i in range(...  77.4 us
    all_to_all x4, starting transfers between devices, to_group(): return lax.all_to_all(array, ('ctx', 'tp'), 0, 0, tiled=True)  33.7 us
    ppermute x15, starting transfers between devices, over_ctx(): lax.ppermute(array, 'ctx', [(ring[i], ring[(i + d) % cs]) for i in range(...  27.7 us
    all_to_all x4, waiting for transfers between devices, to_group(): return lax.all_to_all(array, ('ctx', 'tp'), 0, 0, tiled=True)  27.5 us
    all_to_all x1, waiting for transfers between devices, on_device(): packed = lax.all_to_all(packed, ALL, 0, 0, tiled=True)  26.5 us
    unnamed x115, local copies, waits for them, and re-layouts  17.9 us
    ppermute x11, waiting for transfers between devices, over(): return lax.ppermute(array, ALL, [(i, target(i)) for i in range(devices)])  16.3 us
  transfers between devices with their start and end apart: 48, of which 15 were waited for; matrix products, arithmetic and copies ran while one was open for 11% of the time, Pallas kernels for 35%

profile of v7, /device:TPU:0, one launch (start us, length us, event | category | flops | bytes accessed | tf_op | source)
XLA Modules:
  0.0 534.2 jit_solution(17705242545866499299)
XLA Ops:
  3.8 4.1 collective-permute-start
  11.5 4.5 all-to-all-start
  16.7 1.4 pad_maximum_fusion.1
  18.1 1.5 copy.69
  19.6 26.5 %all-to-all-done = f32[32,1,352]{2,1,0:T(1,128)S(1)} async-done(((f32[32,1,352]{2,1,0:T(1,128)}), f32[32,1,352]{2,1,0:T(1,128)S(1)}, u32[]{:S(2)}, u32[]{:S(2)}) %all-to-all-start) | async-done | bytes 45088 | tf_op jit(solution)/shard_map/all_to_all | solution.py:707
  48.6 1.6 collective-permute-start.3
  50.2 4.3 all-to-all-start.1
  54.5 10.9 %collective-permute-done.3 = bf16[128,2048]{1,0:T(8,128)(2,1)} collective-permute-done((bf16[128,2048]{1,0:T(8,128)(2,1)S(1)}, bf16[128,2048]{1,0:T(8,128)(2,1)}, u32[]{:S(2)}, u32[]{:S(2)}) %collective-permute-start.3) | collective-permute-done | bytes 524320 | tf_op jit(solution)/shard_map/ppermute | solution.py:594
  65.4 3.0 collective-permute-done.5
  68.5 2.2 pad_maximum_fusion.refs_8_.refs_2_.refs_7_.refs_9_.refs_1_
  71.5 5.2 collective-permute-start.7
  82.5 9.5 %collective-permute-done.4 = bf16[128,2048]{1,0:T(8,128)(2,1)} collective-permute-done((bf16[128,2048]{1,0:T(8,128)(2,1)}, bf16[128,2048]{1,0:T(8,128)(2,1)}, u32[]{:S(2)}, u32[]{:S(2)}) %collective-permute-start.4) | collective-permute-done | bytes 524320 | tf_op jit(solution)/shard_map/ppermute | solution.py:594
  95.3 2.2 fusion.refs_1_
  97.5 15.8 %all-to-all-start.2 = ((bf16[16,128,512]{2,1,0:T(8,128)(2,1)}), bf16[16,128,512]{2,1,0:T(8,128)(2,1)}, u32[]{:S(2)}, u32[]{:S(2)}) async-start(bf16[16,128,512]{2,1,0:T(8,128)(2,1)} %bitcast.123), calls=%async_computation.2 | async-start | bytes 4194304 | tf_op jit(solution)/shard_map/all_to_all | solution.py:586
  119.0 5.8 %arrived.1 = (bf16[512,1024]{1,0:T(8,128)(2,1)}, bf16[1024,512]{1,0:T(8,128)(2,1)}, f32[8,128]{1,0:T(8,128)}) custom-call(s32[2]{0:T(128)} %pad_add_fusion.roles_ref, bf16[512,1024]{1,0:T(8,128)(2,1)} %bitcast.8.refs_0_, bf16[1024,1024]{1,0:T(8,128)(2,1)} %fusion.refs_1_, f32[1,1]{1,0:T(1,128)} %bitcast.26.refs_2_, bf16[128,1536]{1,0:T(8,128)(2,1)} %copy-done.23, ...), custom_call_target="tpu_custom_call" | custom-call | flops 1 | bytes 1 | tf_op jit(solution)/shard_map/arrived/pallas_call | solution.py:36
  127.0 27.5 %all-to-all-done.2 = bf16[16,128,512]{2,1,0:T(8,128)(2,1)} async-done(((bf16[16,128,512]{2,1,0:T(8,128)(2,1)}), bf16[16,128,512]{2,1,0:T(8,128)(2,1)}, u32[]{:S(2)}, u32[]{:S(2)}) %all-to-all-start.2) | async-done | bytes 2097184 | tf_op jit(solution)/shard_map/all_to_all | solution.py:586
  154.6 1.7 constant_dynamic-slice_fusion.26
  160.0 14.7 %joined.1 = (f32[512,1024]{1,0:T(8,128)}, bf16[512,1024]{1,0:T(8,128)(2,1)}, bf16[1024,512]{1,0:T(8,128)(2,1)}, bf16[2,512,768]{2,1,0:T(8,128)(2,1)}, bf16[2,512,768]{2,1,0:T(8,128)(2,1)}, /*index=5*/f32[8,128]{1,0:T(8,128)}) custom-call(s32[2]{0:T(128)} %pad_add_fusion.roles_ref, bf16[2,512,512]{2,1,0:T(8,128)(2,1)} %pad_maximum_fusion.8.refs_0_.refs_15_.refs_1_.refs_3_, ...), custom_call_target="tpu_custom_call" | custom-call | flops 1 | bytes 1 | tf_op jit(solution)/shard_map/joined/pallas_call | solution.py:36
  175.6 1.9 slice_bitcast_fusion
  178.2 3.4 collective-permute-start.13
  181.6 1.5 pad_maximum_fusion.3.refs_4_.refs_2_
  184.3 13.3 %attend_forward.2 = (bf16[2,4,1024,512]{3,2,1,0:T(8,128)(2,1)}, bf16[2,512,256]{2,1,0:T(8,128)(2,1)}, f32[8,128]{1,0:T(8,128)}) custom-call(s32[2]{0:T(128)} %pad_add_fusion.roles_ref, bf16[2,512,768]{2,1,0:T(8,128)(2,1)} %get-tuple-element.711.refs_0_, bf16[2,512,768]{2,1,0:T(8,128)(2,1)} %copy-done.14, f32[8,128]{1,0:T(8,128)} %get-tuple-element.581.refs_2_, ...), custom_call_target="tpu_custom_call" | custom-call | flops 1 | bytes 1 | tf_op jit(solution)/shard_map/attend_forward/pallas_call | solution.py:36
  198.5 13.5 %attend_forward.3 = (bf16[2,4,1024,512]{3,2,1,0:T(8,128)(2,1)}, bf16[2,512,256]{2,1,0:T(8,128)(2,1)}, f32[8,128]{1,0:T(8,128)}) custom-call(s32[2]{0:T(128)} %pad_add_fusion.roles_ref, bf16[2,512,768]{2,1,0:T(8,128)(2,1)} %get-tuple-element.684.refs_0_, bf16[2,512,768]{2,1,0:T(8,128)(2,1)} %copy-done.13, f32[8,128]{1,0:T(8,128)} %get-tuple-element.592.refs_2_), custom_call_target="tpu_custom_call" | custom-call | flops 1 | bytes 1 | tf_op jit(solution)/shard_map/attend_forward/pallas_call | solution.py:36
  213.3 7.9 %second.1 = (f32[512,1024]{1,0:T(8,128)}, bf16[512,1024]{1,0:T(8,128)(2,1)}, bf16[1024,512]{1,0:T(8,128)(2,1)}, f32[8,128]{1,0:T(8,128)}) custom-call(s32[2]{0:T(128)} %pad_add_fusion.roles_ref, bf16[2,512,256]{2,1,0:T(8,128)(2,1)} %get-tuple-element.783.refs_0_.refs_3_.refs_5_.refs_7_, bf16[2,512,256]{2,1,0:T(8,128)(2,1)} %get-tuple-element.740.refs_1_.refs_3_, ...), custom_call_target="tpu_custom_call" | custom-call | flops 1 | bytes 1 | tf_op jit(solution)/shard_map/second/pallas_call | solution.py:36
  221.2 7.1 %collective-permute-done.15.refs_3_ = bf16[2,512,1024]{2,1,0:T(8,128)(2,1)} collective-permute-done((bf16[2,512,1024]{2,1,0:T(8,128)(2,1)S(1)}, bf16[2,512,1024]{2,1,0:T(8,128)(2,1)}, u32[]{:S(2)}, u32[]{:S(2)}) %collective-permute-start.15) | collective-permute-done | bytes 2097184 | tf_op jit(solution)/shard_map/ppermute | solution.py:613
  229.6 11.2 %hidden.2 = (bf16[2,512,1024]{2,1,0:T(8,128)(2,1)}, bf16[2,512,1024]{2,1,0:T(8,128)(2,1)}, bf16[2,2,512,1024]{3,2,1,0:T(8,128)(2,1)}, f32[8,128]{1,0:T(8,128)}) custom-call(s32[2]{0:T(128)} %pad_add_fusion.roles_ref, bf16[512,1024]{1,0:T(8,128)(2,1)} %get-tuple-element.636.refs_0_, bf16[1024,512]{1,0:T(8,128)(2,1)} %get-tuple-element.637.refs_1_, ...), custom_call_target="tpu_custom_call" | custom-call | flops 1 | bytes 1 | tf_op jit(solution)/shard_map/hidden/pallas_call | solution.py:36
  242.7 9.8 %hidden_back.2 = (bf16[2,512,1024]{2,1,0:T(8,128)(2,1)}, f32[2,1,1024]{2,1,0:T(1,128)}, bf16[2,2,512,1024]{3,2,1,0:T(8,128)(2,1)}, f32[8,128]{1,0:T(8,128)}) custom-call(s32[2]{0:T(128)} %pad_add_fusion.roles_ref, bf16[512,1024]{1,0:T(8,128)(2,1)} %get-tuple-element.664.refs_0_.refs_7_, bf16[1024,512]{1,0:T(8,128)(2,1)} %get-tuple-element.647.refs_1_, ...), custom_call_target="tpu_custom_call" | custom-call | flops 1 | bytes 1 | tf_op jit(solution)/shard_map/hidden_back/pallas_call | solution.py:36
  252.5 12.3 %hidden.3 = (bf16[2,512,1024]{2,1,0:T(8,128)(2,1)}, bf16[2,512,1024]{2,1,0:T(8,128)(2,1)}, bf16[2,512,1024]{2,1,0:T(8,128)(2,1)}, bf16[2,512,1024]{2,1,0:T(8,128)(2,1)}, f32[8,128]{1,0:T(8,128)}) custom-call(s32[2]{0:T(128)} %pad_add_fusion.roles_ref, bf16[512,1024]{1,0:T(8,128)(2,1)} %get-tuple-element.636.refs_0_, ...), custom_call_target="tpu_custom_call" | custom-call | flops 1 | bytes 1 | tf_op jit(solution)/shard_map/hidden/pallas_call | solution.py:36
  264.8 2.0 collective-permute-start.22
  266.8 2.0 copy-done.18
  268.8 10.4 %hidden_back.3 = (bf16[2,512,1024]{2,1,0:T(8,128)(2,1)}, f32[2,1,1024]{2,1,0:T(1,128)}, bf16[2,512,1024]{2,1,0:T(8,128)(2,1)}, bf16[2,512,1024]{2,1,0:T(8,128)(2,1)}, f32[8,128]{1,0:T(8,128)}) custom-call(s32[2]{0:T(128)} %pad_add_fusion.roles_ref, bf16[512,1024]{1,0:T(8,128)(2,1)} %get-tuple-element.664.refs_0_.refs_7_, ...), custom_call_target="tpu_custom_call" | custom-call | flops 1 | bytes 1 | tf_op jit(solution)/shard_map/hidden_back/pallas_call | solution.py:36
  279.8 17.8 %second_back.1 = (f32[512,1024]{1,0:T(8,128)}, bf16[512,1024]{1,0:T(8,128)(2,1)}, bf16[1024,512]{1,0:T(8,128)(2,1)}, f32[4,1024]{1,0:T(4,128)}, bf16[2,512,256]{...) custom-call(s32[2]{0:T(128)} %pad_add_fusion.roles_ref, ...), custom_call_target="tpu_custom_call" | custom-call | flops 1 | bytes 1 | tf_op jit(solution)/shard_map/second_back/pallas_call | solution.py:36
  297.6 2.1 fusion.4
  300.7 13.9 %attend_backward.2 = (bf16[2,512,768]{2,1,0:T(8,128)(2,1)}, bf16[2,512,512]{2,1,0:T(8,128)(2,1)}, f32[8,128]{1,0:T(8,128)}) custom-call(s32[2]{0:T(128)} %pad_add_fusion.roles_ref, bf16[2,512,768]{2,1,0:T(8,128)(2,1)} %get-tuple-element.684.refs_0_, bf16[2,512,768]{2,1,0:T(8,128)(2,1)} %copy-done.13, bf16[2,4,1024,512]{3,2,1,0:T(8,128)(2,1)} %get-tuple-element.686.refs_2_, ...), custom_call_target="tpu_custom_call" | custom-call | flops 1 | bytes 1 | tf_op jit(solution)/shard_map/attend_backward/pallas_call | solution.py:36
  315.2 10.9 %layer_out.1 = (bf16[512,1024]{1,0:T(8,128)(2,1)}, f32[8,128]{1,0:T(8,128)}) custom-call(s32[2]{0:T(128)} %pad_add_fusion.roles_ref, bf16[2,512,1024]{2,1,0:T(8,128)(2,1)} %get-tuple-element.693.refs_0_, bf16[2,512,1024]{2,1,0:T(8,128)(2,1)} %get-tuple-element.694.refs_1_, bf16[2,512,1024]{2,1,0:T(8,128)(2,1)} %pad_maximum_fusion.3.refs_4_.refs_2_, ...), custom_call_target="tpu_custom_call" | custom-call | flops 1 | bytes 1 | tf_op jit(solution)/shard_map/layer_out/pallas_call | solution.py:36
  326.2 3.6 convolution_convert_fusion.refs_6_
  329.8 2.0 fusion.6
  332.8 14.0 %attend_backward.3 = (bf16[2,512,768]{2,1,0:T(8,128)(2,1)}, bf16[2,512,512]{2,1,0:T(8,128)(2,1)}, f32[8,128]{1,0:T(8,128)}) custom-call(s32[2]{0:T(128)} %pad_add_fusion.roles_ref, bf16[2,512,768]{2,1,0:T(8,128)(2,1)} %get-tuple-element.711.refs_0_, bf16[2,512,768]{2,1,0:T(8,128)(2,1)} %copy-done.14, bf16[2,4,1024,512]{3,2,1,0:T(8,128)(2,1)} %get-tuple-element.713.refs_2_, ...), custom_call_target="tpu_custom_call" | custom-call | flops 1 | bytes 1 | tf_op jit(solution)/shard_map/attend_backward/pallas_call | solution.py:36
  348.5 1.4 pad_maximum_fusion.10
  352.2 7.4 %weight_grad.2 = (bf16[2,2,512,1024]{3,2,1,0:T(8,128)(2,1)}, f32[8,128]{1,0:T(8,128)}) custom-call(s32[2]{0:T(128)} %pad_add_fusion.roles_ref, bf16[1024,512]{1,0:T(8,128)(2,1)} %get-tuple-element.782.refs_0_.refs_2_.refs_4_.refs_6_, bf16[2,512,256]{2,1,0:T(8,128)(2,1)} %get-tuple-element.740.refs_1_.refs_3_, ...), custom_call_target="tpu_custom_call" | custom-call | flops 1 | bytes 1 | tf_op jit(solution)/shard_map/weight_grad/pallas_call | solution.py:36
  360.3 9.4 %all-to-all-start.3 = ((bf16[16,32,1024]{2,1,0:T(8,128)(2,1)}), bf16[16,32,1024]{2,1,0:T(8,128)(2,1)S(1)}, u32[]{:S(2)}, u32[]{:S(2)}) async-start(bf16[16,32,1024]{2,1,0:T(8,128)(2,1)} %bitcast.57), calls=%async_computation.3 | async-start | bytes 2097152 | tf_op jit(solution)/shard_map/all_to_all | solution.py:586
  369.8 1.5 add_convert_fusion.3
  373.1 14.5 %first_back.1 = (bf16[512,1024]{1,0:T(8,128)(2,1)}, bf16[1024,512]{1,0:T(8,128)(2,1)}, f32[4,1024]{1,0:T(4,128)}, bf16[2,2,512,512]{3,2,1,0:T(8,128)(2,1)}, f32[8,128]{1,0:T(8,128)}) custom-call(s32[2]{0:T(128)} %pad_add_fusion.roles_ref, bf16[2,512,768]{2,1,0:T(8,128)(2,1)} %pad_maximum_fusion.7.refs_0_.refs_11_.refs_9_, ...), custom_call_target="tpu_custom_call" | custom-call | flops 1 | bytes 1 | tf_op jit(solution)/shard_map/first_back/pallas_call | solution.py:36
  388.1 5.1 collective-permute-start.29
  393.2 6.6 %inputs_back.1 = (bf16[2,512,512]{2,1,0:T(8,128)(2,1)}, bf16[2,512,512]{2,1,0:T(8,128)(2,1)}, f32[8,128]{1,0:T(8,128)}) custom-call(s32[2]{0:T(128)} %pad_add_fusion.roles_ref, bf16[512,1024]{1,0:T(8,128)(2,1)} %get-tuple-element.768.refs_0_, bf16[2,512,1536]{2,1,0:T(8,128)(2,1)} %copy-done, ...), custom_call_target="tpu_custom_call" | custom-call | flops 1 | bytes 1 | tf_op jit(solution)/shard_map/inputs_back/pallas_call | solution.py:36
  402.1 1.5 copy.72
  404.7 4.2 all-to-all-start.4
  413.5 10.3 %weight_grad.3 = (bf16[2,512,1536]{2,1,0:T(8,128)(2,1)}, bf16[2,512,1536]{2,1,0:T(8,128)(2,1)}, f32[8,128]{1,0:T(8,128)}) custom-call(s32[2]{0:T(128)} %pad_add_fusion.roles_ref, bf16[1024,512]{1,0:T(8,128)(2,1)} %get-tuple-element.780.refs_0_.refs_2_, bf16[2,512,512]{2,1,0:T(8,128)(2,1)} %pad_maximum_fusion.8.refs_0_.refs_15_.refs_1_.refs_3_, ...), custom_call_target="tpu_custom_call" | custom-call | flops 1 | bytes 1 | tf_op jit(solution)/shard_map/weight_grad/pallas_call | solution.py:36
  423.9 2.0 collective-permute-start.34
  426.8 1.5 collective-permute-start.31
  429.7 39.5 %collective-permute-done.31 = bf16[128,2048]{1,0:T(8,128)(2,1)S(1)} collective-permute-done((bf16[128,2048]{1,0:T(8,128)(2,1)}, bf16[128,2048]{1,0:T(8,128)(2,1)S(1)}, u32[]{:S(2)}, u32[]{:S(2)}) %collective-permute-start.31) | collective-permute-done | bytes 524320 | tf_op jit(solution)/shard_map/ppermute | solution.py:594
  470.3 1.6 collective-permute-start.33
  471.8 3.7 fusion.2
  476.7 8.2 %collective-permute-done.32 = bf16[128,2048]{1,0:T(8,128)(2,1)} collective-permute-done((bf16[128,2048]{1,0:T(8,128)(2,1)}, bf16[128,2048]{1,0:T(8,128)(2,1)}, u32[]{:S(2)}, u32[]{:S(2)}) %collective-permute-start.32) | collective-permute-done | bytes 524320 | tf_op jit(solution)/shard_map/ppermute | solution.py:594
  487.4 2.5 fusion.34
  489.9 6.1 %collective-permute-done.35 = bf16[512,1536]{1,0:T(8,128)(2,1)S(1)} collective-permute-done((bf16[512,1536]{1,0:T(8,128)(2,1)S(1)}, bf16[512,1536]{1,0:T(8,128)(2,1)S(1)}, u32[]{:S(2)}, u32[]{:S(2)}) %collective-permute-start.35) | collective-permute-done | bytes 1572896 | tf_op jit(solution)/shard_map/ppermute | solution.py:613
  496.6 3.8 collective-permute-start.36
  501.4 2.6 collective-permute-done.37
  504.0 3.1 collective-permute-done.36
  507.2 2.5 collective-permute-start.38
  515.8 1.7 collective-permute-start.40
  517.5 1.6 collective-permute-start.41
  521.5 2.4 collective-permute-start.42
  526.1 4.1 collective-permute-done.42
  (277 shorter events, 66.3 us)
Async XLA Ops:
  0.6 16.0 %copy-start.31 = (bf16[4,2,256,256]{3,2,1,0:T(8,128)(2,1)S(1)}, bf16[4,2,256,256]{3,2,1,0:T(8,128)(2,1)}, u32[]{:S(2)}) copy-start(bf16[4,2,256,256]{3,2,1,0:T(8,128)(2,1)} %param.30) | copy-start | bytes 3145732
  3.8 42.9 %copy-start.23 = (bf16[128,1536]{1,0:T(8,128)(2,1)}, bf16[128,1536]{1,0:T(8,128)(2,1)S(1)}, u32[]{:S(2)}) copy-start(bf16[128,1536]{1,0:T(8,128)(2,1)S(1)} %pad_maximum_fusion.11.refs_3_) | copy-start | bytes 1179652
  3.8 42.9 %collective-permute-start = (bf16[128,1536]{1,0:T(8,128)(2,1)S(1)}, bf16[128,1536]{1,0:T(8,128)(2,1)S(1)}, u32[]{:S(2)}, u32[]{:S(2)}) collective-permute-start(bf16[128,1536]{1,0:T(8,128)(2,1)S(1)} %pad_maximum_fusion.11.refs_3_), channel_id=1, source_target_pairs={{0,8},{8,12},{12,4},{4,0},{1,9},{9,13},{13,5},{5,1},{2,10},{10,14}... | collective-permute-start | bytes 1179656 | tf_op jit(solution)/shard_map/ppermute | solution.py:594
  7.9 38.8 %collective-permute-start.1 = (bf16[128,1536]{1,0:T(8,128)(2,1)S(1)}, bf16[128,1536]{1,0:T(8,128)(2,1)S(1)}, u32[]{:S(2)}, u32[]{:S(2)}) collective-permute-start(bf16[128,1536]{1,0:T(8,128)(2,1)S(1)} %pad_maximum_fusion.11.refs_3_), channel_id=1, source_target_pairs={{0,12},{8,4},{12,0},{4,8},{1,13},{9,5},{13,1},{5,9},{2,14},{10,6},... | collective-permute-start | bytes 1179656 | tf_op jit(solution)/shard_map/ppermute | solution.py:594
  9.2 37.5 %collective-permute-start.2 = (bf16[128,1536]{1,0:T(8,128)(2,1)S(1)}, bf16[128,1536]{1,0:T(8,128)(2,1)}, u32[]{:S(2)}, u32[]{:S(2)}) collective-permute-start(bf16[128,1536]{1,0:T(8,128)(2,1)S(1)} %pad_maximum_fusion.11.refs_3_), channel_id=1, source_target_pairs={{0,4},{8,0},{12,8},{4,12},{1,5},{9,1},{13,9},{5,13},{2,6},{10,2},{... | collective-permute-start | bytes 1179656 | tf_op jit(solution)/shard_map/ppermute | solution.py:594
  11.5 34.6 %all-to-all-start = ((f32[32,1,352]{2,1,0:T(1,128)}), f32[32,1,352]{2,1,0:T(1,128)S(1)}, u32[]{:S(2)}, u32[]{:S(2)}) async-start(f32[32,1,352]{2,1,0:T(1,128)} %broadcast_in_dim.8), calls=%async_computation | async-start | bytes 98304 | tf_op jit(solution)/shard_map/all_to_all | solution.py:707
  19.6 30.6 %copy-start.24 = (bf16[128,2048]{1,0:T(8,128)(2,1)}, bf16[128,2048]{1,0:T(8,128)(2,1)S(1)}, u32[]{:S(2)}) copy-start(bf16[128,2048]{1,0:T(8,128)(2,1)S(1)} %constant_dynamic-update-slice_fusion.refs_6_) | copy-start | bytes 1572868
  47.9 20.6 %copy-start.12 = (bf16[512,1536]{1,0:T(8,128)(2,1)}, bf16[512,1536]{1,0:T(8,128)(2,1)S(1)}, u32[]{:S(2)}) copy-start(bf16[512,1536]{1,0:T(8,128)(2,1)S(1)} %constant_dynamic-update-slice_fusion.2.refs_7_) | copy-start | bytes 4718596
  47.9 20.6 %collective-permute-start.5 = (bf16[512,1536]{1,0:T(8,128)(2,1)S(1)}, bf16[512,1536]{1,0:T(8,128)(2,1)}, u32[]{:S(2)}, u32[]{:S(2)}) collective-permute-start(bf16[512,1536]{1,0:T(8,128)(2,1)S(1)} %constant_dynamic-update-slice_fusion.2.refs_7_), channel_id=1, source_target_pairs={{0,16},{1,3},{2,18},{3,1},{4,20},{5,7},{6,22},{7,5},{8,24},{9,11},... | collective-permute-start | bytes 4718600 | tf_op jit(solution)/shard_map/ppermute | solution.py:613
  48.6 16.8 %collective-permute-start.3 = (bf16[128,2048]{1,0:T(8,128)(2,1)S(1)}, bf16[128,2048]{1,0:T(8,128)(2,1)}, u32[]{:S(2)}, u32[]{:S(2)}) collective-permute-start(bf16[128,2048]{1,0:T(8,128)(2,1)S(1)} %constant_dynamic-update-slice_fusion.refs_6_), channel_id=1, source_target_pairs={{0,8},{8,12},{12,4},{4,0},{1,9},{9,13},{13,5},{5,1},{2,10},{10,14}... | collective-permute-start | bytes 1572872 | tf_op jit(solution)/shard_map/ppermute | solution.py:594
  50.2 47.3 %all-to-all-start.1 = ((bf16[16,32,1024]{2,1,0:T(8,128)(2,1)}), bf16[16,32,1024]{2,1,0:T(8,128)(2,1)}, u32[]{:S(2)}, u32[]{:S(2)}) async-start(bf16[16,32,1024]{2,1,0:T(8,128)(2,1)} %bitcast.7), calls=%async_computation.1 | async-start | bytes 2097152 | tf_op jit(solution)/shard_map/all_to_all | solution.py:586
  68.5 25.1 %copy-start.41 = (s32[4,2]{0,1:T(2,128)S(1)}, s32[4,2]{0,1:T(2,128)}, u32[]{:S(2)}) copy-start(s32[4,2]{0,1:T(2,128)} %param.44) | copy-start | bytes 100
  70.7 26.8 %copy-start = (bf16[2,512,1536]{2,1,0:T(8,128)(2,1)}, bf16[2,512,1536]{2,1,0:T(8,128)(2,1)S(1)}, u32[]{:S(2)}) copy-start(bf16[2,512,1536]{2,1,0:T(8,128)(2,1)S(1)} %pad_maximum_fusion.refs_8_.refs_2_.refs_7_.refs_9_.refs_1_) | copy-start | bytes 9437188
  70.7 55.1 %collective-permute-start.6 = (bf16[2,512,1536]{2,1,0:T(8,128)(2,1)S(1)}, bf16[2,512,1536]{2,1,0:T(8,128)(2,1)}, u32[]{:S(2)}, u32[]{:S(2)}) collective-permute-start(bf16[2,512,1536]{2,1,0:T(8,128)(2,1)S(1)} %pad_maximum_fusion.refs_8_.refs_2_.refs_7_.refs_9_.refs_1_), channel_id=1, source_target_pairs={{0,2},{1,17},{2,0},{3,19},{4,6},{5,21},{6,4},{7,23},{8,10},{9,25},... | collective-permute-start | bytes 9437192 | tf_op jit(solution)/shard_map/ppermute | solution.py:613
  71.5 54.3 %collective-permute-start.7 = (bf16[2,512,1536]{2,1,0:T(8,128)(2,1)S(1)}, bf16[2,512,1536]{2,1,0:T(8,128)(2,1)}, u32[]{:S(2)}, u32[]{:S(2)}) collective-permute-start(bf16[2,512,1536]{2,1,0:T(8,128)(2,1)S(1)} %pad_maximum_fusion.refs_8_.refs_2_.refs_7_.refs_9_.refs_1_), channel_id=1, source_target_pairs={{0,1},{1,0},{2,3},{3,2},{4,5},{5,4},{6,7},{7,6},{8,9},{9,8},{10,11... | collective-permute-start | bytes 9437192 | tf_op jit(solution)/shard_map/ppermute | solution.py:589
  76.7 15.3 %collective-permute-start.4 = (bf16[128,2048]{1,0:T(8,128)(2,1)}, bf16[128,2048]{1,0:T(8,128)(2,1)}, u32[]{:S(2)}, u32[]{:S(2)}) collective-permute-start(bf16[128,2048]{1,0:T(8,128)(2,1)} %collective-permute-done.3), channel_id=1, source_target_pairs={{0,8},{8,12},{12,4},{4,0},{1,9},{9,13},{13,5},{5,1},{2,10},{10,14}... | collective-permute-start | bytes 1572872 | tf_op jit(solution)/shard_map/ppermute | solution.py:594
  92.0 21.2 %collective-permute-start.8 = (bf16[128,2048]{1,0:T(8,128)(2,1)}, bf16[128,2048]{1,0:T(8,128)(2,1)}, u32[]{:S(2)}, u32[]{:S(2)}) collective-permute-start(bf16[128,2048]{1,0:T(8,128)(2,1)} %collective-permute-done.4), channel_id=1, source_target_pairs={{0,8},{8,12},{12,4},{4,0},{1,9},{9,13},{13,5},{5,1},{2,10},{10,14}... | collective-permute-start | bytes 1572872 | tf_op jit(solution)/shard_map/ppermute | solution.py:594
  97.5 57.1 %all-to-all-start.2 = ((bf16[16,128,512]{2,1,0:T(8,128)(2,1)}), bf16[16,128,512]{2,1,0:T(8,128)(2,1)}, u32[]{:S(2)}, u32[]{:S(2)}) async-start(bf16[16,128,512]{2,1,0:T(8,128)(2,1)} %bitcast.123), calls=%async_computation.2 | async-start | bytes 4194304 | tf_op jit(solution)/shard_map/all_to_all | solution.py:586
  125.2 33.2 %copy-start.32 = (f32[1,7,8,128]{3,1,2,0:T(8,128)}, f32[1,7,8,128]{3,1,2,0:T(8,128)S(1)}, u32[]{:S(2)}) copy-start(f32[1,7,8,128]{3,1,2,0:T(8,128)S(1)} %copy.93) | copy-start | bytes 86020
  125.8 32.6 %collective-permute-start.9 = (bf16[2,512,1536]{2,1,0:T(8,128)(2,1)}, bf16[2,512,1536]{2,1,0:T(8,128)(2,1)S(1)}, u32[]{:S(2)}, u32[]{:S(2)}) collective-permute-start(bf16[2,512,1536]{2,1,0:T(8,128)(2,1)} %collective-permute-done.6.refs_3_.refs_8_.refs_10_.refs_2_), channel_id=1, source_target_pairs={{0,1},{1,0},{2,3},{3,2},{4,5},{5,4},{6,7},{7,6},{8,9},{9,8},{10,11... | collective-permute-start | bytes 9437192 | tf_op jit(solution)/shard_map/ppermute | solution.py:589
  126.4 49.2 %collective-permute-start.12 = (bf16[512,2048]{1,0:T(8,128)(2,1)}, bf16[512,2048]{1,0:T(8,128)(2,1)}, u32[]{:S(2)}, u32[]{:S(2)}) collective-permute-start(bf16[512,2048]{1,0:T(8,128)(2,1)} %copy-done.4), channel_id=1, source_target_pairs={{0,16},{1,3},{2,18},{3,1},{4,20},{5,7},{6,22},{7,5},{8,24},{9,11},... | collective-permute-start | bytes 6291464 | tf_op jit(solution)/shard_map/ppermute | solution.py:613
  174.7 8.4 %collective-permute-start.10 = (bf16[2,512,768]{2,1,0:T(8,128)(2,1)}, bf16[2,512,768]{2,1,0:T(8,128)(2,1)S(1)}, u32[]{:S(2)}, u32[]{:S(2)}) collective-permute-start(bf16[2,512,768]{2,1,0:T(8,128)(2,1)} %get-tuple-element.684.refs_0_), channel_id=1, source_target_pairs={{0,1},{1,0},{2,3},{3,2},{4,5},{5,4},{6,7},{7,6},{8,9},{9,8},{10,11... | collective-permute-start | bytes 4718600 | tf_op jit(solution)/shard_map/ppermute | solution.py:589
  175.5 7.6 %collective-permute-start.11 = (bf16[2,512,768]{2,1,0:T(8,128)(2,1)}, bf16[2,512,768]{2,1,0:T(8,128)(2,1)S(1)}, u32[]{:S(2)}, u32[]{:S(2)}) collective-permute-start(bf16[2,512,768]{2,1,0:T(8,128)(2,1)} %get-tuple-element.711.refs_0_), channel_id=1, source_target_pairs={{0,1},{1,0},{2,3},{3,2},{4,5},{5,4},{6,7},{7,6},{8,9},{9,8},{10,11... | collective-permute-start | bytes 4718600 | tf_op jit(solution)/shard_map/ppermute | solution.py:589
  178.2 33.8 %collective-permute-start.13 = (bf16[2,512,1024]{2,1,0:T(8,128)(2,1)S(1)}, bf16[2,512,1024]{2,1,0:T(8,128)(2,1)}, u32[]{:S(2)}, u32[]{:S(2)}) collective-permute-start(bf16[2,512,1024]{2,1,0:T(8,128)(2,1)S(1)} %pad_maximum_fusion.2.refs_3_.refs_2_), channel_id=1, source_target_pairs={{0,2},{1,17},{2,0},{3,19},{4,6},{5,21},{6,4},{7,23},{8,10},{9,25},... | collective-permute-start | bytes 6291464 | tf_op jit(solution)/shard_map/ppermute | solution.py:613
  183.1 14.6 %copy-start.2 = (bf16[2,512,1024]{2,1,0:T(8,128)(2,1)S(1)}, bf16[2,512,1024]{2,1,0:T(8,128)(2,1)}, u32[]{:S(2)}) copy-start(bf16[2,512,1024]{2,1,0:T(8,128)(2,1)} %pad_maximum_fusion.3.refs_4_.refs_2_) | copy-start | bytes 6291460
  184.3 13.3 %copy-start.13 = (bf16[2,512,768]{2,1,0:T(8,128)(2,1)}, bf16[2,512,768]{2,1,0:T(8,128)(2,1)S(1)}, u32[]{:S(2)}) copy-start(bf16[2,512,768]{2,1,0:T(8,128)(2,1)S(1)} %collective-permute-done.11.refs_1_) | copy-start | bytes 4718596
  197.6 15.0 %copy-start.33 = (f32[1,7,8,128]{3,1,2,0:T(8,128)S(1)}, f32[1,7,8,128]{3,1,2,0:T(8,128)}, u32[]{:S(2)}) copy-start(f32[1,7,8,128]{3,1,2,0:T(8,128)} %copy-done.32) | copy-start | bytes 86020
  197.6 14.4 %collective-permute-start.14 = (bf16[2,512,1024]{2,1,0:T(8,128)(2,1)}, bf16[2,512,1024]{2,1,0:T(8,128)(2,1)S(1)}, u32[]{:S(2)}, u32[]{:S(2)}) collective-permute-start(bf16[2,512,1024]{2,1,0:T(8,128)(2,1)} %copy-done.3), channel_id=1, source_target_pairs={{0,1},{1,0},{2,3},{3,2},{4,5},{5,4},{6,7},{7,6},{8,9},{9,8},{10,11... | collective-permute-start | bytes 6291464 | tf_op jit(solution)/shard_map/ppermute | solution.py:589
  197.7 30.6 %collective-permute-start.15 = (bf16[2,512,1024]{2,1,0:T(8,128)(2,1)S(1)}, bf16[2,512,1024]{2,1,0:T(8,128)(2,1)}, u32[]{:S(2)}, u32[]{:S(2)}) collective-permute-start(bf16[2,512,1024]{2,1,0:T(8,128)(2,1)S(1)} %copy-done.2), channel_id=1, source_target_pairs={{0,2},{1,17},{2,0},{3,19},{4,6},{5,21},{6,4},{7,23},{8,10},{9,25},... | collective-permute-start | bytes 6291464 | tf_op jit(solution)/shard_map/ppermute | solution.py:613
  211.9 16.3 %collective-permute-start.16 = (bf16[2,512,1024]{2,1,0:T(8,128)(2,1)S(1)}, bf16[2,512,1024]{2,1,0:T(8,128)(2,1)}, u32[]{:S(2)}, u32[]{:S(2)}) collective-permute-start(bf16[2,512,1024]{2,1,0:T(8,128)(2,1)S(1)} %copy-done.2), channel_id=1, source_target_pairs={{0,1},{1,0},{2,3},{3,2},{4,5},{5,4},{6,7},{7,6},{8,9},{9,8},{10,11... | collective-permute-start | bytes 6291464 | tf_op jit(solution)/shard_map/ppermute | solution.py:589
  212.0 16.2 %collective-permute-start.17 = (bf16[2,512,1024]{2,1,0:T(8,128)(2,1)}, bf16[2,512,1024]{2,1,0:T(8,128)(2,1)S(1)}, u32[]{:S(2)}, u32[]{:S(2)}) collective-permute-start(bf16[2,512,1024]{2,1,0:T(8,128)(2,1)} %collective-permute-done.13.refs_3_), channel_id=1, source_target_pairs={{0,1},{1,0},{2,3},{3,2},{4,5},{5,4},{6,7},{7,6},{8,9},{9,8},{10,11... | collective-permute-start | bytes 6291464 | tf_op jit(solution)/shard_map/ppermute | solution.py:589
  228.2 13.1 %collective-permute-start.19 = (bf16[2,512,1024]{2,1,0:T(8,128)(2,1)}, bf16[2,512,1024]{2,1,0:T(8,128)(2,1)S(1)}, u32[]{:S(2)}, u32[]{:S(2)}) collective-permute-start(bf16[2,512,1024]{2,1,0:T(8,128)(2,1)} %collective-permute-done.15.refs_3_), channel_id=1, source_target_pairs={{0,1},{1,0},{2,3},{3,2},{4,5},{5,4},{6,7},{7,6},{8,9},{9,8},{10,11... | collective-permute-start | bytes 6291464 | tf_op jit(solution)/shard_map/ppermute | solution.py:589
  240.8 11.7 %collective-permute-start.18 = (bf16[2,2,512,1024]{3,2,1,0:T(8,128)(2,1)}, bf16[2,2,512,1024]{3,2,1,0:T(8,128)(2,1)}, u32[]{:S(2)}, u32[]{:S(2)}) collective-permute-start(bf16[2,2,512,1024]{3,2,1,0:T(8,128)(2,1)} %get-tuple-element.625), channel_id=1, source_target_pairs={{0,1},{1,0},{2,3},{3,2},{4,5},{5,4},{6,7},{7,6},{8,9},{9,8},{10,11... | collective-permute-start | bytes 12582920 | tf_op jit(solution)/shard_map/ppermute | solution.py:589
  252.5 14.3 %collective-permute-start.20 = (bf16[2,2,512,1024]{3,2,1,0:T(8,128)(2,1)}, bf16[2,2,512,1024]{3,2,1,0:T(8,128)(2,1)S(1)}, u32[]{:S(2)}, u32[]{:S(2)}) collective-permute-start(bf16[2,2,512,1024]{3,2,1,0:T(8,128)(2,1)} %get-tuple-element.644), channel_id=1, source_target_pairs={{0,1},{1,0},{2,3},{3,2},{4,5},{5,4},{6,7},{7,6},{8,9},{9,8},{10,11... | collective-permute-start | bytes 12582920 | tf_op jit(solution)/shard_map/ppermute | solution.py:589
  264.8 32.8 %collective-permute-start.22 = (bf16[2,512,1024]{2,1,0:T(8,128)(2,1)}, bf16[2,512,1024]{2,1,0:T(8,128)(2,1)S(1)}, u32[]{:S(2)}, u32[]{:S(2)}) collective-permute-start(bf16[2,512,1024]{2,1,0:T(8,128)(2,1)} %get-tuple-element.679), channel_id=1, source_target_pairs={{0,2},{1,17},{2,0},{3,19},{4,6},{5,21},{6,4},{7,23},{8,10},{9,25},... | collective-permute-start | bytes 6291464 | tf_op jit(solution)/shard_map/ppermute | solution.py:613
  279.2 50.6 %collective-permute-start.21 = (bf16[2,512,1024]{2,1,0:T(8,128)(2,1)}, bf16[2,512,1024]{2,1,0:T(8,128)(2,1)S(1)}, u32[]{:S(2)}, u32[]{:S(2)}) collective-permute-start(bf16[2,512,1024]{2,1,0:T(8,128)(2,1)} %get-tuple-element.673), channel_id=1, source_target_pairs={{0,2},{1,17},{2,0},{3,19},{4,6},{5,21},{6,4},{7,23},{8,10},{9,25},... | collective-permute-start | bytes 6291464 | tf_op jit(solution)/shard_map/ppermute | solution.py:613
  279.8 17.8 %copy-start.26 = (bf16[2,512,1024]{2,1,0:T(8,128)(2,1)S(1)}, bf16[2,512,1024]{2,1,0:T(8,128)(2,1)}, u32[]{:S(2)}) copy-start(bf16[2,512,1024]{2,1,0:T(8,128)(2,1)} %get-tuple-element.682) | copy-start | bytes 6291460
  299.7 47.8 %collective-permute-start.25 = (bf16[512,1024]{1,0:T(8,128)(2,1)S(1)}, bf16[512,1024]{1,0:T(8,128)(2,1)S(1)}, u32[]{:S(2)}, u32[]{:S(2)}) collective-permute-start(bf16[512,1024]{1,0:T(8,128)(2,1)S(1)} %get-tuple-element.691.refs_7_), channel_id=1, source_target_pairs={{0,16},{1,3},{2,18},{3,1},{4,20},{5,7},{6,22},{7,5},{8,24},{9,11},... | collective-permute-start | bytes 3145736 | tf_op jit(solution)/shard_map/ppermute | solution.py:613
  331.8 15.7 %collective-permute-start.26 = (bf16[512,1024]{1,0:T(8,128)(2,1)S(1)}, bf16[512,1024]{1,0:T(8,128)(2,1)S(1)}, u32[]{:S(2)}, u32[]{:S(2)}) collective-permute-start(bf16[512,1024]{1,0:T(8,128)(2,1)S(1)} %get-tuple-element.719.refs_8_), channel_id=1, source_target_pairs={{0,16},{1,3},{2,18},{3,1},{4,20},{5,7},{6,22},{7,5},{8,24},{9,11},... | collective-permute-start | bytes 3145736 | tf_op jit(solution)/shard_map/ppermute | solution.py:613
  332.8 14.7 %copy-start.7 = (bf16[512,1024]{1,0:T(8,128)(2,1)S(1)}, bf16[512,1024]{1,0:T(8,128)(2,1)}, u32[]{:S(2)}) copy-start(bf16[512,1024]{1,0:T(8,128)(2,1)} %get-tuple-element.730.refs_7_) | copy-start | bytes 3145732
  346.8 3.2 collective-permute-start.24
  359.5 53.9 %collective-permute-start.28 = (bf16[2,2,512,1024]{3,2,1,0:T(8,128)(2,1)}, bf16[2,2,512,1024]{3,2,1,0:T(8,128)(2,1)}, u32[]{:S(2)}, u32[]{:S(2)}) collective-permute-start(bf16[2,2,512,1024]{3,2,1,0:T(8,128)(2,1)} %get-tuple-element.778), channel_id=1, source_target_pairs={{0,1},{1,0},{2,3},{3,2},{4,5},{5,4},{6,7},{7,6},{8,9},{9,8},{10,11... | collective-permute-start | bytes 12582920 | tf_op jit(solution)/shard_map/ppermute | solution.py:589
  360.3 9.5 %collective-permute-start.23 = (bf16[2,512,512]{2,1,0:T(8,128)(2,1)}, bf16[2,512,512]{2,1,0:T(8,128)(2,1)}, u32[]{:S(2)}, u32[]{:S(2)}) collective-permute-start(bf16[2,512,512]{2,1,0:T(8,128)(2,1)} %get-tuple-element.721), channel_id=1, source_target_pairs={{0,1},{1,0},{2,3},{3,2},{4,5},{5,4},{6,7},{7,6},{8,9},{9,8},{10,11... | collective-permute-start | bytes 3145736 | tf_op jit(solution)/shard_map/ppermute | solution.py:589
  360.3 43.3 %all-to-all-start.3 = ((bf16[16,32,1024]{2,1,0:T(8,128)(2,1)}), bf16[16,32,1024]{2,1,0:T(8,128)(2,1)S(1)}, u32[]{:S(2)}, u32[]{:S(2)}) async-start(bf16[16,32,1024]{2,1,0:T(8,128)(2,1)} %bitcast.57), calls=%async_computation.3 | async-start | bytes 2097152 | tf_op jit(solution)/shard_map/all_to_all | solution.py:586
  373.1 15.0 %copy-start.27 = (bf16[128,2048]{1,0:T(8,128)(2,1)S(1)}, bf16[128,2048]{1,0:T(8,128)(2,1)}, u32[]{:S(2)}) copy-start(bf16[128,2048]{1,0:T(8,128)(2,1)} %get-tuple-element.747.refs_12_) | copy-start | bytes 1572868
  387.7 25.8 %collective-permute-start.27 = (bf16[2,2,512,512]{3,2,1,0:T(8,128)(2,1)}, bf16[2,2,512,512]{3,2,1,0:T(8,128)(2,1)}, u32[]{:S(2)}, u32[]{:S(2)}) collective-permute-start(bf16[2,2,512,512]{3,2,1,0:T(8,128)(2,1)} %get-tuple-element.777), channel_id=1, source_target_pairs={{0,1},{1,0},{2,3},{3,2},{4,5},{5,4},{6,7},{7,6},{8,9},{9,8},{10,11... | collective-permute-start | bytes 6291464 | tf_op jit(solution)/shard_map/ppermute | solution.py:589
  388.1 25.3 %collective-permute-start.29 = (bf16[128,2048]{1,0:T(8,128)(2,1)S(1)}, bf16[128,2048]{1,0:T(8,128)(2,1)S(1)}, u32[]{:S(2)}, u32[]{:S(2)}) collective-permute-start(bf16[128,2048]{1,0:T(8,128)(2,1)S(1)} %copy-done.27), channel_id=1, source_target_pairs={{0,4},{8,0},{12,8},{4,12},{1,5},{9,1},{13,9},{5,13},{2,6},{10,2},{... | collective-permute-start | bytes 1572872 | tf_op jit(solution)/shard_map/ppermute | solution.py:594
  404.7 67.2 %all-to-all-start.4 = ((bf16[16,128,512]{2,1,0:T(8,128)(2,1)}), bf16[16,128,512]{2,1,0:T(8,128)(2,1)S(1)}, u32[]{:S(2)}, u32[]{:S(2)}) async-start(bf16[16,128,512]{2,1,0:T(8,128)(2,1)} %bitcast.127), calls=%async_computation.4 | async-start | bytes 4194304 | tf_op jit(solution)/shard_map/all_to_all | solution.py:586
  413.5 14.8 %copy-start.37 = (f32[4,1024]{1,0:T(4,128)S(1)}, f32[4,1024]{1,0:T(4,128)}, u32[]{:S(2)}) copy-start(f32[4,1024]{1,0:T(4,128)} %get-tuple-element.803) | copy-start | bytes 49156
  413.5 14.8 %copy-start.38 = (f32[4,1024]{1,0:T(4,128)S(1)}, f32[4,1024]{1,0:T(4,128)}, u32[]{:S(2)}) copy-start(f32[4,1024]{1,0:T(4,128)} %get-tuple-element.802) | copy-start | bytes 49156
  423.9 45.4 %copy-start.15 = (bf16[128,2048]{1,0:T(8,128)(2,1)S(1)}, bf16[128,2048]{1,0:T(8,128)(2,1)}, u32[]{:S(2)}) copy-start(bf16[128,2048]{1,0:T(8,128)(2,1)} %get-tuple-element.807.refs_10_) | copy-start | bytes 1572868
  423.9 48.0 %collective-permute-start.34 = (bf16[2,512,1536]{2,1,0:T(8,128)(2,1)}, bf16[2,512,1536]{2,1,0:T(8,128)(2,1)}, u32[]{:S(2)}, u32[]{:S(2)}) collective-permute-start(bf16[2,512,1536]{2,1,0:T(8,128)(2,1)} %get-tuple-element.814), channel_id=1, source_target_pairs={{0,2},{1,17},{2,0},{3,19},{4,6},{5,21},{6,4},{7,23},{8,10},{9,25},... | collective-permute-start | bytes 9437192 | tf_op jit(solution)/shard_map/ppermute | solution.py:613
  426.8 42.4 %collective-permute-start.31 = (bf16[128,2048]{1,0:T(8,128)(2,1)}, bf16[128,2048]{1,0:T(8,128)(2,1)S(1)}, u32[]{:S(2)}, u32[]{:S(2)}) collective-permute-start(bf16[128,2048]{1,0:T(8,128)(2,1)} %add_convert_fusion.12), channel_id=1, source_target_pairs={{0,4},{8,0},{12,8},{4,12},{1,5},{9,1},{13,9},{5,13},{2,6},{10,2},{... | collective-permute-start | bytes 1572872 | tf_op jit(solution)/shard_map/ppermute | solution.py:594
  429.6 40.6 %collective-permute-start.30 = (f32[2,4,2,352]{3,2,1,0:T(2,128)S(1)}, f32[2,4,2,352]{3,2,1,0:T(2,128)S(1)}, u32[]{:S(2)}, u32[]{:S(2)}) collective-permute-start(f32[2,4,2,352]{3,2,1,0:T(2,128)S(1)} %bitcast.155), channel_id=1, source_target_pairs={{0,1},{1,0},{2,3},{3,2},{4,5},{5,4},{6,7},{7,6},{8,9},{9,8},{10,11... | collective-permute-start | bytes 67592 | tf_op jit(solution)/shard_map/ppermute | solution.py:589
  470.2 14.7 %collective-permute-start.32 = (bf16[128,2048]{1,0:T(8,128)(2,1)}, bf16[128,2048]{1,0:T(8,128)(2,1)}, u32[]{:S(2)}, u32[]{:S(2)}) collective-permute-start(bf16[128,2048]{1,0:T(8,128)(2,1)} %add_convert_fusion.11), channel_id=1, source_target_pairs={{0,4},{8,0},{12,8},{4,12},{1,5},{9,1},{13,9},{5,13},{2,6},{10,2},{... | collective-permute-start | bytes 1572872 | tf_op jit(solution)/shard_map/ppermute | solution.py:594
  470.3 6.4 %collective-permute-start.33 = (f32[2,4,352]{2,1,0:T(4,128)S(1)}, f32[2,4,352]{2,1,0:T(4,128)S(1)}, u32[]{:S(2)}, u32[]{:S(2)}) collective-permute-start(f32[2,4,352]{2,1,0:T(4,128)S(1)} %bitcast.157), channel_id=1, source_target_pairs={{0,2},{1,3},{2,0},{3,1},{4,6},{5,7},{6,4},{7,5},{8,10},{9,11},{10,... | collective-permute-start | bytes 33800 | tf_op jit(solution)/shard_map/ppermute | solution.py:589
  475.6 20.5 %collective-permute-start.35 = (bf16[512,1536]{1,0:T(8,128)(2,1)S(1)}, bf16[512,1536]{1,0:T(8,128)(2,1)S(1)}, u32[]{:S(2)}, u32[]{:S(2)}) collective-permute-start(bf16[512,1536]{1,0:T(8,128)(2,1)S(1)} %get-tuple-element.915), channel_id=1, source_target_pairs={{0,16},{1,3},{2,18},{3,1},{4,20},{5,7},{6,22},{7,5},{8,24},{9,11},... | collective-permute-start | bytes 4718600 | tf_op jit(solution)/shard_map/ppermute | solution.py:613
  496.6 10.5 %collective-permute-start.36 = (bf16[128,1536]{1,0:T(8,128)(2,1)S(1)}, bf16[128,1536]{1,0:T(8,128)(2,1)S(1)}, u32[]{:S(2)}, u32[]{:S(2)}) collective-permute-start(bf16[128,1536]{1,0:T(8,128)(2,1)S(1)} %get-tuple-element.939), channel_id=1, source_target_pairs={{0,4},{8,0},{12,8},{4,12},{1,5},{9,1},{13,9},{5,13},{2,6},{10,2},{... | collective-permute-start | bytes 1179656 | tf_op jit(solution)/shard_map/ppermute | solution.py:594
  500.4 3.6 collective-permute-start.37
  507.2 14.2 %collective-permute-start.38 = (bf16[128,1536]{1,0:T(8,128)(2,1)S(1)}, bf16[128,1536]{1,0:T(8,128)(2,1)S(1)}, u32[]{:S(2)}, u32[]{:S(2)}) collective-permute-start(bf16[128,1536]{1,0:T(8,128)(2,1)S(1)} %add_convert_fusion.14), channel_id=1, source_target_pairs={{0,4},{8,0},{12,8},{4,12},{1,5},{9,1},{13,9},{5,13},{2,6},{10,2},{... | collective-permute-start | bytes 1179656 | tf_op jit(solution)/shard_map/ppermute | solution.py:594
  515.6 4.6 collective-permute-start.39
  515.8 5.5 %collective-permute-start.40 = (f32[352]{0:T(512)S(1)}, f32[352]{0:T(512)S(1)}, u32[]{:S(2)}, u32[]{:S(2)}) collective-permute-start(f32[352]{0:T(512)S(1)} %get-tuple-element.913), channel_id=1, source_target_pairs={{0,12},{8,4},{12,0},{4,8},{1,13},{9,5},{13,1},{5,9},{2,14},{10,6},... | collective-permute-start | bytes 4232 | tf_op jit(solution)/shard_map/ppermute | solution.py:594
  517.5 3.8 collective-permute-start.41
  521.5 8.7 %collective-permute-start.42 = (bf16[128,1536]{1,0:T(8,128)(2,1)S(1)}, bf16[128,1536]{1,0:T(8,128)(2,1)S(1)}, u32[]{:S(2)}, u32[]{:S(2)}) collective-permute-start(bf16[128,1536]{1,0:T(8,128)(2,1)S(1)} %add_convert_fusion.13), channel_id=1, source_target_pairs={{0,4},{8,0},{12,8},{4,12},{1,5},{9,1},{13,9},{5,13},{2,6},{10,2},{... | collective-permute-start | bytes 1179656 | tf_op jit(solution)/shard_map/ppermute | solution.py:594
  (30 other events, 141.3 us)
